TPU v7x, 256 devices: a whole 4x4x8 slice. The times are simulated.
256 devices in a mesh: child: 2 (over y_hi), row: 32 (over z, y_lo, core), col: 4 (over x).
Axes of the slice: x: 4, y: 4 (y_hi: 2, y_lo: 2; y = y_hi * 2 + y_lo), z: 8, core: 2. Of those that a mesh axis runs over, the one named last changes fastest.
Arguments:
- front: bfloat16 [131072, 2048], P(('row', 'child'), 'col'), as said below
- left_factors: bfloat16 [2, 4, 64, 131072], P('child', 'col', None, 'row'), may hold values from -2.5 to 2.5
- right_factors: bfloat16 [2, 256, 64, 2048], P('child', 'row', None, 'col'), may hold values from -2.5 to 2.5
Outputs:
- panel_t: bfloat16 [2048, 131072], P('col', ('row', 'child'))
Inputs may be any that keep to these rules, and one draw needn't show every extreme that they name: The first 2048 rows of front make the symmetric part of the assembled diagonal block positive definite: its diagonal entries exceed the spectral norm of the rest of that part several times.
All inputs are finite; a program needn't handle non-finite values.
Results may differ from a plain program's by a relative error of at most 0.012.
Values may be sent and summed in bfloat16 or wider, within the bound.
No kernel may reach another device: no remote copies, remote signals or barrier semaphores. Data moves between devices by JAX's collectives and lax.ppermute only.
A program may use at most 128 MiB of HBM per device.

v0:
```python
import jax
import jax.numpy as jnp
from jax import lax
from jax.sharding import PartitionSpec as P

TILE = 512
RANK = 64
PW = 2048


def shortened(array):

    def short(part):
        return part.astype(jnp.bfloat16) if part.dtype == jnp.float32 else part

    return jax.tree.map(short, array)


def spread(value, axis, source):
    kept = jnp.where(lax.axis_index(axis) == source, value, 0).astype(value.dtype)
    return lax.psum(kept, axis)


def product_high(left, right):
    return jnp.dot(left, right, precision=lax.Precision.HIGHEST)


def inverse_transpose(top):
    blocks = PW // TILE
    identity = jnp.eye(TILE, dtype=jnp.float32)

    def tile_of(i, j):
        return top[i * TILE : (i + 1) * TILE, j * TILE : (j + 1) * TILE].astype(jnp.float32)

    def sym_tile(i, j):
        return 0.5 * (tile_of(i, j) + tile_of(j, i).T)

    lower = {}
    diag_inv = {}
    for j in range(blocks):
        accum = sym_tile(j, j)
        for k in range(j):
            accum = accum - product_high(lower[j, k], lower[j, k].T)
        lower[j, j] = jnp.linalg.cholesky(accum)
        diag_inv[j] = lax.linalg.triangular_solve(lower[j, j], identity, left_side=True, lower=True)
        for i in range(j + 1, blocks):
            accum = sym_tile(i, j)
            for k in range(j):
                accum = accum - product_high(lower[i, k], lower[j, k].T)
            lower[i, j] = product_high(accum, diag_inv[j].T)
    pieces = {}
    for i in range(blocks):
        pieces[i, i] = diag_inv[i]
    for i in range(blocks):
        for j in range(i):
            acc = jnp.zeros((TILE, TILE), jnp.float32)
            for k in range(j, i):
                acc = acc + product_high(lower[i, k], pieces[k, j])
            pieces[i, j] = -product_high(pieces[i, i], acc)
    zero_tile = jnp.zeros((TILE, TILE), jnp.bfloat16)
    row_list = [
        jnp.concatenate(
            [pieces[b, a].T.astype(jnp.bfloat16) if a <= b else zero_tile for b in range(blocks)],
            axis=1,
        )
        for a in range(blocks)
    ]
    return jnp.concatenate(row_list, axis=0)


def child_term(left_part, right_part):
    left_tiles = left_part.reshape(RANK, right_part.shape[0], TILE)
    result = jnp.einsum("rtk,trn->tkn", left_tiles, right_part, preferred_element_type=jnp.float32)
    return result.reshape(-1, TILE)


def shards(front, left_factors, right_factors):
    side = lax.axis_index("child")
    left_all = left_factors[0, 0]
    right_all = right_factors[0]
    update = lax.psum_scatter(
        child_term(left_all, right_all).astype(jnp.bfloat16),
        "child",
        scatter_dimension=0,
        tiled=True,
    ).astype(jnp.float32)
    panel_rows = (front.astype(jnp.float32) - update).astype(jnp.bfloat16)
    column = lax.axis_index("col")
    is_root = jnp.logical_and(side == 0, lax.axis_index("row") == 0)
    top = lax.all_gather(panel_rows[:PW], "col", axis=1, tiled=True)

    def select_block(matrix):
        return lax.dynamic_slice_in_dim(matrix, column * TILE, TILE, 0)

    empty_shape = (TILE, PW)
    local_block = lax.cond(
        is_root,
        lambda t: select_block(inverse_transpose(t)),
        lambda t: jnp.zeros(empty_shape, jnp.bfloat16),
        top,
    )
    inverse_block = jax.tree.map(
        lambda part, own: part.astype(own.dtype),
        jax.tree.map(lambda part: spread(part, ("child", "row"), 0), shortened(local_block)),
        local_block,
    )
    part = lax.slice_in_dim(inverse_block, 0, lax.axis_size("col") * TILE, axis=1)
    panel_t = lax.psum_scatter(
        lax.dot_general(
            part, panel_rows, (((0,), (1,)), ((), ())), preferred_element_type=jnp.float32
        ),
        "col",
        scatter_dimension=0,
        tiled=True,
    )
    return panel_t.astype(jnp.bfloat16)


def solution(mesh):
    in_specs = (
        P(("row", "child"), "col"),
        P("child", "col", None, "row"),
        P("child", "row", None, "col"),
    )
    out_specs = P("col", ("row", "child"))
    return jax.shard_map(shards, mesh=mesh, in_specs=in_specs, out_specs=out_specs, check_vma=False)
```

profile of v0, /device:TPU:7, one launch (start us, length us, event | category | flops | bytes accessed | tf_op | source)
XLA Modules:
  0.0 1285.8 jit_solution(6734739488787908376)
XLA Ops:
  6.5 0.0 copy-start
  6.5 0.0 reduce-scatter.3.cloned.1.call-start
  6.5 1.3 copy.31
  7.8 0.0 copy-done
  7.8 0.0 copy-start.46
  7.8 3.2 convolution_convert_fusion
  11.1 0.0 reduce-scatter.3.cloned.1.call-update
  11.1 0.0 all-gather.2.cloned.1.call-start
  11.1 63.9 %reduce-scatter.3.cloned.1.call-done = bf16[2048,512]{1,0:T(8,128)(2,1)} async-done(((bf16[4096,512]{1,0:T(8,128)(2,1)}), bf16[2048,512]{1,0:T(8,128)(2,1)}) %reduce-scatter.3.cloned.1.call-update) | async-done | bytes 2097168 | tf_op jit(solution)/shard_map/reduce_scatter | solution.py:81
  75.1 0.0 copy-done.46
  75.1 3.5 subtract_convert_fusion
  78.6 0.0 all-gather.2.cloned.1.call-update
  78.6 0.0 all-reduce.4.cloned.1.call-start
  78.6 83.4 %all-gather.2.cloned.1.call-done = bf16[2048,2048]{1,0:T(8,128)(2,1)} async-done(((bf16[2048,512]{1,0:T(8,128)(2,1)}), bf16[2048,2048]{1,0:T(8,128)(2,1)}) %all-gather.2.cloned.1.call-update) | async-done | bytes 8388624 | tf_op jit(solution)/shard_map/all_gather | solution.py:90
  162.1 1.5 conditional.1
  162.1 1.5 broadcast.134
  163.6 0.0 copy-start.35
  163.6 1.5 broadcast_select_fusion
  165.1 0.0 all-reduce.4.cloned.1.call-update
  165.1 0.0 reduce-scatter.5.cloned.1.call-start
  165.2 951.4 %all-reduce.4.cloned.1.call-done = bf16[512,2048]{0,1:T(8,128)(2,1)} async-done(((bf16[512,2048]{0,1:T(8,128)(2,1)}), bf16[512,2048]{0,1:T(8,128)(2,1)}) %all-reduce.4.cloned.1.call-update) | async-done | bytes 2097168 | tf_op jit(solution)/shard_map/psum | solution.py:21
  1116.6 0.0 copy-done.35
  1116.6 9.7 fusion.185
  1126.3 0.0 reduce-scatter.5.cloned.1.call-update
  1126.3 0.0 copy-start.1
  1126.3 149.1 %reduce-scatter.5.cloned.1.call-done = f32[512,2048]{1,0:T(8,128)} async-done(((f32[2048,2048]{1,0:T(8,128)}), f32[512,2048]{1,0:T(8,128)}) %reduce-scatter.5.cloned.1.call-update) | async-done | bytes 4194320 | tf_op jit(solution)/shard_map/reduce_scatter | solution.py:108
  1275.5 3.8 convert_element_type.129
  1279.3 0.0 copy-done.1
Async XLA Ops:
  6.5 1.3 copy-start
  6.5 68.5 %reduce-scatter.3.cloned.1.call-start = ((), (), s32[]{:S(2)}) async-start(), calls=%async_computation.2 | async-start | bytes 6291456 | tf_op jit(solution)/shard_map/reduce_scatter | solution.py:81
  7.8 67.2 %copy-start.46 = (bf16[2048,512]{1,0:T(8,128)(2,1)S(1)}, bf16[2048,512]{1,0:T(8,128)(2,1)}, u32[]{:S(2)}) copy-start(bf16[2048,512]{1,0:T(8,128)(2,1)} %param.8) | copy-start | bytes 6291460
  11.1 151.0 %all-gather.2.cloned.1.call-start = ((), (), s32[]{:S(2)}) async-start(), calls=%async_computation.3 | async-start | bytes 10485760 | tf_op jit(solution)/shard_map/all_gather | solution.py:90
  78.6 1038.0 %all-reduce.4.cloned.1.call-start = ((), (), s32[]{:S(2)}) async-start(), calls=%async_computation.4 | async-start | bytes 4194304 | tf_op jit(solution)/shard_map/psum | solution.py:21
  163.6 953.0 %copy-start.35 = (bf16[2048,512]{1,0:T(8,128)(2,1)S(1)}, bf16[2048,512]{1,0:T(8,128)(2,1)}, u32[]{:S(2)}) copy-start(bf16[2048,512]{1,0:T(8,128)(2,1)} %subtract_convert_fusion) | copy-start | bytes 6291460
  165.1 1110.4 %reduce-scatter.5.cloned.1.call-start = ((), (), s32[]{:S(2)}) async-start(), calls=%async_computation.5 | async-start | bytes 20971520 | tf_op jit(solution)/shard_map/reduce_scatter | solution.py:108
  1126.3 153.0 %copy-start.1 = (bf16[1,8,64,512]{3,2,1,0:T(8,128)(2,1)S(1)}, bf16[1,8,64,512]{3,2,1,0:T(8,128)(2,1)}, u32[]{:S(2)}) copy-start(bf16[1,8,64,512]{3,2,1,0:T(8,128)(2,1)} %param.10) | copy-start | bytes 1572868
Sparse Core Ops, SparseCore 0:
  11.2 63.8 reduce-scatter.2
  78.7 83.3 all-gather.1
  165.9 950.6 all-reduce.3
  1126.4 148.9 reduce-scatter.4
where the time goes:
time: 1290 us
  waiting for transfers between devices  1250 us (97%)
  between operations  13.2 us (1%)
  matrix products  12.9 us (1%)
    psum x1, waiting for transfers between devices, spread(): return lax.psum(kept, axis)  951 us
    reduce_scatter x1, waiting for transfers between devices, shards(): lax.psum_scatter(lax.dot_general(part, panel_rows, (((0,), (1,)), ((), ()...  149 us
    all_gather x1, waiting for transfers between devices, shards(): top = lax.all_gather(panel_rows[:PW], 'col', axis=1, tiled=True)  83.4 us
    reduce_scatter x1, waiting for transfers between devices, shards(): lax.psum_scatter(child_term(left_all, right_all).astype(jnp.bfloat16), 'c...  63.9 us
  transfers between devices with their start and end apart: 4, of which 4 were waited for; matrix products, arithmetic and copies ran while one was open for 0% of the time, Pallas kernels for 0%

commit v1 on v0

v1 whole, which is shorter than its diff:
```python
import functools

import jax
import jax.numpy as jnp
from jax import lax
from jax.experimental import pallas as pl
from jax.experimental.pallas import tpu as pltpu
from jax.sharding import PartitionSpec as P

TILE = 512
RANK = 64
PW = 2048
BLOCKS = PW // TILE
ROOT_ITERS = 3
ALL = ("child", "row", "col")
NT = (((1,), (1,)), ((), ()))
NN = (((1,), (0,)), ((), ()))


def mxu(left, right, dims):
    return lax.dot_general(
        left.astype(jnp.bfloat16),
        right.astype(jnp.bfloat16),
        dims,
        preferred_element_type=jnp.float32,
    )


def leaf_inverse(tile_ref, x_ref, g_ref, n_ref, e_ref):
    rows = lax.broadcasted_iota(jnp.int32, (TILE, TILE), 0)
    cols = lax.broadcasted_iota(jnp.int32, (TILE, TILE), 1)
    diag = rows == cols
    tile = tile_ref[...]
    picked = jnp.where(diag, tile, 0.0)
    down = lax.rsqrt(jnp.sum(picked, axis=1, keepdims=True))
    across = lax.rsqrt(jnp.sum(picked, axis=0, keepdims=True))
    gram = tile * down * across - diag.astype(jnp.float32)

    def lower(mat):
        return jnp.where(rows > cols, mat, jnp.where(diag, 0.5 * mat, 0.0))

    g_ref[...] = gram
    n_ref[...] = lower(gram)

    def step(_, carry):
        n = n_ref[...]
        e = g_ref[...] - n - mxu(n, g_ref[...], NN)
        e_ref[...] = e.astype(jnp.bfloat16)
        phi = lower(e - n.T - mxu(e_ref[...], n, NT))
        n_ref[...] = n + phi - mxu(phi, n, NN)
        return carry

    lax.fori_loop(0, ROOT_ITERS, step, 0)
    x_ref[...] = ((diag.astype(jnp.float32) - n_ref[...]) * across).astype(jnp.bfloat16)


def factor_kernel(where_ref, own, left, right, far_a, far_b, *refs):
    outs = refs[:8]
    t_ref, s_ref, l_ref, x_ref, r_ref, g_ref, n_ref, e_ref, sems = refs[8:]
    col = where_ref[1]
    half = PW // 2

    @pl.when(where_ref[0] == 1)
    def _():
        far = lax.rem(col + 2, BLOCKS)
        copies = [
            pltpu.make_async_copy(own, t_ref.at[col], sems.at[0]),
            pltpu.make_async_copy(left, t_ref.at[lax.rem(col + 3, BLOCKS)], sems.at[1]),
            pltpu.make_async_copy(right, t_ref.at[lax.rem(col + 1, BLOCKS)], sems.at[2]),
            pltpu.make_async_copy(far_a, t_ref.at[far, pl.ds(0, half)], sems.at[3]),
            pltpu.make_async_copy(far_b, t_ref.at[far, pl.ds(half, half)], sems.at[4]),
        ]
        for copy in copies:
            copy.start()
        for copy in copies:
            copy.wait()

        def rows_of(i):
            return pl.ds(pl.multiple_of(i * TILE, TILE), TILE)

        @pl.loop(0, col + 1)
        def _(i):
            @pl.loop(0, i + 1)
            def _(j):
                low = t_ref[j, rows_of(i), :].astype(jnp.float32)
                high = t_ref[i, rows_of(j), :].astype(jnp.float32)
                s_ref[i, j] = 0.5 * (low + high.T)

        @pl.loop(0, col + 1)
        def _(j):
            leaf_inverse(s_ref.at[j, j], x_ref.at[j], g_ref, n_ref, e_ref)

            @pl.loop(j + 1, col + 1)
            def _(i):
                l_ref[i, j] = mxu(s_ref[i, j], x_ref[j], NT).astype(jnp.bfloat16)

                @pl.loop(j + 1, i + 1)
                def _(k):
                    s_ref[i, k] = s_ref[i, k] - mxu(l_ref[i, j], l_ref[k, j], NT)

        r_ref[col] = x_ref[col]

        @pl.loop(0, BLOCKS)
        def _(step):
            k = BLOCKS - 1 - step

            @pl.when(k > col)
            def _():
                r_ref[k] = jnp.zeros((TILE, TILE), jnp.bfloat16)

            @pl.when(k < col)
            def _():
                n_ref[...] = jnp.zeros((TILE, TILE), jnp.float32)

                @pl.loop(k + 1, col + 1)
                def _(m):
                    n_ref[...] += mxu(r_ref[m], l_ref[m, k], NN)

                r_ref[k] = (-mxu(n_ref[...], x_ref[k], NN)).astype(jnp.bfloat16)

        for z in range(8):
            for k in range(BLOCKS):
                outs[z][:, k * TILE : (k + 1) * TILE] = r_ref[k, z * 64 : (z + 1) * 64, :]


def factor_rows(where, own, left, right, far_a, far_b):
    any_spec = pl.BlockSpec(memory_space=pl.ANY)
    return pl.pallas_call(
        factor_kernel,
        out_shape=[jax.ShapeDtypeStruct((64, PW), jnp.bfloat16)] * 8,
        in_specs=[pl.BlockSpec(memory_space=pltpu.SMEM)] + [any_spec] * 5,
        out_specs=[pl.BlockSpec(memory_space=pltpu.VMEM)] * 8,
        scratch_shapes=[
            pltpu.VMEM((BLOCKS, PW, TILE), jnp.bfloat16),
            pltpu.VMEM((BLOCKS, BLOCKS, TILE, TILE), jnp.float32),
            pltpu.VMEM((BLOCKS, BLOCKS, TILE, TILE), jnp.bfloat16),
            pltpu.VMEM((BLOCKS, TILE, TILE), jnp.bfloat16),
            pltpu.VMEM((BLOCKS, TILE, TILE), jnp.bfloat16),
            pltpu.VMEM((TILE, TILE), jnp.float32),
            pltpu.VMEM((TILE, TILE), jnp.float32),
            pltpu.VMEM((TILE, TILE), jnp.bfloat16),
            pltpu.SemaphoreType.DMA((5,)),
        ],
        compiler_params=pltpu.CompilerParams(vmem_limit_bytes=60 << 20),
        name="factor_rows",
    )(where, own, left, right, far_a, far_b)


def apply_kernel(where_ref, own, left, right, far_a, far_b, *refs):
    chunks = refs[:8]
    out = refs[8]
    p_ref, r_ref, psems, rsems = refs[9:]
    col, z, core = where_ref[1], where_ref[2], where_ref[3]
    half = PW // 2
    sign = 1 - 2 * core
    rcopies = []
    for slot in range(8):
        if slot == 0:
            at = z
        elif slot <= 4:
            at = lax.rem(z - sign * slot + 8, 8)
        else:
            at = lax.rem(z + sign * (slot - 4) + 8, 8)
        rows = pl.ds(pl.multiple_of(at * 64, 64), 64)
        rcopies.append(pltpu.make_async_copy(chunks[slot], r_ref.at[rows], rsems.at[slot]))
    far = lax.rem(col + 2, BLOCKS)
    pcopies = [
        pltpu.make_async_copy(own, p_ref.at[col], psems.at[0]),
        pltpu.make_async_copy(left, p_ref.at[lax.rem(col + 3, BLOCKS)], psems.at[1]),
        pltpu.make_async_copy(right, p_ref.at[lax.rem(col + 1, BLOCKS)], psems.at[2]),
        pltpu.make_async_copy(far_a, p_ref.at[far, pl.ds(0, half)], psems.at[3]),
        pltpu.make_async_copy(far_b, p_ref.at[far, pl.ds(half, half)], psems.at[4]),
    ]
    for copy in rcopies + pcopies:
        copy.start()
    for copy in rcopies + pcopies:
        copy.wait()

    @pl.loop(0, PW // TILE)
    def _(tile):
        at = pl.ds(pl.multiple_of(tile * TILE, TILE), TILE)
        acc = jnp.zeros((TILE, TILE), jnp.float32)
        for k in range(BLOCKS):
            acc = acc + mxu(r_ref[:, k * TILE : (k + 1) * TILE], p_ref[k, at, :], NT)
        out[:, at] = acc.astype(jnp.bfloat16)


def apply_rows(where, own, left, right, far_a, far_b, chunks):
    any_spec = pl.BlockSpec(memory_space=pl.ANY)
    return pl.pallas_call(
        apply_kernel,
        out_shape=jax.ShapeDtypeStruct((TILE, PW), jnp.bfloat16),
        in_specs=[pl.BlockSpec(memory_space=pltpu.SMEM)] + [any_spec] * 13,
        out_specs=pl.BlockSpec(memory_space=pltpu.VMEM),
        scratch_shapes=[
            pltpu.VMEM((BLOCKS, PW, TILE), jnp.bfloat16),
            pltpu.VMEM((TILE, PW), jnp.bfloat16),
            pltpu.SemaphoreType.DMA((5,)),
            pltpu.SemaphoreType.DMA((8,)),
        ],
        compiler_params=pltpu.CompilerParams(vmem_limit_bytes=40 << 20),
        name="apply_rows",
    )(where, own, left, right, far_a, far_b, *chunks)


def device(child, z, ylo, core, col):
    return (child * 32 + z * 4 + ylo * 2 + core) * 4 + col


def pairs_of(move):
    found = []
    for child in range(2):
        for z in range(8):
            for ylo in range(2):
                for core in range(2):
                    for col in range(4):
                        target = move(child, z, ylo, core, col)
                        if target is not None:
                            found.append((device(child, z, ylo, core, col), device(*target)))
    return found


def gather_columns(part):
    def shift(by):
        return pairs_of(lambda c, z, y, k, j: (c, z, y, k, (j + by) % 4))

    half = PW // 2
    left = lax.ppermute(part, ALL, shift(1))
    right = lax.ppermute(part, ALL, shift(3))
    far_a = lax.ppermute(left[:half], ALL, shift(1))
    far_b = lax.ppermute(right[half:], ALL, shift(3))
    return left, right, far_a, far_b


def spread_rows(chunks, z, y, core):
    kept = chunks[0]
    total = None
    for k in range(1, 8):
        pairs = pairs_of(
            lambda c, zz, yy, kk, j: (0, k, 0, 0, j) if (c, zz, yy, kk) == (0, 0, 0, 0) else None
        )
        got = lax.ppermute(chunks[k], ALL, pairs)
        total = got if total is None else total + got
    chunk = jnp.where(z == 0, kept, total)
    total = None
    for to in (1, 3, 2):
        pairs = pairs_of(
            lambda c, zz, yy, kk, j: (to // 2, zz, to % 2, 0, j) if (c, yy, kk) == (0, 0, 0) else None
        )
        got = lax.ppermute(chunk, ALL, pairs)
        total = got if total is None else total + got
    chunk = jnp.where(y == 0, chunk, total)
    got = lax.ppermute(
        chunk, ALL, pairs_of(lambda c, zz, yy, kk, j: (c, zz, yy, 1, j) if kk == 0 else None)
    )
    chunk = jnp.where(core == 0, chunk, got)
    ring = pairs_of(lambda c, zz, yy, kk, j: (c, (zz + 1 - 2 * kk) % 8, yy, kk, j))
    swap = pairs_of(lambda c, zz, yy, kk, j: (c, zz, yy, 1 - kk, j))
    slots = [chunk]
    swapped = []
    current = chunk
    for step in range(4):
        current = lax.ppermute(current, ALL, ring)
        slots.append(current)
        if step < 3:
            swapped.append(lax.ppermute(current, ALL, swap))
    return slots + swapped


def shards(front, left_factors, right_factors):
    side = lax.axis_index("child")
    row = lax.axis_index("row")
    column = lax.axis_index("col")
    z, y, core = row // 4, 2 * side + (row // 2) % 2, row % 2
    left_all = left_factors[0, 0]
    right_all = right_factors[0]
    half = PW
    swap = [(0, 1), (1, 0)]
    tiles = right_all.shape[0] // 2
    got_left = lax.ppermute(
        lax.dynamic_slice_in_dim(left_all, (1 - side) * half, half, 1), "child", swap
    )
    got_right = lax.ppermute(
        lax.dynamic_slice_in_dim(right_all, (1 - side) * tiles, tiles, 0), "child", swap
    )
    own_left = lax.dynamic_slice_in_dim(left_all, side * half, half, 1)
    own_right = lax.dynamic_slice_in_dim(right_all, side * tiles, tiles, 0)
    left = jnp.concatenate([own_left, got_left], axis=0).reshape(2 * RANK, tiles, TILE)
    right = jnp.concatenate([own_right, got_right], axis=1)
    update = jnp.einsum("rtk,trn->tkn", left, right, preferred_element_type=jnp.float32)
    panel_rows = (front.astype(jnp.float32) - update.reshape(PW, TILE)).astype(jnp.bfloat16)
    parts = gather_columns(panel_rows)
    is_root = jnp.logical_and(side == 0, row == 0).astype(jnp.int32)
    where = jnp.stack([is_root, column, z, core]).astype(jnp.int32)
    chunks = factor_rows(where, panel_rows, *parts)
    chunks = spread_rows(chunks, z, y, core)
    return apply_rows(where, panel_rows, *parts, chunks)


def solution(mesh):
    in_specs = (
        P(("row", "child"), "col"),
        P("child", "col", None, "row"),
        P("child", "row", None, "col"),
    )
    out_specs = P("col", ("row", "child"))
    return jax.shard_map(shards, mesh=mesh, in_specs=in_specs, out_specs=out_specs, check_vma=False)
```

time: 1290 us -> 206 us (0.16)
  waiting for transfers between devices: 1250 us -> 140 us
  starting transfers between devices: 0.13 us -> 34.8 us
    psum x1 -> x0, waiting for transfers between devices: 951 us -> none  [spread(): return lax.psum(kept, axis)]
    reduce_scatter x2 -> x0, waiting for transfers between devices: 213 us -> none  [the longest x1 149 us: shards(): lax.psum_scatter(lax.dot_general(part, panel_rows, (((0,), (1,)), ((), ()...]
    ppermute x0 -> x24, waiting for transfers between devices: none -> 140 us  [the longest x1 51.4 us: spread_rows(): lax.ppermute(chunk, ALL, pairs_of(lambda c, zz, yy, kk, j: (c, zz, yy, 1,...]
    all_gather x1 -> x0, waiting for transfers between devices: 83.4 us -> none  [shards(): top = lax.all_gather(panel_rows[:PW], 'col', axis=1, tiled=True)]
    ppermute x0 -> x24, starting transfers between devices: none -> 34.8 us  [the longest x4 9.55 us: spread_rows(): current = lax.ppermute(current, ALL, ring)]
  transfers between devices with their start and end apart: 4 -> 24, of which waited for: 4 -> 11; matrix products, arithmetic and copies ran while one was open for 0% -> 2% of each run, Pallas kernels for 0% -> 0%
where the time goes in v1:
time: 206 us; the launch traced here: 203 us
  waiting for transfers between devices  140 us (68%)
  starting transfers between devices  34.8 us (17%)
  local copies, waits for them, and re-layouts  11.9 us (6%)
  Pallas kernels  11 us (5%)
  other arithmetic  5.06 us (2%)
    ppermute x1, waiting for transfers between devices, spread_rows(): lax.ppermute(chunk, ALL, pairs_of(lambda c, zz, yy, kk, j: (c, zz, yy, 1,...  51.4 us
    ppermute x1, waiting for transfers between devices, gather_columns(): right = lax.ppermute(part, ALL, shift(3))  44.1 us
    ppermute x1, waiting for transfers between devices, gather_columns(): far_b = lax.ppermute(right[half:], ALL, shift(3))  17.9 us
    ppermute x4, waiting for transfers between devices, spread_rows(): current = lax.ppermute(current, ALL, ring)  13.8 us
    ppermute x4, starting transfers between devices, spread_rows(): current = lax.ppermute(current, ALL, ring)  9.55 us
    pallas_call x1, Pallas kernels, apply_rows(): pl.pallas_call(apply_kernel, out_shape=jax.ShapeDtypeStruct((TILE, PW), j...  8.93 us
    unnamed x30, local copies, waits for them, and re-layouts  7.07 us
    ppermute x7, starting transfers between devices, spread_rows(): got = lax.ppermute(chunks[k], ALL, pairs)  6.11 us
  transfers between devices with their start and end apart: 24, of which 11 were waited for; matrix products, arithmetic and copies ran while one was open for 2% of the time, Pallas kernels for 0%

profile of v1, /device:TPU:7, one launch (start us, length us, event | category | flops | bytes accessed | tf_op | source)
XLA Modules:
  0.0 203.5 jit_solution(17982105778967165910)
XLA Ops:
  0.0 1.1 constant_dynamic-slice_fusion
  1.1 3.0 %collective-permute-start = (bf16[64,2048]{1,0:T(8,128)(2,1)S(1)}, bf16[64,2048]{1,0:T(8,128)(2,1)S(1)}, u32[]{:S(2)}, u32[]{:S(2)}) collective-permute-start(bf16[64,2048]{1,0:T(8,128)(2,1)S(1)} %get-tuple-element.24), channel_id=1, source_target_pairs={{0,128},{128,0},{1,129},{129,1},{2,130},{130,2},{3,131},{131,3},{4... | collective-permute-start | bytes 786440 | tf_op jit(solution)/shard_map/ppermute | solution.py:280
  4.1 1.1 dynamic-slice_bitcast_fusion.1
  5.6 4.3 %collective-permute-done = bf16[64,2048]{1,0:T(8,128)(2,1)S(1)} collective-permute-done((bf16[64,2048]{1,0:T(8,128)(2,1)S(1)}, bf16[64,2048]{1,0:T(8,128)(2,1)S(1)}, u32[]{:S(2)}, u32[]{:S(2)}) %collective-permute-start) | collective-permute-done | bytes 262176 | tf_op jit(solution)/shard_map/ppermute | solution.py:280
  10.1 5.3 %collective-permute-done.1 = bf16[4,64,512]{2,1,0:T(8,128)(2,1)S(1)} collective-permute-done((bf16[4,64,512]{2,1,0:T(8,128)(2,1)S(1)}, bf16[4,64,512]{2,1,0:T(8,128)(2,1)S(1)}, u32[]{:S(2)}, u32[]{:S(2)}) %collective-permute-start.1) | collective-permute-done | bytes 262176 | tf_op jit(solution)/shard_map/ppermute | solution.py:283
  15.5 0.8 fusion.1
  16.2 0.8 copy-done.9
  17.0 0.8 fusion.own
  17.8 0.6 collective-permute-start.3
  18.5 2.1 %collective-permute-start.2 = (bf16[2048,512]{1,0:T(8,128)(2,1)S(1)}, bf16[2048,512]{1,0:T(8,128)(2,1)S(1)}, u32[]{:S(2)}, u32[]{:S(2)}) collective-permute-start(bf16[2048,512]{1,0:T(8,128)(2,1)S(1)} %fusion.own), channel_id=1, source_target_pairs={{0,1},{1,2},{2,3},{3,0},{4,5},{5,6},{6,7},{7,4},{8,9},{9,10},{10,1... | collective-permute-start | bytes 6291464 | tf_op jit(solution)/shard_map/ppermute | solution.py:228
  20.6 44.1 %collective-permute-done.3.right = bf16[2048,512]{1,0:T(8,128)(2,1)S(1)} collective-permute-done((bf16[2048,512]{1,0:T(8,128)(2,1)S(1)}, bf16[2048,512]{1,0:T(8,128)(2,1)S(1)}, u32[]{:S(2)}, u32[]{:S(2)}) %collective-permute-start.3) | collective-permute-done | bytes 2097184 | tf_op jit(solution)/shard_map/ppermute | solution.py:229
  64.7 1.1 slice.9
  65.9 1.3 copy-done.4
  67.2 1.0 slice.8
  68.2 2.7 %collective-permute-start.4 = (bf16[1024,512]{1,0:T(8,128)(2,1)}, bf16[1024,512]{1,0:T(8,128)(2,1)}, u32[]{:S(2)}, u32[]{:S(2)}) collective-permute-start(bf16[1024,512]{1,0:T(8,128)(2,1)} %slice.8), channel_id=1, source_target_pairs={{0,1},{1,2},{2,3},{3,0},{4,5},{5,6},{6,7},{7,4},{8,9},{9,10},{10,1... | collective-permute-start | bytes 3145736 | tf_op jit(solution)/shard_map/ppermute | solution.py:230
  70.9 0.6 pad_add_fusion.where_ref
  71.5 17.9 %collective-permute-done.5.far_b = bf16[1024,512]{1,0:T(8,128)(2,1)S(1)} collective-permute-done((bf16[1024,512]{1,0:T(8,128)(2,1)}, bf16[1024,512]{1,0:T(8,128)(2,1)S(1)}, u32[]{:S(2)}, u32[]{:S(2)}) %collective-permute-start.5) | collective-permute-done | bytes 1048608 | tf_op jit(solution)/shard_map/ppermute | solution.py:231
  89.5 1.5 collective-permute-done.4.far_a
  90.9 2.1 %factor_rows.1 = (bf16[64,2048]{1,0:T(8,128)(2,1)}, bf16[64,2048]{1,0:T(8,128)(2,1)}, bf16[64,2048]{1,0:T(8,128)(2,1)}, bf16[64,2048]{1,0:T(8,128)(2,1)}, bf16[6...) custom-call(s32[4]{0:T(128)} %pad_add_fusion.where_ref, ...), custom_call_target="tpu_custom_call" | custom-call | tf_op jit(solution)/shard_map/factor_rows/pallas_call | solution.py:128
  93.0 1.4 collective-permute-start.6
  94.4 1.4 collective-permute-start.7
  95.8 0.7 collective-permute-start.8
  96.4 0.7 collective-permute-start.9
  97.1 0.7 collective-permute-start.10
  97.8 0.7 collective-permute-start.11
  98.5 0.7 collective-permute-start.12
  99.3 0.6 copy-done.10
  100.3 0.7 copy-done.14
  101.0 1.8 add_select_fusion.1
  102.8 1.4 collective-permute-start.15
  104.1 1.4 collective-permute-start.14
  105.5 1.4 collective-permute-start.13
  106.9 1.9 add_select_fusion
  108.7 1.3 collective-permute-start.16
  110.0 51.4 %collective-permute-done.16 = bf16[64,2048]{1,0:T(8,128)(2,1)S(1)} collective-permute-done((bf16[64,2048]{1,0:T(8,128)(2,1)}, bf16[64,2048]{1,0:T(8,128)(2,1)S(1)}, u32[]{:S(2)}, u32[]{:S(2)}) %collective-permute-start.16) | collective-permute-done | bytes 262176 | tf_op jit(solution)/shard_map/ppermute | solution.py:253
  161.5 3.3 %collective-permute-start.17 = (bf16[64,2048]{1,0:T(8,128)(2,1)S(1)}, bf16[64,2048]{1,0:T(8,128)(2,1)S(1)}, u32[]{:S(2)}, u32[]{:S(2)}) collective-permute-start(bf16[64,2048]{1,0:T(8,128)(2,1)S(1)} %broadcast_select_fusion.refs_0_), channel_id=1, source_target_pairs={{0,16},{1,17},{2,18},{3,19},{4,116},{5,117},{6,118},{7,119},{8,24}... | collective-permute-start | bytes 786440 | tf_op jit(solution)/shard_map/ppermute | solution.py:263
  164.8 3.3 %collective-permute-done.17.refs_1_ = bf16[64,2048]{1,0:T(8,128)(2,1)S(1)} collective-permute-done((bf16[64,2048]{1,0:T(8,128)(2,1)S(1)}, bf16[64,2048]{1,0:T(8,128)(2,1)S(1)}, u32[]{:S(2)}, u32[]{:S(2)}) %collective-permute-start.17) | collective-permute-done | bytes 262176 | tf_op jit(solution)/shard_map/ppermute | solution.py:263
  168.1 3.1 %collective-permute-start.18 = (bf16[64,2048]{1,0:T(8,128)(2,1)S(1)}, bf16[64,2048]{1,0:T(8,128)(2,1)S(1)}, u32[]{:S(2)}, u32[]{:S(2)}) collective-permute-start(bf16[64,2048]{1,0:T(8,128)(2,1)S(1)} %collective-permute-done.17.refs_1_), channel_id=1, source_target_pairs={{0,16},{1,17},{2,18},{3,19},{4,116},{5,117},{6,118},{7,119},{8,24}... | collective-permute-start | bytes 786440 | tf_op jit(solution)/shard_map/ppermute | solution.py:263
  171.2 3.3 %collective-permute-done.18.refs_2_ = bf16[64,2048]{1,0:T(8,128)(2,1)S(1)} collective-permute-done((bf16[64,2048]{1,0:T(8,128)(2,1)S(1)}, bf16[64,2048]{1,0:T(8,128)(2,1)S(1)}, u32[]{:S(2)}, u32[]{:S(2)}) %collective-permute-start.18) | collective-permute-done | bytes 262176 | tf_op jit(solution)/shard_map/ppermute | solution.py:263
  174.5 3.1 %collective-permute-start.19 = (bf16[64,2048]{1,0:T(8,128)(2,1)S(1)}, bf16[64,2048]{1,0:T(8,128)(2,1)S(1)}, u32[]{:S(2)}, u32[]{:S(2)}) collective-permute-start(bf16[64,2048]{1,0:T(8,128)(2,1)S(1)} %collective-permute-done.18.refs_2_), channel_id=1, source_target_pairs={{0,16},{1,17},{2,18},{3,19},{4,116},{5,117},{6,118},{7,119},{8,24}... | collective-permute-start | bytes 786440 | tf_op jit(solution)/shard_map/ppermute | solution.py:263
  177.7 0.4 collective-permute-start.21
  178.2 2.8 %collective-permute-done.19.refs_3_ = bf16[64,2048]{1,0:T(8,128)(2,1)S(1)} collective-permute-done((bf16[64,2048]{1,0:T(8,128)(2,1)S(1)}, bf16[64,2048]{1,0:T(8,128)(2,1)S(1)}, u32[]{:S(2)}, u32[]{:S(2)}) %collective-permute-start.19) | collective-permute-done | bytes 262176 | tf_op jit(solution)/shard_map/ppermute | solution.py:263
  181.0 4.7 %collective-permute-start.23 = (bf16[64,2048]{1,0:T(8,128)(2,1)S(1)}, bf16[64,2048]{1,0:T(8,128)(2,1)S(1)}, u32[]{:S(2)}, u32[]{:S(2)}) collective-permute-start(bf16[64,2048]{1,0:T(8,128)(2,1)S(1)} %collective-permute-done.19.refs_3_), channel_id=1, source_target_pairs={{0,4},{1,5},{2,6},{3,7},{4,0},{5,1},{6,2},{7,3},{8,12},{9,13},{10,... | collective-permute-start | bytes 786440 | tf_op jit(solution)/shard_map/ppermute | solution.py:266
  185.7 1.1 collective-permute-done.23.refs_7_
  186.8 4.4 %collective-permute-done.20.refs_4_ = bf16[64,2048]{1,0:T(8,128)(2,1)S(1)} collective-permute-done((bf16[64,2048]{1,0:T(8,128)(2,1)S(1)}, bf16[64,2048]{1,0:T(8,128)(2,1)S(1)}, u32[]{:S(2)}, u32[]{:S(2)}) %collective-permute-start.20) | collective-permute-done | bytes 262176 | tf_op jit(solution)/shard_map/ppermute | solution.py:263
  191.2 1.6 copy-done.3
  192.8 1.6 copy-done.5
  194.4 8.9 %apply_rows.1 = bf16[512,2048]{1,0:T(8,128)(2,1)} custom-call(s32[4]{0:T(128)S(1)} %copy-done.8, bf16[2048,512]{1,0:T(8,128)(2,1)S(1)} %copy-done.1, bf16[2048,512]{1,0:T(8,128)(2,1)S(1)} %copy-done.5, bf16[2048,512]{1,0:T(8,128)(2,1)S(1)} %copy-done.3, bf16[1024,512]{1,0:T(8,128)(2,1)} %collective-permute-done.4.far_a, bf16[1024,512]{1,0:T(8,128)(2,1)S(1)} %copy-done.7, ...), custom_call_target="tpu_custom_call" | custom-call | tf_op jit(solution)/shard_map/apply_rows/pallas_call | solution.py:190
  (44 shorter events, 1.3 us)
Async XLA Ops:
  1.1 8.8 %collective-permute-start = (bf16[64,2048]{1,0:T(8,128)(2,1)S(1)}, bf16[64,2048]{1,0:T(8,128)(2,1)S(1)}, u32[]{:S(2)}, u32[]{:S(2)}) collective-permute-start(bf16[64,2048]{1,0:T(8,128)(2,1)S(1)} %get-tuple-element.24), channel_id=1, source_target_pairs={{0,128},{128,0},{1,129},{129,1},{2,130},{130,2},{3,131},{131,3},{4... | collective-permute-start | bytes 786440 | tf_op jit(solution)/shard_map/ppermute | solution.py:280
  5.1 10.3 %collective-permute-start.1 = (bf16[4,64,512]{2,1,0:T(8,128)(2,1)S(1)}, bf16[4,64,512]{2,1,0:T(8,128)(2,1)S(1)}, u32[]{:S(2)}, u32[]{:S(2)}) collective-permute-start(bf16[4,64,512]{2,1,0:T(8,128)(2,1)S(1)} %get-tuple-element.22), channel_id=1, source_target_pairs={{0,128},{128,0},{1,129},{129,1},{2,130},{130,2},{3,131},{131,3},{4... | collective-permute-start | bytes 786440 | tf_op jit(solution)/shard_map/ppermute | solution.py:283
  15.5 1.6 copy-start.9
  17.8 50.4 %copy-start = (bf16[2048,512]{1,0:T(8,128)(2,1)}, bf16[2048,512]{1,0:T(8,128)(2,1)S(1)}, u32[]{:S(2)}) copy-start(bf16[2048,512]{1,0:T(8,128)(2,1)S(1)} %fusion.own) | copy-start | bytes 6291460
  17.8 46.9 %collective-permute-start.3 = (bf16[2048,512]{1,0:T(8,128)(2,1)S(1)}, bf16[2048,512]{1,0:T(8,128)(2,1)S(1)}, u32[]{:S(2)}, u32[]{:S(2)}) collective-permute-start(bf16[2048,512]{1,0:T(8,128)(2,1)S(1)} %fusion.own), channel_id=1, source_target_pairs={{0,3},{1,0},{2,1},{3,2},{4,7},{5,4},{6,5},{7,6},{8,11},{9,8},{10,9... | collective-permute-start | bytes 6291464 | tf_op jit(solution)/shard_map/ppermute | solution.py:229
  18.5 47.4 %collective-permute-start.2 = (bf16[2048,512]{1,0:T(8,128)(2,1)S(1)}, bf16[2048,512]{1,0:T(8,128)(2,1)S(1)}, u32[]{:S(2)}, u32[]{:S(2)}) collective-permute-start(bf16[2048,512]{1,0:T(8,128)(2,1)S(1)} %fusion.own), channel_id=1, source_target_pairs={{0,1},{1,2},{2,3},{3,0},{4,5},{5,6},{6,7},{7,4},{8,9},{9,10},{10,1... | collective-permute-start | bytes 6291464 | tf_op jit(solution)/shard_map/ppermute | solution.py:228
  64.7 3.5 %copy-start.2 = (bf16[2048,512]{1,0:T(8,128)(2,1)}, bf16[2048,512]{1,0:T(8,128)(2,1)S(1)}, u32[]{:S(2)}) copy-start(bf16[2048,512]{1,0:T(8,128)(2,1)S(1)} %collective-permute-done.3.right) | copy-start | bytes 6291460
  65.8 23.6 %collective-permute-start.5 = (bf16[1024,512]{1,0:T(8,128)(2,1)}, bf16[1024,512]{1,0:T(8,128)(2,1)S(1)}, u32[]{:S(2)}, u32[]{:S(2)}) collective-permute-start(bf16[1024,512]{1,0:T(8,128)(2,1)} %slice.9), channel_id=1, source_target_pairs={{0,3},{1,0},{2,1},{3,2},{4,7},{5,4},{6,5},{7,6},{8,11},{9,8},{10,9... | collective-permute-start | bytes 3145736 | tf_op jit(solution)/shard_map/ppermute | solution.py:231
  65.9 1.3 copy-start.4
  68.2 22.7 %collective-permute-start.4 = (bf16[1024,512]{1,0:T(8,128)(2,1)}, bf16[1024,512]{1,0:T(8,128)(2,1)}, u32[]{:S(2)}, u32[]{:S(2)}) collective-permute-start(bf16[1024,512]{1,0:T(8,128)(2,1)} %slice.8), channel_id=1, source_target_pairs={{0,1},{1,2},{2,3},{3,0},{4,5},{5,6},{6,7},{7,4},{8,9},{9,10},{10,1... | collective-permute-start | bytes 3145736 | tf_op jit(solution)/shard_map/ppermute | solution.py:230
  89.5 1.5 copy-start.6
  93.0 4.8 %collective-permute-start.6 = (bf16[64,2048]{1,0:T(8,128)(2,1)}, bf16[64,2048]{1,0:T(8,128)(2,1)}, u32[]{:S(2)}, u32[]{:S(2)}) collective-permute-start(bf16[64,2048]{1,0:T(8,128)(2,1)} %get-tuple-element.14), channel_id=1, source_target_pairs={{0,16},{1,17},{2,18},{3,19}} | collective-permute-start | bytes 786440 | tf_op jit(solution)/shard_map/ppermute | solution.py:242
  94.4 4.1 %collective-permute-start.7 = (bf16[64,2048]{1,0:T(8,128)(2,1)}, bf16[64,2048]{1,0:T(8,128)(2,1)}, u32[]{:S(2)}, u32[]{:S(2)}) collective-permute-start(bf16[64,2048]{1,0:T(8,128)(2,1)} %get-tuple-element.15), channel_id=1, source_target_pairs={{0,32},{1,33},{2,34},{3,35}} | collective-permute-start | bytes 786440 | tf_op jit(solution)/shard_map/ppermute | solution.py:242
  95.8 3.4 %collective-permute-start.8 = (bf16[64,2048]{1,0:T(8,128)(2,1)}, bf16[64,2048]{1,0:T(8,128)(2,1)S(1)}, u32[]{:S(2)}, u32[]{:S(2)}) collective-permute-start(bf16[64,2048]{1,0:T(8,128)(2,1)} %get-tuple-element.16), channel_id=1, source_target_pairs={{0,48},{1,49},{2,50},{3,51}} | collective-permute-start | bytes 786440 | tf_op jit(solution)/shard_map/ppermute | solution.py:242
  96.4 2.8 %collective-permute-start.9 = (bf16[64,2048]{1,0:T(8,128)(2,1)}, bf16[64,2048]{1,0:T(8,128)(2,1)S(1)}, u32[]{:S(2)}, u32[]{:S(2)}) collective-permute-start(bf16[64,2048]{1,0:T(8,128)(2,1)} %get-tuple-element.17), channel_id=1, source_target_pairs={{0,64},{1,65},{2,66},{3,67}} | collective-permute-start | bytes 786440 | tf_op jit(solution)/shard_map/ppermute | solution.py:242
  97.1 2.1 %collective-permute-start.10 = (bf16[64,2048]{1,0:T(8,128)(2,1)}, bf16[64,2048]{1,0:T(8,128)(2,1)S(1)}, u32[]{:S(2)}, u32[]{:S(2)}) collective-permute-start(bf16[64,2048]{1,0:T(8,128)(2,1)} %get-tuple-element.18), channel_id=1, source_target_pairs={{0,80},{1,81},{2,82},{3,83}} | collective-permute-start | bytes 786440 | tf_op jit(solution)/shard_map/ppermute | solution.py:242
  97.8 1.4 collective-permute-start.11
  98.5 0.8 collective-permute-start.12
  99.2 0.7 copy-start.10
  99.2 0.8 copy-start.11
  99.3 0.9 copy-start.12
  99.3 1.0 copy-start.13
  100.3 0.7 copy-start.14
  101.0 90.2 %copy-start.1 = (bf16[2048,512]{1,0:T(8,128)(2,1)S(1)}, bf16[2048,512]{1,0:T(8,128)(2,1)}, u32[]{:S(2)}) copy-start(bf16[2048,512]{1,0:T(8,128)(2,1)} %copy-done) | copy-start | bytes 6291460
  101.0 90.2 %copy-start.7 = (bf16[1024,512]{1,0:T(8,128)(2,1)S(1)}, bf16[1024,512]{1,0:T(8,128)(2,1)}, u32[]{:S(2)}) copy-start(bf16[1024,512]{1,0:T(8,128)(2,1)} %copy-done.6) | copy-start | bytes 3145732
  101.0 90.2 %copy-start.8 = (s32[4]{0:T(128)S(1)}, s32[4]{0:T(128)}, u32[]{:S(2)}) copy-start(s32[4]{0:T(128)} %pad_add_fusion.where_ref) | copy-start | bytes 52
  102.8 4.1 %collective-permute-start.15 = (bf16[64,2048]{1,0:T(8,128)(2,1)S(1)}, bf16[64,2048]{1,0:T(8,128)(2,1)}, u32[]{:S(2)}, u32[]{:S(2)}) collective-permute-start(bf16[64,2048]{1,0:T(8,128)(2,1)S(1)} %add_select_fusion.1), channel_id=1, source_target_pairs={{0,128},{1,129},{2,130},{3,131},{16,144},{17,145},{18,146},{19,147... | collective-permute-start | bytes 786440 | tf_op jit(solution)/shard_map/ppermute | solution.py:250
  104.1 2.7 %collective-permute-start.14 = (bf16[64,2048]{1,0:T(8,128)(2,1)S(1)}, bf16[64,2048]{1,0:T(8,128)(2,1)}, u32[]{:S(2)}, u32[]{:S(2)}) collective-permute-start(bf16[64,2048]{1,0:T(8,128)(2,1)S(1)} %add_select_fusion.1), channel_id=1, source_target_pairs={{0,136},{1,137},{2,138},{3,139},{16,152},{17,153},{18,154},{19,155... | collective-permute-start | bytes 786440 | tf_op jit(solution)/shard_map/ppermute | solution.py:250
  105.5 1.4 collective-permute-start.13
  108.7 52.7 %collective-permute-start.16 = (bf16[64,2048]{1,0:T(8,128)(2,1)}, bf16[64,2048]{1,0:T(8,128)(2,1)S(1)}, u32[]{:S(2)}, u32[]{:S(2)}) collective-permute-start(bf16[64,2048]{1,0:T(8,128)(2,1)} %add_select_fusion), channel_id=1, source_target_pairs={{0,4},{1,5},{2,6},{3,7},{8,12},{9,13},{10,14},{11,15},{16,20},{17,... | collective-permute-start | bytes 786440 | tf_op jit(solution)/shard_map/ppermute | solution.py:253
  161.5 6.6 %collective-permute-start.17 = (bf16[64,2048]{1,0:T(8,128)(2,1)S(1)}, bf16[64,2048]{1,0:T(8,128)(2,1)S(1)}, u32[]{:S(2)}, u32[]{:S(2)}) collective-permute-start(bf16[64,2048]{1,0:T(8,128)(2,1)S(1)} %broadcast_select_fusion.refs_0_), channel_id=1, source_target_pairs={{0,16},{1,17},{2,18},{3,19},{4,116},{5,117},{6,118},{7,119},{8,24}... | collective-permute-start | bytes 786440 | tf_op jit(solution)/shard_map/ppermute | solution.py:263
  168.1 6.4 %collective-permute-start.18 = (bf16[64,2048]{1,0:T(8,128)(2,1)S(1)}, bf16[64,2048]{1,0:T(8,128)(2,1)S(1)}, u32[]{:S(2)}, u32[]{:S(2)}) collective-permute-start(bf16[64,2048]{1,0:T(8,128)(2,1)S(1)} %collective-permute-done.17.refs_1_), channel_id=1, source_target_pairs={{0,16},{1,17},{2,18},{3,19},{4,116},{5,117},{6,118},{7,119},{8,24}... | collective-permute-start | bytes 786440 | tf_op jit(solution)/shard_map/ppermute | solution.py:263
  174.5 6.4 %collective-permute-start.19 = (bf16[64,2048]{1,0:T(8,128)(2,1)S(1)}, bf16[64,2048]{1,0:T(8,128)(2,1)S(1)}, u32[]{:S(2)}, u32[]{:S(2)}) collective-permute-start(bf16[64,2048]{1,0:T(8,128)(2,1)S(1)} %collective-permute-done.18.refs_2_), channel_id=1, source_target_pairs={{0,16},{1,17},{2,18},{3,19},{4,116},{5,117},{6,118},{7,119},{8,24}... | collective-permute-start | bytes 786440 | tf_op jit(solution)/shard_map/ppermute | solution.py:263
  177.7 8.0 %collective-permute-start.21 = (bf16[64,2048]{1,0:T(8,128)(2,1)S(1)}, bf16[64,2048]{1,0:T(8,128)(2,1)S(1)}, u32[]{:S(2)}, u32[]{:S(2)}) collective-permute-start(bf16[64,2048]{1,0:T(8,128)(2,1)S(1)} %collective-permute-done.17.refs_1_), channel_id=1, source_target_pairs={{0,4},{1,5},{2,6},{3,7},{4,0},{5,1},{6,2},{7,3},{8,12},{9,13},{10,... | collective-permute-start | bytes 786440 | tf_op jit(solution)/shard_map/ppermute | solution.py:266
  178.1 7.6 %collective-permute-start.22 = (bf16[64,2048]{1,0:T(8,128)(2,1)S(1)}, bf16[64,2048]{1,0:T(8,128)(2,1)S(1)}, u32[]{:S(2)}, u32[]{:S(2)}) collective-permute-start(bf16[64,2048]{1,0:T(8,128)(2,1)S(1)} %collective-permute-done.18.refs_2_), channel_id=1, source_target_pairs={{0,4},{1,5},{2,6},{3,7},{4,0},{5,1},{6,2},{7,3},{8,12},{9,13},{10,... | collective-permute-start | bytes 786440 | tf_op jit(solution)/shard_map/ppermute | solution.py:266
  181.0 5.9 %collective-permute-start.23 = (bf16[64,2048]{1,0:T(8,128)(2,1)S(1)}, bf16[64,2048]{1,0:T(8,128)(2,1)S(1)}, u32[]{:S(2)}, u32[]{:S(2)}) collective-permute-start(bf16[64,2048]{1,0:T(8,128)(2,1)S(1)} %collective-permute-done.19.refs_3_), channel_id=1, source_target_pairs={{0,4},{1,5},{2,6},{3,7},{4,0},{5,1},{6,2},{7,3},{8,12},{9,13},{10,... | collective-permute-start | bytes 786440 | tf_op jit(solution)/shard_map/ppermute | solution.py:266
  185.7 5.5 %collective-permute-start.20 = (bf16[64,2048]{1,0:T(8,128)(2,1)S(1)}, bf16[64,2048]{1,0:T(8,128)(2,1)S(1)}, u32[]{:S(2)}, u32[]{:S(2)}) collective-permute-start(bf16[64,2048]{1,0:T(8,128)(2,1)S(1)} %collective-permute-done.19.refs_3_), channel_id=1, source_target_pairs={{0,16},{1,17},{2,18},{3,19},{4,116},{5,117},{6,118},{7,119},{8,24}... | collective-permute-start | bytes 786440 | tf_op jit(solution)/shard_map/ppermute | solution.py:263
  191.2 1.6 copy-start.3
  192.8 1.6 copy-start.5

commit v2 on v1

--- a/solution.py
+++ b/solution.py
@@ -54,25 +54,35 @@
     x_ref[...] = ((diag.astype(jnp.float32) - n_ref[...]) * across).astype(jnp.bfloat16)
 
 
-def factor_kernel(where_ref, own, left, right, far_a, far_b, *refs):
-    outs = refs[:8]
-    t_ref, s_ref, l_ref, x_ref, r_ref, g_ref, n_ref, e_ref, sems = refs[8:]
+def fetch_columns(group, col, own, groups, dest, sems):
+    half = PW // 2
+
+    def copies(parts):
+        found = []
+        for slot, part in enumerate(own + parts):
+            column = lax.rem(col + (0, 3, 1, 2)[slot // 2], BLOCKS)
+            rows = pl.ds((slot % 2) * half, half)
+            found.append(pltpu.make_async_copy(part, dest.at[column, rows], sems.at[slot]))
+        return found
+
+    for index, parts in enumerate(groups):
+
+        @pl.when(group == index)
+        def _():
+            for copy in copies(parts):
+                copy.start()
+
+    return copies(groups[0])
+
+
+def factor_kernel(where_ref, *refs):
+    own, parts, outs = list(refs[:2]), list(refs[2:8]), refs[8:16]
+    t_ref, s_ref, l_ref, x_ref, r_ref, g_ref, n_ref, e_ref, sems = refs[16:]
     col = where_ref[1]
-    half = PW // 2
-
-    @pl.when(where_ref[0] == 1)
+
+    @pl.when(where_ref[0] == 0)
     def _():
-        far = lax.rem(col + 2, BLOCKS)
-        copies = [
-            pltpu.make_async_copy(own, t_ref.at[col], sems.at[0]),
-            pltpu.make_async_copy(left, t_ref.at[lax.rem(col + 3, BLOCKS)], sems.at[1]),
-            pltpu.make_async_copy(right, t_ref.at[lax.rem(col + 1, BLOCKS)], sems.at[2]),
-            pltpu.make_async_copy(far_a, t_ref.at[far, pl.ds(0, half)], sems.at[3]),
-            pltpu.make_async_copy(far_b, t_ref.at[far, pl.ds(half, half)], sems.at[4]),
-        ]
-        for copy in copies:
-            copy.start()
-        for copy in copies:
+        for copy in fetch_columns(0, col, own, [parts], t_ref, sems):
             copy.wait()
 
         def rows_of(i):
@@ -123,12 +133,14 @@
                 outs[z][:, k * TILE : (k + 1) * TILE] = r_ref[k, z * 64 : (z + 1) * 64, :]
 
 
-def factor_rows(where, own, left, right, far_a, far_b):
-    any_spec = pl.BlockSpec(memory_space=pl.ANY)
+HBM = pl.BlockSpec(memory_space=pltpu.HBM)
+
+
+def factor_rows(where, own, parts):
     return pl.pallas_call(
         factor_kernel,
         out_shape=[jax.ShapeDtypeStruct((64, PW), jnp.bfloat16)] * 8,
-        in_specs=[pl.BlockSpec(memory_space=pltpu.SMEM)] + [any_spec] * 5,
+        in_specs=[pl.BlockSpec(memory_space=pltpu.SMEM)] + [HBM] * 8,
         out_specs=[pl.BlockSpec(memory_space=pltpu.VMEM)] * 8,
         scratch_shapes=[
             pltpu.VMEM((BLOCKS, PW, TILE), jnp.bfloat16),
@@ -139,41 +151,39 @@
             pltpu.VMEM((TILE, TILE), jnp.float32),
             pltpu.VMEM((TILE, TILE), jnp.float32),
             pltpu.VMEM((TILE, TILE), jnp.bfloat16),
-            pltpu.SemaphoreType.DMA((5,)),
+            pltpu.SemaphoreType.DMA((8,)),
         ],
-        compiler_params=pltpu.CompilerParams(vmem_limit_bytes=60 << 20),
+        compiler_params=pltpu.CompilerParams(vmem_limit_bytes=56 << 20),
         name="factor_rows",
-    )(where, own, left, right, far_a, far_b)
-
-
-def apply_kernel(where_ref, own, left, right, far_a, far_b, *refs):
-    chunks = refs[:8]
-    out = refs[8]
-    p_ref, r_ref, psems, rsems = refs[9:]
-    col, z, core = where_ref[1], where_ref[2], where_ref[3]
-    half = PW // 2
+    )(where, *own, *parts)
+
+
+CHUNKS = 9
+
+
+def apply_kernel(where_ref, *refs):
+    own = list(refs[:2])
+    groups = [list(refs[2 + 6 * g : 8 + 6 * g]) for g in range(3)]
+    chunks = refs[20 : 20 + CHUNKS]
+    out, p_ref, r_ref, psems, rsems = refs[20 + CHUNKS :]
+    group, col, z, core = where_ref[0], where_ref[1], where_ref[2], where_ref[3]
     sign = 1 - 2 * core
-    rcopies = []
-    for slot in range(8):
-        if slot == 0:
-            at = z
-        elif slot <= 4:
-            at = lax.rem(z - sign * slot + 8, 8)
+    copies = []
+    for slot in range(CHUNKS):
+        size = 64
+        if slot <= 3:
+            at = lax.rem(z - sign * slot + 8, 8) * 64
+        elif slot <= 6:
+            at = lax.rem(z + sign * (slot - 3) + 8, 8) * 64
         else:
-            at = lax.rem(z + sign * (slot - 4) + 8, 8)
-        rows = pl.ds(pl.multiple_of(at * 64, 64), 64)
-        rcopies.append(pltpu.make_async_copy(chunks[slot], r_ref.at[rows], rsems.at[slot]))
-    far = lax.rem(col + 2, BLOCKS)
-    pcopies = [
-        pltpu.make_async_copy(own, p_ref.at[col], psems.at[0]),
-        pltpu.make_async_copy(left, p_ref.at[lax.rem(col + 3, BLOCKS)], psems.at[1]),
-        pltpu.make_async_copy(right, p_ref.at[lax.rem(col + 1, BLOCKS)], psems.at[2]),
-        pltpu.make_async_copy(far_a, p_ref.at[far, pl.ds(0, half)], psems.at[3]),
-        pltpu.make_async_copy(far_b, p_ref.at[far, pl.ds(half, half)], psems.at[4]),
-    ]
-    for copy in rcopies + pcopies:
+            size = 32
+            at = lax.rem(z + 4, 8) * 64 + (core if slot == 7 else 1 - core) * 32
+        rows = pl.ds(pl.multiple_of(at, size), size)
+        copies.append(pltpu.make_async_copy(chunks[slot], r_ref.at[rows], rsems.at[slot]))
+    for copy in copies:
         copy.start()
-    for copy in rcopies + pcopies:
+    copies = copies + fetch_columns(group, col, own, groups, p_ref, psems)
+    for copy in copies:
         copy.wait()
 
     @pl.loop(0, PW // TILE)
@@ -185,22 +195,21 @@
         out[:, at] = acc.astype(jnp.bfloat16)
 
 
-def apply_rows(where, own, left, right, far_a, far_b, chunks):
-    any_spec = pl.BlockSpec(memory_space=pl.ANY)
+def apply_rows(where, own, groups, chunks):
     return pl.pallas_call(
         apply_kernel,
         out_shape=jax.ShapeDtypeStruct((TILE, PW), jnp.bfloat16),
-        in_specs=[pl.BlockSpec(memory_space=pltpu.SMEM)] + [any_spec] * 13,
+        in_specs=[pl.BlockSpec(memory_space=pltpu.SMEM)] + [HBM] * (20 + CHUNKS),
         out_specs=pl.BlockSpec(memory_space=pltpu.VMEM),
         scratch_shapes=[
             pltpu.VMEM((BLOCKS, PW, TILE), jnp.bfloat16),
             pltpu.VMEM((TILE, PW), jnp.bfloat16),
-            pltpu.SemaphoreType.DMA((5,)),
             pltpu.SemaphoreType.DMA((8,)),
+            pltpu.SemaphoreType.DMA((CHUNKS,)),
         ],
         compiler_params=pltpu.CompilerParams(vmem_limit_bytes=40 << 20),
         name="apply_rows",
-    )(where, own, left, right, far_a, far_b, *chunks)
+    )(where, *own, *groups[0], *groups[1], *groups[2], *chunks)
 
 
 def device(child, z, ylo, core, col):
@@ -220,16 +229,26 @@
     return found
 
 
-def gather_columns(part):
+def group_of(child, z, ylo, core):
+    if (child, z, ylo) == (0, 0, 0):
+        return 0 if core == 0 else 2
+    return 1
+
+
+def gather_columns(own, group):
     def shift(by):
-        return pairs_of(lambda c, z, y, k, j: (c, z, y, k, (j + by) % 4))
-
-    half = PW // 2
-    left = lax.ppermute(part, ALL, shift(1))
-    right = lax.ppermute(part, ALL, shift(3))
-    far_a = lax.ppermute(left[:half], ALL, shift(1))
-    far_b = lax.ppermute(right[half:], ALL, shift(3))
-    return left, right, far_a, far_b
+        return pairs_of(
+            lambda c, z, y, k, j: (c, z, y, k, (j + by) % 4) if group_of(c, z, y, k) == group else None
+        )
+
+    upper, lower = own
+    left_a = lax.ppermute(upper, ALL, shift(1))
+    right_b = lax.ppermute(lower, ALL, shift(3))
+    left_b = lax.ppermute(lower, ALL, shift(1))
+    right_a = lax.ppermute(upper, ALL, shift(3))
+    far_a = lax.ppermute(left_a, ALL, shift(1))
+    far_b = lax.ppermute(right_b, ALL, shift(3))
+    return [left_a, left_b, right_a, right_b, far_a, far_b]
 
 
 def spread_rows(chunks, z, y, core):
@@ -254,17 +273,41 @@
         chunk, ALL, pairs_of(lambda c, zz, yy, kk, j: (c, zz, yy, 1, j) if kk == 0 else None)
     )
     chunk = jnp.where(core == 0, chunk, got)
-    ring = pairs_of(lambda c, zz, yy, kk, j: (c, (zz + 1 - 2 * kk) % 8, yy, kk, j))
     swap = pairs_of(lambda c, zz, yy, kk, j: (c, zz, yy, 1 - kk, j))
-    slots = [chunk]
-    swapped = []
-    current = chunk
-    for step in range(4):
-        current = lax.ppermute(current, ALL, ring)
-        slots.append(current)
-        if step < 3:
-            swapped.append(lax.ppermute(current, ALL, swap))
-    return slots + swapped
+    across = pairs_of(lambda c, zz, yy, kk, j: (c, (zz + 4) % 8, yy, kk, j))
+    part = lax.dynamic_slice_in_dim(chunk, core * 32, 32, 0)
+    half = lax.ppermute(part, ALL, across)
+    direct = {}
+    for by in (3, 2, 1):
+        pairs = pairs_of(lambda c, zz, yy, kk, j: (c, (zz + (1 - 2 * kk) * by) % 8, yy, kk, j))
+        direct[by] = lax.ppermute(chunk, ALL, pairs)
+    mine = [direct[by] for by in (1, 2, 3)]
+    theirs = [lax.ppermute(direct[by], ALL, swap) for by in (1, 2, 3)]
+    return [chunk] + mine + theirs + [half, lax.ppermute(half, ALL, swap)]
+
+
+def assemble(front, left, right, got_left, got_right):
+    tiles = right.shape[0]
+    left = jnp.concatenate([left, got_left], axis=0).reshape(2 * RANK, tiles, TILE)
+    right = jnp.concatenate([right, got_right], axis=1)
+    update = jnp.einsum("rtk,trn->tkn", left, right, preferred_element_type=jnp.float32)
+    update = update.reshape(tiles * TILE, TILE)
+    return (front.astype(jnp.float32) - update).astype(jnp.bfloat16)
+
+
+def assemble_halves(front, left, right, got_left, got_right):
+    half = PW // 2
+    tiles = right.shape[0] // 2
+    return [
+        assemble(
+            front[at * half : (at + 1) * half],
+            left[:, at * half : (at + 1) * half],
+            right[at * tiles : (at + 1) * tiles],
+            got_left[:, at * half : (at + 1) * half],
+            got_right[at * tiles : (at + 1) * tiles],
+        )
+        for at in range(2)
+    ]
 
 
 def shards(front, left_factors, right_factors):
@@ -274,27 +317,42 @@
     z, y, core = row // 4, 2 * side + (row // 2) % 2, row % 2
     left_all = left_factors[0, 0]
     right_all = right_factors[0]
-    half = PW
-    swap = [(0, 1), (1, 0)]
     tiles = right_all.shape[0] // 2
-    got_left = lax.ppermute(
-        lax.dynamic_slice_in_dim(left_all, (1 - side) * half, half, 1), "child", swap
-    )
-    got_right = lax.ppermute(
-        lax.dynamic_slice_in_dim(right_all, (1 - side) * tiles, tiles, 0), "child", swap
-    )
-    own_left = lax.dynamic_slice_in_dim(left_all, side * half, half, 1)
+    send_left = lax.dynamic_slice_in_dim(left_all, (1 - side) * PW, PW, 1)
+    send_right = lax.dynamic_slice_in_dim(right_all, (1 - side) * tiles, tiles, 0)
+    own_left = lax.dynamic_slice_in_dim(left_all, side * PW, PW, 1)
     own_right = lax.dynamic_slice_in_dim(right_all, side * tiles, tiles, 0)
-    left = jnp.concatenate([own_left, got_left], axis=0).reshape(2 * RANK, tiles, TILE)
-    right = jnp.concatenate([own_right, got_right], axis=1)
-    update = jnp.einsum("rtk,trn->tkn", left, right, preferred_element_type=jnp.float32)
-    panel_rows = (front.astype(jnp.float32) - update.reshape(PW, TILE)).astype(jnp.bfloat16)
-    parts = gather_columns(panel_rows)
-    is_root = jnp.logical_and(side == 0, row == 0).astype(jnp.int32)
-    where = jnp.stack([is_root, column, z, core]).astype(jnp.int32)
-    chunks = factor_rows(where, panel_rows, *parts)
+
+    def swap(first):
+        return pairs_of(
+            lambda c, zz, yy, kk, j: (1 - c, zz, yy, kk, j)
+            if first == ((c, zz, yy, kk) == (1, 0, 0, 0))
+            else None
+        )
+
+    top_left = lax.ppermute(send_left, ALL, swap(True))
+    top_right = lax.ppermute(send_right, ALL, swap(True))
+    top = assemble_halves(front, own_left, own_right, top_left, top_right)
+    top_parts = gather_columns(top, 0)
+    send_left, send_right, top_left, top_right = lax.optimization_barrier(
+        (send_left, send_right, top_left, top_right)
+    )
+    got_left = lax.ppermute(send_left, ALL, swap(False)) + top_left
+    got_right = lax.ppermute(send_right, ALL, swap(False)) + top_right
+    own = assemble_halves(front, own_left, own_right, got_left, got_right)
+    parts = gather_columns(own, 1)
+    group = jnp.where(jnp.logical_and(y == 0, z == 0), 2 * core, 1)
+    where = jnp.stack([group, column, z, core]).astype(jnp.int32)
+    token = lax.ppermute(
+        top_parts[4][:8, :128] + top_parts[5][:8, :128],
+        ALL,
+        pairs_of(lambda c, zz, yy, kk, j: (c, zz, yy, 1, j) if (c, zz, yy, kk) == (0, 0, 0, 0) else None),
+    )
+    late = lax.optimization_barrier((own[0], own[1], token))[:2]
+    late_parts = gather_columns(late, 2)
+    chunks = factor_rows(where, top, top_parts)
     chunks = spread_rows(chunks, z, y, core)
-    return apply_rows(where, panel_rows, *parts, chunks)
+    return apply_rows(where, own, [top_parts, parts, late_parts], chunks)
 
 
 def solution(mesh):

time: 206 us -> 224 us (1.087)
  starting transfers between devices: 34.8 us -> 82.4 us
  waiting for transfers between devices: 140 us -> 112 us
  local copies, waits for them, and re-layouts: 11.9 us -> 7.51 us
    ppermute x13 -> x30, starting transfers between devices: 23.3 us -> 74.4 us  [the longest x3 15.1 us: spread_rows(): direct[by] = lax.ppermute(chunk, ALL, pairs)]
    ppermute x13 -> x30, waiting for transfers between devices: 88.1 us -> 48.1 us  [the longest x3 17 us: gather_columns(): right_a = lax.ppermute(upper, ALL, shift(3))]
    ppermute x1, waiting for transfers between devices: 51.4 us -> 63.8 us  [spread_rows(): lax.ppermute(chunk, ALL, pairs_of(lambda c, zz, yy, kk, j: (c, zz, yy, 1,...]
    unnamed x30 -> x20, local copies, waits for them, and re-layouts: 7.07 us -> 3.68 us
  transfers between devices with their start and end apart: 24 -> 41, of which waited for: 11 -> 10; matrix products, arithmetic and copies ran while one was open for 2% -> 3% of each run, Pallas kernels for 0% -> 1%
where the time goes in v2:
time: 224 us; the launch traced here: 222 us
  waiting for transfers between devices  112 us (50%)
  starting transfers between devices  82.4 us (37%)
  Pallas kernels  12.8 us (6%)
  local copies, waits for them, and re-layouts  7.51 us (3%)
  other arithmetic  5.32 us (2%)
    ppermute x1, waiting for transfers between devices, spread_rows(): lax.ppermute(chunk, ALL, pairs_of(lambda c, zz, yy, kk, j: (c, zz, yy, 1,...  63.8 us
    ppermute x3, waiting for transfers between devices, gather_columns(): right_a = lax.ppermute(upper, ALL, shift(3))  17 us
    ppermute x3, starting transfers between devices, spread_rows(): direct[by] = lax.ppermute(chunk, ALL, pairs)  15.1 us
    ppermute x3, waiting for transfers between devices, gather_columns(): right_b = lax.ppermute(lower, ALL, shift(3))  14 us
    pallas_call x1, Pallas kernels, apply_rows(): pl.pallas_call(apply_kernel, out_shape=jax.ShapeDtypeStruct((TILE, PW), j...  10.7 us
    ppermute x3, starting transfers between devices, gather_columns(): far_a = lax.ppermute(left_a, ALL, shift(1))  8.72 us
    ppermute x3, waiting for transfers between devices, spread_rows(): direct[by] = lax.ppermute(chunk, ALL, pairs)  8.2 us
    ppermute x3, starting transfers between devices, gather_columns(): left_a = lax.ppermute(upper, ALL, shift(1))  7.35 us
  transfers between devices with their start and end apart: 41, of which 10 were waited for; matrix products, arithmetic and copies ran while one was open for 3% of the time, Pallas kernels for 1%

profile of v2, /device:TPU:7, one launch (start us, length us, event | category | flops | bytes accessed | tf_op | source)
XLA Modules:
  0.0 222.4 jit_solution(15257022769375599013)
XLA Ops:
  0.0 1.0 dynamic-slice_bitcast_fusion
  1.7 1.1 dynamic-slice_bitcast_fusion.1
  2.7 0.7 collective-permute-start
  3.4 1.0 dynamic-slice_bitcast_fusion.3
  4.5 4.8 %collective-permute-start.2 = (bf16[64,2048]{1,0:T(8,128)(2,1)S(1)}, bf16[64,2048]{1,0:T(8,128)(2,1)S(1)}, u32[]{:S(2)}, u32[]{:S(2)}) collective-permute-start(bf16[64,2048]{1,0:T(8,128)(2,1)S(1)} %get-tuple-element.19), channel_id=1, source_target_pairs={{0,128},{1,129},{2,130},{3,131},{4,132},{5,133},{6,134},{7,135},{8... | collective-permute-start | bytes 786440 | tf_op jit(solution)/shard_map/ppermute | solution.py:340
  9.3 2.0 collective-permute-start.3
  11.3 4.9 %collective-permute-done.2 = bf16[64,2048]{1,0:T(8,128)(2,1)S(1)} collective-permute-done((bf16[64,2048]{1,0:T(8,128)(2,1)S(1)}, bf16[64,2048]{1,0:T(8,128)(2,1)S(1)}, u32[]{:S(2)}, u32[]{:S(2)}) %collective-permute-start.2) | collective-permute-done | bytes 262176 | tf_op jit(solution)/shard_map/ppermute | solution.py:340
  17.2 1.9 collective-permute-done.3
  20.9 0.7 copy-done.6
  21.7 2.3 %fusion.3 = (bf16[1024,512]{1,0:T(8,128)(2,1)S(1)}, bf16[1024,512]{1,0:T(8,128)(2,1)}, bf16[1024,512]{1,0:T(8,128)(2,1)S(1)}, bf16[1024,512]{1,0:T(8,128)(2,1)S(1)}) fusion(f32[2,512,512]{2,1,0:T(8,128)S(1)} %fusion.5, bf16[2048,512]{1,0:T(8,128)(2,1)S(1)} %copy-done.6, f32[2,512,512]{2,1,0:T(8,128)S(1)} %fusion.7, f32[2,512,512]{2,1,0:T(8,128)S(1)} %fusion.4, ...), kind=kLoop, calls=%fused_computation.7 | loop fusion | flops 5242880 | bytes 14680064 | tf_op jit(solution)/shard_map/convert_element_type | solution.py:295
  24.0 0.7 collective-permute-start.7
  24.7 1.7 collective-permute-start.4
  26.4 1.6 collective-permute-start.5
  28.0 1.6 collective-permute-start.6
  29.7 1.7 collective-permute-start.9
  31.3 1.6 collective-permute-start.8
  33.0 2.4 %collective-permute-start.18 = (bf16[1024,512]{1,0:T(8,128)(2,1)S(1)}, bf16[1024,512]{1,0:T(8,128)(2,1)}, u32[]{:S(2)}, u32[]{:S(2)}) collective-permute-start(bf16[1024,512]{1,0:T(8,128)(2,1)S(1)} %get-tuple-element.23.refs_0_), channel_id=1, source_target_pairs={{4,7},{5,4},{6,5},{7,6}} | collective-permute-start | bytes 3145736 | tf_op jit(solution)/shard_map/ppermute | solution.py:248
  35.5 4.0 %collective-permute-start.16 = (bf16[1024,512]{1,0:T(8,128)(2,1)S(1)}, bf16[1024,512]{1,0:T(8,128)(2,1)}, u32[]{:S(2)}, u32[]{:S(2)}) collective-permute-start(bf16[1024,512]{1,0:T(8,128)(2,1)S(1)} %get-tuple-element.23.refs_0_), channel_id=1, source_target_pairs={{4,5},{5,6},{6,7},{7,4}} | collective-permute-start | bytes 3145736 | tf_op jit(solution)/shard_map/ppermute | solution.py:245
  40.2 2.1 factor_rows.1
  44.4 17.0 %collective-permute-done.18.refs_16_ = bf16[1024,512]{1,0:T(8,128)(2,1)} collective-permute-done((bf16[1024,512]{1,0:T(8,128)(2,1)S(1)}, bf16[1024,512]{1,0:T(8,128)(2,1)}, u32[]{:S(2)}, u32[]{:S(2)}) %collective-permute-start.18) | collective-permute-done | bytes 1048608 | tf_op jit(solution)/shard_map/ppermute | solution.py:248
  61.4 1.9 collective-permute-start.19
  63.3 4.6 %collective-permute-start.17 = (bf16[1024,512]{1,0:T(8,128)(2,1)S(1)}, bf16[1024,512]{1,0:T(8,128)(2,1)S(1)}, u32[]{:S(2)}, u32[]{:S(2)}) collective-permute-start(bf16[1024,512]{1,0:T(8,128)(2,1)S(1)} %get-tuple-element.24.refs_1_), channel_id=1, source_target_pairs={{4,5},{5,6},{6,7},{7,4}} | collective-permute-start | bytes 3145736 | tf_op jit(solution)/shard_map/ppermute | solution.py:247
  67.9 1.6 collective-permute-start.13
  72.3 0.7 collective-permute-start.11
  73.1 1.6 collective-permute-start.10
  74.7 1.1 add_select_fusion.1
  75.8 14.0 %collective-permute-done.19.refs_17_ = bf16[1024,512]{1,0:T(8,128)(2,1)} collective-permute-done((bf16[1024,512]{1,0:T(8,128)(2,1)S(1)}, bf16[1024,512]{1,0:T(8,128)(2,1)}, u32[]{:S(2)}, u32[]{:S(2)}) %collective-permute-start.19) | collective-permute-done | bytes 1048608 | tf_op jit(solution)/shard_map/ppermute | solution.py:246
  92.3 1.7 collective-permute-start.12
  94.0 5.4 %collective-permute-start.20 = (bf16[1024,512]{1,0:T(8,128)(2,1)}, bf16[1024,512]{1,0:T(8,128)(2,1)}, u32[]{:S(2)}, u32[]{:S(2)}) collective-permute-start(bf16[1024,512]{1,0:T(8,128)(2,1)} %collective-permute-done.16.refs_14_), channel_id=1, source_target_pairs={{4,5},{5,6},{6,7},{7,4}} | collective-permute-start | bytes 3145736 | tf_op jit(solution)/shard_map/ppermute | solution.py:249
  99.5 1.9 collective-permute-start.21
  101.5 1.0 copy-done.2
  102.5 1.6 collective-permute-start.15
  104.1 1.3 collective-permute-start.32
  105.4 63.8 %collective-permute-done.32 = bf16[64,2048]{1,0:T(8,128)(2,1)S(1)} collective-permute-done((bf16[64,2048]{1,0:T(8,128)(2,1)S(1)}, bf16[64,2048]{1,0:T(8,128)(2,1)S(1)}, u32[]{:S(2)}, u32[]{:S(2)}) %collective-permute-start.32) | collective-permute-done | bytes 262176 | tf_op jit(solution)/shard_map/ppermute | solution.py:272
  169.2 0.7 copy-done.9
  169.9 1.7 collective-permute-start.14
  171.6 1.0 broadcast_select_fusion.refs_20_
  172.6 13.8 %collective-permute-start.35 = (bf16[64,2048]{1,0:T(8,128)(2,1)S(1)}, bf16[64,2048]{1,0:T(8,128)(2,1)}, u32[]{:S(2)}, u32[]{:S(2)}) collective-permute-start(bf16[64,2048]{1,0:T(8,128)(2,1)S(1)} %broadcast_select_fusion.refs_20_), channel_id=1, source_target_pairs={{0,48},{1,49},{2,50},{3,51},{4,84},{5,85},{6,86},{7,87},{8,56},{9,... | collective-permute-start | bytes 786440 | tf_op jit(solution)/shard_map/ppermute | solution.py:283
  186.4 1.3 collective-permute-start.34
  187.7 5.6 %collective-permute-start.39 = (bf16[32,2048]{1,0:T(8,128)(2,1)S(1)}, bf16[32,2048]{1,0:T(8,128)(2,1)S(1)}, u32[]{:S(2)}, u32[]{:S(2)}) collective-permute-start(bf16[32,2048]{1,0:T(8,128)(2,1)S(1)} %constant_dynamic-slice_fusion), channel_id=1, source_target_pairs={{0,64},{1,65},{2,66},{3,67},{4,68},{5,69},{6,70},{7,71},{8,72},{9,... | collective-permute-start | bytes 393224 | tf_op jit(solution)/shard_map/ppermute | solution.py:279
  193.4 3.9 %collective-permute-start.38 = (bf16[64,2048]{1,0:T(8,128)(2,1)}, bf16[64,2048]{1,0:T(8,128)(2,1)S(1)}, u32[]{:S(2)}, u32[]{:S(2)}) collective-permute-start(bf16[64,2048]{1,0:T(8,128)(2,1)} %collective-permute-done.35.refs_23_), channel_id=1, source_target_pairs={{0,4},{1,5},{2,6},{3,7},{4,0},{5,1},{6,2},{7,3},{8,12},{9,13},{10,... | collective-permute-start | bytes 786440 | tf_op jit(solution)/shard_map/ppermute | solution.py:285
  197.3 4.9 %collective-permute-done.34.refs_22_ = bf16[64,2048]{1,0:T(8,128)(2,1)} collective-permute-done((bf16[64,2048]{1,0:T(8,128)(2,1)S(1)}, bf16[64,2048]{1,0:T(8,128)(2,1)}, u32[]{:S(2)}, u32[]{:S(2)}) %collective-permute-start.34) | collective-permute-done | bytes 262176 | tf_op jit(solution)/shard_map/ppermute | solution.py:283
  202.2 2.3 %collective-permute-start.37 = (bf16[64,2048]{1,0:T(8,128)(2,1)}, bf16[64,2048]{1,0:T(8,128)(2,1)S(1)}, u32[]{:S(2)}, u32[]{:S(2)}) collective-permute-start(bf16[64,2048]{1,0:T(8,128)(2,1)} %collective-permute-done.34.refs_22_), channel_id=1, source_target_pairs={{0,4},{1,5},{2,6},{3,7},{4,0},{5,1},{6,2},{7,3},{8,12},{9,13},{10,... | collective-permute-start | bytes 786440 | tf_op jit(solution)/shard_map/ppermute | solution.py:285
  204.6 3.3 %collective-permute-done.33.refs_21_ = bf16[64,2048]{1,0:T(8,128)(2,1)} collective-permute-done((bf16[64,2048]{1,0:T(8,128)(2,1)S(1)}, bf16[64,2048]{1,0:T(8,128)(2,1)}, u32[]{:S(2)}, u32[]{:S(2)}) %collective-permute-start.33) | collective-permute-done | bytes 262176 | tf_op jit(solution)/shard_map/ppermute | solution.py:283
  207.8 0.9 collective-permute-start.36
  208.7 1.3 collective-permute-done.40.refs_28_
  210.3 1.2 copy-done.3
  211.5 10.7 %apply_rows.1 = bf16[512,2048]{1,0:T(8,128)(2,1)} custom-call(s32[4]{0:T(128)S(1)} %copy-done.4, bf16[1024,512]{1,0:T(8,128)(2,1)S(1)} %get-tuple-element.23.refs_0_, bf16[1024,512]{1,0:T(8,128)(2,1)S(1)} %get-tuple-element.24.refs_1_, bf16[1024,512]{1,0:T(8,128)(2,1)} %collective-permute-done.4.refs_2_, bf16[1024,512]{1,0:T(8,128)(2,1)} %collective-permute-done.5.refs_3_, ...), custom_call_target="tpu_custom_call" | custom-call | tf_op jit(solution)/shard_map/apply_rows/pallas_call | solution.py:199
  (81 shorter events, 11.5 us)
Async XLA Ops:
  1.0 3.5 %collective-permute-start.1 = (bf16[4,64,512]{2,1,0:T(8,128)(2,1)S(1)}, bf16[4,64,512]{2,1,0:T(8,128)(2,1)S(1)}, u32[]{:S(2)}, u32[]{:S(2)}) collective-permute-start(bf16[4,64,512]{2,1,0:T(8,128)(2,1)S(1)} %dynamic-slice_bitcast_fusion), channel_id=1, source_target_pairs={{128,0},{129,1},{130,2},{131,3}} | collective-permute-start | bytes 786440 | tf_op jit(solution)/shard_map/ppermute | solution.py:334
  2.7 1.7 collective-permute-start
  4.5 11.8 %collective-permute-start.2 = (bf16[64,2048]{1,0:T(8,128)(2,1)S(1)}, bf16[64,2048]{1,0:T(8,128)(2,1)S(1)}, u32[]{:S(2)}, u32[]{:S(2)}) collective-permute-start(bf16[64,2048]{1,0:T(8,128)(2,1)S(1)} %get-tuple-element.19), channel_id=1, source_target_pairs={{0,128},{1,129},{2,130},{3,131},{4,132},{5,133},{6,134},{7,135},{8... | collective-permute-start | bytes 786440 | tf_op jit(solution)/shard_map/ppermute | solution.py:340
  9.3 9.8 %collective-permute-start.3 = (bf16[4,64,512]{2,1,0:T(8,128)(2,1)S(1)}, bf16[4,64,512]{2,1,0:T(8,128)(2,1)S(1)}, u32[]{:S(2)}, u32[]{:S(2)}) collective-permute-start(bf16[4,64,512]{2,1,0:T(8,128)(2,1)S(1)} %dynamic-slice_bitcast_fusion), channel_id=1, source_target_pairs={{0,128},{1,129},{2,130},{3,131},{4,132},{5,133},{6,134},{7,135},{8... | collective-permute-start | bytes 786440 | tf_op jit(solution)/shard_map/ppermute | solution.py:341
  20.1 1.6 copy-start.6
  24.0 11.5 %copy-start.5 = (bf16[1024,512]{1,0:T(8,128)(2,1)}, bf16[1024,512]{1,0:T(8,128)(2,1)S(1)}, u32[]{:S(2)}) copy-start(bf16[1024,512]{1,0:T(8,128)(2,1)S(1)} %get-tuple-element.33.refs_1_) | copy-start | bytes 3145732
  24.0 5.7 %collective-permute-start.7 = (bf16[1024,512]{1,0:T(8,128)(2,1)S(1)}, bf16[1024,512]{1,0:T(8,128)(2,1)S(1)}, u32[]{:S(2)}, u32[]{:S(2)}) collective-permute-start(bf16[1024,512]{1,0:T(8,128)(2,1)S(1)} %get-tuple-element.33.refs_1_), channel_id=1, source_target_pairs={{0,3},{1,0},{2,1},{3,2}} | collective-permute-start | bytes 3145736 | tf_op jit(solution)/shard_map/ppermute | solution.py:246
  24.7 6.6 %collective-permute-start.4 = (bf16[1024,512]{1,0:T(8,128)(2,1)}, bf16[1024,512]{1,0:T(8,128)(2,1)}, u32[]{:S(2)}, u32[]{:S(2)}) collective-permute-start(bf16[1024,512]{1,0:T(8,128)(2,1)} %get-tuple-element.34.refs_0_), channel_id=1, source_target_pairs={{0,1},{1,2},{2,3},{3,0}} | collective-permute-start | bytes 3145736 | tf_op jit(solution)/shard_map/ppermute | solution.py:245
  26.4 9.1 %collective-permute-start.5 = (bf16[1024,512]{1,0:T(8,128)(2,1)S(1)}, bf16[1024,512]{1,0:T(8,128)(2,1)}, u32[]{:S(2)}, u32[]{:S(2)}) collective-permute-start(bf16[1024,512]{1,0:T(8,128)(2,1)S(1)} %get-tuple-element.33.refs_1_), channel_id=1, source_target_pairs={{0,1},{1,2},{2,3},{3,0}} | collective-permute-start | bytes 3145736 | tf_op jit(solution)/shard_map/ppermute | solution.py:247
  28.0 12.1 %collective-permute-start.6 = (bf16[1024,512]{1,0:T(8,128)(2,1)}, bf16[1024,512]{1,0:T(8,128)(2,1)}, u32[]{:S(2)}, u32[]{:S(2)}) collective-permute-start(bf16[1024,512]{1,0:T(8,128)(2,1)} %get-tuple-element.34.refs_0_), channel_id=1, source_target_pairs={{0,3},{1,0},{2,1},{3,2}} | collective-permute-start | bytes 3145736 | tf_op jit(solution)/shard_map/ppermute | solution.py:248
  29.7 10.5 %copy-start = (bf16[1024,512]{1,0:T(8,128)(2,1)}, bf16[1024,512]{1,0:T(8,128)(2,1)S(1)}, u32[]{:S(2)}) copy-start(bf16[1024,512]{1,0:T(8,128)(2,1)S(1)} %collective-permute-done.7.refs_5_) | copy-start | bytes 3145732
  29.7 10.5 %collective-permute-start.9 = (bf16[1024,512]{1,0:T(8,128)(2,1)S(1)}, bf16[1024,512]{1,0:T(8,128)(2,1)}, u32[]{:S(2)}, u32[]{:S(2)}) collective-permute-start(bf16[1024,512]{1,0:T(8,128)(2,1)S(1)} %collective-permute-done.7.refs_5_), channel_id=1, source_target_pairs={{0,3},{1,0},{2,1},{3,2}} | collective-permute-start | bytes 3145736 | tf_op jit(solution)/shard_map/ppermute | solution.py:250
  31.3 8.8 %collective-permute-start.8 = (bf16[1024,512]{1,0:T(8,128)(2,1)}, bf16[1024,512]{1,0:T(8,128)(2,1)}, u32[]{:S(2)}, u32[]{:S(2)}) collective-permute-start(bf16[1024,512]{1,0:T(8,128)(2,1)} %collective-permute-done.4.refs_2_), channel_id=1, source_target_pairs={{0,1},{1,2},{2,3},{3,0}} | collective-permute-start | bytes 3145736 | tf_op jit(solution)/shard_map/ppermute | solution.py:249
  33.0 28.4 %collective-permute-start.18 = (bf16[1024,512]{1,0:T(8,128)(2,1)S(1)}, bf16[1024,512]{1,0:T(8,128)(2,1)}, u32[]{:S(2)}, u32[]{:S(2)}) collective-permute-start(bf16[1024,512]{1,0:T(8,128)(2,1)S(1)} %get-tuple-element.23.refs_0_), channel_id=1, source_target_pairs={{4,7},{5,4},{6,5},{7,6}} | collective-permute-start | bytes 3145736 | tf_op jit(solution)/shard_map/ppermute | solution.py:248
  35.5 27.9 %collective-permute-start.16 = (bf16[1024,512]{1,0:T(8,128)(2,1)S(1)}, bf16[1024,512]{1,0:T(8,128)(2,1)}, u32[]{:S(2)}, u32[]{:S(2)}) collective-permute-start(bf16[1024,512]{1,0:T(8,128)(2,1)S(1)} %get-tuple-element.23.refs_0_), channel_id=1, source_target_pairs={{4,5},{5,6},{6,7},{7,4}} | collective-permute-start | bytes 3145736 | tf_op jit(solution)/shard_map/ppermute | solution.py:245
  42.3 25.6 %collective-permute-start.22 = (bf16[64,2048]{1,0:T(8,128)(2,1)}, bf16[64,2048]{1,0:T(8,128)(2,1)S(1)}, u32[]{:S(2)}, u32[]{:S(2)}) collective-permute-start(bf16[64,2048]{1,0:T(8,128)(2,1)} %get-tuple-element.26), channel_id=1, source_target_pairs={{0,16},{1,17},{2,18},{3,19}} | collective-permute-start | bytes 786440 | tf_op jit(solution)/shard_map/ppermute | solution.py:261
  43.0 26.5 %collective-permute-start.23 = (bf16[64,2048]{1,0:T(8,128)(2,1)}, bf16[64,2048]{1,0:T(8,128)(2,1)S(1)}, u32[]{:S(2)}, u32[]{:S(2)}) collective-permute-start(bf16[64,2048]{1,0:T(8,128)(2,1)} %get-tuple-element.27), channel_id=1, source_target_pairs={{0,32},{1,33},{2,34},{3,35}} | collective-permute-start | bytes 786440 | tf_op jit(solution)/shard_map/ppermute | solution.py:261
  43.7 26.5 %collective-permute-start.24 = (bf16[64,2048]{1,0:T(8,128)(2,1)}, bf16[64,2048]{1,0:T(8,128)(2,1)S(1)}, u32[]{:S(2)}, u32[]{:S(2)}) collective-permute-start(bf16[64,2048]{1,0:T(8,128)(2,1)} %get-tuple-element.28), channel_id=1, source_target_pairs={{0,48},{1,49},{2,50},{3,51}} | collective-permute-start | bytes 786440 | tf_op jit(solution)/shard_map/ppermute | solution.py:261
  61.4 28.4 %collective-permute-start.19 = (bf16[1024,512]{1,0:T(8,128)(2,1)S(1)}, bf16[1024,512]{1,0:T(8,128)(2,1)}, u32[]{:S(2)}, u32[]{:S(2)}) collective-permute-start(bf16[1024,512]{1,0:T(8,128)(2,1)S(1)} %get-tuple-element.24.refs_1_), channel_id=1, source_target_pairs={{4,7},{5,4},{6,5},{7,6}} | collective-permute-start | bytes 3145736 | tf_op jit(solution)/shard_map/ppermute | solution.py:246
  63.3 27.6 %collective-permute-start.17 = (bf16[1024,512]{1,0:T(8,128)(2,1)S(1)}, bf16[1024,512]{1,0:T(8,128)(2,1)S(1)}, u32[]{:S(2)}, u32[]{:S(2)}) collective-permute-start(bf16[1024,512]{1,0:T(8,128)(2,1)S(1)} %get-tuple-element.24.refs_1_), channel_id=1, source_target_pairs={{4,5},{5,6},{6,7},{7,4}} | collective-permute-start | bytes 3145736 | tf_op jit(solution)/shard_map/ppermute | solution.py:247
  67.9 23.7 %collective-permute-start.13 = (bf16[1024,512]{1,0:T(8,128)(2,1)S(1)}, bf16[1024,512]{1,0:T(8,128)(2,1)}, u32[]{:S(2)}, u32[]{:S(2)}) collective-permute-start(bf16[1024,512]{1,0:T(8,128)(2,1)S(1)} %get-tuple-element.24.refs_1_), channel_id=1, source_target_pairs={{8,11},{9,8},{10,9},{11,10},{12,15},{13,12},{14,13},{15,14},{16,19... | collective-permute-start | bytes 3145736 | tf_op jit(solution)/shard_map/ppermute | solution.py:246
  69.5 1.4 collective-permute-start.25
  70.2 1.4 collective-permute-start.26
  70.9 1.4 collective-permute-start.27
  71.6 1.4 collective-permute-start.28
  72.3 29.1 %collective-permute-start.11 = (bf16[1024,512]{1,0:T(8,128)(2,1)S(1)}, bf16[1024,512]{1,0:T(8,128)(2,1)S(1)}, u32[]{:S(2)}, u32[]{:S(2)}) collective-permute-start(bf16[1024,512]{1,0:T(8,128)(2,1)S(1)} %get-tuple-element.24.refs_1_), channel_id=1, source_target_pairs={{8,9},{9,10},{10,11},{11,8},{12,13},{13,14},{14,15},{15,12},{16,17... | collective-permute-start | bytes 3145736 | tf_op jit(solution)/shard_map/ppermute | solution.py:247
  73.1 31.0 %collective-permute-start.10 = (bf16[1024,512]{1,0:T(8,128)(2,1)S(1)}, bf16[1024,512]{1,0:T(8,128)(2,1)}, u32[]{:S(2)}, u32[]{:S(2)}) collective-permute-start(bf16[1024,512]{1,0:T(8,128)(2,1)S(1)} %get-tuple-element.23.refs_0_), channel_id=1, source_target_pairs={{8,9},{9,10},{10,11},{11,8},{12,13},{13,14},{14,15},{15,12},{16,17... | collective-permute-start | bytes 3145736 | tf_op jit(solution)/shard_map/ppermute | solution.py:245
  74.7 135.6 %copy-start.1 = (bf16[1024,512]{1,0:T(8,128)(2,1)S(1)}, bf16[1024,512]{1,0:T(8,128)(2,1)}, u32[]{:S(2)}) copy-start(bf16[1024,512]{1,0:T(8,128)(2,1)} %copy-done) | copy-start | bytes 3145732
  74.7 135.6 %copy-start.4 = (s32[4]{0:T(128)S(1)}, s32[4]{0:T(128)}, u32[]{:S(2)}) copy-start(s32[4]{0:T(128)} %pad_add_fusion.where_ref) | copy-start | bytes 52
  89.8 2.5 %collective-permute-start.31 = (bf16[64,2048]{1,0:T(8,128)(2,1)S(1)}, bf16[64,2048]{1,0:T(8,128)(2,1)S(1)}, u32[]{:S(2)}, u32[]{:S(2)}) collective-permute-start(bf16[64,2048]{1,0:T(8,128)(2,1)S(1)} %add_select_fusion.1), channel_id=1, source_target_pairs={{0,128},{1,129},{2,130},{3,131},{16,144},{17,145},{18,146},{19,147... | collective-permute-start | bytes 786440 | tf_op jit(solution)/shard_map/ppermute | solution.py:269
  90.9 13.2 %copy-start.7 = (bf16[1024,512]{1,0:T(8,128)(2,1)}, bf16[1024,512]{1,0:T(8,128)(2,1)S(1)}, u32[]{:S(2)}) copy-start(bf16[1024,512]{1,0:T(8,128)(2,1)S(1)} %collective-permute-done.17.refs_15_) | copy-start | bytes 3145732
  90.9 3.1 %collective-permute-start.30 = (bf16[64,2048]{1,0:T(8,128)(2,1)S(1)}, bf16[64,2048]{1,0:T(8,128)(2,1)S(1)}, u32[]{:S(2)}, u32[]{:S(2)}) collective-permute-start(bf16[64,2048]{1,0:T(8,128)(2,1)S(1)} %add_select_fusion.1), channel_id=1, source_target_pairs={{0,136},{1,137},{2,138},{3,139},{16,152},{17,153},{18,154},{19,155... | collective-permute-start | bytes 786440 | tf_op jit(solution)/shard_map/ppermute | solution.py:269
  91.6 7.8 %collective-permute-start.29 = (bf16[64,2048]{1,0:T(8,128)(2,1)S(1)}, bf16[64,2048]{1,0:T(8,128)(2,1)S(1)}, u32[]{:S(2)}, u32[]{:S(2)}) collective-permute-start(bf16[64,2048]{1,0:T(8,128)(2,1)S(1)} %add_select_fusion.1), channel_id=1, source_target_pairs={{0,8},{1,9},{2,10},{3,11},{16,24},{17,25},{18,26},{19,27},{32,40},... | collective-permute-start | bytes 786440 | tf_op jit(solution)/shard_map/ppermute | solution.py:269
  92.3 80.3 %collective-permute-start.12 = (bf16[1024,512]{1,0:T(8,128)(2,1)S(1)}, bf16[1024,512]{1,0:T(8,128)(2,1)}, u32[]{:S(2)}, u32[]{:S(2)}) collective-permute-start(bf16[1024,512]{1,0:T(8,128)(2,1)S(1)} %get-tuple-element.23.refs_0_), channel_id=1, source_target_pairs={{8,11},{9,8},{10,9},{11,10},{12,15},{13,12},{14,13},{15,14},{16,19... | collective-permute-start | bytes 3145736 | tf_op jit(solution)/shard_map/ppermute | solution.py:248
  94.0 92.3 %collective-permute-start.20 = (bf16[1024,512]{1,0:T(8,128)(2,1)}, bf16[1024,512]{1,0:T(8,128)(2,1)}, u32[]{:S(2)}, u32[]{:S(2)}) collective-permute-start(bf16[1024,512]{1,0:T(8,128)(2,1)} %collective-permute-done.16.refs_14_), channel_id=1, source_target_pairs={{4,5},{5,6},{6,7},{7,4}} | collective-permute-start | bytes 3145736 | tf_op jit(solution)/shard_map/ppermute | solution.py:249
  99.5 88.2 %collective-permute-start.21 = (bf16[1024,512]{1,0:T(8,128)(2,1)}, bf16[1024,512]{1,0:T(8,128)(2,1)}, u32[]{:S(2)}, u32[]{:S(2)}) collective-permute-start(bf16[1024,512]{1,0:T(8,128)(2,1)} %collective-permute-done.19.refs_17_), channel_id=1, source_target_pairs={{4,7},{5,4},{6,5},{7,6}} | collective-permute-start | bytes 3145736 | tf_op jit(solution)/shard_map/ppermute | solution.py:250
  101.4 4.0 %copy-start.8 = (bf16[64,2048]{1,0:T(8,128)(2,1)}, bf16[64,2048]{1,0:T(8,128)(2,1)S(1)}, u32[]{:S(2)}) copy-start(bf16[64,2048]{1,0:T(8,128)(2,1)S(1)} %add_select_fusion) | copy-start | bytes 786436
  102.5 85.2 %collective-permute-start.15 = (bf16[1024,512]{1,0:T(8,128)(2,1)}, bf16[1024,512]{1,0:T(8,128)(2,1)}, u32[]{:S(2)}, u32[]{:S(2)}) collective-permute-start(bf16[1024,512]{1,0:T(8,128)(2,1)} %collective-permute-done.13.refs_11_), channel_id=1, source_target_pairs={{8,11},{9,8},{10,9},{11,10},{12,15},{13,12},{14,13},{15,14},{16,19... | collective-permute-start | bytes 3145736 | tf_op jit(solution)/shard_map/ppermute | solution.py:250
  104.1 65.1 %collective-permute-start.32 = (bf16[64,2048]{1,0:T(8,128)(2,1)S(1)}, bf16[64,2048]{1,0:T(8,128)(2,1)S(1)}, u32[]{:S(2)}, u32[]{:S(2)}) collective-permute-start(bf16[64,2048]{1,0:T(8,128)(2,1)S(1)} %add_select_fusion), channel_id=1, source_target_pairs={{0,4},{1,5},{2,6},{3,7},{8,12},{9,13},{10,14},{11,15},{16,20},{17,... | collective-permute-start | bytes 786440 | tf_op jit(solution)/shard_map/ppermute | solution.py:272
  169.9 38.8 %collective-permute-start.14 = (bf16[1024,512]{1,0:T(8,128)(2,1)}, bf16[1024,512]{1,0:T(8,128)(2,1)}, u32[]{:S(2)}, u32[]{:S(2)}) collective-permute-start(bf16[1024,512]{1,0:T(8,128)(2,1)} %collective-permute-done.10.refs_8_), channel_id=1, source_target_pairs={{8,9},{9,10},{10,11},{11,8},{12,13},{13,14},{14,15},{15,12},{16,17... | collective-permute-start | bytes 3145736 | tf_op jit(solution)/shard_map/ppermute | solution.py:249
  172.6 20.8 %collective-permute-start.35 = (bf16[64,2048]{1,0:T(8,128)(2,1)S(1)}, bf16[64,2048]{1,0:T(8,128)(2,1)}, u32[]{:S(2)}, u32[]{:S(2)}) collective-permute-start(bf16[64,2048]{1,0:T(8,128)(2,1)S(1)} %broadcast_select_fusion.refs_20_), channel_id=1, source_target_pairs={{0,48},{1,49},{2,50},{3,51},{4,84},{5,85},{6,86},{7,87},{8,56},{9,... | collective-permute-start | bytes 786440 | tf_op jit(solution)/shard_map/ppermute | solution.py:283
  186.4 15.9 %collective-permute-start.34 = (bf16[64,2048]{1,0:T(8,128)(2,1)S(1)}, bf16[64,2048]{1,0:T(8,128)(2,1)}, u32[]{:S(2)}, u32[]{:S(2)}) collective-permute-start(bf16[64,2048]{1,0:T(8,128)(2,1)S(1)} %broadcast_select_fusion.refs_20_), channel_id=1, source_target_pairs={{0,32},{1,33},{2,34},{3,35},{4,100},{5,101},{6,102},{7,103},{8,40}... | collective-permute-start | bytes 786440 | tf_op jit(solution)/shard_map/ppermute | solution.py:283
  187.7 20.1 %collective-permute-start.33 = (bf16[64,2048]{1,0:T(8,128)(2,1)S(1)}, bf16[64,2048]{1,0:T(8,128)(2,1)}, u32[]{:S(2)}, u32[]{:S(2)}) collective-permute-start(bf16[64,2048]{1,0:T(8,128)(2,1)S(1)} %broadcast_select_fusion.refs_20_), channel_id=1, source_target_pairs={{0,16},{1,17},{2,18},{3,19},{4,116},{5,117},{6,118},{7,119},{8,24}... | collective-permute-start | bytes 786440 | tf_op jit(solution)/shard_map/ppermute | solution.py:283
  187.7 21.0 %collective-permute-start.39 = (bf16[32,2048]{1,0:T(8,128)(2,1)S(1)}, bf16[32,2048]{1,0:T(8,128)(2,1)S(1)}, u32[]{:S(2)}, u32[]{:S(2)}) collective-permute-start(bf16[32,2048]{1,0:T(8,128)(2,1)S(1)} %constant_dynamic-slice_fusion), channel_id=1, source_target_pairs={{0,64},{1,65},{2,66},{3,67},{4,68},{5,69},{6,70},{7,71},{8,72},{9,... | collective-permute-start | bytes 393224 | tf_op jit(solution)/shard_map/ppermute | solution.py:279
  193.4 16.7 %collective-permute-start.38 = (bf16[64,2048]{1,0:T(8,128)(2,1)}, bf16[64,2048]{1,0:T(8,128)(2,1)S(1)}, u32[]{:S(2)}, u32[]{:S(2)}) collective-permute-start(bf16[64,2048]{1,0:T(8,128)(2,1)} %collective-permute-done.35.refs_23_), channel_id=1, source_target_pairs={{0,4},{1,5},{2,6},{3,7},{4,0},{5,1},{6,2},{7,3},{8,12},{9,13},{10,... | collective-permute-start | bytes 786440 | tf_op jit(solution)/shard_map/ppermute | solution.py:285
  202.2 7.9 %collective-permute-start.37 = (bf16[64,2048]{1,0:T(8,128)(2,1)}, bf16[64,2048]{1,0:T(8,128)(2,1)S(1)}, u32[]{:S(2)}, u32[]{:S(2)}) collective-permute-start(bf16[64,2048]{1,0:T(8,128)(2,1)} %collective-permute-done.34.refs_22_), channel_id=1, source_target_pairs={{0,4},{1,5},{2,6},{3,7},{4,0},{5,1},{6,2},{7,3},{8,12},{9,13},{10,... | collective-permute-start | bytes 786440 | tf_op jit(solution)/shard_map/ppermute | solution.py:285
  207.8 2.5 %collective-permute-start.36 = (bf16[64,2048]{1,0:T(8,128)(2,1)}, bf16[64,2048]{1,0:T(8,128)(2,1)S(1)}, u32[]{:S(2)}, u32[]{:S(2)}) collective-permute-start(bf16[64,2048]{1,0:T(8,128)(2,1)} %collective-permute-done.33.refs_21_), channel_id=1, source_target_pairs={{0,4},{1,5},{2,6},{3,7},{4,0},{5,1},{6,2},{7,3},{8,12},{9,13},{10,... | collective-permute-start | bytes 786440 | tf_op jit(solution)/shard_map/ppermute | solution.py:285
  208.7 1.3 collective-permute-start.40
  (3 other events, 2.9 us)

commit v3 on v2

--- a/solution.py
+++ b/solution.py
@@ -54,36 +54,50 @@
     x_ref[...] = ((diag.astype(jnp.float32) - n_ref[...]) * across).astype(jnp.bfloat16)
 
 
-def fetch_columns(group, col, own, groups, dest, sems):
-    half = PW // 2
-
-    def copies(parts):
-        found = []
-        for slot, part in enumerate(own + parts):
-            column = lax.rem(col + (0, 3, 1, 2)[slot // 2], BLOCKS)
-            rows = pl.ds((slot % 2) * half, half)
-            found.append(pltpu.make_async_copy(part, dest.at[column, rows], sems.at[slot]))
-        return found
-
-    for index, parts in enumerate(groups):
-
-        @pl.when(group == index)
+HALF = PW // 2
+HBM = pl.BlockSpec(memory_space=pltpu.HBM)
+
+
+def column_copies(col, next_parts, wrap_parts, far_parts, dest, sems):
+    size = PW // len(next_parts)
+    found = {1: [], 2: [], 3: []}
+    for at in range(len(next_parts)):
+        rows = pl.ds(at * size, size)
+        slots = [3 * at, 3 * at + 1, 3 * at + 2]
+        found[1].append(
+            pltpu.make_async_copy(next_parts[at], dest.at[col - 1, rows], sems.at[slots[0]])
+        )
+        found[2].append(
+            pltpu.make_async_copy(far_parts[at], dest.at[col - 2, rows], sems.at[slots[1]])
+        )
+        found[3].append(pltpu.make_async_copy(wrap_parts[at], dest.at[0, rows], sems.at[slots[2]]))
+
+    for least in (1, 2, 3):
+
+        @pl.when(col >= least)
         def _():
-            for copy in copies(parts):
+            for copy in found[least]:
                 copy.start()
 
-    return copies(groups[0])
-
-
-def factor_kernel(where_ref, *refs):
-    own, parts, outs = list(refs[:2]), list(refs[2:8]), refs[8:16]
-    t_ref, s_ref, l_ref, x_ref, r_ref, g_ref, n_ref, e_ref, sems = refs[16:]
+    for least in (1, 2, 3):
+
+        @pl.when(col >= least)
+        def _():
+            for copy in found[least]:
+                copy.wait()
+
+
+def factor_kernel(where_ref, own, *refs):
+    tops, outs = refs[:6], refs[6:14]
+    t_ref, s_ref, l_ref, x_ref, r_ref, g_ref, n_ref, e_ref, sems = refs[14:]
     col = where_ref[1]
 
     @pl.when(where_ref[0] == 0)
     def _():
-        for copy in fetch_columns(0, col, own, [parts], t_ref, sems):
-            copy.wait()
+        mine = pltpu.make_async_copy(own, t_ref.at[col], sems.at[6])
+        mine.start()
+        column_copies(col, tops[0:2], tops[2:4], tops[4:6], t_ref, sems)
+        mine.wait()
 
         def rows_of(i):
             return pl.ds(pl.multiple_of(i * TILE, TILE), TILE)
@@ -136,11 +150,11 @@
 HBM = pl.BlockSpec(memory_space=pltpu.HBM)
 
 
-def factor_rows(where, own, parts):
+def factor_rows(where, own, tops):
     return pl.pallas_call(
         factor_kernel,
         out_shape=[jax.ShapeDtypeStruct((64, PW), jnp.bfloat16)] * 8,
-        in_specs=[pl.BlockSpec(memory_space=pltpu.SMEM)] + [HBM] * 8,
+        in_specs=[pl.BlockSpec(memory_space=pltpu.SMEM)] + [HBM] * 7,
         out_specs=[pl.BlockSpec(memory_space=pltpu.VMEM)] * 8,
         scratch_shapes=[
             pltpu.VMEM((BLOCKS, PW, TILE), jnp.bfloat16),
@@ -151,21 +165,20 @@
             pltpu.VMEM((TILE, TILE), jnp.float32),
             pltpu.VMEM((TILE, TILE), jnp.float32),
             pltpu.VMEM((TILE, TILE), jnp.bfloat16),
-            pltpu.SemaphoreType.DMA((8,)),
+            pltpu.SemaphoreType.DMA((7,)),
         ],
         compiler_params=pltpu.CompilerParams(vmem_limit_bytes=56 << 20),
         name="factor_rows",
-    )(where, *own, *parts)
+    )(where, own, *tops)
 
 
 CHUNKS = 9
 
 
-def apply_kernel(where_ref, *refs):
-    own = list(refs[:2])
-    groups = [list(refs[2 + 6 * g : 8 + 6 * g]) for g in range(3)]
-    chunks = refs[20 : 20 + CHUNKS]
-    out, p_ref, r_ref, psems, rsems = refs[20 + CHUNKS :]
+def apply_kernel(where_ref, own, *refs):
+    main, late, tops = refs[:3], refs[3:6], refs[6:12]
+    chunks = refs[12 : 12 + CHUNKS]
+    out, p_ref, r_ref, acc_ref, psems, rsems = refs[13 + CHUNKS :]
     group, col, z, core = where_ref[0], where_ref[1], where_ref[2], where_ref[3]
     sign = 1 - 2 * core
     copies = []
@@ -180,36 +193,52 @@
             at = lax.rem(z + 4, 8) * 64 + (core if slot == 7 else 1 - core) * 32
         rows = pl.ds(pl.multiple_of(at, size), size)
         copies.append(pltpu.make_async_copy(chunks[slot], r_ref.at[rows], rsems.at[slot]))
+    copies.append(pltpu.make_async_copy(own, p_ref.at[col], psems.at[6]))
     for copy in copies:
         copy.start()
-    copies = copies + fetch_columns(group, col, own, groups, p_ref, psems)
+
+    @pl.when(group == 0)
+    def _():
+        column_copies(col, tops[0:2], tops[2:4], tops[4:6], p_ref, psems)
+
+    for index, parts in ((1, main), (2, late)):
+
+        @pl.when(group == index)
+        def _():
+            column_copies(col, parts[0:1], parts[1:2], parts[2:3], p_ref, psems)
+
     for copy in copies:
         copy.wait()
 
     @pl.loop(0, PW // TILE)
     def _(tile):
         at = pl.ds(pl.multiple_of(tile * TILE, TILE), TILE)
-        acc = jnp.zeros((TILE, TILE), jnp.float32)
-        for k in range(BLOCKS):
-            acc = acc + mxu(r_ref[:, k * TILE : (k + 1) * TILE], p_ref[k, at, :], NT)
-        out[:, at] = acc.astype(jnp.bfloat16)
-
-
-def apply_rows(where, own, groups, chunks):
+        acc_ref[...] = mxu(r_ref[:, :TILE], p_ref[0, at, :], NT)
+        for k in range(1, BLOCKS):
+
+            @pl.when(k <= col)
+            def _():
+                acc_ref[...] += mxu(r_ref[:, k * TILE : (k + 1) * TILE], p_ref[k, at, :], NT)
+
+        out[:, at] = acc_ref[...].astype(jnp.bfloat16)
+
+
+def apply_rows(where, own, main, late, tops, chunks, token):
     return pl.pallas_call(
         apply_kernel,
         out_shape=jax.ShapeDtypeStruct((TILE, PW), jnp.bfloat16),
-        in_specs=[pl.BlockSpec(memory_space=pltpu.SMEM)] + [HBM] * (20 + CHUNKS),
+        in_specs=[pl.BlockSpec(memory_space=pltpu.SMEM)] + [HBM] * (14 + CHUNKS),
         out_specs=pl.BlockSpec(memory_space=pltpu.VMEM),
         scratch_shapes=[
             pltpu.VMEM((BLOCKS, PW, TILE), jnp.bfloat16),
             pltpu.VMEM((TILE, PW), jnp.bfloat16),
-            pltpu.SemaphoreType.DMA((8,)),
+            pltpu.VMEM((TILE, TILE), jnp.float32),
+            pltpu.SemaphoreType.DMA((7,)),
             pltpu.SemaphoreType.DMA((CHUNKS,)),
         ],
         compiler_params=pltpu.CompilerParams(vmem_limit_bytes=40 << 20),
         name="apply_rows",
-    )(where, *own, *groups[0], *groups[1], *groups[2], *chunks)
+    )(where, own, *main, *late, *tops, *chunks, token)
 
 
 def device(child, z, ylo, core, col):
@@ -229,29 +258,41 @@
     return found
 
 
-def group_of(child, z, ylo, core):
-    if (child, z, ylo) == (0, 0, 0):
-        return 0 if core == 0 else 2
-    return 1
-
-
-def gather_columns(own, group):
-    def shift(by):
-        return pairs_of(
-            lambda c, z, y, k, j: (c, z, y, k, (j + by) % 4) if group_of(c, z, y, k) == group else None
-        )
-
-    upper, lower = own
-    left_a = lax.ppermute(upper, ALL, shift(1))
-    right_b = lax.ppermute(lower, ALL, shift(3))
-    left_b = lax.ppermute(lower, ALL, shift(1))
-    right_a = lax.ppermute(upper, ALL, shift(3))
-    far_a = lax.ppermute(left_a, ALL, shift(1))
-    far_b = lax.ppermute(right_b, ALL, shift(3))
-    return [left_a, left_b, right_a, right_b, far_a, far_b]
-
-
-def spread_rows(chunks, z, y, core):
+def owner(core, col):
+    return device(0, 0, 0, core, col)
+
+
+def up_pairs(member, least, step=1):
+    return pairs_of(
+        lambda c, z, y, k, j: (c, z, y, k, (j + step) % 4)
+        if member(c, z, y, k) and least <= j <= (2 if step == 1 else 0)
+        else None
+    )
+
+
+def is_first(c, z, y, k):
+    return (c, z, y, k) == (0, 0, 0, 0)
+
+
+def is_second(c, z, y, k):
+    return (c, z, y, k) == (0, 0, 0, 1)
+
+
+def is_other(c, z, y, k):
+    return (c, z, y) != (0, 0, 0)
+
+
+def gather_part(part, member):
+    near = lax.ppermute(part, ALL, up_pairs(member, 0))
+    wrap = lax.ppermute(part, ALL, up_pairs(member, 0, 3))
+    return near, wrap
+
+
+def forward_part(near, member):
+    return lax.ppermute(near, ALL, up_pairs(member, 1))
+
+
+def spread_rows(chunks, z, y, core, far_a, far_b):
     kept = chunks[0]
     total = None
     for k in range(1, 8):
@@ -261,6 +302,7 @@
         got = lax.ppermute(chunks[k], ALL, pairs)
         total = got if total is None else total + got
     chunk = jnp.where(z == 0, kept, total)
+    chunk, far_a, far_b = lax.optimization_barrier((chunk, far_a, far_b))
     total = None
     for to in (1, 3, 2):
         pairs = pairs_of(
@@ -283,7 +325,7 @@
         direct[by] = lax.ppermute(chunk, ALL, pairs)
     mine = [direct[by] for by in (1, 2, 3)]
     theirs = [lax.ppermute(direct[by], ALL, swap) for by in (1, 2, 3)]
-    return [chunk] + mine + theirs + [half, lax.ppermute(half, ALL, swap)]
+    return [chunk] + mine + theirs + [half, lax.ppermute(half, ALL, swap)], far_a, far_b
 
 
 def assemble(front, left, right, got_left, got_right):
@@ -293,21 +335,6 @@
     update = jnp.einsum("rtk,trn->tkn", left, right, preferred_element_type=jnp.float32)
     update = update.reshape(tiles * TILE, TILE)
     return (front.astype(jnp.float32) - update).astype(jnp.bfloat16)
-
-
-def assemble_halves(front, left, right, got_left, got_right):
-    half = PW // 2
-    tiles = right.shape[0] // 2
-    return [
-        assemble(
-            front[at * half : (at + 1) * half],
-            left[:, at * half : (at + 1) * half],
-            right[at * tiles : (at + 1) * tiles],
-            got_left[:, at * half : (at + 1) * half],
-            got_right[at * tiles : (at + 1) * tiles],
-        )
-        for at in range(2)
-    ]
 
 
 def shards(front, left_factors, right_factors):
@@ -323,36 +350,34 @@
     own_left = lax.dynamic_slice_in_dim(left_all, side * PW, PW, 1)
     own_right = lax.dynamic_slice_in_dim(right_all, side * tiles, tiles, 0)
 
-    def swap(first):
-        return pairs_of(
-            lambda c, zz, yy, kk, j: (1 - c, zz, yy, kk, j)
-            if first == ((c, zz, yy, kk) == (1, 0, 0, 0))
-            else None
-        )
-
-    top_left = lax.ppermute(send_left, ALL, swap(True))
-    top_right = lax.ppermute(send_right, ALL, swap(True))
-    top = assemble_halves(front, own_left, own_right, top_left, top_right)
-    top_parts = gather_columns(top, 0)
-    send_left, send_right, top_left, top_right = lax.optimization_barrier(
-        (send_left, send_right, top_left, top_right)
-    )
-    got_left = lax.ppermute(send_left, ALL, swap(False)) + top_left
-    got_right = lax.ppermute(send_right, ALL, swap(False)) + top_right
-    own = assemble_halves(front, own_left, own_right, got_left, got_right)
-    parts = gather_columns(own, 1)
+    swap = pairs_of(lambda c, zz, yy, kk, j: (1 - c, zz, yy, kk, j))
+    got_left = lax.ppermute(send_left, ALL, swap)
+    got_right = lax.ppermute(send_right, ALL, swap)
+    own = assemble(front, own_left, own_right, got_left, got_right)
+    near_a, wrap_a = gather_part(own[:HALF], is_first)
+    near_b, wrap_b = gather_part(own[HALF:], is_first)
+    far_a = forward_part(near_a, is_first)
+    far_b = forward_part(near_b, is_first)
+    tops = [near_a, near_b, wrap_a, wrap_b, far_a, far_b]
+    near, wrap = gather_part(own, is_other)
+    far = forward_part(near, is_other)
+    token = lax.ppermute(
+        near[:8, :128],
+        ALL,
+        [(device(0, 1, 0, 1, j), owner(1, j)) for j in range(1, 4)]
+        + [(device(0, 1, 0, 0, 1), owner(1, 0))],
+    )
+    own_late, token = lax.optimization_barrier((own, token))
+    late_near, late_wrap = gather_part(own_late, is_second)
     group = jnp.where(jnp.logical_and(y == 0, z == 0), 2 * core, 1)
     where = jnp.stack([group, column, z, core]).astype(jnp.int32)
-    token = lax.ppermute(
-        top_parts[4][:8, :128] + top_parts[5][:8, :128],
-        ALL,
-        pairs_of(lambda c, zz, yy, kk, j: (c, zz, yy, 1, j) if (c, zz, yy, kk) == (0, 0, 0, 0) else None),
-    )
-    late = lax.optimization_barrier((own[0], own[1], token))[:2]
-    late_parts = gather_columns(late, 2)
-    chunks = factor_rows(where, top, top_parts)
-    chunks = spread_rows(chunks, z, y, core)
-    return apply_rows(where, own, [top_parts, parts, late_parts], chunks)
+    where, near, wrap, late_near = lax.optimization_barrier((where, near, wrap, late_near))
+    late_far = forward_part(late_near, is_second)
+    chunks = factor_rows(where, own, tops)
+    chunks, far, late_wrap = spread_rows(chunks, z, y, core, far, late_wrap)
+    main = [near, wrap, far]
+    late = [late_near, late_wrap, late_far]
+    return apply_rows(where, own, main, late, tops, chunks, token)
 
 
 def solution(mesh):

time: 224 us -> 231 us (1.031)
  waiting for transfers between devices: 112 us -> 155 us
  starting transfers between devices: 82.4 us -> 45.1 us
  Pallas kernels: 12.8 us -> 15.7 us
    ppermute x23 -> x16, waiting for transfers between devices: 39.7 us -> 93.5 us  [the longest x1 46.7 us: shards(): lax.ppermute(near[:8, :128], ALL, [(device(0, 1, 0, 1, j), owner(1, j)) f...]
    ppermute x23 -> x16, starting transfers between devices: 46.4 us -> 23.9 us  [the longest x4 6.57 us: forward_part(): return lax.ppermute(near, ALL, up_pairs(member, 1))]
    ppermute x1, waiting for transfers between devices: 63.8 us -> 45 us  [spread_rows(): lax.ppermute(chunk, ALL, pairs_of(lambda c, zz, yy, kk, j: (c, zz, yy, 1,...]
    ppermute x3, waiting for transfers between devices: 8.2 us -> 16.4 us  [spread_rows(): direct[by] = lax.ppermute(chunk, ALL, pairs)]
    ppermute x3, starting transfers between devices: 15.1 us -> 7.27 us  [spread_rows(): direct[by] = lax.ppermute(chunk, ALL, pairs)]
    ppermute x3, starting transfers between devices: 7.18 us -> 1.27 us  [spread_rows(): theirs = [lax.ppermute(direct[by], ALL, swap) for by in (1, 2, 3)]]
    pallas_call x1, Pallas kernels: 10.7 us -> 13.7 us  [apply_rows(): pl.pallas_call(apply_kernel, out_shape=jax.ShapeDtypeStruct((TILE, PW), j...]
    unnamed x20 -> x16, local copies, waits for them, and re-layouts: 3.68 us -> 0.85 us
  transfers between devices with their start and end apart: 41 -> 34, of which waited for: 10 -> 10; matrix products, arithmetic and copies ran while one was open for 3% -> 3% of each run, Pallas kernels for 1% -> 1%
where the time goes in v3:
time: 231 us; the launch traced here: 230 us
  waiting for transfers between devices  155 us (67%)
  starting transfers between devices  45.1 us (20%)
  Pallas kernels  15.7 us (7%)
  local copies, waits for them, and re-layouts  6.86 us (3%)
  other arithmetic  5.73 us (2%)
    ppermute x1, waiting for transfers between devices, shards(): lax.ppermute(near[:8, :128], ALL, [(device(0, 1, 0, 1, j), owner(1, j)) f...  46.7 us
    ppermute x1, waiting for transfers between devices, spread_rows(): lax.ppermute(chunk, ALL, pairs_of(lambda c, zz, yy, kk, j: (c, zz, yy, 1,...  45 us
    ppermute x4, waiting for transfers between devices, gather_part(): near = lax.ppermute(part, ALL, up_pairs(member, 0))  19.3 us
    ppermute x4, waiting for transfers between devices, gather_part(): wrap = lax.ppermute(part, ALL, up_pairs(member, 0, 3))  16.8 us
    ppermute x3, waiting for transfers between devices, spread_rows(): direct[by] = lax.ppermute(chunk, ALL, pairs)  16.4 us
    pallas_call x1, Pallas kernels, apply_rows(): pl.pallas_call(apply_kernel, out_shape=jax.ShapeDtypeStruct((TILE, PW), j...  13.7 us
    ppermute x3, starting transfers between devices, spread_rows(): direct[by] = lax.ppermute(chunk, ALL, pairs)  7.27 us
    ppermute x4, starting transfers between devices, forward_part(): return lax.ppermute(near, ALL, up_pairs(member, 1))  6.57 us
  transfers between devices with their start and end apart: 34, of which 10 were waited for; matrix products, arithmetic and copies ran while one was open for 3% of the time, Pallas kernels for 1%

profile of v3, /device:TPU:7, one launch (start us, length us, event | category | flops | bytes accessed | tf_op | source)
XLA Modules:
  0.0 229.7 jit_solution(12462026891295218728)
XLA Ops:
  0.0 1.1 constant_dynamic-slice_fusion.1
  1.1 3.0 %collective-permute-start = (bf16[64,2048]{1,0:T(8,128)(2,1)S(1)}, bf16[64,2048]{1,0:T(8,128)(2,1)S(1)}, u32[]{:S(2)}, u32[]{:S(2)}) collective-permute-start(bf16[64,2048]{1,0:T(8,128)(2,1)S(1)} %get-tuple-element.44), channel_id=1, source_target_pairs={{0,128},{1,129},{2,130},{3,131},{4,132},{5,133},{6,134},{7,135},{8... | collective-permute-start | bytes 786440 | tf_op jit(solution)/shard_map/ppermute | solution.py:354
  4.1 1.1 dynamic-slice_bitcast_fusion.1
  5.6 4.3 %collective-permute-done = bf16[64,2048]{1,0:T(8,128)(2,1)S(1)} collective-permute-done((bf16[64,2048]{1,0:T(8,128)(2,1)S(1)}, bf16[64,2048]{1,0:T(8,128)(2,1)S(1)}, u32[]{:S(2)}, u32[]{:S(2)}) %collective-permute-start) | collective-permute-done | bytes 262176 | tf_op jit(solution)/shard_map/ppermute | solution.py:354
  10.1 5.3 %collective-permute-done.1 = bf16[4,64,512]{2,1,0:T(8,128)(2,1)S(1)} collective-permute-done((bf16[4,64,512]{2,1,0:T(8,128)(2,1)S(1)}, bf16[4,64,512]{2,1,0:T(8,128)(2,1)S(1)}, u32[]{:S(2)}, u32[]{:S(2)}) %collective-permute-start.1) | collective-permute-done | bytes 262176 | tf_op jit(solution)/shard_map/ppermute | solution.py:355
  15.5 0.8 fusion.1
  16.2 0.8 copy-done.7
  17.0 2.2 fusion.own
  19.2 2.0 collective-permute-start.2
  21.9 1.3 collective-permute-start.4
  23.2 2.0 collective-permute-start.3
  25.2 46.7 %collective-permute-done.4.refs_21_ = bf16[8,128]{1,0:T(8,128)(2,1)S(1)} collective-permute-done((bf16[8,128]{1,0:T(8,128)(2,1)S(1)}, bf16[8,128]{1,0:T(8,128)(2,1)S(1)}, u32[]{:S(2)}, u32[]{:S(2)}) %collective-permute-start.4) | collective-permute-done | bytes 2080 | tf_op jit(solution)/shard_map/ppermute | solution.py:364
  71.9 1.3 collective-permute-start.5
  73.2 2.6 %fusion.9 = (bf16[1024,512]{1,0:T(8,128)(2,1)S(1)}, bf16[1024,512]{1,0:T(8,128)(2,1)}) fusion(bf16[2048,512]{1,0:T(8,128)(2,1)} %fusion.own), kind=kLoop, calls=%fused_computation.19 | loop fusion | bytes 4194304 | tf_op jit(solution)/shard_map/slice | solution.py:358
  75.9 0.7 collective-permute-start.9
  76.6 0.7 collective-permute-start.7
  77.3 0.7 collective-permute-start.6
  78.1 1.7 collective-permute-start.8
  79.8 1.6 collective-permute-start.11
  81.4 1.7 collective-permute-start.10
  83.1 2.0 collective-permute-start.19
  85.1 19.3 %collective-permute-done.5.refs_3_ = bf16[2048,512]{1,0:T(8,128)(2,1)} collective-permute-done((bf16[2048,512]{1,0:T(8,128)(2,1)}, bf16[2048,512]{1,0:T(8,128)(2,1)}, u32[]{:S(2)}, u32[]{:S(2)}) %collective-permute-start.5) | collective-permute-done | bytes 2097184 | tf_op jit(solution)/shard_map/ppermute | solution.py:286
  104.4 1.3 collective-permute-start.20
  106.4 2.0 factor_rows.1
  108.5 0.7 collective-permute-start.12
  109.1 0.7 collective-permute-start.13
  109.8 0.7 collective-permute-start.14
  110.5 0.7 collective-permute-start.15
  111.2 0.7 collective-permute-start.16
  111.9 0.7 collective-permute-start.17
  112.6 0.7 collective-permute-start.18
  113.3 1.3 collective-permute-start.21
  114.7 1.2 add_select_fusion.1
  115.9 16.8 %collective-permute-done.20.refs_4_ = bf16[2048,512]{1,0:T(8,128)(2,1)} collective-permute-done((bf16[2048,512]{1,0:T(8,128)(2,1)}, bf16[2048,512]{1,0:T(8,128)(2,1)}, u32[]{:S(2)}, u32[]{:S(2)}) %collective-permute-start.20) | collective-permute-done | bytes 2097184 | tf_op jit(solution)/shard_map/ppermute | solution.py:287
  133.4 0.7 collective-permute-start.23
  134.8 0.8 add_select_fusion
  135.5 1.3 collective-permute-start.25
  136.8 45.0 %collective-permute-done.25 = bf16[64,2048]{1,0:T(8,128)(2,1)} collective-permute-done((bf16[64,2048]{1,0:T(8,128)(2,1)}, bf16[64,2048]{1,0:T(8,128)(2,1)}, u32[]{:S(2)}, u32[]{:S(2)}) %collective-permute-start.25) | collective-permute-done | bytes 262176 | tf_op jit(solution)/shard_map/ppermute | solution.py:314
  181.8 1.0 broadcast_select_fusion.refs_12_
  182.8 6.5 %collective-permute-start.28 = (bf16[64,2048]{1,0:T(8,128)(2,1)S(1)}, bf16[64,2048]{1,0:T(8,128)(2,1)}, u32[]{:S(2)}, u32[]{:S(2)}) collective-permute-start(bf16[64,2048]{1,0:T(8,128)(2,1)S(1)} %broadcast_select_fusion.refs_12_), channel_id=1, source_target_pairs={{0,48},{1,49},{2,50},{3,51},{4,84},{5,85},{6,86},{7,87},{8,56},{9,... | collective-permute-start | bytes 786440 | tf_op jit(solution)/shard_map/ppermute | solution.py:325
  190.1 4.6 %collective-permute-start.32 = (bf16[32,2048]{1,0:T(8,128)(2,1)S(1)}, bf16[32,2048]{1,0:T(8,128)(2,1)S(1)}, u32[]{:S(2)}, u32[]{:S(2)}) collective-permute-start(bf16[32,2048]{1,0:T(8,128)(2,1)S(1)} %constant_dynamic-slice_fusion), channel_id=1, source_target_pairs={{0,64},{1,65},{2,66},{3,67},{4,68},{5,69},{6,70},{7,71},{8,72},{9,... | collective-permute-start | bytes 393224 | tf_op jit(solution)/shard_map/ppermute | solution.py:321
  194.6 7.0 %collective-permute-done.28.refs_15_ = bf16[64,2048]{1,0:T(8,128)(2,1)} collective-permute-done((bf16[64,2048]{1,0:T(8,128)(2,1)S(1)}, bf16[64,2048]{1,0:T(8,128)(2,1)}, u32[]{:S(2)}, u32[]{:S(2)}) %collective-permute-start.28) | collective-permute-done | bytes 262176 | tf_op jit(solution)/shard_map/ppermute | solution.py:325
  201.6 5.1 %collective-permute-done.27.refs_14_ = bf16[64,2048]{1,0:T(8,128)(2,1)} collective-permute-done((bf16[64,2048]{1,0:T(8,128)(2,1)S(1)}, bf16[64,2048]{1,0:T(8,128)(2,1)}, u32[]{:S(2)}, u32[]{:S(2)}) %collective-permute-start.27) | collective-permute-done | bytes 262176 | tf_op jit(solution)/shard_map/ppermute | solution.py:325
  206.7 1.3 collective-permute-start.30
  208.0 4.4 %collective-permute-done.26.refs_13_ = bf16[64,2048]{1,0:T(8,128)(2,1)} collective-permute-done((bf16[64,2048]{1,0:T(8,128)(2,1)S(1)}, bf16[64,2048]{1,0:T(8,128)(2,1)}, u32[]{:S(2)}, u32[]{:S(2)}) %collective-permute-start.26) | collective-permute-done | bytes 262176 | tf_op jit(solution)/shard_map/ppermute | solution.py:325
  212.3 2.5 %collective-permute-start.33 = (bf16[32,2048]{1,0:T(8,128)(2,1)S(1)}, bf16[32,2048]{1,0:T(8,128)(2,1)S(1)}, u32[]{:S(2)}, u32[]{:S(2)}) collective-permute-start(bf16[32,2048]{1,0:T(8,128)(2,1)S(1)} %collective-permute-done.32.refs_19_), channel_id=1, source_target_pairs={{0,4},{1,5},{2,6},{3,7},{4,0},{5,1},{6,2},{7,3},{8,12},{9,13},{10,... | collective-permute-start | bytes 393224 | tf_op jit(solution)/shard_map/ppermute | solution.py:328
  214.8 1.0 collective-permute-done.33.refs_20_
  215.8 13.7 %apply_rows.1 = bf16[512,2048]{1,0:T(8,128)(2,1)} custom-call(s32[4]{0:T(128)S(1)} %copy-done.6, bf16[2048,512]{1,0:T(8,128)(2,1)} %fusion.own, bf16[2048,512]{1,0:T(8,128)(2,1)} %collective-permute-done.2.refs_0_, bf16[2048,512]{1,0:T(8,128)(2,1)} %collective-permute-done.3.refs_1_, bf16[2048,512]{1,0:T(8,128)(2,1)} %collective-permute-done.19.refs_2_, ...), custom_call_target="tpu_custom_call" | custom-call | tf_op jit(solution)/shard_map/apply_rows/pallas_call | solution.py:227
  (51 shorter events, 4.2 us)
Async XLA Ops:
  1.1 8.8 %collective-permute-start = (bf16[64,2048]{1,0:T(8,128)(2,1)S(1)}, bf16[64,2048]{1,0:T(8,128)(2,1)S(1)}, u32[]{:S(2)}, u32[]{:S(2)}) collective-permute-start(bf16[64,2048]{1,0:T(8,128)(2,1)S(1)} %get-tuple-element.44), channel_id=1, source_target_pairs={{0,128},{1,129},{2,130},{3,131},{4,132},{5,133},{6,134},{7,135},{8... | collective-permute-start | bytes 786440 | tf_op jit(solution)/shard_map/ppermute | solution.py:354
  5.1 10.3 %collective-permute-start.1 = (bf16[4,64,512]{2,1,0:T(8,128)(2,1)S(1)}, bf16[4,64,512]{2,1,0:T(8,128)(2,1)S(1)}, u32[]{:S(2)}, u32[]{:S(2)}) collective-permute-start(bf16[4,64,512]{2,1,0:T(8,128)(2,1)S(1)} %get-tuple-element.42), channel_id=1, source_target_pairs={{0,128},{1,129},{2,130},{3,131},{4,132},{5,133},{6,134},{7,135},{8... | collective-permute-start | bytes 786440 | tf_op jit(solution)/shard_map/ppermute | solution.py:355
  15.5 1.6 copy-start.7
  19.2 2.0 collective-permute-start.2
  21.9 50.1 %collective-permute-start.4 = (bf16[8,128]{1,0:T(8,128)(2,1)S(1)}, bf16[8,128]{1,0:T(8,128)(2,1)S(1)}, u32[]{:S(2)}, u32[]{:S(2)}) collective-permute-start(bf16[8,128]{1,0:T(8,128)(2,1)S(1)} %slice.12), channel_id=1, source_target_pairs={{21,5},{22,6},{23,7},{17,4}} | collective-permute-start | bytes 6152 | tf_op jit(solution)/shard_map/ppermute | solution.py:364
  23.2 59.9 %collective-permute-start.3 = (bf16[2048,512]{1,0:T(8,128)(2,1)}, bf16[2048,512]{1,0:T(8,128)(2,1)}, u32[]{:S(2)}, u32[]{:S(2)}) collective-permute-start(bf16[2048,512]{1,0:T(8,128)(2,1)} %fusion.own), channel_id=1, source_target_pairs={{8,11},{12,15},{16,19},{20,23},{24,27},{28,31},{32,35},{36,39},{40... | collective-permute-start | bytes 6291464 | tf_op jit(solution)/shard_map/ppermute | solution.py:287
  71.9 32.5 %collective-permute-start.5 = (bf16[2048,512]{1,0:T(8,128)(2,1)}, bf16[2048,512]{1,0:T(8,128)(2,1)}, u32[]{:S(2)}, u32[]{:S(2)}) collective-permute-start(bf16[2048,512]{1,0:T(8,128)(2,1)} %fusion.own), channel_id=1, source_target_pairs={{4,5},{5,6},{6,7}} | collective-permute-start | bytes 6291464 | tf_op jit(solution)/shard_map/ppermute | solution.py:286
  75.9 2.2 collective-permute-start.9
  76.6 3.2 %collective-permute-start.7 = (bf16[1024,512]{1,0:T(8,128)(2,1)S(1)}, bf16[1024,512]{1,0:T(8,128)(2,1)S(1)}, u32[]{:S(2)}, u32[]{:S(2)}) collective-permute-start(bf16[1024,512]{1,0:T(8,128)(2,1)S(1)} %get-tuple-element.39), channel_id=1, source_target_pairs={{0,1},{1,2},{2,3}} | collective-permute-start | bytes 3145736 | tf_op jit(solution)/shard_map/ppermute | solution.py:286
  77.3 4.1 %collective-permute-start.6 = (bf16[1024,512]{1,0:T(8,128)(2,1)}, bf16[1024,512]{1,0:T(8,128)(2,1)S(1)}, u32[]{:S(2)}, u32[]{:S(2)}) collective-permute-start(bf16[1024,512]{1,0:T(8,128)(2,1)} %get-tuple-element.40), channel_id=1, source_target_pairs={{0,1},{1,2},{2,3}} | collective-permute-start | bytes 3145736 | tf_op jit(solution)/shard_map/ppermute | solution.py:286
  78.1 28.3 %copy-start = (bf16[1024,512]{1,0:T(8,128)(2,1)}, bf16[1024,512]{1,0:T(8,128)(2,1)S(1)}, u32[]{:S(2)}) copy-start(bf16[1024,512]{1,0:T(8,128)(2,1)S(1)} %collective-permute-done.9.refs_3_.refs_9_) | copy-start | bytes 3145732
  78.1 28.3 %collective-permute-start.8 = (bf16[1024,512]{1,0:T(8,128)(2,1)}, bf16[1024,512]{1,0:T(8,128)(2,1)}, u32[]{:S(2)}, u32[]{:S(2)}) collective-permute-start(bf16[1024,512]{1,0:T(8,128)(2,1)} %get-tuple-element.40), channel_id=1, source_target_pairs={{0,3}} | collective-permute-start | bytes 3145736 | tf_op jit(solution)/shard_map/ppermute | solution.py:287
  79.8 26.6 %copy-start.2 = (bf16[1024,512]{1,0:T(8,128)(2,1)}, bf16[1024,512]{1,0:T(8,128)(2,1)S(1)}, u32[]{:S(2)}) copy-start(bf16[1024,512]{1,0:T(8,128)(2,1)S(1)} %collective-permute-done.7.refs_1_.refs_7_) | copy-start | bytes 3145732
  79.8 26.6 %collective-permute-start.11 = (bf16[1024,512]{1,0:T(8,128)(2,1)S(1)}, bf16[1024,512]{1,0:T(8,128)(2,1)}, u32[]{:S(2)}, u32[]{:S(2)}) collective-permute-start(bf16[1024,512]{1,0:T(8,128)(2,1)S(1)} %collective-permute-done.7.refs_1_.refs_7_), channel_id=1, source_target_pairs={{1,2},{2,3}} | collective-permute-start | bytes 3145736 | tf_op jit(solution)/shard_map/ppermute | solution.py:292
  81.4 25.0 %copy-start.4 = (bf16[1024,512]{1,0:T(8,128)(2,1)}, bf16[1024,512]{1,0:T(8,128)(2,1)S(1)}, u32[]{:S(2)}) copy-start(bf16[1024,512]{1,0:T(8,128)(2,1)S(1)} %collective-permute-done.6.refs_0_.refs_6_) | copy-start | bytes 3145732
  81.4 25.0 %collective-permute-start.10 = (bf16[1024,512]{1,0:T(8,128)(2,1)S(1)}, bf16[1024,512]{1,0:T(8,128)(2,1)}, u32[]{:S(2)}, u32[]{:S(2)}) collective-permute-start(bf16[1024,512]{1,0:T(8,128)(2,1)S(1)} %collective-permute-done.6.refs_0_.refs_6_), channel_id=1, source_target_pairs={{1,2},{2,3}} | collective-permute-start | bytes 3145736 | tf_op jit(solution)/shard_map/ppermute | solution.py:292
  83.1 32.8 %collective-permute-start.19 = (bf16[2048,512]{1,0:T(8,128)(2,1)}, bf16[2048,512]{1,0:T(8,128)(2,1)}, u32[]{:S(2)}, u32[]{:S(2)}) collective-permute-start(bf16[2048,512]{1,0:T(8,128)(2,1)} %collective-permute-done.2.refs_0_), channel_id=1, source_target_pairs={{9,10},{10,11},{13,14},{14,15},{17,18},{18,19},{21,22},{22,23},{25... | collective-permute-start | bytes 6291464 | tf_op jit(solution)/shard_map/ppermute | solution.py:292
  104.4 28.3 %collective-permute-start.20 = (bf16[2048,512]{1,0:T(8,128)(2,1)}, bf16[2048,512]{1,0:T(8,128)(2,1)}, u32[]{:S(2)}, u32[]{:S(2)}) collective-permute-start(bf16[2048,512]{1,0:T(8,128)(2,1)} %fusion.own), channel_id=1, source_target_pairs={{4,7}} | collective-permute-start | bytes 6291464 | tf_op jit(solution)/shard_map/ppermute | solution.py:287
  108.5 2.1 collective-permute-start.12
  109.1 2.1 collective-permute-start.13
  109.8 2.1 collective-permute-start.14
  110.5 2.1 collective-permute-start.15
  111.2 2.1 collective-permute-start.16
  111.9 2.7 %collective-permute-start.17 = (bf16[64,2048]{1,0:T(8,128)(2,1)}, bf16[64,2048]{1,0:T(8,128)(2,1)S(1)}, u32[]{:S(2)}, u32[]{:S(2)}) collective-permute-start(bf16[64,2048]{1,0:T(8,128)(2,1)} %get-tuple-element.32), channel_id=1, source_target_pairs={{0,96},{1,97},{2,98},{3,99}} | collective-permute-start | bytes 786440 | tf_op jit(solution)/shard_map/ppermute | solution.py:302
  112.6 2.0 collective-permute-start.18
  113.3 102.5 %collective-permute-start.21 = (bf16[2048,512]{1,0:T(8,128)(2,1)}, bf16[2048,512]{1,0:T(8,128)(2,1)}, u32[]{:S(2)}, u32[]{:S(2)}) collective-permute-start(bf16[2048,512]{1,0:T(8,128)(2,1)} %collective-permute-done.5.refs_3_), channel_id=1, source_target_pairs={{5,6},{6,7}} | collective-permute-start | bytes 6291464 | tf_op jit(solution)/shard_map/ppermute | solution.py:292
  114.6 101.1 %copy-start.1 = (bf16[1024,512]{1,0:T(8,128)(2,1)S(1)}, bf16[1024,512]{1,0:T(8,128)(2,1)}, u32[]{:S(2)}) copy-start(bf16[1024,512]{1,0:T(8,128)(2,1)} %copy-done) | copy-start | bytes 3145732
  114.6 101.1 %copy-start.3 = (bf16[1024,512]{1,0:T(8,128)(2,1)S(1)}, bf16[1024,512]{1,0:T(8,128)(2,1)}, u32[]{:S(2)}) copy-start(bf16[1024,512]{1,0:T(8,128)(2,1)} %copy-done.2) | copy-start | bytes 3145732
  114.7 101.1 %copy-start.5 = (bf16[1024,512]{1,0:T(8,128)(2,1)S(1)}, bf16[1024,512]{1,0:T(8,128)(2,1)}, u32[]{:S(2)}) copy-start(bf16[1024,512]{1,0:T(8,128)(2,1)} %copy-done.4) | copy-start | bytes 3145732
  114.7 101.1 %copy-start.6 = (s32[4]{0:T(128)S(1)}, s32[4]{0:T(128)}, u32[]{:S(2)}) copy-start(s32[4]{0:T(128)} %pad_add_fusion.where_ref) | copy-start | bytes 52
  132.7 2.0 collective-permute-start.24
  133.4 1.4 collective-permute-start.23
  134.1 0.7 collective-permute-start.22
  135.5 46.3 %collective-permute-start.25 = (bf16[64,2048]{1,0:T(8,128)(2,1)}, bf16[64,2048]{1,0:T(8,128)(2,1)}, u32[]{:S(2)}, u32[]{:S(2)}) collective-permute-start(bf16[64,2048]{1,0:T(8,128)(2,1)} %add_select_fusion), channel_id=1, source_target_pairs={{0,4},{1,5},{2,6},{3,7},{8,12},{9,13},{10,14},{11,15},{16,20},{17,... | collective-permute-start | bytes 786440 | tf_op jit(solution)/shard_map/ppermute | solution.py:314
  182.8 18.8 %collective-permute-start.28 = (bf16[64,2048]{1,0:T(8,128)(2,1)S(1)}, bf16[64,2048]{1,0:T(8,128)(2,1)}, u32[]{:S(2)}, u32[]{:S(2)}) collective-permute-start(bf16[64,2048]{1,0:T(8,128)(2,1)S(1)} %broadcast_select_fusion.refs_12_), channel_id=1, source_target_pairs={{0,48},{1,49},{2,50},{3,51},{4,84},{5,85},{6,86},{7,87},{8,56},{9,... | collective-permute-start | bytes 786440 | tf_op jit(solution)/shard_map/ppermute | solution.py:325
  189.3 17.4 %collective-permute-start.27 = (bf16[64,2048]{1,0:T(8,128)(2,1)S(1)}, bf16[64,2048]{1,0:T(8,128)(2,1)}, u32[]{:S(2)}, u32[]{:S(2)}) collective-permute-start(bf16[64,2048]{1,0:T(8,128)(2,1)S(1)} %broadcast_select_fusion.refs_12_), channel_id=1, source_target_pairs={{0,32},{1,33},{2,34},{3,35},{4,100},{5,101},{6,102},{7,103},{8,40}... | collective-permute-start | bytes 786440 | tf_op jit(solution)/shard_map/ppermute | solution.py:325
  189.6 22.7 %collective-permute-start.26 = (bf16[64,2048]{1,0:T(8,128)(2,1)S(1)}, bf16[64,2048]{1,0:T(8,128)(2,1)}, u32[]{:S(2)}, u32[]{:S(2)}) collective-permute-start(bf16[64,2048]{1,0:T(8,128)(2,1)S(1)} %broadcast_select_fusion.refs_12_), channel_id=1, source_target_pairs={{0,16},{1,17},{2,18},{3,19},{4,116},{5,117},{6,118},{7,119},{8,24}... | collective-permute-start | bytes 786440 | tf_op jit(solution)/shard_map/ppermute | solution.py:325
  190.1 22.2 %collective-permute-start.32 = (bf16[32,2048]{1,0:T(8,128)(2,1)S(1)}, bf16[32,2048]{1,0:T(8,128)(2,1)S(1)}, u32[]{:S(2)}, u32[]{:S(2)}) collective-permute-start(bf16[32,2048]{1,0:T(8,128)(2,1)S(1)} %constant_dynamic-slice_fusion), channel_id=1, source_target_pairs={{0,64},{1,65},{2,66},{3,67},{4,68},{5,69},{6,70},{7,71},{8,72},{9,... | collective-permute-start | bytes 393224 | tf_op jit(solution)/shard_map/ppermute | solution.py:321
  201.6 14.2 %collective-permute-start.31 = (bf16[64,2048]{1,0:T(8,128)(2,1)}, bf16[64,2048]{1,0:T(8,128)(2,1)S(1)}, u32[]{:S(2)}, u32[]{:S(2)}) collective-permute-start(bf16[64,2048]{1,0:T(8,128)(2,1)} %collective-permute-done.28.refs_15_), channel_id=1, source_target_pairs={{0,4},{1,5},{2,6},{3,7},{4,0},{5,1},{6,2},{7,3},{8,12},{9,13},{10,... | collective-permute-start | bytes 786440 | tf_op jit(solution)/shard_map/ppermute | solution.py:327
  206.7 9.1 %collective-permute-start.30 = (bf16[64,2048]{1,0:T(8,128)(2,1)}, bf16[64,2048]{1,0:T(8,128)(2,1)S(1)}, u32[]{:S(2)}, u32[]{:S(2)}) collective-permute-start(bf16[64,2048]{1,0:T(8,128)(2,1)} %collective-permute-done.27.refs_14_), channel_id=1, source_target_pairs={{0,4},{1,5},{2,6},{3,7},{4,0},{5,1},{6,2},{7,3},{8,12},{9,13},{10,... | collective-permute-start | bytes 786440 | tf_op jit(solution)/shard_map/ppermute | solution.py:327
  212.3 3.5 %collective-permute-start.29 = (bf16[64,2048]{1,0:T(8,128)(2,1)}, bf16[64,2048]{1,0:T(8,128)(2,1)S(1)}, u32[]{:S(2)}, u32[]{:S(2)}) collective-permute-start(bf16[64,2048]{1,0:T(8,128)(2,1)} %collective-permute-done.26.refs_13_), channel_id=1, source_target_pairs={{0,4},{1,5},{2,6},{3,7},{4,0},{5,1},{6,2},{7,3},{8,12},{9,13},{10,... | collective-permute-start | bytes 786440 | tf_op jit(solution)/shard_map/ppermute | solution.py:327
  212.3 3.4 %collective-permute-start.33 = (bf16[32,2048]{1,0:T(8,128)(2,1)S(1)}, bf16[32,2048]{1,0:T(8,128)(2,1)S(1)}, u32[]{:S(2)}, u32[]{:S(2)}) collective-permute-start(bf16[32,2048]{1,0:T(8,128)(2,1)S(1)} %collective-permute-done.32.refs_19_), channel_id=1, source_target_pairs={{0,4},{1,5},{2,6},{3,7},{4,0},{5,1},{6,2},{7,3},{8,12},{9,13},{10,... | collective-permute-start | bytes 393224 | tf_op jit(solution)/shard_map/ppermute | solution.py:328

commit v4 on v3

--- a/solution.py
+++ b/solution.py
@@ -58,45 +58,62 @@
 HBM = pl.BlockSpec(memory_space=pltpu.HBM)
 
 
-def column_copies(col, next_parts, wrap_parts, far_parts, dest, sems):
-    size = PW // len(next_parts)
-    found = {1: [], 2: [], 3: []}
-    for at in range(len(next_parts)):
-        rows = pl.ds(at * size, size)
-        slots = [3 * at, 3 * at + 1, 3 * at + 2]
-        found[1].append(
-            pltpu.make_async_copy(next_parts[at], dest.at[col - 1, rows], sems.at[slots[0]])
-        )
-        found[2].append(
-            pltpu.make_async_copy(far_parts[at], dest.at[col - 2, rows], sems.at[slots[1]])
-        )
-        found[3].append(pltpu.make_async_copy(wrap_parts[at], dest.at[0, rows], sems.at[slots[2]]))
-
-    for least in (1, 2, 3):
-
-        @pl.when(col >= least)
+def run_copies(found, dest, sems):
+    copies = [
+        pltpu.make_async_copy(part, dest.at[column, pl.ds(at * HALF, size)], sems.at[slot])
+        for slot, (part, column, at, size) in enumerate(found)
+    ]
+    for copy in copies:
+        copy.start()
+    for copy in copies:
+        copy.wait()
+
+
+def fetch_tops(col, tops, dest, sems):
+    u0, u2_u1, w0_w1, w2, w1, u1_u0, w0, u0_next, w0_next = tops
+    found = {
+        1: [(u0_next, 0, 0, HALF), (w0_next, 0, 1, HALF)],
+        2: [(u2_u1, 1, 0, HALF), (w0_w1, 1, 1, HALF), (u1_u0, 0, 0, HALF), (w0, 0, 1, HALF)],
+        3: [
+            (u0, 0, 0, HALF),
+            (w0_w1, 0, 1, HALF),
+            (u2_u1, 2, 0, HALF),
+            (w2, 2, 1, HALF),
+            (u1_u0, 1, 0, HALF),
+            (w1, 1, 1, HALF),
+        ],
+    }
+    for column, parts in found.items():
+
+        @pl.when(col == column)
         def _():
-            for copy in found[least]:
-                copy.start()
-
-    for least in (1, 2, 3):
-
-        @pl.when(col >= least)
+            run_copies(parts, dest, sems)
+
+
+def fetch_rows(col, parts, dest, sems):
+    near, wrap, upper, lower = parts
+    found = {
+        1: [(near, 0, 0, PW)],
+        2: [(near, 1, 0, PW), (upper, 0, 0, HALF), (lower, 0, 1, HALF)],
+        3: [(near, 2, 0, PW), (wrap, 0, 0, PW), (upper, 1, 0, HALF), (lower, 1, 1, HALF)],
+    }
+    for column, parts in found.items():
+
+        @pl.when(col == column)
         def _():
-            for copy in found[least]:
-                copy.wait()
+            run_copies(parts, dest, sems)
 
 
 def factor_kernel(where_ref, own, *refs):
-    tops, outs = refs[:6], refs[6:14]
-    t_ref, s_ref, l_ref, x_ref, r_ref, g_ref, n_ref, e_ref, sems = refs[14:]
+    tops, outs = refs[:9], refs[9:17]
+    t_ref, s_ref, l_ref, x_ref, r_ref, g_ref, n_ref, e_ref, sems = refs[17:]
     col = where_ref[1]
 
     @pl.when(where_ref[0] == 0)
     def _():
         mine = pltpu.make_async_copy(own, t_ref.at[col], sems.at[6])
         mine.start()
-        column_copies(col, tops[0:2], tops[2:4], tops[4:6], t_ref, sems)
+        fetch_tops(col, tops, t_ref, sems)
         mine.wait()
 
         def rows_of(i):
@@ -154,7 +171,7 @@
     return pl.pallas_call(
         factor_kernel,
         out_shape=[jax.ShapeDtypeStruct((64, PW), jnp.bfloat16)] * 8,
-        in_specs=[pl.BlockSpec(memory_space=pltpu.SMEM)] + [HBM] * 7,
+        in_specs=[pl.BlockSpec(memory_space=pltpu.SMEM)] + [HBM] * 10,
         out_specs=[pl.BlockSpec(memory_space=pltpu.VMEM)] * 8,
         scratch_shapes=[
             pltpu.VMEM((BLOCKS, PW, TILE), jnp.bfloat16),
@@ -176,9 +193,9 @@
 
 
 def apply_kernel(where_ref, own, *refs):
-    main, late, tops = refs[:3], refs[3:6], refs[6:12]
-    chunks = refs[12 : 12 + CHUNKS]
-    out, p_ref, r_ref, acc_ref, psems, rsems = refs[13 + CHUNKS :]
+    main, late, tops = refs[:4], refs[4:8], refs[8:17]
+    chunks = refs[17 : 17 + CHUNKS]
+    out, p_ref, r_ref, acc_ref, psems, rsems = refs[18 + CHUNKS :]
     group, col, z, core = where_ref[0], where_ref[1], where_ref[2], where_ref[3]
     sign = 1 - 2 * core
     copies = []
@@ -199,13 +216,13 @@
 
     @pl.when(group == 0)
     def _():
-        column_copies(col, tops[0:2], tops[2:4], tops[4:6], p_ref, psems)
+        fetch_tops(col, tops, p_ref, psems)
 
     for index, parts in ((1, main), (2, late)):
 
         @pl.when(group == index)
         def _():
-            column_copies(col, parts[0:1], parts[1:2], parts[2:3], p_ref, psems)
+            fetch_rows(col, parts, p_ref, psems)
 
     for copy in copies:
         copy.wait()
@@ -227,7 +244,7 @@
     return pl.pallas_call(
         apply_kernel,
         out_shape=jax.ShapeDtypeStruct((TILE, PW), jnp.bfloat16),
-        in_specs=[pl.BlockSpec(memory_space=pltpu.SMEM)] + [HBM] * (14 + CHUNKS),
+        in_specs=[pl.BlockSpec(memory_space=pltpu.SMEM)] + [HBM] * (19 + CHUNKS),
         out_specs=pl.BlockSpec(memory_space=pltpu.VMEM),
         scratch_shapes=[
             pltpu.VMEM((BLOCKS, PW, TILE), jnp.bfloat16),
@@ -262,11 +279,10 @@
     return device(0, 0, 0, core, col)
 
 
-def up_pairs(member, least, step=1):
+def moves(member, *steps):
+    allowed = dict(steps)
     return pairs_of(
-        lambda c, z, y, k, j: (c, z, y, k, (j + step) % 4)
-        if member(c, z, y, k) and least <= j <= (2 if step == 1 else 0)
-        else None
+        lambda c, z, y, k, j: (c, z, y, k, allowed[j]) if member(c, z, y, k) and j in allowed else None
     )
 
 
@@ -283,16 +299,37 @@
 
 
 def gather_part(part, member):
-    near = lax.ppermute(part, ALL, up_pairs(member, 0))
-    wrap = lax.ppermute(part, ALL, up_pairs(member, 0, 3))
+    wrap = lax.ppermute(part, ALL, moves(member, (0, 3), (1, 0)))
+    near = lax.ppermute(part, ALL, moves(member, (0, 1), (1, 2), (2, 3)))
     return near, wrap
 
 
-def forward_part(near, member):
-    return lax.ppermute(near, ALL, up_pairs(member, 1))
-
-
-def spread_rows(chunks, z, y, core, far_a, far_b):
+def forward_part(near, wrap, member):
+    upper = lax.ppermute(near[:HALF], ALL, moves(member, (1, 2), (2, 3)))
+    lower = lax.ppermute(wrap[HALF:], ALL, moves(member, (0, 3), (3, 2)))
+    return upper, lower
+
+
+def gather_top(own, column):
+    def send(part, *steps):
+        return lax.ppermute(part, ALL, moves(is_first, *steps))
+
+    upper, lower = own[:HALF], own[HALF:]
+    first = jnp.where(column == 1, lower, upper)
+    u0 = send(first, (0, 3), (1, 0))
+    u2_u1 = send(upper, (2, 3), (1, 2))
+    w0_w1 = send(lower, (0, 3), (1, 2))
+    w2 = send(lower, (2, 3))
+    w1 = send(u0, (0, 3))
+    u1_u0 = send(jnp.where(column == 3, u0, u2_u1), (2, 3), (3, 2))
+    w0 = send(w0_w1, (3, 2))
+    upper, lower, w1 = lax.optimization_barrier((upper, lower, w1))
+    u0_next = send(upper, (0, 1))
+    w0_next = send(lower, (0, 1))
+    return [u0, u2_u1, w0_w1, w2, w1, u1_u0, w0, u0_next, w0_next]
+
+
+def spread_rows(chunks, z, y, core, early):
     kept = chunks[0]
     total = None
     for k in range(1, 8):
@@ -302,7 +339,7 @@
         got = lax.ppermute(chunks[k], ALL, pairs)
         total = got if total is None else total + got
     chunk = jnp.where(z == 0, kept, total)
-    chunk, far_a, far_b = lax.optimization_barrier((chunk, far_a, far_b))
+    chunk, *early = lax.optimization_barrier((chunk, *early))
     total = None
     for to in (1, 3, 2):
         pairs = pairs_of(
@@ -325,7 +362,7 @@
         direct[by] = lax.ppermute(chunk, ALL, pairs)
     mine = [direct[by] for by in (1, 2, 3)]
     theirs = [lax.ppermute(direct[by], ALL, swap) for by in (1, 2, 3)]
-    return [chunk] + mine + theirs + [half, lax.ppermute(half, ALL, swap)], far_a, far_b
+    return [chunk] + mine + theirs + [half, lax.ppermute(half, ALL, swap)], *early
 
 
 def assemble(front, left, right, got_left, got_right):
@@ -354,29 +391,24 @@
     got_left = lax.ppermute(send_left, ALL, swap)
     got_right = lax.ppermute(send_right, ALL, swap)
     own = assemble(front, own_left, own_right, got_left, got_right)
-    near_a, wrap_a = gather_part(own[:HALF], is_first)
-    near_b, wrap_b = gather_part(own[HALF:], is_first)
-    far_a = forward_part(near_a, is_first)
-    far_b = forward_part(near_b, is_first)
-    tops = [near_a, near_b, wrap_a, wrap_b, far_a, far_b]
+    tops = gather_top(own, column)
     near, wrap = gather_part(own, is_other)
-    far = forward_part(near, is_other)
+    upper, lower = forward_part(near, wrap, is_other)
     token = lax.ppermute(
-        near[:8, :128],
+        near[:8, :128] + wrap[:8, :128],
         ALL,
-        [(device(0, 1, 0, 1, j), owner(1, j)) for j in range(1, 4)]
-        + [(device(0, 1, 0, 0, 1), owner(1, 0))],
+        [(device(0, 1, 0, 0, j), owner(1, j)) for j in range(4)],
     )
     own_late, token = lax.optimization_barrier((own, token))
     late_near, late_wrap = gather_part(own_late, is_second)
     group = jnp.where(jnp.logical_and(y == 0, z == 0), 2 * core, 1)
     where = jnp.stack([group, column, z, core]).astype(jnp.int32)
     where, near, wrap, late_near = lax.optimization_barrier((where, near, wrap, late_near))
-    late_far = forward_part(late_near, is_second)
+    late_upper, late_lower = forward_part(late_near, late_wrap, is_second)
     chunks = factor_rows(where, own, tops)
-    chunks, far, late_wrap = spread_rows(chunks, z, y, core, far, late_wrap)
-    main = [near, wrap, far]
-    late = [late_near, late_wrap, late_far]
+    chunks, upper, lower, late_wrap = spread_rows(chunks, z, y, core, (upper, lower, late_wrap))
+    main = [near, wrap, upper, lower]
+    late = [late_near, late_wrap, late_upper, late_lower]
     return apply_rows(where, own, main, late, tops, chunks, token)
 
 

time: 231 us -> 223 us (0.965)
  waiting for transfers between devices: 155 us -> 109 us
  starting transfers between devices: 45.1 us -> 80.1 us
  other arithmetic: 5.73 us -> 8.89 us
    ppermute x1, waiting for transfers between devices: 45 us -> 0.01 us  [spread_rows(): lax.ppermute(chunk, ALL, pairs_of(lambda c, zz, yy, kk, j: (c, zz, yy, 1,...]
    ppermute x3, waiting for transfers between devices: 16.4 us -> 3.9 us  [spread_rows(): direct[by] = lax.ppermute(chunk, ALL, pairs)]
    ppermute x1, starting transfers between devices: 0.14 us -> 11.9 us  [shards(): got_right = lax.ppermute(send_right, ALL, swap)]
    ppermute x1, waiting for transfers between devices: 0.01 us -> 10.4 us  [spread_rows(): half = lax.ppermute(part, ALL, across)]
    ppermute x1, starting transfers between devices: 3 us -> 13.2 us  [shards(): got_left = lax.ppermute(send_left, ALL, swap)]
    ppermute x3, starting transfers between devices: 1.27 us -> 8.51 us  [spread_rows(): theirs = [lax.ppermute(direct[by], ALL, swap) for by in (1, 2, 3)]]
    ppermute x13 -> x18, starting transfers between devices: 18.3 us -> 23.7 us  [the longest x9 12.1 us: send(): return lax.ppermute(part, ALL, moves(is_first, *steps))]
    ppermute x1, waiting for transfers between devices: 4.26 us -> 0.01 us  [shards(): got_left = lax.ppermute(send_left, ALL, swap)]
  transfers between devices with their start and end apart: 34 -> 39, of which waited for: 10 -> 8; matrix products, arithmetic and copies ran while one was open for 3% -> 6% of each run, Pallas kernels for 1% -> 1%
where the time goes in v4:
time: 223 us; the launch traced here: 222 us
  waiting for transfers between devices  109 us (49%)
  starting transfers between devices  80.1 us (36%)
  Pallas kernels  15.3 us (7%)
  other arithmetic  8.89 us (4%)
  local copies, waits for them, and re-layouts  7.53 us (3%)
    ppermute x1, waiting for transfers between devices, shards(): lax.ppermute(near[:8, :128] + wrap[:8, :128], ALL, [(device(0, 1, 0, 0, j...  47.5 us
    ppermute x2, waiting for transfers between devices, gather_part(): wrap = lax.ppermute(part, ALL, moves(member, (0, 3), (1, 0)))  23.7 us
    ppermute x2, waiting for transfers between devices, gather_part(): near = lax.ppermute(part, ALL, moves(member, (0, 1), (1, 2), (2, 3)))  13.2 us
    ppermute x1, starting transfers between devices, shards(): got_left = lax.ppermute(send_left, ALL, swap)  13.2 us
    pallas_call x1, Pallas kernels, apply_rows(): pl.pallas_call(apply_kernel, out_shape=jax.ShapeDtypeStruct((TILE, PW), j...  13.1 us
    ppermute x9, starting transfers between devices, send(): return lax.ppermute(part, ALL, moves(is_first, *steps))  12.1 us
    ppermute x1, starting transfers between devices, shards(): got_right = lax.ppermute(send_right, ALL, swap)  11.9 us
    ppermute x1, waiting for transfers between devices, spread_rows(): half = lax.ppermute(part, ALL, across)  10.4 us
  transfers between devices with their start and end apart: 39, of which 8 were waited for; matrix products, arithmetic and copies ran while one was open for 6% of the time, Pallas kernels for 1%

profile of v4, /device:TPU:7, one launch (start us, length us, event | category | flops | bytes accessed | tf_op | source)
XLA Modules:
  0.0 222.2 jit_solution(5967082144614828525)
XLA Ops:
  0.0 1.1 constant_dynamic-slice_fusion.1
  1.1 13.2 %collective-permute-start = (bf16[64,2048]{1,0:T(8,128)(2,1)S(1)}, bf16[64,2048]{1,0:T(8,128)(2,1)S(1)}, u32[]{:S(2)}, u32[]{:S(2)}) collective-permute-start(bf16[64,2048]{1,0:T(8,128)(2,1)S(1)} %get-tuple-element.53), channel_id=1, source_target_pairs={{0,128},{1,129},{2,130},{3,131},{4,132},{5,133},{6,134},{7,135},{8... | collective-permute-start | bytes 786440 | tf_op jit(solution)/shard_map/ppermute | solution.py:391
  14.2 1.1 dynamic-slice_bitcast_fusion.1
  15.3 11.9 %collective-permute-start.1 = (bf16[4,64,512]{2,1,0:T(8,128)(2,1)S(1)}, bf16[4,64,512]{2,1,0:T(8,128)(2,1)S(1)}, u32[]{:S(2)}, u32[]{:S(2)}) collective-permute-start(bf16[4,64,512]{2,1,0:T(8,128)(2,1)S(1)} %get-tuple-element.51), channel_id=1, source_target_pairs={{0,128},{1,129},{2,130},{3,131},{4,132},{5,133},{6,134},{7,135},{8... | collective-permute-start | bytes 786440 | tf_op jit(solution)/shard_map/ppermute | solution.py:392
  27.8 8.5 %collective-permute-done.1 = bf16[4,64,512]{2,1,0:T(8,128)(2,1)S(1)} collective-permute-done((bf16[4,64,512]{2,1,0:T(8,128)(2,1)S(1)}, bf16[4,64,512]{2,1,0:T(8,128)(2,1)S(1)}, u32[]{:S(2)}, u32[]{:S(2)}) %collective-permute-start.1) | collective-permute-done | bytes 262176 | tf_op jit(solution)/shard_map/ppermute | solution.py:392
  36.3 0.8 fusion.1
  37.1 0.8 copy-done.9
  37.9 2.2 fusion.own
  40.1 0.8 collective-permute-start.3
  40.9 2.0 collective-permute-start.2
  42.9 3.1 %fusion.9 = (bf16[1024,512]{1,0:T(8,128)(2,1)}, bf16[1024,512]{1,0:T(8,128)(2,1)S(1)}, bf16[1024,512]{1,0:T(8,128)(2,1)}) fusion(bf16[2048,512]{1,0:T(8,128)(2,1)} %fusion.own, pred[]{:T(512)S(6)} %eq.22), kind=kLoop, calls=%fused_computation.22 | loop fusion | flops 524288 | bytes 5242881 | tf_op jit(solution)/shard_map/slice | solution.py:317
  46.0 0.7 collective-permute-start.6
  47.4 1.3 collective-permute-start.4
  48.7 47.5 %collective-permute-done.4.refs_26_ = bf16[8,128]{1,0:T(8,128)(2,1)S(1)} collective-permute-done((bf16[8,128]{1,0:T(8,128)(2,1)S(1)}, bf16[8,128]{1,0:T(8,128)(2,1)S(1)}, u32[]{:S(2)}, u32[]{:S(2)}) %collective-permute-start.4) | collective-permute-done | bytes 2080 | tf_op jit(solution)/shard_map/ppermute | solution.py:397
  96.2 1.3 collective-permute-start.5
  97.5 0.7 collective-permute-start.7
  98.2 0.7 collective-permute-start.8
  99.0 1.7 collective-permute-start.10
  100.7 1.6 collective-permute-start.9
  102.3 1.2 broadcast_select_fusion
  103.5 1.6 collective-permute-start.11
  105.2 1.6 collective-permute-start.12
  106.8 1.7 collective-permute-start.13
  108.5 1.6 collective-permute-start.14
  110.1 13.2 %collective-permute-done.5.refs_4_ = bf16[2048,512]{1,0:T(8,128)(2,1)} collective-permute-done((bf16[2048,512]{1,0:T(8,128)(2,1)}, bf16[2048,512]{1,0:T(8,128)(2,1)}, u32[]{:S(2)}, u32[]{:S(2)}) %collective-permute-start.5) | collective-permute-done | bytes 2097184 | tf_op jit(solution)/shard_map/ppermute | solution.py:303
  123.3 1.3 collective-permute-start.24
  125.3 2.2 factor_rows.1
  129.0 0.8 collective-permute-start.17
  129.9 0.7 collective-permute-start.23
  130.6 1.3 slice.36
  131.9 0.7 collective-permute-start.22
  132.7 0.7 collective-permute-start.18
  134.1 0.7 collective-permute-start.20
  135.6 23.7 %collective-permute-done.24.refs_5_ = bf16[2048,512]{1,0:T(8,128)(2,1)} collective-permute-done((bf16[2048,512]{1,0:T(8,128)(2,1)}, bf16[2048,512]{1,0:T(8,128)(2,1)}, u32[]{:S(2)}, u32[]{:S(2)}) %collective-permute-start.24) | collective-permute-done | bytes 2097184 | tf_op jit(solution)/shard_map/ppermute | solution.py:302
  161.5 1.3 collective-permute-start.30
  162.8 1.3 slice.38
  164.1 2.2 collective-permute-start.26
  166.3 1.3 slice.30
  167.6 1.3 collective-permute-start.25
  168.9 1.0 broadcast_select_fusion.2.refs_17_
  169.9 8.6 %collective-permute-start.37 = (bf16[32,2048]{1,0:T(8,128)(2,1)S(1)}, bf16[32,2048]{1,0:T(8,128)(2,1)S(1)}, u32[]{:S(2)}, u32[]{:S(2)}) collective-permute-start(bf16[32,2048]{1,0:T(8,128)(2,1)S(1)} %constant_dynamic-slice_fusion), channel_id=1, source_target_pairs={{0,64},{1,65},{2,66},{3,67},{4,68},{5,69},{6,70},{7,71},{8,72},{9,... | collective-permute-start | bytes 393224 | tf_op jit(solution)/shard_map/ppermute | solution.py:358
  178.5 5.4 %collective-permute-start.33 = (bf16[64,2048]{1,0:T(8,128)(2,1)S(1)}, bf16[64,2048]{1,0:T(8,128)(2,1)S(1)}, u32[]{:S(2)}, u32[]{:S(2)}) collective-permute-start(bf16[64,2048]{1,0:T(8,128)(2,1)S(1)} %broadcast_select_fusion.2.refs_17_), channel_id=1, source_target_pairs={{0,48},{1,49},{2,50},{3,51},{4,84},{5,85},{6,86},{7,87},{8,56},{9,... | collective-permute-start | bytes 786440 | tf_op jit(solution)/shard_map/ppermute | solution.py:362
  184.6 10.4 %collective-permute-done.37.refs_24_ = bf16[32,2048]{1,0:T(8,128)(2,1)S(1)} collective-permute-done((bf16[32,2048]{1,0:T(8,128)(2,1)S(1)}, bf16[32,2048]{1,0:T(8,128)(2,1)S(1)}, u32[]{:S(2)}, u32[]{:S(2)}) %collective-permute-start.37) | collective-permute-done | bytes 131104 | tf_op jit(solution)/shard_map/ppermute | solution.py:358
  195.1 4.3 %collective-permute-start.36 = (bf16[64,2048]{1,0:T(8,128)(2,1)S(1)}, bf16[64,2048]{1,0:T(8,128)(2,1)S(1)}, u32[]{:S(2)}, u32[]{:S(2)}) collective-permute-start(bf16[64,2048]{1,0:T(8,128)(2,1)S(1)} %collective-permute-done.33.refs_20_), channel_id=1, source_target_pairs={{0,4},{1,5},{2,6},{3,7},{4,0},{5,1},{6,2},{7,3},{8,12},{9,13},{10,... | collective-permute-start | bytes 786440 | tf_op jit(solution)/shard_map/ppermute | solution.py:364
  199.4 3.6 %collective-permute-done.32.refs_19_ = bf16[64,2048]{1,0:T(8,128)(2,1)S(1)} collective-permute-done((bf16[64,2048]{1,0:T(8,128)(2,1)S(1)}, bf16[64,2048]{1,0:T(8,128)(2,1)S(1)}, u32[]{:S(2)}, u32[]{:S(2)}) %collective-permute-start.32) | collective-permute-done | bytes 262176 | tf_op jit(solution)/shard_map/ppermute | solution.py:362
  203.3 4.2 %collective-permute-start.34 = (bf16[64,2048]{1,0:T(8,128)(2,1)S(1)}, bf16[64,2048]{1,0:T(8,128)(2,1)S(1)}, u32[]{:S(2)}, u32[]{:S(2)}) collective-permute-start(bf16[64,2048]{1,0:T(8,128)(2,1)S(1)} %collective-permute-done.31.refs_18_), channel_id=1, source_target_pairs={{0,4},{1,5},{2,6},{3,7},{4,0},{5,1},{6,2},{7,3},{8,12},{9,13},{10,... | collective-permute-start | bytes 786440 | tf_op jit(solution)/shard_map/ppermute | solution.py:364
  207.5 1.3 collective-permute-done.38.refs_25_
  208.9 13.1 %apply_rows.1 = bf16[512,2048]{1,0:T(8,128)(2,1)} custom-call(s32[4]{0:T(128)S(1)} %copy-done.6, bf16[2048,512]{1,0:T(8,128)(2,1)} %fusion.own, bf16[2048,512]{1,0:T(8,128)(2,1)} %collective-permute-done.2.refs_0_, bf16[2048,512]{1,0:T(8,128)(2,1)} %copy-done.7, bf16[1024,512]{1,0:T(8,128)(2,1)S(1)} %collective-permute-done.22.refs_2_, ...), custom_call_target="tpu_custom_call" | custom-call | tf_op jit(solution)/shard_map/apply_rows/pallas_call | solution.py:244
  (80 shorter events, 7.9 us)
Async XLA Ops:
  1.1 26.5 %collective-permute-start = (bf16[64,2048]{1,0:T(8,128)(2,1)S(1)}, bf16[64,2048]{1,0:T(8,128)(2,1)S(1)}, u32[]{:S(2)}, u32[]{:S(2)}) collective-permute-start(bf16[64,2048]{1,0:T(8,128)(2,1)S(1)} %get-tuple-element.53), channel_id=1, source_target_pairs={{0,128},{1,129},{2,130},{3,131},{4,132},{5,133},{6,134},{7,135},{8... | collective-permute-start | bytes 786440 | tf_op jit(solution)/shard_map/ppermute | solution.py:391
  15.3 21.0 %collective-permute-start.1 = (bf16[4,64,512]{2,1,0:T(8,128)(2,1)S(1)}, bf16[4,64,512]{2,1,0:T(8,128)(2,1)S(1)}, u32[]{:S(2)}, u32[]{:S(2)}) collective-permute-start(bf16[4,64,512]{2,1,0:T(8,128)(2,1)S(1)} %get-tuple-element.51), channel_id=1, source_target_pairs={{0,128},{1,129},{2,130},{3,131},{4,132},{5,133},{6,134},{7,135},{8... | collective-permute-start | bytes 786440 | tf_op jit(solution)/shard_map/ppermute | solution.py:392
  40.1 6.6 %collective-permute-start.3 = (bf16[2048,512]{1,0:T(8,128)(2,1)}, bf16[2048,512]{1,0:T(8,128)(2,1)S(1)}, u32[]{:S(2)}, u32[]{:S(2)}) collective-permute-start(bf16[2048,512]{1,0:T(8,128)(2,1)} %fusion.own), channel_id=1, source_target_pairs={{8,11},{9,8},{12,15},{13,12},{16,19},{17,16},{20,23},{21,20},{24,2... | collective-permute-start | bytes 6291464 | tf_op jit(solution)/shard_map/ppermute | solution.py:302
  40.9 5.8 %collective-permute-start.2 = (bf16[2048,512]{1,0:T(8,128)(2,1)}, bf16[2048,512]{1,0:T(8,128)(2,1)}, u32[]{:S(2)}, u32[]{:S(2)}) collective-permute-start(bf16[2048,512]{1,0:T(8,128)(2,1)} %fusion.own), channel_id=1, source_target_pairs={{8,9},{9,10},{10,11},{12,13},{13,14},{14,15},{16,17},{17,18},{18,1... | collective-permute-start | bytes 6291464 | tf_op jit(solution)/shard_map/ppermute | solution.py:303
  46.0 53.0 %collective-permute-start.6 = (bf16[1024,512]{1,0:T(8,128)(2,1)S(1)}, bf16[1024,512]{1,0:T(8,128)(2,1)S(1)}, u32[]{:S(2)}, u32[]{:S(2)}) collective-permute-start(bf16[1024,512]{1,0:T(8,128)(2,1)S(1)} %get-tuple-element.48), channel_id=1, source_target_pairs={{0,3},{1,0}} | collective-permute-start | bytes 3145736 | tf_op jit(solution)/shard_map/ppermute | solution.py:315
  46.7 50.8 %copy-start.7 = (bf16[2048,512]{1,0:T(8,128)(2,1)}, bf16[2048,512]{1,0:T(8,128)(2,1)S(1)}, u32[]{:S(2)}) copy-start(bf16[2048,512]{1,0:T(8,128)(2,1)S(1)} %collective-permute-done.3.refs_1_) | copy-start | bytes 6291460
  47.4 48.8 %collective-permute-start.4 = (bf16[8,128]{1,0:T(8,128)(2,1)S(1)}, bf16[8,128]{1,0:T(8,128)(2,1)S(1)}, u32[]{:S(2)}, u32[]{:S(2)}) collective-permute-start(bf16[8,128]{1,0:T(8,128)(2,1)S(1)} %slice_add_fusion), channel_id=1, source_target_pairs={{16,4},{17,5},{18,6},{19,7}} | collective-permute-start | bytes 6152 | tf_op jit(solution)/shard_map/ppermute | solution.py:397
  96.2 27.1 %collective-permute-start.5 = (bf16[2048,512]{1,0:T(8,128)(2,1)}, bf16[2048,512]{1,0:T(8,128)(2,1)}, u32[]{:S(2)}, u32[]{:S(2)}) collective-permute-start(bf16[2048,512]{1,0:T(8,128)(2,1)} %fusion.own), channel_id=1, source_target_pairs={{4,5},{5,6},{6,7}} | collective-permute-start | bytes 6291464 | tf_op jit(solution)/shard_map/ppermute | solution.py:303
  97.5 4.8 %collective-permute-start.7 = (bf16[1024,512]{1,0:T(8,128)(2,1)}, bf16[1024,512]{1,0:T(8,128)(2,1)S(1)}, u32[]{:S(2)}, u32[]{:S(2)}) collective-permute-start(bf16[1024,512]{1,0:T(8,128)(2,1)} %get-tuple-element.31), channel_id=1, source_target_pairs={{1,2},{2,3}} | collective-permute-start | bytes 3145736 | tf_op jit(solution)/shard_map/ppermute | solution.py:315
  98.2 6.9 %collective-permute-start.8 = (bf16[1024,512]{1,0:T(8,128)(2,1)}, bf16[1024,512]{1,0:T(8,128)(2,1)S(1)}, u32[]{:S(2)}, u32[]{:S(2)}) collective-permute-start(bf16[1024,512]{1,0:T(8,128)(2,1)} %get-tuple-element.32), channel_id=1, source_target_pairs={{0,3},{1,2}} | collective-permute-start | bytes 3145736 | tf_op jit(solution)/shard_map/ppermute | solution.py:315
  99.0 26.3 %copy-start = (bf16[1024,512]{1,0:T(8,128)(2,1)}, bf16[1024,512]{1,0:T(8,128)(2,1)S(1)}, u32[]{:S(2)}) copy-start(bf16[1024,512]{1,0:T(8,128)(2,1)S(1)} %collective-permute-done.6.refs_0_.refs_8_) | copy-start | bytes 3145732
  99.0 7.8 %collective-permute-start.10 = (bf16[1024,512]{1,0:T(8,128)(2,1)S(1)}, bf16[1024,512]{1,0:T(8,128)(2,1)}, u32[]{:S(2)}, u32[]{:S(2)}) collective-permute-start(bf16[1024,512]{1,0:T(8,128)(2,1)S(1)} %collective-permute-done.6.refs_0_.refs_8_), channel_id=1, source_target_pairs={{0,3}} | collective-permute-start | bytes 3145736 | tf_op jit(solution)/shard_map/ppermute | solution.py:315
  100.7 7.8 %collective-permute-start.9 = (bf16[1024,512]{1,0:T(8,128)(2,1)}, bf16[1024,512]{1,0:T(8,128)(2,1)}, u32[]{:S(2)}, u32[]{:S(2)}) collective-permute-start(bf16[1024,512]{1,0:T(8,128)(2,1)} %get-tuple-element.32), channel_id=1, source_target_pairs={{2,3}} | collective-permute-start | bytes 3145736 | tf_op jit(solution)/shard_map/ppermute | solution.py:315
  102.3 23.0 %copy-start.2 = (bf16[1024,512]{1,0:T(8,128)(2,1)}, bf16[1024,512]{1,0:T(8,128)(2,1)S(1)}, u32[]{:S(2)}) copy-start(bf16[1024,512]{1,0:T(8,128)(2,1)S(1)} %collective-permute-done.7.refs_1_.refs_9_) | copy-start | bytes 3145732
  103.5 21.8 %collective-permute-start.11 = (bf16[1024,512]{1,0:T(8,128)(2,1)}, bf16[1024,512]{1,0:T(8,128)(2,1)}, u32[]{:S(2)}, u32[]{:S(2)}) collective-permute-start(bf16[1024,512]{1,0:T(8,128)(2,1)} %broadcast_select_fusion), channel_id=1, source_target_pairs={{2,3},{3,2}} | collective-permute-start | bytes 3145736 | tf_op jit(solution)/shard_map/ppermute | solution.py:315
  105.2 20.2 %copy-start.4 = (bf16[1024,512]{1,0:T(8,128)(2,1)}, bf16[1024,512]{1,0:T(8,128)(2,1)S(1)}, u32[]{:S(2)}) copy-start(bf16[1024,512]{1,0:T(8,128)(2,1)S(1)} %collective-permute-done.8.refs_2_.refs_10_) | copy-start | bytes 3145732
  105.2 20.1 %collective-permute-start.12 = (bf16[1024,512]{1,0:T(8,128)(2,1)S(1)}, bf16[1024,512]{1,0:T(8,128)(2,1)}, u32[]{:S(2)}, u32[]{:S(2)}) collective-permute-start(bf16[1024,512]{1,0:T(8,128)(2,1)S(1)} %collective-permute-done.8.refs_2_.refs_10_), channel_id=1, source_target_pairs={{3,2}} | collective-permute-start | bytes 3145736 | tf_op jit(solution)/shard_map/ppermute | solution.py:315
  106.8 18.5 %collective-permute-start.13 = (bf16[1024,512]{1,0:T(8,128)(2,1)}, bf16[1024,512]{1,0:T(8,128)(2,1)}, u32[]{:S(2)}, u32[]{:S(2)}) collective-permute-start(bf16[1024,512]{1,0:T(8,128)(2,1)} %get-tuple-element.31), channel_id=1, source_target_pairs={{0,1}} | collective-permute-start | bytes 3145736 | tf_op jit(solution)/shard_map/ppermute | solution.py:315
  108.5 16.8 %collective-permute-start.14 = (bf16[1024,512]{1,0:T(8,128)(2,1)}, bf16[1024,512]{1,0:T(8,128)(2,1)}, u32[]{:S(2)}, u32[]{:S(2)}) collective-permute-start(bf16[1024,512]{1,0:T(8,128)(2,1)} %get-tuple-element.32), channel_id=1, source_target_pairs={{0,1}} | collective-permute-start | bytes 3145736 | tf_op jit(solution)/shard_map/ppermute | solution.py:315
  123.3 36.0 %collective-permute-start.24 = (bf16[2048,512]{1,0:T(8,128)(2,1)}, bf16[2048,512]{1,0:T(8,128)(2,1)}, u32[]{:S(2)}, u32[]{:S(2)}) collective-permute-start(bf16[2048,512]{1,0:T(8,128)(2,1)} %fusion.own), channel_id=1, source_target_pairs={{4,7},{5,4}} | collective-permute-start | bytes 6291464 | tf_op jit(solution)/shard_map/ppermute | solution.py:302
  127.5 4.4 %collective-permute-start.15 = (bf16[64,2048]{1,0:T(8,128)(2,1)}, bf16[64,2048]{1,0:T(8,128)(2,1)S(1)}, u32[]{:S(2)}, u32[]{:S(2)}) collective-permute-start(bf16[64,2048]{1,0:T(8,128)(2,1)} %get-tuple-element.34), channel_id=1, source_target_pairs={{0,16},{1,17},{2,18},{3,19}} | collective-permute-start | bytes 786440 | tf_op jit(solution)/shard_map/ppermute | solution.py:339
  128.2 4.4 %collective-permute-start.16 = (bf16[64,2048]{1,0:T(8,128)(2,1)}, bf16[64,2048]{1,0:T(8,128)(2,1)S(1)}, u32[]{:S(2)}, u32[]{:S(2)}) collective-permute-start(bf16[64,2048]{1,0:T(8,128)(2,1)} %get-tuple-element.35), channel_id=1, source_target_pairs={{0,32},{1,33},{2,34},{3,35}} | collective-permute-start | bytes 786440 | tf_op jit(solution)/shard_map/ppermute | solution.py:339
  128.9 6.5 %copy-start.10 = (bf16[64,2048]{1,0:T(8,128)(2,1)S(1)}, bf16[64,2048]{1,0:T(8,128)(2,1)}, u32[]{:S(2)}) copy-start(bf16[64,2048]{1,0:T(8,128)(2,1)} %get-tuple-element.33) | copy-start | bytes 786436
  129.0 4.4 %collective-permute-start.17 = (bf16[64,2048]{1,0:T(8,128)(2,1)}, bf16[64,2048]{1,0:T(8,128)(2,1)S(1)}, u32[]{:S(2)}, u32[]{:S(2)}) collective-permute-start(bf16[64,2048]{1,0:T(8,128)(2,1)} %get-tuple-element.36), channel_id=1, source_target_pairs={{0,48},{1,49},{2,50},{3,51}} | collective-permute-start | bytes 786440 | tf_op jit(solution)/shard_map/ppermute | solution.py:339
  129.9 5.7 %collective-permute-start.23 = (bf16[1024,512]{1,0:T(8,128)(2,1)S(1)}, bf16[1024,512]{1,0:T(8,128)(2,1)S(1)}, u32[]{:S(2)}, u32[]{:S(2)}) collective-permute-start(bf16[1024,512]{1,0:T(8,128)(2,1)S(1)} %slice.37), channel_id=1, source_target_pairs={{8,11},{11,10},{12,15},{15,14},{16,19},{19,18},{20,23},{23,22},{24... | collective-permute-start | bytes 3145736 | tf_op jit(solution)/shard_map/ppermute | solution.py:309
  131.9 3.7 %collective-permute-start.22 = (bf16[1024,512]{1,0:T(8,128)(2,1)S(1)}, bf16[1024,512]{1,0:T(8,128)(2,1)S(1)}, u32[]{:S(2)}, u32[]{:S(2)}) collective-permute-start(bf16[1024,512]{1,0:T(8,128)(2,1)S(1)} %slice.36), channel_id=1, source_target_pairs={{9,10},{10,11},{13,14},{14,15},{17,18},{18,19},{21,22},{22,23},{25... | collective-permute-start | bytes 3145736 | tf_op jit(solution)/shard_map/ppermute | solution.py:308
  132.7 1.4 collective-permute-start.18
  133.4 1.4 collective-permute-start.19
  134.1 1.4 collective-permute-start.20
  134.8 0.7 collective-permute-start.21
  159.3 2.0 collective-permute-start.29
  160.0 1.4 collective-permute-start.28
  160.7 0.7 collective-permute-start.27
  161.5 7.4 %collective-permute-start.30 = (bf16[64,2048]{1,0:T(8,128)(2,1)S(1)}, bf16[64,2048]{1,0:T(8,128)(2,1)}, u32[]{:S(2)}, u32[]{:S(2)}) collective-permute-start(bf16[64,2048]{1,0:T(8,128)(2,1)S(1)} %add_select_fusion), channel_id=1, source_target_pairs={{0,4},{1,5},{2,6},{3,7},{8,12},{9,13},{10,14},{11,15},{16,20},{17,... | collective-permute-start | bytes 786440 | tf_op jit(solution)/shard_map/ppermute | solution.py:351
  164.1 44.8 %copy-start.1 = (bf16[1024,512]{1,0:T(8,128)(2,1)S(1)}, bf16[1024,512]{1,0:T(8,128)(2,1)}, u32[]{:S(2)}) copy-start(bf16[1024,512]{1,0:T(8,128)(2,1)} %copy-done) | copy-start | bytes 3145732
  164.1 44.8 %copy-start.3 = (bf16[1024,512]{1,0:T(8,128)(2,1)S(1)}, bf16[1024,512]{1,0:T(8,128)(2,1)}, u32[]{:S(2)}) copy-start(bf16[1024,512]{1,0:T(8,128)(2,1)} %copy-done.2) | copy-start | bytes 3145732
  164.1 44.8 %copy-start.5 = (bf16[1024,512]{1,0:T(8,128)(2,1)S(1)}, bf16[1024,512]{1,0:T(8,128)(2,1)}, u32[]{:S(2)}) copy-start(bf16[1024,512]{1,0:T(8,128)(2,1)} %copy-done.4) | copy-start | bytes 3145732
  164.1 44.8 %copy-start.6 = (s32[4]{0:T(128)S(1)}, s32[4]{0:T(128)}, u32[]{:S(2)}) copy-start(s32[4]{0:T(128)} %pad_add_fusion.where_ref) | copy-start | bytes 52
  164.1 43.4 %collective-permute-start.26 = (bf16[1024,512]{1,0:T(8,128)(2,1)S(1)}, bf16[1024,512]{1,0:T(8,128)(2,1)S(1)}, u32[]{:S(2)}, u32[]{:S(2)}) collective-permute-start(bf16[1024,512]{1,0:T(8,128)(2,1)S(1)} %slice.38), channel_id=1, source_target_pairs={{4,7},{7,6}} | collective-permute-start | bytes 3145736 | tf_op jit(solution)/shard_map/ppermute | solution.py:309
  167.6 39.9 %collective-permute-start.25 = (bf16[1024,512]{1,0:T(8,128)(2,1)S(1)}, bf16[1024,512]{1,0:T(8,128)(2,1)S(1)}, u32[]{:S(2)}, u32[]{:S(2)}) collective-permute-start(bf16[1024,512]{1,0:T(8,128)(2,1)S(1)} %slice.30), channel_id=1, source_target_pairs={{5,6},{6,7}} | collective-permute-start | bytes 3145736 | tf_op jit(solution)/shard_map/ppermute | solution.py:308
  169.9 25.1 %collective-permute-start.37 = (bf16[32,2048]{1,0:T(8,128)(2,1)S(1)}, bf16[32,2048]{1,0:T(8,128)(2,1)S(1)}, u32[]{:S(2)}, u32[]{:S(2)}) collective-permute-start(bf16[32,2048]{1,0:T(8,128)(2,1)S(1)} %constant_dynamic-slice_fusion), channel_id=1, source_target_pairs={{0,64},{1,65},{2,66},{3,67},{4,68},{5,69},{6,70},{7,71},{8,72},{9,... | collective-permute-start | bytes 393224 | tf_op jit(solution)/shard_map/ppermute | solution.py:358
  178.5 16.5 %collective-permute-start.33 = (bf16[64,2048]{1,0:T(8,128)(2,1)S(1)}, bf16[64,2048]{1,0:T(8,128)(2,1)S(1)}, u32[]{:S(2)}, u32[]{:S(2)}) collective-permute-start(bf16[64,2048]{1,0:T(8,128)(2,1)S(1)} %broadcast_select_fusion.2.refs_17_), channel_id=1, source_target_pairs={{0,48},{1,49},{2,50},{3,51},{4,84},{5,85},{6,86},{7,87},{8,56},{9,... | collective-permute-start | bytes 786440 | tf_op jit(solution)/shard_map/ppermute | solution.py:362
  184.0 19.0 %collective-permute-start.32 = (bf16[64,2048]{1,0:T(8,128)(2,1)S(1)}, bf16[64,2048]{1,0:T(8,128)(2,1)S(1)}, u32[]{:S(2)}, u32[]{:S(2)}) collective-permute-start(bf16[64,2048]{1,0:T(8,128)(2,1)S(1)} %broadcast_select_fusion.2.refs_17_), channel_id=1, source_target_pairs={{0,32},{1,33},{2,34},{3,35},{4,100},{5,101},{6,102},{7,103},{8,40}... | collective-permute-start | bytes 786440 | tf_op jit(solution)/shard_map/ppermute | solution.py:362
  195.1 8.2 %collective-permute-start.31 = (bf16[64,2048]{1,0:T(8,128)(2,1)S(1)}, bf16[64,2048]{1,0:T(8,128)(2,1)S(1)}, u32[]{:S(2)}, u32[]{:S(2)}) collective-permute-start(bf16[64,2048]{1,0:T(8,128)(2,1)S(1)} %broadcast_select_fusion.2.refs_17_), channel_id=1, source_target_pairs={{0,16},{1,17},{2,18},{3,19},{4,116},{5,117},{6,118},{7,119},{8,24}... | collective-permute-start | bytes 786440 | tf_op jit(solution)/shard_map/ppermute | solution.py:362
  195.1 13.8 %collective-permute-start.36 = (bf16[64,2048]{1,0:T(8,128)(2,1)S(1)}, bf16[64,2048]{1,0:T(8,128)(2,1)S(1)}, u32[]{:S(2)}, u32[]{:S(2)}) collective-permute-start(bf16[64,2048]{1,0:T(8,128)(2,1)S(1)} %collective-permute-done.33.refs_20_), channel_id=1, source_target_pairs={{0,4},{1,5},{2,6},{3,7},{4,0},{5,1},{6,2},{7,3},{8,12},{9,13},{10,... | collective-permute-start | bytes 786440 | tf_op jit(solution)/shard_map/ppermute | solution.py:364
  203.0 5.8 %collective-permute-start.35 = (bf16[64,2048]{1,0:T(8,128)(2,1)S(1)}, bf16[64,2048]{1,0:T(8,128)(2,1)S(1)}, u32[]{:S(2)}, u32[]{:S(2)}) collective-permute-start(bf16[64,2048]{1,0:T(8,128)(2,1)S(1)} %collective-permute-done.32.refs_19_), channel_id=1, source_target_pairs={{0,4},{1,5},{2,6},{3,7},{4,0},{5,1},{6,2},{7,3},{8,12},{9,13},{10,... | collective-permute-start | bytes 786440 | tf_op jit(solution)/shard_map/ppermute | solution.py:364
  203.3 5.5 %collective-permute-start.34 = (bf16[64,2048]{1,0:T(8,128)(2,1)S(1)}, bf16[64,2048]{1,0:T(8,128)(2,1)S(1)}, u32[]{:S(2)}, u32[]{:S(2)}) collective-permute-start(bf16[64,2048]{1,0:T(8,128)(2,1)S(1)} %collective-permute-done.31.refs_18_), channel_id=1, source_target_pairs={{0,4},{1,5},{2,6},{3,7},{4,0},{5,1},{6,2},{7,3},{8,12},{9,13},{10,... | collective-permute-start | bytes 786440 | tf_op jit(solution)/shard_map/ppermute | solution.py:364
  207.5 1.3 collective-permute-start.38
  (6 other events, 25.3 us)

commit v5 on v4

--- a/solution.py
+++ b/solution.py
@@ -91,11 +91,15 @@
 
 
 def fetch_rows(col, parts, dest, sems):
-    near, wrap, upper, lower = parts
+    near, wrap = parts[:2]
+    if len(parts) == 4:
+        far = [(parts[2], 0, HALF), (parts[3], 1, HALF)]
+    else:
+        far = [(parts[2], 0, PW)]
     found = {
         1: [(near, 0, 0, PW)],
-        2: [(near, 1, 0, PW), (upper, 0, 0, HALF), (lower, 0, 1, HALF)],
-        3: [(near, 2, 0, PW), (wrap, 0, 0, PW), (upper, 1, 0, HALF), (lower, 1, 1, HALF)],
+        2: [(near, 1, 0, PW)] + [(part, 0, at, size) for part, at, size in far],
+        3: [(near, 2, 0, PW), (wrap, 0, 0, PW)] + [(part, 1, at, size) for part, at, size in far],
     }
     for column, parts in found.items():
 
@@ -189,27 +193,28 @@
     )(where, own, *tops)
 
 
-CHUNKS = 9
+CHUNKS = 6
 
 
 def apply_kernel(where_ref, own, *refs):
-    main, late, tops = refs[:4], refs[4:8], refs[8:17]
-    chunks = refs[17 : 17 + CHUNKS]
-    out, p_ref, r_ref, acc_ref, psems, rsems = refs[18 + CHUNKS :]
+    main, late, tops = refs[:4], refs[4:7], refs[7:16]
+    chunks = refs[16 : 16 + CHUNKS]
+    out, p_ref, r_ref, acc_ref, psems, rsems = refs[17 + CHUNKS :]
     group, col, z, core = where_ref[0], where_ref[1], where_ref[2], where_ref[3]
     sign = 1 - 2 * core
     copies = []
-    for slot in range(CHUNKS):
-        size = 64
-        if slot <= 3:
-            at = lax.rem(z - sign * slot + 8, 8) * 64
-        elif slot <= 6:
-            at = lax.rem(z + sign * (slot - 3) + 8, 8) * 64
-        else:
-            size = 32
-            at = lax.rem(z + 4, 8) * 64 + (core if slot == 7 else 1 - core) * 32
+
+    def place(part, at, size):
         rows = pl.ds(pl.multiple_of(at, size), size)
-        copies.append(pltpu.make_async_copy(chunks[slot], r_ref.at[rows], rsems.at[slot]))
+        copies.append(pltpu.make_async_copy(part, r_ref.at[rows], rsems.at[len(copies)]))
+
+    swapped = chunks[5]
+    place(chunks[0], z * 64, 64)
+    for by in range(1, 4):
+        place(chunks[by], lax.rem(z - sign * by + 8, 8) * 64, 64)
+        place(swapped.at[pl.ds(by * 64 - 64, 64)], lax.rem(z + sign * by + 8, 8) * 64, 64)
+    place(chunks[4], lax.rem(z + 4, 8) * 64 + core * 32, 32)
+    place(swapped.at[pl.ds(192, 32)], lax.rem(z + 4, 8) * 64 + (1 - core) * 32, 32)
     copies.append(pltpu.make_async_copy(own, p_ref.at[col], psems.at[6]))
     for copy in copies:
         copy.start()
@@ -244,14 +249,14 @@
     return pl.pallas_call(
         apply_kernel,
         out_shape=jax.ShapeDtypeStruct((TILE, PW), jnp.bfloat16),
-        in_specs=[pl.BlockSpec(memory_space=pltpu.SMEM)] + [HBM] * (19 + CHUNKS),
+        in_specs=[pl.BlockSpec(memory_space=pltpu.SMEM)] + [HBM] * (18 + CHUNKS),
         out_specs=pl.BlockSpec(memory_space=pltpu.VMEM),
         scratch_shapes=[
             pltpu.VMEM((BLOCKS, PW, TILE), jnp.bfloat16),
             pltpu.VMEM((TILE, PW), jnp.bfloat16),
             pltpu.VMEM((TILE, TILE), jnp.float32),
             pltpu.SemaphoreType.DMA((7,)),
-            pltpu.SemaphoreType.DMA((CHUNKS,)),
+            pltpu.SemaphoreType.DMA((9,)),
         ],
         compiler_params=pltpu.CompilerParams(vmem_limit_bytes=40 << 20),
         name="apply_rows",
@@ -302,12 +307,6 @@
     wrap = lax.ppermute(part, ALL, moves(member, (0, 3), (1, 0)))
     near = lax.ppermute(part, ALL, moves(member, (0, 1), (1, 2), (2, 3)))
     return near, wrap
-
-
-def forward_part(near, wrap, member):
-    upper = lax.ppermute(near[:HALF], ALL, moves(member, (1, 2), (2, 3)))
-    lower = lax.ppermute(wrap[HALF:], ALL, moves(member, (0, 3), (3, 2)))
-    return upper, lower
 
 
 def gather_top(own, column):
@@ -360,18 +359,9 @@
     for by in (3, 2, 1):
         pairs = pairs_of(lambda c, zz, yy, kk, j: (c, (zz + (1 - 2 * kk) * by) % 8, yy, kk, j))
         direct[by] = lax.ppermute(chunk, ALL, pairs)
-    mine = [direct[by] for by in (1, 2, 3)]
-    theirs = [lax.ppermute(direct[by], ALL, swap) for by in (1, 2, 3)]
-    return [chunk] + mine + theirs + [half, lax.ppermute(half, ALL, swap)], *early
-
-
-def assemble(front, left, right, got_left, got_right):
-    tiles = right.shape[0]
-    left = jnp.concatenate([left, got_left], axis=0).reshape(2 * RANK, tiles, TILE)
-    right = jnp.concatenate([right, got_right], axis=1)
-    update = jnp.einsum("rtk,trn->tkn", left, right, preferred_element_type=jnp.float32)
-    update = update.reshape(tiles * TILE, TILE)
-    return (front.astype(jnp.float32) - update).astype(jnp.bfloat16)
+    mine = [direct[by] for by in (1, 2, 3)] + [half]
+    theirs = lax.ppermute(jnp.concatenate(mine, axis=0), ALL, swap)
+    return [chunk] + mine + [theirs], *early
 
 
 def shards(front, left_factors, right_factors):
@@ -379,36 +369,41 @@
     row = lax.axis_index("row")
     column = lax.axis_index("col")
     z, y, core = row // 4, 2 * side + (row // 2) % 2, row % 2
-    left_all = left_factors[0, 0]
-    right_all = right_factors[0]
-    tiles = right_all.shape[0] // 2
-    send_left = lax.dynamic_slice_in_dim(left_all, (1 - side) * PW, PW, 1)
-    send_right = lax.dynamic_slice_in_dim(right_all, (1 - side) * tiles, tiles, 0)
-    own_left = lax.dynamic_slice_in_dim(left_all, side * PW, PW, 1)
-    own_right = lax.dynamic_slice_in_dim(right_all, side * tiles, tiles, 0)
-
-    swap = pairs_of(lambda c, zz, yy, kk, j: (1 - c, zz, yy, kk, j))
-    got_left = lax.ppermute(send_left, ALL, swap)
-    got_right = lax.ppermute(send_right, ALL, swap)
-    own = assemble(front, own_left, own_right, got_left, got_right)
+    tiles = right_factors.shape[1] // 2
+    left_all = left_factors[0, 0].reshape(RANK, 2 * tiles, TILE).transpose(1, 0, 2)
+    both = jnp.stack([left_all, right_factors[0]])
+    sent = lax.dynamic_slice_in_dim(both, (1 - side) * tiles, tiles, 1)
+    kept = lax.dynamic_slice_in_dim(both, side * tiles, tiles, 1)
+    got = lax.ppermute(
+        sent, ALL, pairs_of(lambda c, zz, yy, kk, j: (1 - c, zz, yy, kk, j))
+    )
+    factors = jnp.concatenate([kept, got], axis=2)
+    update = jnp.einsum("trk,trn->tkn", factors[0], factors[1], preferred_element_type=jnp.float32)
+    own = (front.astype(jnp.float32) - update.reshape(PW, TILE)).astype(jnp.bfloat16)
     tops = gather_top(own, column)
     near, wrap = gather_part(own, is_other)
-    upper, lower = forward_part(near, wrap, is_other)
     token = lax.ppermute(
         near[:8, :128] + wrap[:8, :128],
         ALL,
         [(device(0, 1, 0, 0, j), owner(1, j)) for j in range(4)],
     )
     own_late, token = lax.optimization_barrier((own, token))
-    late_near, late_wrap = gather_part(own_late, is_second)
+    late_near = lax.ppermute(own_late, ALL, moves(is_second, (0, 1), (1, 2), (2, 3)))
+    late_wrap = lax.ppermute(own_late, ALL, moves(is_second, (0, 3)))
     group = jnp.where(jnp.logical_and(y == 0, z == 0), 2 * core, 1)
     where = jnp.stack([group, column, z, core]).astype(jnp.int32)
-    where, near, wrap, late_near = lax.optimization_barrier((where, near, wrap, late_near))
-    late_upper, late_lower = forward_part(late_near, late_wrap, is_second)
+    where, near, wrap, near_a, wrap_b, late_near = lax.optimization_barrier(
+        (where, near, wrap, near[:HALF], wrap[HALF:], late_near)
+    )
+    upper = lax.ppermute(near_a, ALL, moves(is_other, (1, 2), (2, 3)))
+    lower = lax.ppermute(wrap_b, ALL, moves(is_other, (0, 3), (3, 2)))
+    late_far = lax.ppermute(late_near, ALL, moves(is_second, (1, 2), (2, 3)))
     chunks = factor_rows(where, own, tops)
-    chunks, upper, lower, late_wrap = spread_rows(chunks, z, y, core, (upper, lower, late_wrap))
+    chunks, upper, lower, late_wrap, late_far = spread_rows(
+        chunks, z, y, core, (upper, lower, late_wrap, late_far)
+    )
     main = [near, wrap, upper, lower]
-    late = [late_near, late_wrap, late_upper, late_lower]
+    late = [late_near, late_wrap, late_far]
     return apply_rows(where, own, main, late, tops, chunks, token)
 
 

time: 223 us -> 203 us (0.910)
  starting transfers between devices: 80.1 us -> 46.1 us
  waiting for transfers between devices: 109 us -> 115 us
  local copies, waits for them, and re-layouts: 7.53 us -> 12.1 us
    ppermute x10 -> x7, waiting for transfers between devices: 9.9 us -> 53.3 us  [the longest x1 24.9 us: shards(): late_wrap = lax.ppermute(own_late, ALL, moves(is_second, (0, 3)))]
    ppermute x10 -> x7, starting transfers between devices: 38.5 us -> 14.5 us  [the longest x1 6.22 us: spread_rows(): theirs = lax.ppermute(jnp.concatenate(mine, axis=0), ALL, swap)]
    ppermute x2 -> x1, waiting for transfers between devices: 23.7 us -> 0.01 us  [gather_part(): wrap = lax.ppermute(part, ALL, moves(member, (0, 3), (1, 0)))]
    ppermute x2 -> x1, waiting for transfers between devices: 13.2 us -> 0.01 us  [gather_part(): near = lax.ppermute(part, ALL, moves(member, (0, 1), (1, 2), (2, 3)))]
    ppermute x1, starting transfers between devices: 8.61 us -> 0.27 us  [spread_rows(): half = lax.ppermute(part, ALL, across)]
    unnamed x30 -> x33, local copies, waits for them, and re-layouts: 0.88 us -> 7.39 us
    dynamic_slice x3 -> x0, local copies, waits for them, and re-layouts: 2.41 us -> none  [the longest x2 1.33 us: shards(): own_left = lax.dynamic_slice_in_dim(left_all, side * PW, PW, 1)]
    ppermute x1, waiting for transfers between devices: 0.01 us -> 2.24 us  [spread_rows(): lax.ppermute(chunk, ALL, pairs_of(lambda c, zz, yy, kk, j: (c, zz, yy, 1,...]
  transfers between devices with their start and end apart: 39 -> 34, of which waited for: 8 -> 9; matrix products, arithmetic and copies ran while one was open for 6% -> 5% of each run, Pallas kernels for 1% -> 1%
where the time goes in v5:
time: 203 us; the launch traced here: 200 us
  waiting for transfers between devices  115 us (57%)
  starting transfers between devices  46.1 us (23%)
  Pallas kernels  15.8 us (8%)
  local copies, waits for them, and re-layouts  12.1 us (6%)
  other arithmetic  9.92 us (5%)
    ppermute x1, waiting for transfers between devices, shards(): lax.ppermute(near[:8, :128] + wrap[:8, :128], ALL, [(device(0, 1, 0, 0, j...  47.7 us
    ppermute x1, waiting for transfers between devices, shards(): late_wrap = lax.ppermute(own_late, ALL, moves(is_second, (0, 3)))  24.9 us
    ppermute x1, waiting for transfers between devices, shards(): lax.ppermute(own_late, ALL, moves(is_second, (0, 1), (1, 2), (2, 3)))  14.9 us
    pallas_call x1, Pallas kernels, apply_rows(): pl.pallas_call(apply_kernel, out_shape=jax.ShapeDtypeStruct((TILE, PW), j...  13.6 us
    ppermute x9, starting transfers between devices, send(): return lax.ppermute(part, ALL, moves(is_first, *steps))  12.1 us
    ppermute x1, waiting for transfers between devices, shards(): lax.ppermute(sent, ALL, pairs_of(lambda c, zz, yy, kk, j: (1 - c, zz, yy,...  11.4 us
    ppermute x1, waiting for transfers between devices, spread_rows(): half = lax.ppermute(part, ALL, across)  9.64 us
    unnamed x33, local copies, waits for them, and re-layouts  7.39 us
  transfers between devices with their start and end apart: 34, of which 9 were waited for; matrix products, arithmetic and copies ran while one was open for 5% of the time, Pallas kernels for 1%

profile of v5, /device:TPU:7, one launch (start us, length us, event | category | flops | bytes accessed | tf_op | source)
XLA Modules:
  0.0 200.4 jit_solution(8728755250428014456)
XLA Ops:
  0.0 1.3 copy.8
  1.6 3.0 %collective-permute-start = (bf16[2,4,64,512]{3,2,1,0:T(8,128)(2,1)S(1)}, bf16[2,4,64,512]{3,2,1,0:T(8,128)(2,1)S(1)}, u32[]{:S(2)}, u32[]{:S(2)}) collective-permute-start(bf16[2,4,64,512]{3,2,1,0:T(8,128)(2,1)S(1)} %get-tuple-element.56), channel_id=1, source_target_pairs={{0,128},{1,129},{2,130},{3,131},{4,132},{5,133},{6,134},{7,135},{8... | collective-permute-start | bytes 1572872 | tf_op jit(solution)/shard_map/ppermute | solution.py:377
  4.6 11.4 %collective-permute-done = bf16[2,4,64,512]{3,2,1,0:T(8,128)(2,1)S(1)} collective-permute-done((bf16[2,4,64,512]{3,2,1,0:T(8,128)(2,1)S(1)}, bf16[2,4,64,512]{3,2,1,0:T(8,128)(2,1)S(1)}, u32[]{:S(2)}, u32[]{:S(2)}) %collective-permute-start) | collective-permute-done | bytes 524320 | tf_op jit(solution)/shard_map/ppermute | solution.py:377
  15.9 0.7 fusion.3
  16.7 0.8 copy-done.12
  17.5 2.0 %fusion.own = bf16[2048,512]{1,0:T(8,128)(2,1)} fusion(f32[4,512,512]{2,1,0:T(8,128)S(1)} %fusion.3, bf16[2048,512]{1,0:T(8,128)(2,1)S(1)} %copy-done.12), kind=kLoop, calls=%fused_computation.1 | loop fusion | flops 3145728 | bytes 8388608 | tf_op jit(solution)/shard_map/convert_element_type | solution.py:382
  19.6 0.8 collective-permute-start.2
  20.4 2.0 %collective-permute-start.1 = (bf16[2048,512]{1,0:T(8,128)(2,1)}, bf16[2048,512]{1,0:T(8,128)(2,1)}, u32[]{:S(2)}, u32[]{:S(2)}) collective-permute-start(bf16[2048,512]{1,0:T(8,128)(2,1)} %fusion.own), channel_id=1, source_target_pairs={{8,9},{9,10},{10,11},{12,13},{13,14},{14,15},{16,17},{17,18},{18,1... | collective-permute-start | bytes 6291464 | tf_op jit(solution)/shard_map/ppermute | solution.py:308
  23.1 1.3 collective-permute-start.3
  24.3 3.1 %fusion.11 = (bf16[1024,512]{1,0:T(8,128)(2,1)}, bf16[1024,512]{1,0:T(8,128)(2,1)S(1)}, bf16[1024,512]{1,0:T(8,128)(2,1)}) fusion(bf16[2048,512]{1,0:T(8,128)(2,1)} %fusion.own, pred[]{:T(512)S(6)} %eq.22), kind=kLoop, calls=%fused_computation.27 | loop fusion | flops 524288 | bytes 5242881 | tf_op jit(solution)/shard_map/slice | solution.py:316
  27.4 0.7 collective-permute-start.5
  28.2 47.7 %collective-permute-done.3.refs_22_ = bf16[8,128]{1,0:T(8,128)(2,1)S(1)} collective-permute-done((bf16[8,128]{1,0:T(8,128)(2,1)S(1)}, bf16[8,128]{1,0:T(8,128)(2,1)S(1)}, u32[]{:S(2)}, u32[]{:S(2)}) %collective-permute-start.3) | collective-permute-done | bytes 2080 | tf_op jit(solution)/shard_map/ppermute | solution.py:385
  75.9 1.3 collective-permute-start.4
  77.2 0.7 collective-permute-start.6
  77.9 0.7 collective-permute-start.7
  78.6 1.6 collective-permute-start.9
  80.3 1.6 collective-permute-start.8
  81.9 1.2 broadcast_select_fusion
  83.1 1.7 collective-permute-start.10
  84.8 1.7 collective-permute-start.11
  86.4 1.7 collective-permute-start.12
  88.1 14.9 %collective-permute-done.4.refs_4_ = bf16[2048,512]{1,0:T(8,128)(2,1)} collective-permute-done((bf16[2048,512]{1,0:T(8,128)(2,1)}, bf16[2048,512]{1,0:T(8,128)(2,1)}, u32[]{:S(2)}, u32[]{:S(2)}) %collective-permute-start.4) | collective-permute-done | bytes 2097184 | tf_op jit(solution)/shard_map/ppermute | solution.py:391
  103.0 1.6 collective-permute-start.13
  105.2 2.2 %slice.35 = bf16[1024,512]{1,0:T(8,128)(2,1)} slice(bf16[2048,512]{1,0:T(8,128)(2,1)} %copy-done.11), slice={[1024:2048], [0:512]} | slice | bytes 2097152 | tf_op jit(solution)/shard_map/slice | solution.py:396
  107.5 2.3 %slice.34 = bf16[1024,512]{1,0:T(8,128)(2,1)} slice(bf16[2048,512]{1,0:T(8,128)(2,1)} %collective-permute-done.1.refs_0_), slice={[0:1024], [0:512]} | slice | bytes 2097152 | tf_op jit(solution)/shard_map/slice | solution.py:396
  109.8 1.3 collective-permute-start.23
  111.1 1.3 collective-permute-start.24
  112.4 2.1 %factor_rows.1 = (bf16[64,2048]{1,0:T(8,128)(2,1)}, bf16[64,2048]{1,0:T(8,128)(2,1)}, bf16[64,2048]{1,0:T(8,128)(2,1)}, bf16[64,2048]{1,0:T(8,128)(2,1)}, bf16[6...) custom-call(s32[4]{0:T(128)} %pad_add_fusion.where_ref, ...), custom_call_target="tpu_custom_call" | custom-call | tf_op jit(solution)/shard_map/factor_rows/pallas_call | solution.py:175
  115.2 0.7 collective-permute-start.15
  115.9 0.7 collective-permute-start.16
  118.0 0.7 collective-permute-start.21
  118.7 0.7 collective-permute-start.22
  120.9 1.1 add_select_fusion.1
  122.0 24.9 %collective-permute-done.23.refs_5_ = bf16[2048,512]{1,0:T(8,128)(2,1)S(1)} collective-permute-done((bf16[2048,512]{1,0:T(8,128)(2,1)}, bf16[2048,512]{1,0:T(8,128)(2,1)S(1)}, u32[]{:S(2)}, u32[]{:S(2)}) %collective-permute-start.23) | collective-permute-done | bytes 2097184 | tf_op jit(solution)/shard_map/ppermute | solution.py:392
  146.9 1.0 copy-done.6
  148.5 1.0 copy-done.8
  149.5 1.4 copy-done.14
  153.1 1.3 collective-permute-start.28
  154.4 2.2 %collective-permute-done.28 = bf16[64,2048]{1,0:T(8,128)(2,1)} collective-permute-done((bf16[64,2048]{1,0:T(8,128)(2,1)S(1)}, bf16[64,2048]{1,0:T(8,128)(2,1)}, u32[]{:S(2)}, u32[]{:S(2)}) %collective-permute-start.28) | collective-permute-done | bytes 262176 | tf_op jit(solution)/shard_map/ppermute | solution.py:350
  156.6 1.0 broadcast_select_fusion.2.refs_16_
  157.7 5.5 %collective-permute-start.30 = (bf16[64,2048]{1,0:T(8,128)(2,1)S(1)}, bf16[64,2048]{1,0:T(8,128)(2,1)S(1)}, u32[]{:S(2)}, u32[]{:S(2)}) collective-permute-start(bf16[64,2048]{1,0:T(8,128)(2,1)S(1)} %broadcast_select_fusion.2.refs_16_), channel_id=1, source_target_pairs={{0,32},{1,33},{2,34},{3,35},{4,100},{5,101},{6,102},{7,103},{8,40}... | collective-permute-start | bytes 786440 | tf_op jit(solution)/shard_map/ppermute | solution.py:361
  163.3 1.5 collective-permute-start.29
  165.1 9.6 %collective-permute-done.32.refs_20_ = bf16[32,2048]{1,0:T(8,128)(2,1)S(1)} collective-permute-done((bf16[32,2048]{1,0:T(8,128)(2,1)S(1)}, bf16[32,2048]{1,0:T(8,128)(2,1)S(1)}, u32[]{:S(2)}, u32[]{:S(2)}) %collective-permute-start.32) | collective-permute-done | bytes 131104 | tf_op jit(solution)/shard_map/ppermute | solution.py:357
  174.9 2.1 %collective-permute-done.29.refs_17_ = bf16[64,2048]{1,0:T(8,128)(2,1)S(1)} collective-permute-done((bf16[64,2048]{1,0:T(8,128)(2,1)S(1)}, bf16[64,2048]{1,0:T(8,128)(2,1)S(1)}, u32[]{:S(2)}, u32[]{:S(2)}) %collective-permute-start.29) | collective-permute-done | bytes 262176 | tf_op jit(solution)/shard_map/ppermute | solution.py:361
  177.1 6.2 %collective-permute-start.33 = (bf16[224,2048]{1,0:T(8,128)(2,1)S(1)}, bf16[224,2048]{1,0:T(8,128)(2,1)S(1)}, u32[]{:S(2)}, u32[]{:S(2)}) collective-permute-start(bf16[224,2048]{1,0:T(8,128)(2,1)S(1)} %pad_maximum_fusion), channel_id=1, source_target_pairs={{0,4},{1,5},{2,6},{3,7},{4,0},{5,1},{6,2},{7,3},{8,12},{9,13},{10,... | collective-permute-start | bytes 2752520 | tf_op jit(solution)/shard_map/ppermute | solution.py:363
  183.3 2.1 %collective-permute-done.33.refs_21_ = bf16[224,2048]{1,0:T(8,128)(2,1)S(1)} collective-permute-done((bf16[224,2048]{1,0:T(8,128)(2,1)S(1)}, bf16[224,2048]{1,0:T(8,128)(2,1)S(1)}, u32[]{:S(2)}, u32[]{:S(2)}) %collective-permute-start.33) | collective-permute-done | bytes 917536 | tf_op jit(solution)/shard_map/ppermute | solution.py:363
  185.4 1.2 copy-done.9
  186.6 13.6 %apply_rows.1 = bf16[512,2048]{1,0:T(8,128)(2,1)} custom-call(s32[4]{0:T(128)S(1)} %copy-done.10, bf16[2048,512]{1,0:T(8,128)(2,1)} %fusion.own, bf16[2048,512]{1,0:T(8,128)(2,1)} %collective-permute-done.1.refs_0_, bf16[2048,512]{1,0:T(8,128)(2,1)} %copy-done.11, bf16[1024,512]{1,0:T(8,128)(2,1)S(1)} %copy-done.7, bf16[1024,512]{1,0:T(8,128)(2,1)S(1)} %copy-done.9, ...), custom_call_target="tpu_custom_call" | custom-call | tf_op jit(solution)/shard_map/apply_rows/pallas_call | solution.py:249
  (70 shorter events, 8.4 us)
Async XLA Ops:
  0.0 1.4 copy-start.15
  1.6 14.4 %collective-permute-start = (bf16[2,4,64,512]{3,2,1,0:T(8,128)(2,1)S(1)}, bf16[2,4,64,512]{3,2,1,0:T(8,128)(2,1)S(1)}, u32[]{:S(2)}, u32[]{:S(2)}) collective-permute-start(bf16[2,4,64,512]{3,2,1,0:T(8,128)(2,1)S(1)} %get-tuple-element.56), channel_id=1, source_target_pairs={{0,128},{1,129},{2,130},{3,131},{4,132},{5,133},{6,134},{7,135},{8... | collective-permute-start | bytes 1572872 | tf_op jit(solution)/shard_map/ppermute | solution.py:377
  15.9 1.6 copy-start.12
  19.6 2.8 %collective-permute-start.2 = (bf16[2048,512]{1,0:T(8,128)(2,1)}, bf16[2048,512]{1,0:T(8,128)(2,1)S(1)}, u32[]{:S(2)}, u32[]{:S(2)}) collective-permute-start(bf16[2048,512]{1,0:T(8,128)(2,1)} %fusion.own), channel_id=1, source_target_pairs={{8,11},{9,8},{12,15},{13,12},{16,19},{17,16},{20,23},{21,20},{24,2... | collective-permute-start | bytes 6291464 | tf_op jit(solution)/shard_map/ppermute | solution.py:307
  20.4 2.0 %collective-permute-start.1 = (bf16[2048,512]{1,0:T(8,128)(2,1)}, bf16[2048,512]{1,0:T(8,128)(2,1)}, u32[]{:S(2)}, u32[]{:S(2)}) collective-permute-start(bf16[2048,512]{1,0:T(8,128)(2,1)} %fusion.own), channel_id=1, source_target_pairs={{8,9},{9,10},{10,11},{12,13},{13,14},{14,15},{16,17},{17,18},{18,1... | collective-permute-start | bytes 6291464 | tf_op jit(solution)/shard_map/ppermute | solution.py:308
  22.4 5.0 %copy-start.11 = (bf16[2048,512]{1,0:T(8,128)(2,1)}, bf16[2048,512]{1,0:T(8,128)(2,1)S(1)}, u32[]{:S(2)}) copy-start(bf16[2048,512]{1,0:T(8,128)(2,1)S(1)} %collective-permute-done.2.refs_1_) | copy-start | bytes 6291460
  23.1 52.8 %collective-permute-start.3 = (bf16[8,128]{1,0:T(8,128)(2,1)S(1)}, bf16[8,128]{1,0:T(8,128)(2,1)S(1)}, u32[]{:S(2)}, u32[]{:S(2)}) collective-permute-start(bf16[8,128]{1,0:T(8,128)(2,1)S(1)} %slice_add_fusion), channel_id=1, source_target_pairs={{16,4},{17,5},{18,6},{19,7}} | collective-permute-start | bytes 6152 | tf_op jit(solution)/shard_map/ppermute | solution.py:385
  27.4 51.2 %collective-permute-start.5 = (bf16[1024,512]{1,0:T(8,128)(2,1)S(1)}, bf16[1024,512]{1,0:T(8,128)(2,1)S(1)}, u32[]{:S(2)}, u32[]{:S(2)}) collective-permute-start(bf16[1024,512]{1,0:T(8,128)(2,1)S(1)} %get-tuple-element.54), channel_id=1, source_target_pairs={{0,3},{1,0}} | collective-permute-start | bytes 3145736 | tf_op jit(solution)/shard_map/ppermute | solution.py:314
  75.9 27.1 %collective-permute-start.4 = (bf16[2048,512]{1,0:T(8,128)(2,1)}, bf16[2048,512]{1,0:T(8,128)(2,1)}, u32[]{:S(2)}, u32[]{:S(2)}) collective-permute-start(bf16[2048,512]{1,0:T(8,128)(2,1)} %fusion.own), channel_id=1, source_target_pairs={{4,5},{5,6},{6,7}} | collective-permute-start | bytes 6291464 | tf_op jit(solution)/shard_map/ppermute | solution.py:391
  77.2 4.8 %collective-permute-start.6 = (bf16[1024,512]{1,0:T(8,128)(2,1)}, bf16[1024,512]{1,0:T(8,128)(2,1)S(1)}, u32[]{:S(2)}, u32[]{:S(2)}) collective-permute-start(bf16[1024,512]{1,0:T(8,128)(2,1)} %get-tuple-element.34), channel_id=1, source_target_pairs={{1,2},{2,3}} | collective-permute-start | bytes 3145736 | tf_op jit(solution)/shard_map/ppermute | solution.py:314
  77.9 6.9 %collective-permute-start.7 = (bf16[1024,512]{1,0:T(8,128)(2,1)}, bf16[1024,512]{1,0:T(8,128)(2,1)S(1)}, u32[]{:S(2)}, u32[]{:S(2)}) collective-permute-start(bf16[1024,512]{1,0:T(8,128)(2,1)} %get-tuple-element.35), channel_id=1, source_target_pairs={{0,3},{1,2}} | collective-permute-start | bytes 3145736 | tf_op jit(solution)/shard_map/ppermute | solution.py:314
  78.6 28.9 %copy-start = (bf16[1024,512]{1,0:T(8,128)(2,1)}, bf16[1024,512]{1,0:T(8,128)(2,1)S(1)}, u32[]{:S(2)}) copy-start(bf16[1024,512]{1,0:T(8,128)(2,1)S(1)} %collective-permute-done.5.refs_0_.refs_7_) | copy-start | bytes 3145732
  78.6 7.8 %collective-permute-start.9 = (bf16[1024,512]{1,0:T(8,128)(2,1)S(1)}, bf16[1024,512]{1,0:T(8,128)(2,1)}, u32[]{:S(2)}, u32[]{:S(2)}) collective-permute-start(bf16[1024,512]{1,0:T(8,128)(2,1)S(1)} %collective-permute-done.5.refs_0_.refs_7_), channel_id=1, source_target_pairs={{0,3}} | collective-permute-start | bytes 3145736 | tf_op jit(solution)/shard_map/ppermute | solution.py:314
  80.3 29.5 %collective-permute-start.8 = (bf16[1024,512]{1,0:T(8,128)(2,1)}, bf16[1024,512]{1,0:T(8,128)(2,1)}, u32[]{:S(2)}, u32[]{:S(2)}) collective-permute-start(bf16[1024,512]{1,0:T(8,128)(2,1)} %get-tuple-element.35), channel_id=1, source_target_pairs={{2,3}} | collective-permute-start | bytes 3145736 | tf_op jit(solution)/shard_map/ppermute | solution.py:314
  81.9 25.6 %copy-start.2 = (bf16[1024,512]{1,0:T(8,128)(2,1)}, bf16[1024,512]{1,0:T(8,128)(2,1)S(1)}, u32[]{:S(2)}) copy-start(bf16[1024,512]{1,0:T(8,128)(2,1)S(1)} %collective-permute-done.6.refs_1_.refs_8_) | copy-start | bytes 3145732
  83.1 28.0 %collective-permute-start.10 = (bf16[1024,512]{1,0:T(8,128)(2,1)}, bf16[1024,512]{1,0:T(8,128)(2,1)}, u32[]{:S(2)}, u32[]{:S(2)}) collective-permute-start(bf16[1024,512]{1,0:T(8,128)(2,1)} %broadcast_select_fusion), channel_id=1, source_target_pairs={{2,3},{3,2}} | collective-permute-start | bytes 3145736 | tf_op jit(solution)/shard_map/ppermute | solution.py:314
  84.8 25.0 %copy-start.4 = (bf16[1024,512]{1,0:T(8,128)(2,1)}, bf16[1024,512]{1,0:T(8,128)(2,1)S(1)}, u32[]{:S(2)}) copy-start(bf16[1024,512]{1,0:T(8,128)(2,1)S(1)} %collective-permute-done.7.refs_2_.refs_9_) | copy-start | bytes 3145732
  84.8 27.6 %collective-permute-start.11 = (bf16[1024,512]{1,0:T(8,128)(2,1)S(1)}, bf16[1024,512]{1,0:T(8,128)(2,1)}, u32[]{:S(2)}, u32[]{:S(2)}) collective-permute-start(bf16[1024,512]{1,0:T(8,128)(2,1)S(1)} %collective-permute-done.7.refs_2_.refs_9_), channel_id=1, source_target_pairs={{3,2}} | collective-permute-start | bytes 3145736 | tf_op jit(solution)/shard_map/ppermute | solution.py:314
  86.4 26.0 %collective-permute-start.12 = (bf16[1024,512]{1,0:T(8,128)(2,1)}, bf16[1024,512]{1,0:T(8,128)(2,1)}, u32[]{:S(2)}, u32[]{:S(2)}) collective-permute-start(bf16[1024,512]{1,0:T(8,128)(2,1)} %get-tuple-element.34), channel_id=1, source_target_pairs={{0,1}} | collective-permute-start | bytes 3145736 | tf_op jit(solution)/shard_map/ppermute | solution.py:314
  103.0 9.4 %collective-permute-start.13 = (bf16[1024,512]{1,0:T(8,128)(2,1)}, bf16[1024,512]{1,0:T(8,128)(2,1)}, u32[]{:S(2)}, u32[]{:S(2)}) collective-permute-start(bf16[1024,512]{1,0:T(8,128)(2,1)} %get-tuple-element.35), channel_id=1, source_target_pairs={{0,1}} | collective-permute-start | bytes 3145736 | tf_op jit(solution)/shard_map/ppermute | solution.py:314
  109.8 37.1 %collective-permute-start.23 = (bf16[2048,512]{1,0:T(8,128)(2,1)}, bf16[2048,512]{1,0:T(8,128)(2,1)S(1)}, u32[]{:S(2)}, u32[]{:S(2)}) collective-permute-start(bf16[2048,512]{1,0:T(8,128)(2,1)} %fusion.own), channel_id=1, source_target_pairs={{4,7}} | collective-permute-start | bytes 6291464 | tf_op jit(solution)/shard_map/ppermute | solution.py:392
  111.1 38.5 %collective-permute-start.24 = (bf16[2048,512]{1,0:T(8,128)(2,1)}, bf16[2048,512]{1,0:T(8,128)(2,1)S(1)}, u32[]{:S(2)}, u32[]{:S(2)}) collective-permute-start(bf16[2048,512]{1,0:T(8,128)(2,1)} %collective-permute-done.4.refs_4_), channel_id=1, source_target_pairs={{5,6},{6,7}} | collective-permute-start | bytes 6291464 | tf_op jit(solution)/shard_map/ppermute | solution.py:400
  114.5 2.1 %collective-permute-start.14 = (bf16[64,2048]{1,0:T(8,128)(2,1)}, bf16[64,2048]{1,0:T(8,128)(2,1)S(1)}, u32[]{:S(2)}, u32[]{:S(2)}) collective-permute-start(bf16[64,2048]{1,0:T(8,128)(2,1)} %get-tuple-element.37), channel_id=1, source_target_pairs={{0,16},{1,17},{2,18},{3,19}} | collective-permute-start | bytes 786440 | tf_op jit(solution)/shard_map/ppermute | solution.py:338
  115.2 2.1 %collective-permute-start.15 = (bf16[64,2048]{1,0:T(8,128)(2,1)}, bf16[64,2048]{1,0:T(8,128)(2,1)S(1)}, u32[]{:S(2)}, u32[]{:S(2)}) collective-permute-start(bf16[64,2048]{1,0:T(8,128)(2,1)} %get-tuple-element.38), channel_id=1, source_target_pairs={{0,32},{1,33},{2,34},{3,35}} | collective-permute-start | bytes 786440 | tf_op jit(solution)/shard_map/ppermute | solution.py:338
  115.9 2.1 %collective-permute-start.16 = (bf16[64,2048]{1,0:T(8,128)(2,1)}, bf16[64,2048]{1,0:T(8,128)(2,1)S(1)}, u32[]{:S(2)}, u32[]{:S(2)}) collective-permute-start(bf16[64,2048]{1,0:T(8,128)(2,1)} %get-tuple-element.39), channel_id=1, source_target_pairs={{0,48},{1,49},{2,50},{3,51}} | collective-permute-start | bytes 786440 | tf_op jit(solution)/shard_map/ppermute | solution.py:338
  116.6 2.1 %collective-permute-start.17 = (bf16[64,2048]{1,0:T(8,128)(2,1)}, bf16[64,2048]{1,0:T(8,128)(2,1)S(1)}, u32[]{:S(2)}, u32[]{:S(2)}) collective-permute-start(bf16[64,2048]{1,0:T(8,128)(2,1)} %get-tuple-element.40), channel_id=1, source_target_pairs={{0,64},{1,65},{2,66},{3,67}} | collective-permute-start | bytes 786440 | tf_op jit(solution)/shard_map/ppermute | solution.py:338
  117.3 2.2 %collective-permute-start.18 = (bf16[64,2048]{1,0:T(8,128)(2,1)}, bf16[64,2048]{1,0:T(8,128)(2,1)S(1)}, u32[]{:S(2)}, u32[]{:S(2)}) collective-permute-start(bf16[64,2048]{1,0:T(8,128)(2,1)} %get-tuple-element.41), channel_id=1, source_target_pairs={{0,80},{1,81},{2,82},{3,83}} | collective-permute-start | bytes 786440 | tf_op jit(solution)/shard_map/ppermute | solution.py:338
  118.0 28.9 %collective-permute-start.21 = (bf16[1024,512]{1,0:T(8,128)(2,1)}, bf16[1024,512]{1,0:T(8,128)(2,1)S(1)}, u32[]{:S(2)}, u32[]{:S(2)}) collective-permute-start(bf16[1024,512]{1,0:T(8,128)(2,1)} %slice.34), channel_id=1, source_target_pairs={{9,10},{10,11},{13,14},{14,15},{17,18},{18,19},{21,22},{22,23},{25... | collective-permute-start | bytes 3145736 | tf_op jit(solution)/shard_map/ppermute | solution.py:398
  118.7 29.2 %collective-permute-start.22 = (bf16[1024,512]{1,0:T(8,128)(2,1)}, bf16[1024,512]{1,0:T(8,128)(2,1)S(1)}, u32[]{:S(2)}, u32[]{:S(2)}) collective-permute-start(bf16[1024,512]{1,0:T(8,128)(2,1)} %slice.35), channel_id=1, source_target_pairs={{8,11},{11,10},{12,15},{15,14},{16,19},{19,18},{20,23},{23,22},{24... | collective-permute-start | bytes 3145736 | tf_op jit(solution)/shard_map/ppermute | solution.py:399
  119.5 0.7 collective-permute-start.19
  120.2 0.7 collective-permute-start.20
  121.9 63.4 %copy-start.1 = (bf16[1024,512]{1,0:T(8,128)(2,1)S(1)}, bf16[1024,512]{1,0:T(8,128)(2,1)}, u32[]{:S(2)}) copy-start(bf16[1024,512]{1,0:T(8,128)(2,1)} %copy-done) | copy-start | bytes 3145732
  122.0 63.4 %copy-start.3 = (bf16[1024,512]{1,0:T(8,128)(2,1)S(1)}, bf16[1024,512]{1,0:T(8,128)(2,1)}, u32[]{:S(2)}) copy-start(bf16[1024,512]{1,0:T(8,128)(2,1)} %copy-done.2) | copy-start | bytes 3145732
  122.0 63.4 %copy-start.5 = (bf16[1024,512]{1,0:T(8,128)(2,1)S(1)}, bf16[1024,512]{1,0:T(8,128)(2,1)}, u32[]{:S(2)}) copy-start(bf16[1024,512]{1,0:T(8,128)(2,1)} %copy-done.4) | copy-start | bytes 3145732
  122.0 63.4 %copy-start.10 = (s32[4]{0:T(128)S(1)}, s32[4]{0:T(128)}, u32[]{:S(2)}) copy-start(s32[4]{0:T(128)} %pad_add_fusion.where_ref) | copy-start | bytes 52
  146.9 1.6 copy-start.13
  149.5 1.4 copy-start.14
  150.9 2.0 %collective-permute-start.27 = (bf16[64,2048]{1,0:T(8,128)(2,1)S(1)}, bf16[64,2048]{1,0:T(8,128)(2,1)S(1)}, u32[]{:S(2)}, u32[]{:S(2)}) collective-permute-start(bf16[64,2048]{1,0:T(8,128)(2,1)S(1)} %add_select_fusion.1), channel_id=1, source_target_pairs={{0,128},{1,129},{2,130},{3,131},{16,144},{17,145},{18,146},{19,147... | collective-permute-start | bytes 786440 | tf_op jit(solution)/shard_map/ppermute | solution.py:347
  151.6 1.4 collective-permute-start.26
  152.3 0.7 collective-permute-start.25
  153.1 3.6 %collective-permute-start.28 = (bf16[64,2048]{1,0:T(8,128)(2,1)S(1)}, bf16[64,2048]{1,0:T(8,128)(2,1)}, u32[]{:S(2)}, u32[]{:S(2)}) collective-permute-start(bf16[64,2048]{1,0:T(8,128)(2,1)S(1)} %add_select_fusion), channel_id=1, source_target_pairs={{0,4},{1,5},{2,6},{3,7},{8,12},{9,13},{10,14},{11,15},{16,20},{17,... | collective-permute-start | bytes 786440 | tf_op jit(solution)/shard_map/ppermute | solution.py:350
  154.4 31.0 %copy-start.7 = (bf16[1024,512]{1,0:T(8,128)(2,1)S(1)}, bf16[1024,512]{1,0:T(8,128)(2,1)}, u32[]{:S(2)}) copy-start(bf16[1024,512]{1,0:T(8,128)(2,1)} %copy-done.6) | copy-start | bytes 3145732
  157.6 17.1 %collective-permute-start.31 = (bf16[64,2048]{1,0:T(8,128)(2,1)S(1)}, bf16[64,2048]{1,0:T(8,128)(2,1)S(1)}, u32[]{:S(2)}, u32[]{:S(2)}) collective-permute-start(bf16[64,2048]{1,0:T(8,128)(2,1)S(1)} %broadcast_select_fusion.2.refs_16_), channel_id=1, source_target_pairs={{0,48},{1,49},{2,50},{3,51},{4,84},{5,85},{6,86},{7,87},{8,56},{9,... | collective-permute-start | bytes 786440 | tf_op jit(solution)/shard_map/ppermute | solution.py:361
  157.7 17.2 %collective-permute-start.30 = (bf16[64,2048]{1,0:T(8,128)(2,1)S(1)}, bf16[64,2048]{1,0:T(8,128)(2,1)S(1)}, u32[]{:S(2)}, u32[]{:S(2)}) collective-permute-start(bf16[64,2048]{1,0:T(8,128)(2,1)S(1)} %broadcast_select_fusion.2.refs_16_), channel_id=1, source_target_pairs={{0,32},{1,33},{2,34},{3,35},{4,100},{5,101},{6,102},{7,103},{8,40}... | collective-permute-start | bytes 786440 | tf_op jit(solution)/shard_map/ppermute | solution.py:361
  163.3 13.7 %collective-permute-start.29 = (bf16[64,2048]{1,0:T(8,128)(2,1)S(1)}, bf16[64,2048]{1,0:T(8,128)(2,1)S(1)}, u32[]{:S(2)}, u32[]{:S(2)}) collective-permute-start(bf16[64,2048]{1,0:T(8,128)(2,1)S(1)} %broadcast_select_fusion.2.refs_16_), channel_id=1, source_target_pairs={{0,16},{1,17},{2,18},{3,19},{4,116},{5,117},{6,118},{7,119},{8,24}... | collective-permute-start | bytes 786440 | tf_op jit(solution)/shard_map/ppermute | solution.py:361
  164.8 9.9 %collective-permute-start.32 = (bf16[32,2048]{1,0:T(8,128)(2,1)S(1)}, bf16[32,2048]{1,0:T(8,128)(2,1)S(1)}, u32[]{:S(2)}, u32[]{:S(2)}) collective-permute-start(bf16[32,2048]{1,0:T(8,128)(2,1)S(1)} %constant_dynamic-slice_fusion), channel_id=1, source_target_pairs={{0,64},{1,65},{2,66},{3,67},{4,68},{5,69},{6,70},{7,71},{8,72},{9,... | collective-permute-start | bytes 393224 | tf_op jit(solution)/shard_map/ppermute | solution.py:357
  177.1 8.3 %collective-permute-start.33 = (bf16[224,2048]{1,0:T(8,128)(2,1)S(1)}, bf16[224,2048]{1,0:T(8,128)(2,1)S(1)}, u32[]{:S(2)}, u32[]{:S(2)}) collective-permute-start(bf16[224,2048]{1,0:T(8,128)(2,1)S(1)} %pad_maximum_fusion), channel_id=1, source_target_pairs={{0,4},{1,5},{2,6},{3,7},{4,0},{5,1},{6,2},{7,3},{8,12},{9,13},{10,... | collective-permute-start | bytes 2752520 | tf_op jit(solution)/shard_map/ppermute | solution.py:363
  185.4 1.2 copy-start.9
  (2 other events, 2.0 us)

commit v6 on v5

--- a/solution.py
+++ b/solution.py
@@ -69,55 +69,30 @@
         copy.wait()
 
 
-def fetch_tops(col, tops, dest, sems):
-    u0, u2_u1, w0_w1, w2, w1, u1_u0, w0, u0_next, w0_next = tops
+def fetch_rows(col, parts, dest, sems):
+    near, wrap, far = parts
     found = {
-        1: [(u0_next, 0, 0, HALF), (w0_next, 0, 1, HALF)],
-        2: [(u2_u1, 1, 0, HALF), (w0_w1, 1, 1, HALF), (u1_u0, 0, 0, HALF), (w0, 0, 1, HALF)],
-        3: [
-            (u0, 0, 0, HALF),
-            (w0_w1, 0, 1, HALF),
-            (u2_u1, 2, 0, HALF),
-            (w2, 2, 1, HALF),
-            (u1_u0, 1, 0, HALF),
-            (w1, 1, 1, HALF),
-        ],
+        1: [(near, 0, 0, PW)],
+        2: [(near, 1, 0, PW), (far, 0, 0, PW)],
+        3: [(near, 2, 0, PW), (wrap, 0, 0, PW), (far, 1, 0, PW)],
     }
-    for column, parts in found.items():
+    for column, copies in found.items():
 
         @pl.when(col == column)
         def _():
-            run_copies(parts, dest, sems)
-
-
-def fetch_rows(col, parts, dest, sems):
-    near, wrap = parts[:2]
-    if len(parts) == 4:
-        far = [(parts[2], 0, HALF), (parts[3], 1, HALF)]
-    else:
-        far = [(parts[2], 0, PW)]
-    found = {
-        1: [(near, 0, 0, PW)],
-        2: [(near, 1, 0, PW)] + [(part, 0, at, size) for part, at, size in far],
-        3: [(near, 2, 0, PW), (wrap, 0, 0, PW)] + [(part, 1, at, size) for part, at, size in far],
-    }
-    for column, parts in found.items():
-
-        @pl.when(col == column)
-        def _():
-            run_copies(parts, dest, sems)
+            run_copies(copies, dest, sems)
 
 
 def factor_kernel(where_ref, own, *refs):
-    tops, outs = refs[:9], refs[9:17]
-    t_ref, s_ref, l_ref, x_ref, r_ref, g_ref, n_ref, e_ref, sems = refs[17:]
-    col = where_ref[1]
-
-    @pl.when(where_ref[0] == 0)
+    parts, outs = refs[:3], refs[3:11]
+    t_ref, s_ref, l_ref, x_ref, r_ref, g_ref, n_ref, e_ref, sems = refs[11:]
+    col = where_ref[2]
+
+    @pl.when(where_ref[0] == 1)
     def _():
-        mine = pltpu.make_async_copy(own, t_ref.at[col], sems.at[6])
+        mine = pltpu.make_async_copy(own, t_ref.at[col], sems.at[3])
         mine.start()
-        fetch_tops(col, tops, t_ref, sems)
+        fetch_rows(col, parts, t_ref, sems)
         mine.wait()
 
         def rows_of(i):
@@ -171,11 +146,11 @@
 HBM = pl.BlockSpec(memory_space=pltpu.HBM)
 
 
-def factor_rows(where, own, tops):
+def factor_rows(where, own, parts):
     return pl.pallas_call(
         factor_kernel,
         out_shape=[jax.ShapeDtypeStruct((64, PW), jnp.bfloat16)] * 8,
-        in_specs=[pl.BlockSpec(memory_space=pltpu.SMEM)] + [HBM] * 10,
+        in_specs=[pl.BlockSpec(memory_space=pltpu.SMEM)] + [HBM] * 4,
         out_specs=[pl.BlockSpec(memory_space=pltpu.VMEM)] * 8,
         scratch_shapes=[
             pltpu.VMEM((BLOCKS, PW, TILE), jnp.bfloat16),
@@ -186,21 +161,21 @@
             pltpu.VMEM((TILE, TILE), jnp.float32),
             pltpu.VMEM((TILE, TILE), jnp.float32),
             pltpu.VMEM((TILE, TILE), jnp.bfloat16),
-            pltpu.SemaphoreType.DMA((7,)),
+            pltpu.SemaphoreType.DMA((4,)),
         ],
         compiler_params=pltpu.CompilerParams(vmem_limit_bytes=56 << 20),
         name="factor_rows",
-    )(where, own, *tops)
+    )(where, own, *parts)
 
 
 CHUNKS = 6
 
 
 def apply_kernel(where_ref, own, *refs):
-    main, late, tops = refs[:4], refs[4:7], refs[7:16]
-    chunks = refs[16 : 16 + CHUNKS]
-    out, p_ref, r_ref, acc_ref, psems, rsems = refs[17 + CHUNKS :]
-    group, col, z, core = where_ref[0], where_ref[1], where_ref[2], where_ref[3]
+    main, late = refs[:3], refs[3:6]
+    chunks = refs[6 : 6 + CHUNKS]
+    out, p_ref, r_ref, psems, rsems = refs[7 + CHUNKS :]
+    second, col, z, core = where_ref[1], where_ref[2], where_ref[3], where_ref[4]
     sign = 1 - 2 * core
     copies = []
 
@@ -215,52 +190,47 @@
         place(swapped.at[pl.ds(by * 64 - 64, 64)], lax.rem(z + sign * by + 8, 8) * 64, 64)
     place(chunks[4], lax.rem(z + 4, 8) * 64 + core * 32, 32)
     place(swapped.at[pl.ds(192, 32)], lax.rem(z + 4, 8) * 64 + (1 - core) * 32, 32)
-    copies.append(pltpu.make_async_copy(own, p_ref.at[col], psems.at[6]))
+    copies.append(pltpu.make_async_copy(own, p_ref.at[col], psems.at[3]))
     for copy in copies:
         copy.start()
 
-    @pl.when(group == 0)
-    def _():
-        fetch_tops(col, tops, p_ref, psems)
-
-    for index, parts in ((1, main), (2, late)):
-
-        @pl.when(group == index)
+    for index, parts in ((0, main), (1, late)):
+
+        @pl.when(second == index)
         def _():
             fetch_rows(col, parts, p_ref, psems)
 
     for copy in copies:
         copy.wait()
 
-    @pl.loop(0, PW // TILE)
-    def _(tile):
-        at = pl.ds(pl.multiple_of(tile * TILE, TILE), TILE)
-        acc_ref[...] = mxu(r_ref[:, :TILE], p_ref[0, at, :], NT)
-        for k in range(1, BLOCKS):
-
-            @pl.when(k <= col)
-            def _():
-                acc_ref[...] += mxu(r_ref[:, k * TILE : (k + 1) * TILE], p_ref[k, at, :], NT)
-
-        out[:, at] = acc_ref[...].astype(jnp.bfloat16)
-
-
-def apply_rows(where, own, main, late, tops, chunks, token):
+    for last in range(BLOCKS):
+
+        @pl.when(col == last)
+        def _():
+            @pl.loop(0, PW // TILE)
+            def _(tile):
+                at = pl.ds(pl.multiple_of(tile * TILE, TILE), TILE)
+                acc = mxu(r_ref[:, :TILE], p_ref[0, at, :], NT)
+                for k in range(1, last + 1):
+                    acc = acc + mxu(r_ref[:, k * TILE : (k + 1) * TILE], p_ref[k, at, :], NT)
+                out[:, at] = acc.astype(jnp.bfloat16)
+
+
+def apply_rows(where, own, main, late, chunks, token):
     return pl.pallas_call(
         apply_kernel,
         out_shape=jax.ShapeDtypeStruct((TILE, PW), jnp.bfloat16),
-        in_specs=[pl.BlockSpec(memory_space=pltpu.SMEM)] + [HBM] * (18 + CHUNKS),
+        in_specs=[pl.BlockSpec(memory_space=pltpu.SMEM)] + [HBM] * (8 + CHUNKS),
         out_specs=pl.BlockSpec(memory_space=pltpu.VMEM),
         scratch_shapes=[
             pltpu.VMEM((BLOCKS, PW, TILE), jnp.bfloat16),
             pltpu.VMEM((TILE, PW), jnp.bfloat16),
-            pltpu.VMEM((TILE, TILE), jnp.float32),
-            pltpu.SemaphoreType.DMA((7,)),
+            pltpu.SemaphoreType.DMA((4,)),
             pltpu.SemaphoreType.DMA((9,)),
         ],
         compiler_params=pltpu.CompilerParams(vmem_limit_bytes=40 << 20),
         name="apply_rows",
-    )(where, own, *main, *late, *tops, *chunks, token)
+    )(where, own, *main, *late, *chunks, token)
 
 
 def device(child, z, ylo, core, col):
@@ -291,44 +261,23 @@
     )
 
 
-def is_first(c, z, y, k):
-    return (c, z, y, k) == (0, 0, 0, 0)
-
-
 def is_second(c, z, y, k):
     return (c, z, y, k) == (0, 0, 0, 1)
 
 
 def is_other(c, z, y, k):
-    return (c, z, y) != (0, 0, 0)
-
-
-def gather_part(part, member):
-    wrap = lax.ppermute(part, ALL, moves(member, (0, 3), (1, 0)))
+    return (c, z, y, k) != (0, 0, 0, 1)
+
+
+def gather(part, member):
     near = lax.ppermute(part, ALL, moves(member, (0, 1), (1, 2), (2, 3)))
-    return near, wrap
-
-
-def gather_top(own, column):
-    def send(part, *steps):
-        return lax.ppermute(part, ALL, moves(is_first, *steps))
-
-    upper, lower = own[:HALF], own[HALF:]
-    first = jnp.where(column == 1, lower, upper)
-    u0 = send(first, (0, 3), (1, 0))
-    u2_u1 = send(upper, (2, 3), (1, 2))
-    w0_w1 = send(lower, (0, 3), (1, 2))
-    w2 = send(lower, (2, 3))
-    w1 = send(u0, (0, 3))
-    u1_u0 = send(jnp.where(column == 3, u0, u2_u1), (2, 3), (3, 2))
-    w0 = send(w0_w1, (3, 2))
-    upper, lower, w1 = lax.optimization_barrier((upper, lower, w1))
-    u0_next = send(upper, (0, 1))
-    w0_next = send(lower, (0, 1))
-    return [u0, u2_u1, w0_w1, w2, w1, u1_u0, w0, u0_next, w0_next]
-
-
-def spread_rows(chunks, z, y, core, early):
+    wrap = lax.ppermute(part, ALL, moves(member, (0, 3)))
+    near, wrap = lax.optimization_barrier((near, wrap))
+    far = lax.ppermute(near, ALL, moves(member, (1, 2), (2, 3)))
+    return [near, wrap, far]
+
+
+def spread_rows(chunks, z, y, core):
     kept = chunks[0]
     total = None
     for k in range(1, 8):
@@ -338,7 +287,6 @@
         got = lax.ppermute(chunks[k], ALL, pairs)
         total = got if total is None else total + got
     chunk = jnp.where(z == 0, kept, total)
-    chunk, *early = lax.optimization_barrier((chunk, *early))
     total = None
     for to in (1, 3, 2):
         pairs = pairs_of(
@@ -361,7 +309,7 @@
         direct[by] = lax.ppermute(chunk, ALL, pairs)
     mine = [direct[by] for by in (1, 2, 3)] + [half]
     theirs = lax.ppermute(jnp.concatenate(mine, axis=0), ALL, swap)
-    return [chunk] + mine + [theirs], *early
+    return [chunk] + mine + [theirs]
 
 
 def shards(front, left_factors, right_factors):
@@ -380,31 +328,22 @@
     factors = jnp.concatenate([kept, got], axis=2)
     update = jnp.einsum("trk,trn->tkn", factors[0], factors[1], preferred_element_type=jnp.float32)
     own = (front.astype(jnp.float32) - update.reshape(PW, TILE)).astype(jnp.bfloat16)
-    tops = gather_top(own, column)
-    near, wrap = gather_part(own, is_other)
+    main = gather(own, is_other)
     token = lax.ppermute(
-        near[:8, :128] + wrap[:8, :128],
+        main[0][:8, :128] + main[1][:8, :128],
         ALL,
-        [(device(0, 1, 0, 0, j), owner(1, j)) for j in range(4)],
+        [(device(0, 1, 0, 0, j), device(0, 0, 0, 1, j)) for j in range(4)],
     )
     own_late, token = lax.optimization_barrier((own, token))
-    late_near = lax.ppermute(own_late, ALL, moves(is_second, (0, 1), (1, 2), (2, 3)))
-    late_wrap = lax.ppermute(own_late, ALL, moves(is_second, (0, 3)))
-    group = jnp.where(jnp.logical_and(y == 0, z == 0), 2 * core, 1)
-    where = jnp.stack([group, column, z, core]).astype(jnp.int32)
-    where, near, wrap, near_a, wrap_b, late_near = lax.optimization_barrier(
-        (where, near, wrap, near[:HALF], wrap[HALF:], late_near)
-    )
-    upper = lax.ppermute(near_a, ALL, moves(is_other, (1, 2), (2, 3)))
-    lower = lax.ppermute(wrap_b, ALL, moves(is_other, (0, 3), (3, 2)))
-    late_far = lax.ppermute(late_near, ALL, moves(is_second, (1, 2), (2, 3)))
-    chunks = factor_rows(where, own, tops)
-    chunks, upper, lower, late_wrap, late_far = spread_rows(
-        chunks, z, y, core, (upper, lower, late_wrap, late_far)
-    )
-    main = [near, wrap, upper, lower]
-    late = [late_near, late_wrap, late_far]
-    return apply_rows(where, own, main, late, tops, chunks, token)
+    late = gather(own_late, is_second)
+    second = jnp.logical_and(jnp.logical_and(y == 0, z == 0), core == 1)
+    first = jnp.logical_and(jnp.logical_and(y == 0, z == 0), core == 0)
+    where = jnp.stack([first, second, column, z, core]).astype(jnp.int32)
+    where, *gathered = lax.optimization_barrier((where, *main, *late))
+    main, late = gathered[:3], gathered[3:]
+    chunks = factor_rows(where, own, main)
+    chunks = spread_rows(chunks, z, y, core)
+    return apply_rows(where, own, main, late, chunks, token)
 
 
 def solution(mesh):

time: 203 us -> 201 us (level)
  waiting for transfers between devices: 115 us -> 144 us
  starting transfers between devices: 46.1 us -> 35.3 us
  local copies, waits for them, and re-layouts: 12.1 us -> 3.64 us
  other arithmetic: 9.92 us -> 2.79 us
  Pallas kernels: 15.8 us -> 12.7 us
    ppermute x17 -> x7, waiting for transfers between devices: 87.5 us -> 101 us  [the longest x1 51.7 us: shards(): lax.ppermute(main[0][:8, :128] + main[1][:8, :128], ALL, [(device(0, 1, 0...]
    ppermute x1, waiting for transfers between devices: 2.24 us -> 14.7 us  [spread_rows(): lax.ppermute(chunk, ALL, pairs_of(lambda c, zz, yy, kk, j: (c, zz, yy, 1,...]
    ppermute x17 -> x7, starting transfers between devices: 21.4 us -> 9.94 us  [the longest x2 3.32 us: gather(): near = lax.ppermute(part, ALL, moves(member, (0, 1), (1, 2), (2, 3)))]
    ppermute x1, starting transfers between devices: 0.27 us -> 5.28 us  [spread_rows(): half = lax.ppermute(part, ALL, across)]
    ppermute x3, starting transfers between devices: 7.14 us -> 2.61 us  [spread_rows(): direct[by] = lax.ppermute(chunk, ALL, pairs)]
    slice x2 -> x0, local copies, waits for them, and re-layouts: 4.51 us -> none  [the longest x1 2.26 us: shards(): near[:HALF]]
    unnamed x33 -> x17, local copies, waits for them, and re-layouts: 7.39 us -> 2.9 us
    slice x1 -> x0, other arithmetic: 3.09 us -> none  [gather_top(): upper, lower = (own[:HALF], own[HALF:])]
  transfers between devices with their start and end apart: 34 -> 24, of which waited for: 9 -> 10; matrix products, arithmetic and copies ran while one was open for 5% -> 0% of each run, Pallas kernels for 1% -> 0%
where the time goes in v6:
time: 201 us; the launch traced here: 200 us
  waiting for transfers between devices  144 us (72%)
  starting transfers between devices  35.3 us (18%)
  Pallas kernels  12.7 us (6%)
  local copies, waits for them, and re-layouts  3.64 us (2%)
  other arithmetic  2.79 us (1%)
    ppermute x1, waiting for transfers between devices, shards(): lax.ppermute(main[0][:8, :128] + main[1][:8, :128], ALL, [(device(0, 1, 0...  51.7 us
    ppermute x2, waiting for transfers between devices, gather(): far = lax.ppermute(near, ALL, moves(member, (1, 2), (2, 3)))  25.2 us
    ppermute x2, waiting for transfers between devices, gather(): wrap = lax.ppermute(part, ALL, moves(member, (0, 3)))  23.4 us
    ppermute x1, waiting for transfers between devices, spread_rows(): lax.ppermute(chunk, ALL, pairs_of(lambda c, zz, yy, kk, j: (c, zz, yy, 1,...  14.7 us
    ppermute x1, waiting for transfers between devices, shards(): lax.ppermute(sent, ALL, pairs_of(lambda c, zz, yy, kk, j: (1 - c, zz, yy,...  11.4 us
    pallas_call x1, Pallas kernels, apply_rows(): pl.pallas_call(apply_kernel, out_shape=jax.ShapeDtypeStruct((TILE, PW), j...  10.6 us
    ppermute x1, waiting for transfers between devices, spread_rows(): half = lax.ppermute(part, ALL, across)  10.3 us
    ppermute x1, starting transfers between devices, spread_rows(): theirs = lax.ppermute(jnp.concatenate(mine, axis=0), ALL, swap)  6.29 us
  transfers between devices with their start and end apart: 24, of which 10 were waited for; matrix products, arithmetic and copies ran while one was open for 0% of the time, Pallas kernels for 0%

profile of v6, /device:TPU:7, one launch (start us, length us, event | category | flops | bytes accessed | tf_op | source)
XLA Modules:
  0.0 199.7 jit_solution(4703144718447761663)
XLA Ops:
  0.0 1.3 copy.8
  1.3 0.2 copy.10
  1.5 0.1 fusion.5
  1.6 3.0 %collective-permute-start = (bf16[2,4,64,512]{3,2,1,0:T(8,128)(2,1)S(1)}, bf16[2,4,64,512]{3,2,1,0:T(8,128)(2,1)S(1)}, u32[]{:S(2)}, u32[]{:S(2)}) collective-permute-start(bf16[2,4,64,512]{3,2,1,0:T(8,128)(2,1)S(1)} %get-tuple-element.47), channel_id=1, source_target_pairs={{0,128},{1,129},{2,130},{3,131},{4,132},{5,133},{6,134},{7,135},{8... | collective-permute-start | bytes 1572872 | tf_op jit(solution)/shard_map/ppermute | solution.py:325
  4.6 11.4 %collective-permute-done = bf16[2,4,64,512]{3,2,1,0:T(8,128)(2,1)S(1)} collective-permute-done((bf16[2,4,64,512]{3,2,1,0:T(8,128)(2,1)S(1)}, bf16[2,4,64,512]{3,2,1,0:T(8,128)(2,1)S(1)}, u32[]{:S(2)}, u32[]{:S(2)}) %collective-permute-start) | collective-permute-done | bytes 524320 | tf_op jit(solution)/shard_map/ppermute | solution.py:325
  15.9 0.8 fusion.3
  16.7 0.8 copy-done.6
  17.5 0.8 fusion.own
  18.3 0.8 collective-permute-start.2
  19.1 2.0 %collective-permute-start.1 = (bf16[2048,512]{1,0:T(8,128)(2,1)S(1)}, bf16[2048,512]{1,0:T(8,128)(2,1)}, u32[]{:S(2)}, u32[]{:S(2)}) collective-permute-start(bf16[2048,512]{1,0:T(8,128)(2,1)S(1)} %fusion.own), channel_id=1, source_target_pairs={{0,1},{1,2},{2,3},{8,9},{9,10},{10,11},{12,13},{13,14},{14,15},{16... | collective-permute-start | bytes 6291464 | tf_op jit(solution)/shard_map/ppermute | solution.py:273
  21.2 0.7 slice_add_fusion
  21.9 1.3 collective-permute-start.4
  23.1 51.7 %collective-permute-done.4.refs_12_ = bf16[8,128]{1,0:T(8,128)(2,1)S(1)} collective-permute-done((bf16[8,128]{1,0:T(8,128)(2,1)S(1)}, bf16[8,128]{1,0:T(8,128)(2,1)S(1)}, u32[]{:S(2)}, u32[]{:S(2)}) %collective-permute-start.4) | collective-permute-done | bytes 2080 | tf_op jit(solution)/shard_map/ppermute | solution.py:332
  74.8 1.3 collective-permute-start.6
  76.1 1.3 collective-permute-start.5
  77.4 2.0 collective-permute-start.3
  79.4 23.4 %collective-permute-done.6.refs_4_ = bf16[2048,512]{1,0:T(8,128)(2,1)S(1)} collective-permute-done((bf16[2048,512]{1,0:T(8,128)(2,1)S(1)}, bf16[2048,512]{1,0:T(8,128)(2,1)S(1)}, u32[]{:S(2)}, u32[]{:S(2)}) %collective-permute-start.6) | collective-permute-done | bytes 2097184 | tf_op jit(solution)/shard_map/ppermute | solution.py:274
  102.8 0.6 collective-permute-done.5.refs_3_
  103.5 0.8 copy-done.5
  104.2 1.3 collective-permute-start.7
  105.6 0.6 stack.37.where_ref
  106.1 25.2 %collective-permute-done.7.refs_5_ = bf16[2048,512]{1,0:T(8,128)(2,1)} collective-permute-done((bf16[2048,512]{1,0:T(8,128)(2,1)}, bf16[2048,512]{1,0:T(8,128)(2,1)}, u32[]{:S(2)}, u32[]{:S(2)}) %collective-permute-start.7) | collective-permute-done | bytes 2097184 | tf_op jit(solution)/shard_map/ppermute | solution.py:276
  131.3 2.0 %factor_rows.1 = (bf16[64,2048]{1,0:T(8,128)(2,1)}, bf16[64,2048]{1,0:T(8,128)(2,1)}, bf16[64,2048]{1,0:T(8,128)(2,1)}, bf16[64,2048]{1,0:T(8,128)(2,1)}, bf16[6...) custom-call(s32[5]{0:T(128)} %stack.37.where_ref, ...), custom_call_target="tpu_custom_call" | custom-call | tf_op jit(solution)/shard_map/factor_rows/pallas_call | solution.py:150
  133.3 0.7 collective-permute-start.8
  134.0 0.7 collective-permute-start.9
  134.7 0.7 collective-permute-start.10
  135.4 0.7 collective-permute-start.11
  136.1 0.7 collective-permute-start.12
  136.8 0.7 collective-permute-start.13
  137.5 0.7 collective-permute-start.14
  138.2 1.1 add_select_fusion.1
  139.3 0.8 collective-permute-start.17
  140.1 0.7 collective-permute-start.16
  140.8 0.7 collective-permute-start.15
  141.5 0.1 add_select_fusion
  141.6 1.3 collective-permute-start.18
  142.9 14.7 %collective-permute-done.18 = bf16[64,2048]{1,0:T(8,128)(2,1)S(1)} collective-permute-done((bf16[64,2048]{1,0:T(8,128)(2,1)S(1)}, bf16[64,2048]{1,0:T(8,128)(2,1)S(1)}, u32[]{:S(2)}, u32[]{:S(2)}) %collective-permute-start.18) | collective-permute-done | bytes 262176 | tf_op jit(solution)/shard_map/ppermute | solution.py:298
  157.6 0.1 collective-permute-start.21
  157.6 0.5 collective-permute-start.20
  158.2 2.0 collective-permute-start.19
  160.2 5.3 %collective-permute-start.22 = (bf16[32,2048]{1,0:T(8,128)(2,1)S(1)}, bf16[32,2048]{1,0:T(8,128)(2,1)S(1)}, u32[]{:S(2)}, u32[]{:S(2)}) collective-permute-start(bf16[32,2048]{1,0:T(8,128)(2,1)S(1)} %constant_dynamic-slice_fusion), channel_id=1, source_target_pairs={{0,64},{1,65},{2,66},{3,67},{4,68},{5,69},{6,70},{7,71},{8,72},{9,... | collective-permute-start | bytes 393224 | tf_op jit(solution)/shard_map/ppermute | solution.py:305
  165.5 10.3 %collective-permute-done.22.refs_10_ = bf16[32,2048]{1,0:T(8,128)(2,1)S(1)} collective-permute-done((bf16[32,2048]{1,0:T(8,128)(2,1)S(1)}, bf16[32,2048]{1,0:T(8,128)(2,1)S(1)}, u32[]{:S(2)}, u32[]{:S(2)}) %collective-permute-start.22) | collective-permute-done | bytes 131104 | tf_op jit(solution)/shard_map/ppermute | solution.py:305
  175.8 3.0 %collective-permute-done.20.refs_8_ = bf16[64,2048]{1,0:T(8,128)(2,1)S(1)} collective-permute-done((bf16[64,2048]{1,0:T(8,128)(2,1)S(1)}, bf16[64,2048]{1,0:T(8,128)(2,1)S(1)}, u32[]{:S(2)}, u32[]{:S(2)}) %collective-permute-start.20) | collective-permute-done | bytes 262176 | tf_op jit(solution)/shard_map/ppermute | solution.py:309
  178.8 1.8 collective-permute-done.19.refs_7_
  180.6 0.1 pad_maximum_fusion
  180.7 6.3 %collective-permute-start.23 = (bf16[224,2048]{1,0:T(8,128)(2,1)S(1)}, bf16[224,2048]{1,0:T(8,128)(2,1)S(1)}, u32[]{:S(2)}, u32[]{:S(2)}) collective-permute-start(bf16[224,2048]{1,0:T(8,128)(2,1)S(1)} %pad_maximum_fusion), channel_id=1, source_target_pairs={{0,4},{1,5},{2,6},{3,7},{4,0},{5,1},{6,2},{7,3},{8,12},{9,13},{10,... | collective-permute-start | bytes 2752520 | tf_op jit(solution)/shard_map/ppermute | solution.py:311
  187.0 2.1 %collective-permute-done.23.refs_11_ = bf16[224,2048]{1,0:T(8,128)(2,1)S(1)} collective-permute-done((bf16[224,2048]{1,0:T(8,128)(2,1)S(1)}, bf16[224,2048]{1,0:T(8,128)(2,1)S(1)}, u32[]{:S(2)}, u32[]{:S(2)}) %collective-permute-start.23) | collective-permute-done | bytes 917536 | tf_op jit(solution)/shard_map/ppermute | solution.py:311
  189.1 10.6 %apply_rows.1 = bf16[512,2048]{1,0:T(8,128)(2,1)} custom-call(s32[5]{0:T(128)S(1)} %copy-done.4, bf16[2048,512]{1,0:T(8,128)(2,1)S(1)} %copy-done.1, bf16[2048,512]{1,0:T(8,128)(2,1)} %collective-permute-done.1.refs_0_, bf16[2048,512]{1,0:T(8,128)(2,1)S(1)} %copy-done.3, bf16[2048,512]{1,0:T(8,128)(2,1)} %collective-permute-done.3.refs_2_, ...), custom_call_target="tpu_custom_call" | custom-call | tf_op jit(solution)/shard_map/apply_rows/pallas_call | solution.py:220
  (30 shorter events, 0.1 us)
Async XLA Ops:
  0.0 1.4 copy-start.7
  1.6 14.4 %collective-permute-start = (bf16[2,4,64,512]{3,2,1,0:T(8,128)(2,1)S(1)}, bf16[2,4,64,512]{3,2,1,0:T(8,128)(2,1)S(1)}, u32[]{:S(2)}, u32[]{:S(2)}) collective-permute-start(bf16[2,4,64,512]{3,2,1,0:T(8,128)(2,1)S(1)} %get-tuple-element.47), channel_id=1, source_target_pairs={{0,128},{1,129},{2,130},{3,131},{4,132},{5,133},{6,134},{7,135},{8... | collective-permute-start | bytes 1572872 | tf_op jit(solution)/shard_map/ppermute | solution.py:325
  15.9 1.6 copy-start.6
  18.3 113.0 %copy-start = (bf16[2048,512]{1,0:T(8,128)(2,1)}, bf16[2048,512]{1,0:T(8,128)(2,1)S(1)}, u32[]{:S(2)}) copy-start(bf16[2048,512]{1,0:T(8,128)(2,1)S(1)} %fusion.own) | copy-start | bytes 6291460
  18.3 2.8 %collective-permute-start.2 = (bf16[2048,512]{1,0:T(8,128)(2,1)S(1)}, bf16[2048,512]{1,0:T(8,128)(2,1)S(1)}, u32[]{:S(2)}, u32[]{:S(2)}) collective-permute-start(bf16[2048,512]{1,0:T(8,128)(2,1)S(1)} %fusion.own), channel_id=1, source_target_pairs={{0,3},{8,11},{12,15},{16,19},{20,23},{24,27},{28,31},{32,35},{36,3... | collective-permute-start | bytes 6291464 | tf_op jit(solution)/shard_map/ppermute | solution.py:274
  19.1 2.0 %collective-permute-start.1 = (bf16[2048,512]{1,0:T(8,128)(2,1)S(1)}, bf16[2048,512]{1,0:T(8,128)(2,1)}, u32[]{:S(2)}, u32[]{:S(2)}) collective-permute-start(bf16[2048,512]{1,0:T(8,128)(2,1)S(1)} %fusion.own), channel_id=1, source_target_pairs={{0,1},{1,2},{2,3},{8,9},{9,10},{10,11},{12,13},{13,14},{14,15},{16... | collective-permute-start | bytes 6291464 | tf_op jit(solution)/shard_map/ppermute | solution.py:273
  21.2 82.3 %copy-start.2 = (bf16[2048,512]{1,0:T(8,128)(2,1)}, bf16[2048,512]{1,0:T(8,128)(2,1)S(1)}, u32[]{:S(2)}) copy-start(bf16[2048,512]{1,0:T(8,128)(2,1)S(1)} %collective-permute-done.2.refs_1_) | copy-start | bytes 6291460
  21.9 53.0 %collective-permute-start.4 = (bf16[8,128]{1,0:T(8,128)(2,1)S(1)}, bf16[8,128]{1,0:T(8,128)(2,1)S(1)}, u32[]{:S(2)}, u32[]{:S(2)}) collective-permute-start(bf16[8,128]{1,0:T(8,128)(2,1)S(1)} %slice_add_fusion), channel_id=1, source_target_pairs={{16,4},{17,5},{18,6},{19,7}} | collective-permute-start | bytes 6152 | tf_op jit(solution)/shard_map/ppermute | solution.py:332
  74.8 28.0 %collective-permute-start.6 = (bf16[2048,512]{1,0:T(8,128)(2,1)S(1)}, bf16[2048,512]{1,0:T(8,128)(2,1)S(1)}, u32[]{:S(2)}, u32[]{:S(2)}) collective-permute-start(bf16[2048,512]{1,0:T(8,128)(2,1)S(1)} %fusion.own), channel_id=1, source_target_pairs={{4,7}} | collective-permute-start | bytes 6291464 | tf_op jit(solution)/shard_map/ppermute | solution.py:274
  76.1 27.3 %collective-permute-start.5 = (bf16[2048,512]{1,0:T(8,128)(2,1)S(1)}, bf16[2048,512]{1,0:T(8,128)(2,1)}, u32[]{:S(2)}, u32[]{:S(2)}) collective-permute-start(bf16[2048,512]{1,0:T(8,128)(2,1)S(1)} %fusion.own), channel_id=1, source_target_pairs={{4,5},{5,6},{6,7}} | collective-permute-start | bytes 6291464 | tf_op jit(solution)/shard_map/ppermute | solution.py:273
  77.4 28.7 %collective-permute-start.3 = (bf16[2048,512]{1,0:T(8,128)(2,1)}, bf16[2048,512]{1,0:T(8,128)(2,1)}, u32[]{:S(2)}, u32[]{:S(2)}) collective-permute-start(bf16[2048,512]{1,0:T(8,128)(2,1)} %collective-permute-done.1.refs_0_), channel_id=1, source_target_pairs={{1,2},{2,3},{9,10},{10,11},{13,14},{14,15},{17,18},{18,19},{21,22}... | collective-permute-start | bytes 6291464 | tf_op jit(solution)/shard_map/ppermute | solution.py:276
  102.8 1.4 copy-start.5
  104.2 27.1 %collective-permute-start.7 = (bf16[2048,512]{1,0:T(8,128)(2,1)}, bf16[2048,512]{1,0:T(8,128)(2,1)}, u32[]{:S(2)}, u32[]{:S(2)}) collective-permute-start(bf16[2048,512]{1,0:T(8,128)(2,1)} %collective-permute-done.5.refs_3_), channel_id=1, source_target_pairs={{5,6},{6,7}} | collective-permute-start | bytes 6291464 | tf_op jit(solution)/shard_map/ppermute | solution.py:276
  133.3 3.4 %collective-permute-start.8 = (bf16[64,2048]{1,0:T(8,128)(2,1)}, bf16[64,2048]{1,0:T(8,128)(2,1)S(1)}, u32[]{:S(2)}, u32[]{:S(2)}) collective-permute-start(bf16[64,2048]{1,0:T(8,128)(2,1)} %get-tuple-element.39), channel_id=1, source_target_pairs={{0,16},{1,17},{2,18},{3,19}} | collective-permute-start | bytes 786440 | tf_op jit(solution)/shard_map/ppermute | solution.py:287
  134.0 3.4 %collective-permute-start.9 = (bf16[64,2048]{1,0:T(8,128)(2,1)}, bf16[64,2048]{1,0:T(8,128)(2,1)S(1)}, u32[]{:S(2)}, u32[]{:S(2)}) collective-permute-start(bf16[64,2048]{1,0:T(8,128)(2,1)} %get-tuple-element.40), channel_id=1, source_target_pairs={{0,32},{1,33},{2,34},{3,35}} | collective-permute-start | bytes 786440 | tf_op jit(solution)/shard_map/ppermute | solution.py:287
  134.7 3.5 %collective-permute-start.10 = (bf16[64,2048]{1,0:T(8,128)(2,1)}, bf16[64,2048]{1,0:T(8,128)(2,1)S(1)}, u32[]{:S(2)}, u32[]{:S(2)}) collective-permute-start(bf16[64,2048]{1,0:T(8,128)(2,1)} %get-tuple-element.41), channel_id=1, source_target_pairs={{0,48},{1,49},{2,50},{3,51}} | collective-permute-start | bytes 786440 | tf_op jit(solution)/shard_map/ppermute | solution.py:287
  135.4 2.8 %collective-permute-start.11 = (bf16[64,2048]{1,0:T(8,128)(2,1)}, bf16[64,2048]{1,0:T(8,128)(2,1)S(1)}, u32[]{:S(2)}, u32[]{:S(2)}) collective-permute-start(bf16[64,2048]{1,0:T(8,128)(2,1)} %get-tuple-element.42), channel_id=1, source_target_pairs={{0,64},{1,65},{2,66},{3,67}} | collective-permute-start | bytes 786440 | tf_op jit(solution)/shard_map/ppermute | solution.py:287
  136.1 2.1 %collective-permute-start.12 = (bf16[64,2048]{1,0:T(8,128)(2,1)}, bf16[64,2048]{1,0:T(8,128)(2,1)S(1)}, u32[]{:S(2)}, u32[]{:S(2)}) collective-permute-start(bf16[64,2048]{1,0:T(8,128)(2,1)} %get-tuple-element.43), channel_id=1, source_target_pairs={{0,80},{1,81},{2,82},{3,83}} | collective-permute-start | bytes 786440 | tf_op jit(solution)/shard_map/ppermute | solution.py:287
  136.8 1.4 collective-permute-start.13
  137.5 0.7 collective-permute-start.14
  139.3 49.8 %copy-start.1 = (bf16[2048,512]{1,0:T(8,128)(2,1)S(1)}, bf16[2048,512]{1,0:T(8,128)(2,1)}, u32[]{:S(2)}) copy-start(bf16[2048,512]{1,0:T(8,128)(2,1)} %copy-done) | copy-start | bytes 6291460
  139.3 49.8 %copy-start.4 = (s32[5]{0:T(128)S(1)}, s32[5]{0:T(128)}, u32[]{:S(2)}) copy-start(s32[5]{0:T(128)} %stack.37.where_ref) | copy-start | bytes 64
  139.3 2.2 %collective-permute-start.17 = (bf16[64,2048]{1,0:T(8,128)(2,1)S(1)}, bf16[64,2048]{1,0:T(8,128)(2,1)S(1)}, u32[]{:S(2)}, u32[]{:S(2)}) collective-permute-start(bf16[64,2048]{1,0:T(8,128)(2,1)S(1)} %add_select_fusion.1), channel_id=1, source_target_pairs={{0,128},{1,129},{2,130},{3,131},{16,144},{17,145},{18,146},{19,147... | collective-permute-start | bytes 786440 | tf_op jit(solution)/shard_map/ppermute | solution.py:295
  140.1 1.4 collective-permute-start.16
  140.8 0.7 collective-permute-start.15
  141.6 16.0 %collective-permute-start.18 = (bf16[64,2048]{1,0:T(8,128)(2,1)S(1)}, bf16[64,2048]{1,0:T(8,128)(2,1)S(1)}, u32[]{:S(2)}, u32[]{:S(2)}) collective-permute-start(bf16[64,2048]{1,0:T(8,128)(2,1)S(1)} %add_select_fusion), channel_id=1, source_target_pairs={{0,4},{1,5},{2,6},{3,7},{8,12},{9,13},{10,14},{11,15},{16,20},{17,... | collective-permute-start | bytes 786440 | tf_op jit(solution)/shard_map/ppermute | solution.py:298
  142.9 46.2 %copy-start.3 = (bf16[2048,512]{1,0:T(8,128)(2,1)S(1)}, bf16[2048,512]{1,0:T(8,128)(2,1)}, u32[]{:S(2)}) copy-start(bf16[2048,512]{1,0:T(8,128)(2,1)} %copy-done.2) | copy-start | bytes 6291460
  157.6 18.2 %collective-permute-start.21 = (bf16[64,2048]{1,0:T(8,128)(2,1)S(1)}, bf16[64,2048]{1,0:T(8,128)(2,1)S(1)}, u32[]{:S(2)}, u32[]{:S(2)}) collective-permute-start(bf16[64,2048]{1,0:T(8,128)(2,1)S(1)} %broadcast_select_fusion.refs_6_), channel_id=1, source_target_pairs={{0,48},{1,49},{2,50},{3,51},{4,84},{5,85},{6,86},{7,87},{8,56},{9,... | collective-permute-start | bytes 786440 | tf_op jit(solution)/shard_map/ppermute | solution.py:309
  157.6 21.1 %collective-permute-start.20 = (bf16[64,2048]{1,0:T(8,128)(2,1)S(1)}, bf16[64,2048]{1,0:T(8,128)(2,1)S(1)}, u32[]{:S(2)}, u32[]{:S(2)}) collective-permute-start(bf16[64,2048]{1,0:T(8,128)(2,1)S(1)} %broadcast_select_fusion.refs_6_), channel_id=1, source_target_pairs={{0,32},{1,33},{2,34},{3,35},{4,100},{5,101},{6,102},{7,103},{8,40}... | collective-permute-start | bytes 786440 | tf_op jit(solution)/shard_map/ppermute | solution.py:309
  158.2 22.4 %collective-permute-start.19 = (bf16[64,2048]{1,0:T(8,128)(2,1)S(1)}, bf16[64,2048]{1,0:T(8,128)(2,1)S(1)}, u32[]{:S(2)}, u32[]{:S(2)}) collective-permute-start(bf16[64,2048]{1,0:T(8,128)(2,1)S(1)} %broadcast_select_fusion.refs_6_), channel_id=1, source_target_pairs={{0,16},{1,17},{2,18},{3,19},{4,116},{5,117},{6,118},{7,119},{8,24}... | collective-permute-start | bytes 786440 | tf_op jit(solution)/shard_map/ppermute | solution.py:309
  160.2 15.6 %collective-permute-start.22 = (bf16[32,2048]{1,0:T(8,128)(2,1)S(1)}, bf16[32,2048]{1,0:T(8,128)(2,1)S(1)}, u32[]{:S(2)}, u32[]{:S(2)}) collective-permute-start(bf16[32,2048]{1,0:T(8,128)(2,1)S(1)} %constant_dynamic-slice_fusion), channel_id=1, source_target_pairs={{0,64},{1,65},{2,66},{3,67},{4,68},{5,69},{6,70},{7,71},{8,72},{9,... | collective-permute-start | bytes 393224 | tf_op jit(solution)/shard_map/ppermute | solution.py:305
  180.7 8.4 %collective-permute-start.23 = (bf16[224,2048]{1,0:T(8,128)(2,1)S(1)}, bf16[224,2048]{1,0:T(8,128)(2,1)S(1)}, u32[]{:S(2)}, u32[]{:S(2)}) collective-permute-start(bf16[224,2048]{1,0:T(8,128)(2,1)S(1)} %pad_maximum_fusion), channel_id=1, source_target_pairs={{0,4},{1,5},{2,6},{3,7},{4,0},{5,1},{6,2},{7,3},{8,12},{9,13},{10,... | collective-permute-start | bytes 2752520 | tf_op jit(solution)/shard_map/ppermute | solution.py:311

commit v7 on v6

--- a/solution.py
+++ b/solution.py
@@ -250,10 +250,6 @@
     return found
 
 
-def owner(core, col):
-    return device(0, 0, 0, core, col)
-
-
 def moves(member, *steps):
     allowed = dict(steps)
     return pairs_of(
@@ -262,11 +258,11 @@
 
 
 def is_second(c, z, y, k):
-    return (c, z, y, k) == (0, 0, 0, 1)
+    return (c, y, k) == (0, 0, 1)
 
 
 def is_other(c, z, y, k):
-    return (c, z, y, k) != (0, 0, 0, 1)
+    return (c, y, k) != (0, 0, 1)
 
 
 def gather(part, member):
@@ -332,11 +328,11 @@
     token = lax.ppermute(
         main[0][:8, :128] + main[1][:8, :128],
         ALL,
-        [(device(0, 1, 0, 0, j), device(0, 0, 0, 1, j)) for j in range(4)],
+        pairs_of(lambda c, zz, yy, kk, j: (0, zz, 0, 1, j) if (c, yy, kk) == (0, 1, 0) else None),
     )
     own_late, token = lax.optimization_barrier((own, token))
     late = gather(own_late, is_second)
-    second = jnp.logical_and(jnp.logical_and(y == 0, z == 0), core == 1)
+    second = jnp.logical_and(y == 0, core == 1)
     first = jnp.logical_and(jnp.logical_and(y == 0, z == 0), core == 0)
     where = jnp.stack([first, second, column, z, core]).astype(jnp.int32)
     where, *gathered = lax.optimization_barrier((where, *main, *late))

time: 201 us -> 189 us (0.940)
  waiting for transfers between devices: 144 us -> 134 us
    ppermute x1, waiting for transfers between devices: 14.7 us -> 2.11 us  [spread_rows(): lax.ppermute(chunk, ALL, pairs_of(lambda c, zz, yy, kk, j: (c, zz, yy, 1,...]
    ppermute x1, starting transfers between devices: 6.29 us -> 2.56 us  [spread_rows(): theirs = lax.ppermute(jnp.concatenate(mine, axis=0), ALL, swap)]
    ppermute x3, starting transfers between devices: 2.61 us -> 6.33 us  [spread_rows(): direct[by] = lax.ppermute(chunk, ALL, pairs)]
    ppermute x3, waiting for transfers between devices: 4.79 us -> 7.79 us  [spread_rows(): direct[by] = lax.ppermute(chunk, ALL, pairs)]
where the time goes in v7:
time: 189 us
  waiting for transfers between devices  134 us (71%)
  starting transfers between devices  34.6 us (18%)
  Pallas kernels  12.7 us (7%)
  local copies, waits for them, and re-layouts  3.29 us (2%)
  other arithmetic  2.79 us (1%)
    ppermute x1, waiting for transfers between devices, shards(): lax.ppermute(main[0][:8, :128] + main[1][:8, :128], ALL, pairs_of(lambda...  51.4 us
    ppermute x2, waiting for transfers between devices, gather(): far = lax.ppermute(near, ALL, moves(member, (1, 2), (2, 3)))  25.2 us
    ppermute x2, waiting for transfers between devices, gather(): wrap = lax.ppermute(part, ALL, moves(member, (0, 3)))  23.4 us
    ppermute x1, waiting for transfers between devices, shards(): lax.ppermute(sent, ALL, pairs_of(lambda c, zz, yy, kk, j: (1 - c, zz, yy,...  11.4 us
    pallas_call x1, Pallas kernels, apply_rows(): pl.pallas_call(apply_kernel, out_shape=jax.ShapeDtypeStruct((TILE, PW), j...  10.6 us
    ppermute x1, waiting for transfers between devices, spread_rows(): half = lax.ppermute(part, ALL, across)  9.87 us
    ppermute x3, waiting for transfers between devices, spread_rows(): direct[by] = lax.ppermute(chunk, ALL, pairs)  7.79 us
    ppermute x3, starting transfers between devices, spread_rows(): direct[by] = lax.ppermute(chunk, ALL, pairs)  6.33 us
  transfers between devices with their start and end apart: 24, of which 10 were waited for; matrix products, arithmetic and copies ran while one was open for 0% of the time, Pallas kernels for 0%

profile of v7, /device:TPU:7, one launch (start us, length us, event | category | flops | bytes accessed | tf_op | source)
XLA Modules:
  0.0 188.7 jit_solution(15283011597867738075)
XLA Ops:
  0.0 1.3 copy.8
  1.3 0.2 copy.10
  1.5 0.1 fusion.5
  1.6 3.0 %collective-permute-start = (bf16[2,4,64,512]{3,2,1,0:T(8,128)(2,1)S(1)}, bf16[2,4,64,512]{3,2,1,0:T(8,128)(2,1)S(1)}, u32[]{:S(2)}, u32[]{:S(2)}) collective-permute-start(bf16[2,4,64,512]{3,2,1,0:T(8,128)(2,1)S(1)} %get-tuple-element.47), channel_id=1, source_target_pairs={{0,128},{1,129},{2,130},{3,131},{4,132},{5,133},{6,134},{7,135},{8... | collective-permute-start | bytes 1572872 | tf_op jit(solution)/shard_map/ppermute | solution.py:321
  4.6 11.4 %collective-permute-done = bf16[2,4,64,512]{3,2,1,0:T(8,128)(2,1)S(1)} collective-permute-done((bf16[2,4,64,512]{3,2,1,0:T(8,128)(2,1)S(1)}, bf16[2,4,64,512]{3,2,1,0:T(8,128)(2,1)S(1)}, u32[]{:S(2)}, u32[]{:S(2)}) %collective-permute-start) | collective-permute-done | bytes 524320 | tf_op jit(solution)/shard_map/ppermute | solution.py:321
  15.9 0.8 fusion.3
  16.7 0.8 copy-done.6
  17.5 0.8 fusion.own
  18.3 0.8 collective-permute-start.2
  19.1 2.0 %collective-permute-start.1 = (bf16[2048,512]{1,0:T(8,128)(2,1)S(1)}, bf16[2048,512]{1,0:T(8,128)(2,1)}, u32[]{:S(2)}, u32[]{:S(2)}) collective-permute-start(bf16[2048,512]{1,0:T(8,128)(2,1)S(1)} %fusion.own), channel_id=1, source_target_pairs={{0,1},{1,2},{2,3},{8,9},{9,10},{10,11},{12,13},{13,14},{14,15},{16... | collective-permute-start | bytes 6291464 | tf_op jit(solution)/shard_map/ppermute | solution.py:269
  21.2 0.7 slice_add_fusion
  21.9 1.3 collective-permute-start.4
  23.1 51.4 %collective-permute-done.4.refs_12_ = bf16[8,128]{1,0:T(8,128)(2,1)S(1)} collective-permute-done((bf16[8,128]{1,0:T(8,128)(2,1)S(1)}, bf16[8,128]{1,0:T(8,128)(2,1)S(1)}, u32[]{:S(2)}, u32[]{:S(2)}) %collective-permute-start.4) | collective-permute-done | bytes 2080 | tf_op jit(solution)/shard_map/ppermute | solution.py:328
  74.5 1.3 collective-permute-start.6
  75.8 1.3 collective-permute-start.5
  77.1 2.0 %collective-permute-start.3 = (bf16[2048,512]{1,0:T(8,128)(2,1)}, bf16[2048,512]{1,0:T(8,128)(2,1)}, u32[]{:S(2)}, u32[]{:S(2)}) collective-permute-start(bf16[2048,512]{1,0:T(8,128)(2,1)} %collective-permute-done.1.refs_0_), channel_id=1, source_target_pairs={{1,2},{2,3},{9,10},{10,11},{13,14},{14,15},{17,18},{18,19},{25,26}... | collective-permute-start | bytes 6291464 | tf_op jit(solution)/shard_map/ppermute | solution.py:272
  79.1 23.4 %collective-permute-done.6.refs_4_ = bf16[2048,512]{1,0:T(8,128)(2,1)S(1)} collective-permute-done((bf16[2048,512]{1,0:T(8,128)(2,1)S(1)}, bf16[2048,512]{1,0:T(8,128)(2,1)S(1)}, u32[]{:S(2)}, u32[]{:S(2)}) %collective-permute-start.6) | collective-permute-done | bytes 2097184 | tf_op jit(solution)/shard_map/ppermute | solution.py:270
  102.5 1.0 collective-permute-done.5.refs_3_
  103.5 0.4 copy-done.5
  103.9 1.3 collective-permute-start.7
  105.2 0.6 stack.37.where_ref
  105.8 25.2 %collective-permute-done.7.refs_5_ = bf16[2048,512]{1,0:T(8,128)(2,1)} collective-permute-done((bf16[2048,512]{1,0:T(8,128)(2,1)}, bf16[2048,512]{1,0:T(8,128)(2,1)}, u32[]{:S(2)}, u32[]{:S(2)}) %collective-permute-start.7) | collective-permute-done | bytes 2097184 | tf_op jit(solution)/shard_map/ppermute | solution.py:272
  131.0 2.0 %factor_rows.1 = (bf16[64,2048]{1,0:T(8,128)(2,1)}, bf16[64,2048]{1,0:T(8,128)(2,1)}, bf16[64,2048]{1,0:T(8,128)(2,1)}, bf16[64,2048]{1,0:T(8,128)(2,1)}, bf16[6...) custom-call(s32[5]{0:T(128)} %stack.37.where_ref, ...), custom_call_target="tpu_custom_call" | custom-call | tf_op jit(solution)/shard_map/factor_rows/pallas_call | solution.py:150
  133.0 0.7 collective-permute-start.8
  133.7 0.7 collective-permute-start.9
  134.3 0.7 collective-permute-start.10
  135.0 0.7 collective-permute-start.11
  135.7 0.7 collective-permute-start.12
  136.4 0.7 collective-permute-start.13
  137.1 0.7 collective-permute-start.14
  137.8 1.1 add_select_fusion.1
  138.9 0.8 collective-permute-start.17
  139.7 0.7 collective-permute-start.16
  140.4 0.7 collective-permute-start.15
  141.2 0.1 add_select_fusion
  141.2 1.3 collective-permute-start.18
  142.5 2.1 %collective-permute-done.18 = bf16[64,2048]{1,0:T(8,128)(2,1)S(1)} collective-permute-done((bf16[64,2048]{1,0:T(8,128)(2,1)S(1)}, bf16[64,2048]{1,0:T(8,128)(2,1)S(1)}, u32[]{:S(2)}, u32[]{:S(2)}) %collective-permute-start.18) | collective-permute-done | bytes 262176 | tf_op jit(solution)/shard_map/ppermute | solution.py:294
  144.7 5.6 %collective-permute-start.21 = (bf16[64,2048]{1,0:T(8,128)(2,1)S(1)}, bf16[64,2048]{1,0:T(8,128)(2,1)S(1)}, u32[]{:S(2)}, u32[]{:S(2)}) collective-permute-start(bf16[64,2048]{1,0:T(8,128)(2,1)S(1)} %broadcast_select_fusion.refs_6_), channel_id=1, source_target_pairs={{0,48},{1,49},{2,50},{3,51},{4,84},{5,85},{6,86},{7,87},{8,56},{9,... | collective-permute-start | bytes 786440 | tf_op jit(solution)/shard_map/ppermute | solution.py:305
  150.3 0.3 collective-permute-start.20
  150.5 0.5 collective-permute-start.19
  151.0 4.6 %collective-permute-start.22 = (bf16[32,2048]{1,0:T(8,128)(2,1)S(1)}, bf16[32,2048]{1,0:T(8,128)(2,1)S(1)}, u32[]{:S(2)}, u32[]{:S(2)}) collective-permute-start(bf16[32,2048]{1,0:T(8,128)(2,1)S(1)} %constant_dynamic-slice_fusion), channel_id=1, source_target_pairs={{0,64},{1,65},{2,66},{3,67},{4,68},{5,69},{6,70},{7,71},{8,72},{9,... | collective-permute-start | bytes 393224 | tf_op jit(solution)/shard_map/ppermute | solution.py:301
  155.6 9.9 %collective-permute-done.22.refs_10_ = bf16[32,2048]{1,0:T(8,128)(2,1)S(1)} collective-permute-done((bf16[32,2048]{1,0:T(8,128)(2,1)S(1)}, bf16[32,2048]{1,0:T(8,128)(2,1)S(1)}, u32[]{:S(2)}, u32[]{:S(2)}) %collective-permute-start.22) | collective-permute-done | bytes 131104 | tf_op jit(solution)/shard_map/ppermute | solution.py:301
  165.5 2.2 %collective-permute-done.20.refs_8_ = bf16[64,2048]{1,0:T(8,128)(2,1)S(1)} collective-permute-done((bf16[64,2048]{1,0:T(8,128)(2,1)S(1)}, bf16[64,2048]{1,0:T(8,128)(2,1)S(1)}, u32[]{:S(2)}, u32[]{:S(2)}) %collective-permute-start.20) | collective-permute-done | bytes 262176 | tf_op jit(solution)/shard_map/ppermute | solution.py:305
  167.6 5.6 %collective-permute-done.19.refs_7_ = bf16[64,2048]{1,0:T(8,128)(2,1)S(1)} collective-permute-done((bf16[64,2048]{1,0:T(8,128)(2,1)S(1)}, bf16[64,2048]{1,0:T(8,128)(2,1)S(1)}, u32[]{:S(2)}, u32[]{:S(2)}) %collective-permute-start.19) | collective-permute-done | bytes 262176 | tf_op jit(solution)/shard_map/ppermute | solution.py:305
  173.3 0.1 pad_maximum_fusion
  173.3 2.6 %collective-permute-start.23 = (bf16[224,2048]{1,0:T(8,128)(2,1)S(1)}, bf16[224,2048]{1,0:T(8,128)(2,1)S(1)}, u32[]{:S(2)}, u32[]{:S(2)}) collective-permute-start(bf16[224,2048]{1,0:T(8,128)(2,1)S(1)} %pad_maximum_fusion), channel_id=1, source_target_pairs={{0,4},{1,5},{2,6},{3,7},{4,0},{5,1},{6,2},{7,3},{8,12},{9,13},{10,... | collective-permute-start | bytes 2752520 | tf_op jit(solution)/shard_map/ppermute | solution.py:307
  175.9 2.1 %collective-permute-done.23.refs_11_ = bf16[224,2048]{1,0:T(8,128)(2,1)S(1)} collective-permute-done((bf16[224,2048]{1,0:T(8,128)(2,1)S(1)}, bf16[224,2048]{1,0:T(8,128)(2,1)S(1)}, u32[]{:S(2)}, u32[]{:S(2)}) %collective-permute-start.23) | collective-permute-done | bytes 917536 | tf_op jit(solution)/shard_map/ppermute | solution.py:307
  178.0 10.6 %apply_rows.1 = bf16[512,2048]{1,0:T(8,128)(2,1)} custom-call(s32[5]{0:T(128)S(1)} %copy-done.4, bf16[2048,512]{1,0:T(8,128)(2,1)S(1)} %copy-done.1, bf16[2048,512]{1,0:T(8,128)(2,1)} %collective-permute-done.1.refs_0_, bf16[2048,512]{1,0:T(8,128)(2,1)S(1)} %copy-done.3, bf16[2048,512]{1,0:T(8,128)(2,1)} %collective-permute-done.3.refs_2_, ...), custom_call_target="tpu_custom_call" | custom-call | tf_op jit(solution)/shard_map/apply_rows/pallas_call | solution.py:220
  (30 shorter events, 0.1 us)
Async XLA Ops:
  0.0 1.4 copy-start.7
  1.6 14.4 %collective-permute-start = (bf16[2,4,64,512]{3,2,1,0:T(8,128)(2,1)S(1)}, bf16[2,4,64,512]{3,2,1,0:T(8,128)(2,1)S(1)}, u32[]{:S(2)}, u32[]{:S(2)}) collective-permute-start(bf16[2,4,64,512]{3,2,1,0:T(8,128)(2,1)S(1)} %get-tuple-element.47), channel_id=1, source_target_pairs={{0,128},{1,129},{2,130},{3,131},{4,132},{5,133},{6,134},{7,135},{8... | collective-permute-start | bytes 1572872 | tf_op jit(solution)/shard_map/ppermute | solution.py:321
  15.9 1.6 copy-start.6
  18.3 112.6 %copy-start = (bf16[2048,512]{1,0:T(8,128)(2,1)}, bf16[2048,512]{1,0:T(8,128)(2,1)S(1)}, u32[]{:S(2)}) copy-start(bf16[2048,512]{1,0:T(8,128)(2,1)S(1)} %fusion.own) | copy-start | bytes 6291460
  18.3 2.8 %collective-permute-start.2 = (bf16[2048,512]{1,0:T(8,128)(2,1)S(1)}, bf16[2048,512]{1,0:T(8,128)(2,1)S(1)}, u32[]{:S(2)}, u32[]{:S(2)}) collective-permute-start(bf16[2048,512]{1,0:T(8,128)(2,1)S(1)} %fusion.own), channel_id=1, source_target_pairs={{0,3},{8,11},{12,15},{16,19},{24,27},{28,31},{32,35},{40,43},{44,4... | collective-permute-start | bytes 6291464 | tf_op jit(solution)/shard_map/ppermute | solution.py:270
  19.1 2.0 %collective-permute-start.1 = (bf16[2048,512]{1,0:T(8,128)(2,1)S(1)}, bf16[2048,512]{1,0:T(8,128)(2,1)}, u32[]{:S(2)}, u32[]{:S(2)}) collective-permute-start(bf16[2048,512]{1,0:T(8,128)(2,1)S(1)} %fusion.own), channel_id=1, source_target_pairs={{0,1},{1,2},{2,3},{8,9},{9,10},{10,11},{12,13},{13,14},{14,15},{16... | collective-permute-start | bytes 6291464 | tf_op jit(solution)/shard_map/ppermute | solution.py:269
  21.2 82.3 %copy-start.2 = (bf16[2048,512]{1,0:T(8,128)(2,1)}, bf16[2048,512]{1,0:T(8,128)(2,1)S(1)}, u32[]{:S(2)}) copy-start(bf16[2048,512]{1,0:T(8,128)(2,1)S(1)} %collective-permute-done.2.refs_1_) | copy-start | bytes 6291460
  21.9 52.6 %collective-permute-start.4 = (bf16[8,128]{1,0:T(8,128)(2,1)S(1)}, bf16[8,128]{1,0:T(8,128)(2,1)S(1)}, u32[]{:S(2)}, u32[]{:S(2)}) collective-permute-start(bf16[8,128]{1,0:T(8,128)(2,1)S(1)} %slice_add_fusion), channel_id=1, source_target_pairs={{8,4},{9,5},{10,6},{11,7},{24,20},{25,21},{26,22},{27,23},{40,36},... | collective-permute-start | bytes 6152 | tf_op jit(solution)/shard_map/ppermute | solution.py:328
  74.5 28.0 %collective-permute-start.6 = (bf16[2048,512]{1,0:T(8,128)(2,1)S(1)}, bf16[2048,512]{1,0:T(8,128)(2,1)S(1)}, u32[]{:S(2)}, u32[]{:S(2)}) collective-permute-start(bf16[2048,512]{1,0:T(8,128)(2,1)S(1)} %fusion.own), channel_id=1, source_target_pairs={{4,7},{20,23},{36,39},{52,55},{68,71},{84,87},{100,103},{116,119}} | collective-permute-start | bytes 6291464 | tf_op jit(solution)/shard_map/ppermute | solution.py:270
  75.8 27.7 %collective-permute-start.5 = (bf16[2048,512]{1,0:T(8,128)(2,1)S(1)}, bf16[2048,512]{1,0:T(8,128)(2,1)}, u32[]{:S(2)}, u32[]{:S(2)}) collective-permute-start(bf16[2048,512]{1,0:T(8,128)(2,1)S(1)} %fusion.own), channel_id=1, source_target_pairs={{4,5},{5,6},{6,7},{20,21},{21,22},{22,23},{36,37},{37,38},{38,39},... | collective-permute-start | bytes 6291464 | tf_op jit(solution)/shard_map/ppermute | solution.py:269
  77.1 28.7 %collective-permute-start.3 = (bf16[2048,512]{1,0:T(8,128)(2,1)}, bf16[2048,512]{1,0:T(8,128)(2,1)}, u32[]{:S(2)}, u32[]{:S(2)}) collective-permute-start(bf16[2048,512]{1,0:T(8,128)(2,1)} %collective-permute-done.1.refs_0_), channel_id=1, source_target_pairs={{1,2},{2,3},{9,10},{10,11},{13,14},{14,15},{17,18},{18,19},{25,26}... | collective-permute-start | bytes 6291464 | tf_op jit(solution)/shard_map/ppermute | solution.py:272
  102.5 1.4 copy-start.5
  103.9 27.1 %collective-permute-start.7 = (bf16[2048,512]{1,0:T(8,128)(2,1)}, bf16[2048,512]{1,0:T(8,128)(2,1)}, u32[]{:S(2)}, u32[]{:S(2)}) collective-permute-start(bf16[2048,512]{1,0:T(8,128)(2,1)} %collective-permute-done.5.refs_3_), channel_id=1, source_target_pairs={{5,6},{6,7},{21,22},{22,23},{37,38},{38,39},{53,54},{54,55},{69,70... | collective-permute-start | bytes 6291464 | tf_op jit(solution)/shard_map/ppermute | solution.py:272
  133.0 3.4 %collective-permute-start.8 = (bf16[64,2048]{1,0:T(8,128)(2,1)}, bf16[64,2048]{1,0:T(8,128)(2,1)S(1)}, u32[]{:S(2)}, u32[]{:S(2)}) collective-permute-start(bf16[64,2048]{1,0:T(8,128)(2,1)} %get-tuple-element.39), channel_id=1, source_target_pairs={{0,16},{1,17},{2,18},{3,19}} | collective-permute-start | bytes 786440 | tf_op jit(solution)/shard_map/ppermute | solution.py:283
  133.7 3.4 %collective-permute-start.9 = (bf16[64,2048]{1,0:T(8,128)(2,1)}, bf16[64,2048]{1,0:T(8,128)(2,1)S(1)}, u32[]{:S(2)}, u32[]{:S(2)}) collective-permute-start(bf16[64,2048]{1,0:T(8,128)(2,1)} %get-tuple-element.40), channel_id=1, source_target_pairs={{0,32},{1,33},{2,34},{3,35}} | collective-permute-start | bytes 786440 | tf_op jit(solution)/shard_map/ppermute | solution.py:283
  134.3 3.5 %collective-permute-start.10 = (bf16[64,2048]{1,0:T(8,128)(2,1)}, bf16[64,2048]{1,0:T(8,128)(2,1)S(1)}, u32[]{:S(2)}, u32[]{:S(2)}) collective-permute-start(bf16[64,2048]{1,0:T(8,128)(2,1)} %get-tuple-element.41), channel_id=1, source_target_pairs={{0,48},{1,49},{2,50},{3,51}} | collective-permute-start | bytes 786440 | tf_op jit(solution)/shard_map/ppermute | solution.py:283
  135.0 2.8 %collective-permute-start.11 = (bf16[64,2048]{1,0:T(8,128)(2,1)}, bf16[64,2048]{1,0:T(8,128)(2,1)S(1)}, u32[]{:S(2)}, u32[]{:S(2)}) collective-permute-start(bf16[64,2048]{1,0:T(8,128)(2,1)} %get-tuple-element.42), channel_id=1, source_target_pairs={{0,64},{1,65},{2,66},{3,67}} | collective-permute-start | bytes 786440 | tf_op jit(solution)/shard_map/ppermute | solution.py:283
  135.7 2.1 %collective-permute-start.12 = (bf16[64,2048]{1,0:T(8,128)(2,1)}, bf16[64,2048]{1,0:T(8,128)(2,1)S(1)}, u32[]{:S(2)}, u32[]{:S(2)}) collective-permute-start(bf16[64,2048]{1,0:T(8,128)(2,1)} %get-tuple-element.43), channel_id=1, source_target_pairs={{0,80},{1,81},{2,82},{3,83}} | collective-permute-start | bytes 786440 | tf_op jit(solution)/shard_map/ppermute | solution.py:283
  136.4 1.4 collective-permute-start.13
  137.1 0.7 collective-permute-start.14
  138.9 39.1 %copy-start.1 = (bf16[2048,512]{1,0:T(8,128)(2,1)S(1)}, bf16[2048,512]{1,0:T(8,128)(2,1)}, u32[]{:S(2)}) copy-start(bf16[2048,512]{1,0:T(8,128)(2,1)} %copy-done) | copy-start | bytes 6291460
  138.9 39.1 %copy-start.4 = (s32[5]{0:T(128)S(1)}, s32[5]{0:T(128)}, u32[]{:S(2)}) copy-start(s32[5]{0:T(128)} %stack.37.where_ref) | copy-start | bytes 64
  138.9 2.2 %collective-permute-start.17 = (bf16[64,2048]{1,0:T(8,128)(2,1)S(1)}, bf16[64,2048]{1,0:T(8,128)(2,1)S(1)}, u32[]{:S(2)}, u32[]{:S(2)}) collective-permute-start(bf16[64,2048]{1,0:T(8,128)(2,1)S(1)} %add_select_fusion.1), channel_id=1, source_target_pairs={{0,128},{1,129},{2,130},{3,131},{16,144},{17,145},{18,146},{19,147... | collective-permute-start | bytes 786440 | tf_op jit(solution)/shard_map/ppermute | solution.py:291
  139.7 1.4 collective-permute-start.16
  140.4 0.7 collective-permute-start.15
  141.2 3.4 %collective-permute-start.18 = (bf16[64,2048]{1,0:T(8,128)(2,1)S(1)}, bf16[64,2048]{1,0:T(8,128)(2,1)S(1)}, u32[]{:S(2)}, u32[]{:S(2)}) collective-permute-start(bf16[64,2048]{1,0:T(8,128)(2,1)S(1)} %add_select_fusion), channel_id=1, source_target_pairs={{0,4},{1,5},{2,6},{3,7},{8,12},{9,13},{10,14},{11,15},{16,20},{17,... | collective-permute-start | bytes 786440 | tf_op jit(solution)/shard_map/ppermute | solution.py:294
  142.5 35.5 %copy-start.3 = (bf16[2048,512]{1,0:T(8,128)(2,1)S(1)}, bf16[2048,512]{1,0:T(8,128)(2,1)}, u32[]{:S(2)}) copy-start(bf16[2048,512]{1,0:T(8,128)(2,1)} %copy-done.2) | copy-start | bytes 6291460
  144.7 20.8 %collective-permute-start.21 = (bf16[64,2048]{1,0:T(8,128)(2,1)S(1)}, bf16[64,2048]{1,0:T(8,128)(2,1)S(1)}, u32[]{:S(2)}, u32[]{:S(2)}) collective-permute-start(bf16[64,2048]{1,0:T(8,128)(2,1)S(1)} %broadcast_select_fusion.refs_6_), channel_id=1, source_target_pairs={{0,48},{1,49},{2,50},{3,51},{4,84},{5,85},{6,86},{7,87},{8,56},{9,... | collective-permute-start | bytes 786440 | tf_op jit(solution)/shard_map/ppermute | solution.py:305
  150.3 17.4 %collective-permute-start.20 = (bf16[64,2048]{1,0:T(8,128)(2,1)S(1)}, bf16[64,2048]{1,0:T(8,128)(2,1)S(1)}, u32[]{:S(2)}, u32[]{:S(2)}) collective-permute-start(bf16[64,2048]{1,0:T(8,128)(2,1)S(1)} %broadcast_select_fusion.refs_6_), channel_id=1, source_target_pairs={{0,32},{1,33},{2,34},{3,35},{4,100},{5,101},{6,102},{7,103},{8,40}... | collective-permute-start | bytes 786440 | tf_op jit(solution)/shard_map/ppermute | solution.py:305
  150.5 22.7 %collective-permute-start.19 = (bf16[64,2048]{1,0:T(8,128)(2,1)S(1)}, bf16[64,2048]{1,0:T(8,128)(2,1)S(1)}, u32[]{:S(2)}, u32[]{:S(2)}) collective-permute-start(bf16[64,2048]{1,0:T(8,128)(2,1)S(1)} %broadcast_select_fusion.refs_6_), channel_id=1, source_target_pairs={{0,16},{1,17},{2,18},{3,19},{4,116},{5,117},{6,118},{7,119},{8,24}... | collective-permute-start | bytes 786440 | tf_op jit(solution)/shard_map/ppermute | solution.py:305
  151.0 14.4 %collective-permute-start.22 = (bf16[32,2048]{1,0:T(8,128)(2,1)S(1)}, bf16[32,2048]{1,0:T(8,128)(2,1)S(1)}, u32[]{:S(2)}, u32[]{:S(2)}) collective-permute-start(bf16[32,2048]{1,0:T(8,128)(2,1)S(1)} %constant_dynamic-slice_fusion), channel_id=1, source_target_pairs={{0,64},{1,65},{2,66},{3,67},{4,68},{5,69},{6,70},{7,71},{8,72},{9,... | collective-permute-start | bytes 393224 | tf_op jit(solution)/shard_map/ppermute | solution.py:301
  173.3 4.7 %collective-permute-start.23 = (bf16[224,2048]{1,0:T(8,128)(2,1)S(1)}, bf16[224,2048]{1,0:T(8,128)(2,1)S(1)}, u32[]{:S(2)}, u32[]{:S(2)}) collective-permute-start(bf16[224,2048]{1,0:T(8,128)(2,1)S(1)} %pad_maximum_fusion), channel_id=1, source_target_pairs={{0,4},{1,5},{2,6},{3,7},{4,0},{5,1},{6,2},{7,3},{8,12},{9,13},{10,... | collective-permute-start | bytes 2752520 | tf_op jit(solution)/shard_map/ppermute | solution.py:307

commit v8 on v7

--- a/solution.py
+++ b/solution.py
@@ -26,36 +26,76 @@
     )
 
 
-def leaf_inverse(tile_ref, x_ref, g_ref, n_ref, e_ref):
-    rows = lax.broadcasted_iota(jnp.int32, (TILE, TILE), 0)
-    cols = lax.broadcasted_iota(jnp.int32, (TILE, TILE), 1)
-    diag = rows == cols
-    tile = tile_ref[...]
-    picked = jnp.where(diag, tile, 0.0)
-    down = lax.rsqrt(jnp.sum(picked, axis=1, keepdims=True))
-    across = lax.rsqrt(jnp.sum(picked, axis=0, keepdims=True))
-    gram = tile * down * across - diag.astype(jnp.float32)
+def leaf_inverse(tile_ref, x_ref, g_ref, n_ref, nb_ref):
+    part = TILE // 2
+    top, low = slice(0, part), slice(part, TILE)
+    diag = lax.broadcasted_iota(jnp.int32, (part, part), 0) == lax.broadcasted_iota(
+        jnp.int32, (part, part), 1
+    )
+    under = lax.broadcasted_iota(jnp.int32, (part, part), 0) > lax.broadcasted_iota(
+        jnp.int32, (part, part), 1
+    )
 
     def lower(mat):
-        return jnp.where(rows > cols, mat, jnp.where(diag, 0.5 * mat, 0.0))
-
-    g_ref[...] = gram
-    n_ref[...] = lower(gram)
+        return jnp.where(under, mat, jnp.where(diag, 0.5 * mat, 0.0))
+
+    def scales(block):
+        picked = jnp.where(diag, tile_ref[block, block], 0.0)
+        return (
+            lax.rsqrt(jnp.sum(picked, axis=1, keepdims=True)),
+            lax.rsqrt(jnp.sum(picked, axis=0, keepdims=True)),
+        )
+
+    (down0, across0), (down1, across1) = scales(top), scales(low)
+    eye = diag.astype(jnp.float32)
+    g00 = tile_ref[top, top] * down0 * across0 - eye
+    g10 = tile_ref[low, top] * down1 * across0
+    g01 = tile_ref[top, low] * down0 * across1
+    g11 = tile_ref[low, low] * down1 * across1 - eye
+    g_ref[top, top] = g00.astype(jnp.bfloat16)
+    g_ref[low, top] = g10.astype(jnp.bfloat16)
+    g_ref[top, low] = g01.astype(jnp.bfloat16)
+    g_ref[low, low] = g11.astype(jnp.bfloat16)
+    n_ref[top, top] = lower(g00)
+    n_ref[low, top] = g10
+    n_ref[low, low] = lower(g11)
+    nb_ref[top, top] = lower(g00).astype(jnp.bfloat16)
+    nb_ref[low, top] = g10.astype(jnp.bfloat16)
+    nb_ref[low, low] = lower(g11).astype(jnp.bfloat16)
 
     def step(_, carry):
-        n = n_ref[...]
-        e = g_ref[...] - n - mxu(n, g_ref[...], NN)
-        e_ref[...] = e.astype(jnp.bfloat16)
-        phi = lower(e - n.T - mxu(e_ref[...], n, NT))
-        n_ref[...] = n + phi - mxu(phi, n, NN)
+        n00, n10, n11 = n_ref[top, top], n_ref[low, top], n_ref[low, low]
+        b00, b10, b11 = nb_ref[top, top], nb_ref[low, top], nb_ref[low, low]
+        scaled00 = tile_ref[top, top] * down0 * across0 - eye
+        scaled10 = tile_ref[low, top] * down1 * across0
+        scaled11 = tile_ref[low, low] * down1 * across1 - eye
+        e00 = scaled00 - n00 - mxu(b00, g_ref[top, top], NN)
+        e10 = scaled10 - n10 - mxu(nb_ref[low, :], g_ref[:, top], NN)
+        e11 = scaled11 - n11 - mxu(nb_ref[low, :], g_ref[:, low], NN)
+        c00, c10, c11 = e00.astype(jnp.bfloat16), e10.astype(jnp.bfloat16), e11.astype(jnp.bfloat16)
+        p00 = lower(e00 - jnp.where(diag, n00, 0.0) - mxu(c00, b00, NT))
+        p10 = e10 - mxu(c10, b00, NT)
+        p11 = lower(
+            e11 - jnp.where(diag, n11, 0.0) - mxu(c10, b10, NT) - mxu(c11, b11, NT)
+        )
+        f00, f10, f11 = p00.astype(jnp.bfloat16), p10.astype(jnp.bfloat16), p11.astype(jnp.bfloat16)
+        n00 = n00 + p00 - mxu(f00, b00, NN)
+        n10 = n10 + p10 - mxu(f10, b00, NN) - mxu(f11, b10, NN)
+        n11 = n11 + p11 - mxu(f11, b11, NN)
+        n_ref[top, top], n_ref[low, top], n_ref[low, low] = n00, n10, n11
+        nb_ref[top, top] = n00.astype(jnp.bfloat16)
+        nb_ref[low, top] = n10.astype(jnp.bfloat16)
+        nb_ref[low, low] = n11.astype(jnp.bfloat16)
         return carry
 
     lax.fori_loop(0, ROOT_ITERS, step, 0)
-    x_ref[...] = ((diag.astype(jnp.float32) - n_ref[...]) * across).astype(jnp.bfloat16)
+    x_ref[top, top] = ((eye - n_ref[top, top]) * across0).astype(jnp.bfloat16)
+    x_ref[top, low] = jnp.zeros((part, part), jnp.bfloat16)
+    x_ref[low, top] = (-n_ref[low, top] * across0).astype(jnp.bfloat16)
+    x_ref[low, low] = ((eye - n_ref[low, low]) * across1).astype(jnp.bfloat16)
 
 
 HALF = PW // 2
-HBM = pl.BlockSpec(memory_space=pltpu.HBM)
 
 
 def run_copies(found, dest, sems):
@@ -70,11 +110,11 @@
 
 
 def fetch_rows(col, parts, dest, sems):
-    near, wrap, far = parts
+    near, wrap, upper, lower = parts
     found = {
         1: [(near, 0, 0, PW)],
-        2: [(near, 1, 0, PW), (far, 0, 0, PW)],
-        3: [(near, 2, 0, PW), (wrap, 0, 0, PW), (far, 1, 0, PW)],
+        2: [(near, 1, 0, PW), (upper, 0, 0, HALF), (lower, 0, 1, HALF)],
+        3: [(near, 2, 0, PW), (wrap, 0, 0, PW), (upper, 1, 0, HALF), (lower, 1, 1, HALF)],
     }
     for column, copies in found.items():
 
@@ -84,13 +124,13 @@
 
 
 def factor_kernel(where_ref, own, *refs):
-    parts, outs = refs[:3], refs[3:11]
-    t_ref, s_ref, l_ref, x_ref, r_ref, g_ref, n_ref, e_ref, sems = refs[11:]
+    parts, outs = refs[:4], refs[4:12]
+    t_ref, s_ref, l_ref, x_ref, r_ref, g_ref, n_ref, e_ref, sems = refs[12:]
     col = where_ref[2]
 
     @pl.when(where_ref[0] == 1)
     def _():
-        mine = pltpu.make_async_copy(own, t_ref.at[col], sems.at[3])
+        mine = pltpu.make_async_copy(own, t_ref.at[col], sems.at[4])
         mine.start()
         fetch_rows(col, parts, t_ref, sems)
         mine.wait()
@@ -150,7 +190,7 @@
     return pl.pallas_call(
         factor_kernel,
         out_shape=[jax.ShapeDtypeStruct((64, PW), jnp.bfloat16)] * 8,
-        in_specs=[pl.BlockSpec(memory_space=pltpu.SMEM)] + [HBM] * 4,
+        in_specs=[pl.BlockSpec(memory_space=pltpu.SMEM)] + [HBM] * 5,
         out_specs=[pl.BlockSpec(memory_space=pltpu.VMEM)] * 8,
         scratch_shapes=[
             pltpu.VMEM((BLOCKS, PW, TILE), jnp.bfloat16),
@@ -158,10 +198,10 @@
             pltpu.VMEM((BLOCKS, BLOCKS, TILE, TILE), jnp.bfloat16),
             pltpu.VMEM((BLOCKS, TILE, TILE), jnp.bfloat16),
             pltpu.VMEM((BLOCKS, TILE, TILE), jnp.bfloat16),
-            pltpu.VMEM((TILE, TILE), jnp.float32),
+            pltpu.VMEM((TILE, TILE), jnp.bfloat16),
             pltpu.VMEM((TILE, TILE), jnp.float32),
             pltpu.VMEM((TILE, TILE), jnp.bfloat16),
-            pltpu.SemaphoreType.DMA((4,)),
+            pltpu.SemaphoreType.DMA((5,)),
         ],
         compiler_params=pltpu.CompilerParams(vmem_limit_bytes=56 << 20),
         name="factor_rows",
@@ -172,9 +212,9 @@
 
 
 def apply_kernel(where_ref, own, *refs):
-    main, late = refs[:3], refs[3:6]
-    chunks = refs[6 : 6 + CHUNKS]
-    out, p_ref, r_ref, psems, rsems = refs[7 + CHUNKS :]
+    main, late = refs[:4], refs[4:8]
+    chunks = refs[8 : 8 + CHUNKS]
+    out, p_ref, r_ref, psems, rsems = refs[9 + CHUNKS :]
     second, col, z, core = where_ref[1], where_ref[2], where_ref[3], where_ref[4]
     sign = 1 - 2 * core
     copies = []
@@ -190,7 +230,7 @@
         place(swapped.at[pl.ds(by * 64 - 64, 64)], lax.rem(z + sign * by + 8, 8) * 64, 64)
     place(chunks[4], lax.rem(z + 4, 8) * 64 + core * 32, 32)
     place(swapped.at[pl.ds(192, 32)], lax.rem(z + 4, 8) * 64 + (1 - core) * 32, 32)
-    copies.append(pltpu.make_async_copy(own, p_ref.at[col], psems.at[3]))
+    copies.append(pltpu.make_async_copy(own, p_ref.at[col], psems.at[4]))
     for copy in copies:
         copy.start()
 
@@ -220,12 +260,12 @@
     return pl.pallas_call(
         apply_kernel,
         out_shape=jax.ShapeDtypeStruct((TILE, PW), jnp.bfloat16),
-        in_specs=[pl.BlockSpec(memory_space=pltpu.SMEM)] + [HBM] * (8 + CHUNKS),
+        in_specs=[pl.BlockSpec(memory_space=pltpu.SMEM)] + [HBM] * (10 + CHUNKS),
         out_specs=pl.BlockSpec(memory_space=pltpu.VMEM),
         scratch_shapes=[
             pltpu.VMEM((BLOCKS, PW, TILE), jnp.bfloat16),
             pltpu.VMEM((TILE, PW), jnp.bfloat16),
-            pltpu.SemaphoreType.DMA((4,)),
+            pltpu.SemaphoreType.DMA((5,)),
             pltpu.SemaphoreType.DMA((9,)),
         ],
         compiler_params=pltpu.CompilerParams(vmem_limit_bytes=40 << 20),
@@ -265,12 +305,15 @@
     return (c, y, k) != (0, 0, 1)
 
 
-def gather(part, member):
+def gather(part, member, column):
     near = lax.ppermute(part, ALL, moves(member, (0, 1), (1, 2), (2, 3)))
     wrap = lax.ppermute(part, ALL, moves(member, (0, 3)))
-    near, wrap = lax.optimization_barrier((near, wrap))
-    far = lax.ppermute(near, ALL, moves(member, (1, 2), (2, 3)))
-    return [near, wrap, far]
+    back = lax.ppermute(part[HALF:], ALL, moves(member, (1, 0)))
+    near, wrap, back = lax.optimization_barrier((near, wrap, back))
+    upper = lax.ppermute(near[:HALF], ALL, moves(member, (1, 2), (2, 3)))
+    mixed = jnp.where(column == 0, back, wrap[HALF:])
+    lower = lax.ppermute(mixed, ALL, moves(member, (0, 3), (3, 2)))
+    return [near, wrap, upper, lower]
 
 
 def spread_rows(chunks, z, y, core):
@@ -324,19 +367,19 @@
     factors = jnp.concatenate([kept, got], axis=2)
     update = jnp.einsum("trk,trn->tkn", factors[0], factors[1], preferred_element_type=jnp.float32)
     own = (front.astype(jnp.float32) - update.reshape(PW, TILE)).astype(jnp.bfloat16)
-    main = gather(own, is_other)
+    main = gather(own, is_other, column)
     token = lax.ppermute(
         main[0][:8, :128] + main[1][:8, :128],
         ALL,
         pairs_of(lambda c, zz, yy, kk, j: (0, zz, 0, 1, j) if (c, yy, kk) == (0, 1, 0) else None),
     )
     own_late, token = lax.optimization_barrier((own, token))
-    late = gather(own_late, is_second)
+    late = gather(own_late, is_second, column)
     second = jnp.logical_and(y == 0, core == 1)
     first = jnp.logical_and(jnp.logical_and(y == 0, z == 0), core == 0)
     where = jnp.stack([first, second, column, z, core]).astype(jnp.int32)
     where, *gathered = lax.optimization_barrier((where, *main, *late))
-    main, late = gathered[:3], gathered[3:]
+    main, late = gathered[:4], gathered[4:]
     chunks = factor_rows(where, own, main)
     chunks = spread_rows(chunks, z, y, core)
     return apply_rows(where, own, main, late, chunks, token)

time: 189 us -> 187 us (0.989)
  waiting for transfers between devices: 134 us -> 113 us
  local copies, waits for them, and re-layouts: 3.29 us -> 13.8 us
  starting transfers between devices: 34.6 us -> 39.2 us
  other arithmetic: 2.79 us -> 6.56 us
    ppermute x2 -> x6, waiting for transfers between devices: 25.2 us -> 12.3 us  [the longest x2 7.41 us: gather(): upper = lax.ppermute(near[:HALF], ALL, moves(member, (1, 2), (2, 3)))]
    ppermute x2 -> x6, starting transfers between devices: 3.27 us -> 9.95 us  [the longest x2 5.61 us: gather(): lower = lax.ppermute(mixed, ALL, moves(member, (0, 3), (3, 2)))]
    ppermute x2, waiting for transfers between devices: 23.4 us -> 17 us  [gather(): wrap = lax.ppermute(part, ALL, moves(member, (0, 3)))]
    slice x0 -> x4, local copies, waits for them, and re-layouts: none -> 5.84 us  [the longest x2 4.68 us: gather(): upper = lax.ppermute(near[:HALF], ALL, moves(member, (1, 2), (2, 3)))]
    unnamed x17 -> x35, local copies, waits for them, and re-layouts: 2.55 us -> 7.15 us
    select_n x0 -> x2, other arithmetic: none -> 3.46 us  [gather(): mixed = jnp.where(column == 0, back, wrap[HALF:])]
  transfers between devices with their start and end apart: 24 -> 28, of which waited for: 10 -> 10; matrix products, arithmetic and copies ran while one was open for 0% -> 5% of each run, Pallas kernels for 0% -> 0%
where the time goes in v8:
time: 187 us; the launch traced here: 186 us
  waiting for transfers between devices  113 us (60%)
  starting transfers between devices  39.2 us (21%)
  local copies, waits for them, and re-layouts  13.8 us (7%)
  Pallas kernels  12.1 us (6%)
  other arithmetic  6.56 us (4%)
    ppermute x1, waiting for transfers between devices, shards(): lax.ppermute(main[0][:8, :128] + main[1][:8, :128], ALL, pairs_of(lambda...  50.6 us
    ppermute x2, waiting for transfers between devices, gather(): wrap = lax.ppermute(part, ALL, moves(member, (0, 3)))  17 us
    ppermute x1, waiting for transfers between devices, shards(): lax.ppermute(sent, ALL, pairs_of(lambda c, zz, yy, kk, j: (1 - c, zz, yy,...  11.4 us
    pallas_call x1, Pallas kernels, apply_rows(): pl.pallas_call(apply_kernel, out_shape=jax.ShapeDtypeStruct((TILE, PW), j...  10.1 us
    ppermute x1, waiting for transfers between devices, spread_rows(): half = lax.ppermute(part, ALL, across)  9.25 us
    ppermute x3, waiting for transfers between devices, spread_rows(): direct[by] = lax.ppermute(chunk, ALL, pairs)  8.41 us
    ppermute x2, waiting for transfers between devices, gather(): upper = lax.ppermute(near[:HALF], ALL, moves(member, (1, 2), (2, 3)))  7.41 us
    unnamed x35, local copies, waits for them, and re-layouts  7.15 us
  transfers between devices with their start and end apart: 28, of which 10 were waited for; matrix products, arithmetic and copies ran while one was open for 5% of the time, Pallas kernels for 0%

profile of v8, /device:TPU:7, one launch (start us, length us, event | category | flops | bytes accessed | tf_op | source)
XLA Modules:
  0.0 186.4 jit_solution(14009594375277973088)
XLA Ops:
  0.0 1.3 copy.8
  1.6 3.0 %collective-permute-start = (bf16[2,4,64,512]{3,2,1,0:T(8,128)(2,1)S(1)}, bf16[2,4,64,512]{3,2,1,0:T(8,128)(2,1)S(1)}, u32[]{:S(2)}, u32[]{:S(2)}) collective-permute-start(bf16[2,4,64,512]{3,2,1,0:T(8,128)(2,1)S(1)} %get-tuple-element.55), channel_id=1, source_target_pairs={{0,128},{1,129},{2,130},{3,131},{4,132},{5,133},{6,134},{7,135},{8... | collective-permute-start | bytes 1572872 | tf_op jit(solution)/shard_map/ppermute | solution.py:364
  4.6 11.4 %collective-permute-done = bf16[2,4,64,512]{3,2,1,0:T(8,128)(2,1)S(1)} collective-permute-done((bf16[2,4,64,512]{3,2,1,0:T(8,128)(2,1)S(1)}, bf16[2,4,64,512]{3,2,1,0:T(8,128)(2,1)S(1)}, u32[]{:S(2)}, u32[]{:S(2)}) %collective-permute-start) | collective-permute-done | bytes 524320 | tf_op jit(solution)/shard_map/ppermute | solution.py:364
  15.9 0.7 fusion.3
  16.7 0.8 copy-done.14
  17.5 0.7 fusion.own
  18.3 0.8 collective-permute-start.2
  19.1 0.8 collective-permute-start.1
  19.9 0.7 collective-permute-start.3
  20.7 1.0 copy-done.15
  21.7 1.3 collective-permute-start.6
  23.0 50.6 %collective-permute-done.6.refs_14_ = bf16[8,128]{1,0:T(8,128)(2,1)S(1)} collective-permute-done((bf16[8,128]{1,0:T(8,128)(2,1)S(1)}, bf16[8,128]{1,0:T(8,128)(2,1)S(1)}, u32[]{:S(2)}, u32[]{:S(2)}) %collective-permute-start.6) | collective-permute-done | bytes 2080 | tf_op jit(solution)/shard_map/ppermute | solution.py:371
  73.6 1.3 collective-permute-start.8
  74.9 1.3 collective-permute-start.7
  76.2 1.1 slice.37
  77.3 1.6 collective-permute-start.9
  78.9 2.4 %slice.33 = bf16[1024,512]{1,0:T(8,128)(2,1)} slice(bf16[2048,512]{1,0:T(8,128)(2,1)} %copy-done.5), slice={[0:1024], [0:512]} | slice | bytes 2097152 | tf_op jit(solution)/shard_map/slice | solution.py:313
  81.4 0.7 collective-permute-start.4
  82.1 1.1 slice_select_fusion.1
  83.2 1.6 collective-permute-start.5
  84.8 17.0 %collective-permute-done.8.refs_5_ = bf16[2048,512]{1,0:T(8,128)(2,1)} collective-permute-done((bf16[2048,512]{1,0:T(8,128)(2,1)S(1)}, bf16[2048,512]{1,0:T(8,128)(2,1)}, u32[]{:S(2)}, u32[]{:S(2)}) %collective-permute-start.8) | collective-permute-done | bytes 2097184 | tf_op jit(solution)/shard_map/ppermute | solution.py:310
  101.8 2.3 %slice.38 = bf16[1024,512]{1,0:T(8,128)(2,1)} slice(bf16[2048,512]{1,0:T(8,128)(2,1)} %collective-permute-done.7.refs_4_), slice={[0:1024], [0:512]} | slice | bytes 2097152 | tf_op jit(solution)/shard_map/slice | solution.py:313
  104.1 1.3 collective-permute-start.10
  105.4 2.4 %slice_select_fusion = bf16[1024,512]{1,0:T(8,128)(2,1)} fusion(bf16[1024,512]{1,0:T(8,128)(2,1)} %collective-permute-done.9, bf16[2048,512]{1,0:T(8,128)(2,1)} %collective-permute-done.8.refs_5_, pred[]{:T(512)S(6)} %eq.27), kind=kLoop, calls=%fused_computation.8 | loop fusion | flops 524288 | bytes 3145729 | tf_op jit(solution)/shard_map/jit(_where)/select_n | solution.py:314
  107.8 4.0 %collective-permute-start.11 = (bf16[1024,512]{1,0:T(8,128)(2,1)}, bf16[1024,512]{1,0:T(8,128)(2,1)S(1)}, u32[]{:S(2)}, u32[]{:S(2)}) collective-permute-start(bf16[1024,512]{1,0:T(8,128)(2,1)} %slice_select_fusion), channel_id=1, source_target_pairs={{4,7},{7,6},{20,23},{23,22},{36,39},{39,38},{52,55},{55,54},{68,71... | collective-permute-start | bytes 3145736 | tf_op jit(solution)/shard_map/ppermute | solution.py:315
  112.4 7.4 %collective-permute-done.10.refs_6_ = bf16[1024,512]{1,0:T(8,128)(2,1)S(1)} collective-permute-done((bf16[1024,512]{1,0:T(8,128)(2,1)}, bf16[1024,512]{1,0:T(8,128)(2,1)S(1)}, u32[]{:S(2)}, u32[]{:S(2)}) %collective-permute-start.10) | collective-permute-done | bytes 1048608 | tf_op jit(solution)/shard_map/ppermute | solution.py:313
  119.8 4.9 %collective-permute-done.11.refs_7_ = bf16[1024,512]{1,0:T(8,128)(2,1)S(1)} collective-permute-done((bf16[1024,512]{1,0:T(8,128)(2,1)}, bf16[1024,512]{1,0:T(8,128)(2,1)S(1)}, u32[]{:S(2)}, u32[]{:S(2)}) %collective-permute-start.11) | collective-permute-done | bytes 1048608 | tf_op jit(solution)/shard_map/ppermute | solution.py:315
  124.7 2.0 %factor_rows.1 = (bf16[64,2048]{1,0:T(8,128)(2,1)}, bf16[64,2048]{1,0:T(8,128)(2,1)}, bf16[64,2048]{1,0:T(8,128)(2,1)}, bf16[64,2048]{1,0:T(8,128)(2,1)}, bf16[6...) custom-call(s32[5]{0:T(128)} %stack.37.where_ref, ...), custom_call_target="tpu_custom_call" | custom-call | tf_op jit(solution)/shard_map/factor_rows/pallas_call | solution.py:190
  128.2 0.7 collective-permute-start.14
  128.8 0.7 collective-permute-start.15
  129.5 0.7 collective-permute-start.16
  130.9 0.7 collective-permute-start.18
  131.7 1.2 add_select_fusion.1
  132.9 0.8 collective-permute-start.21
  135.1 1.3 collective-permute-start.22
  136.5 2.2 %collective-permute-done.22 = bf16[64,2048]{1,0:T(8,128)(2,1)} collective-permute-done((bf16[64,2048]{1,0:T(8,128)(2,1)S(1)}, bf16[64,2048]{1,0:T(8,128)(2,1)}, u32[]{:S(2)}, u32[]{:S(2)}) %collective-permute-start.22) | collective-permute-done | bytes 262176 | tf_op jit(solution)/shard_map/ppermute | solution.py:337
  138.7 1.0 broadcast_select_fusion.refs_8_
  139.7 5.5 %collective-permute-start.25 = (bf16[64,2048]{1,0:T(8,128)(2,1)S(1)}, bf16[64,2048]{1,0:T(8,128)(2,1)S(1)}, u32[]{:S(2)}, u32[]{:S(2)}) collective-permute-start(bf16[64,2048]{1,0:T(8,128)(2,1)S(1)} %broadcast_select_fusion.refs_8_), channel_id=1, source_target_pairs={{0,48},{1,49},{2,50},{3,51},{4,84},{5,85},{6,86},{7,87},{8,56},{9,... | collective-permute-start | bytes 786440 | tf_op jit(solution)/shard_map/ppermute | solution.py:348
  145.9 4.6 %collective-permute-start.26 = (bf16[32,2048]{1,0:T(8,128)(2,1)S(1)}, bf16[32,2048]{1,0:T(8,128)(2,1)S(1)}, u32[]{:S(2)}, u32[]{:S(2)}) collective-permute-start(bf16[32,2048]{1,0:T(8,128)(2,1)S(1)} %constant_dynamic-slice_fusion), channel_id=1, source_target_pairs={{0,64},{1,65},{2,66},{3,67},{4,68},{5,69},{6,70},{7,71},{8,72},{9,... | collective-permute-start | bytes 393224 | tf_op jit(solution)/shard_map/ppermute | solution.py:344
  150.5 9.3 %collective-permute-done.26.refs_12_ = bf16[32,2048]{1,0:T(8,128)(2,1)S(1)} collective-permute-done((bf16[32,2048]{1,0:T(8,128)(2,1)S(1)}, bf16[32,2048]{1,0:T(8,128)(2,1)S(1)}, u32[]{:S(2)}, u32[]{:S(2)}) %collective-permute-start.26) | collective-permute-done | bytes 131104 | tf_op jit(solution)/shard_map/ppermute | solution.py:344
  159.8 2.8 %collective-permute-done.24.refs_10_ = bf16[64,2048]{1,0:T(8,128)(2,1)S(1)} collective-permute-done((bf16[64,2048]{1,0:T(8,128)(2,1)S(1)}, bf16[64,2048]{1,0:T(8,128)(2,1)S(1)}, u32[]{:S(2)}, u32[]{:S(2)}) %collective-permute-start.24) | collective-permute-done | bytes 262176 | tf_op jit(solution)/shard_map/ppermute | solution.py:348
  162.6 5.6 %collective-permute-done.23.refs_9_ = bf16[64,2048]{1,0:T(8,128)(2,1)S(1)} collective-permute-done((bf16[64,2048]{1,0:T(8,128)(2,1)S(1)}, bf16[64,2048]{1,0:T(8,128)(2,1)S(1)}, u32[]{:S(2)}, u32[]{:S(2)}) %collective-permute-start.23) | collective-permute-done | bytes 262176 | tf_op jit(solution)/shard_map/ppermute | solution.py:348
  168.3 1.8 collective-permute-start.27
  170.1 2.1 %collective-permute-done.27.refs_13_ = bf16[224,2048]{1,0:T(8,128)(2,1)S(1)} collective-permute-done((bf16[224,2048]{1,0:T(8,128)(2,1)S(1)}, bf16[224,2048]{1,0:T(8,128)(2,1)S(1)}, u32[]{:S(2)}, u32[]{:S(2)}) %collective-permute-start.27) | collective-permute-done | bytes 917536 | tf_op jit(solution)/shard_map/ppermute | solution.py:350
  172.2 1.6 copy-done.6
  173.8 1.2 copy-done.10
  175.0 1.2 copy-done.12
  176.2 10.1 %apply_rows.1 = bf16[512,2048]{1,0:T(8,128)(2,1)} custom-call(s32[5]{0:T(128)S(1)} %copy-done.13, bf16[2048,512]{1,0:T(8,128)(2,1)S(1)} %copy-done.1, bf16[2048,512]{1,0:T(8,128)(2,1)S(1)} %copy-done.6, bf16[2048,512]{1,0:T(8,128)(2,1)S(1)} %copy-done.4, bf16[1024,512]{1,0:T(8,128)(2,1)S(1)} %copy-done.8, bf16[1024,512]{1,0:T(8,128)(2,1)} %collective-permute-done.5.refs_3_, ...), custom_call_target="tpu_custom_call" | custom-call | tf_op jit(solution)/shard_map/apply_rows/pallas_call | solution.py:260
  (62 shorter events, 5.3 us)
Async XLA Ops:
  0.0 1.4 copy-start.16
  1.6 14.4 %collective-permute-start = (bf16[2,4,64,512]{3,2,1,0:T(8,128)(2,1)S(1)}, bf16[2,4,64,512]{3,2,1,0:T(8,128)(2,1)S(1)}, u32[]{:S(2)}, u32[]{:S(2)}) collective-permute-start(bf16[2,4,64,512]{3,2,1,0:T(8,128)(2,1)S(1)} %get-tuple-element.55), channel_id=1, source_target_pairs={{0,128},{1,129},{2,130},{3,131},{4,132},{5,133},{6,134},{7,135},{8... | collective-permute-start | bytes 1572872 | tf_op jit(solution)/shard_map/ppermute | solution.py:364
  15.9 1.6 copy-start.14
  18.3 59.1 %copy-start = (bf16[2048,512]{1,0:T(8,128)(2,1)}, bf16[2048,512]{1,0:T(8,128)(2,1)S(1)}, u32[]{:S(2)}) copy-start(bf16[2048,512]{1,0:T(8,128)(2,1)S(1)} %fusion.own) | copy-start | bytes 6291460
  18.3 2.4 %collective-permute-start.2 = (bf16[2048,512]{1,0:T(8,128)(2,1)S(1)}, bf16[2048,512]{1,0:T(8,128)(2,1)S(1)}, u32[]{:S(2)}, u32[]{:S(2)}) collective-permute-start(bf16[2048,512]{1,0:T(8,128)(2,1)S(1)} %fusion.own), channel_id=1, source_target_pairs={{0,3},{8,11},{12,15},{16,19},{24,27},{28,31},{32,35},{40,43},{44,4... | collective-permute-start | bytes 6291464 | tf_op jit(solution)/shard_map/ppermute | solution.py:310
  19.1 2.6 %collective-permute-start.1 = (bf16[2048,512]{1,0:T(8,128)(2,1)S(1)}, bf16[2048,512]{1,0:T(8,128)(2,1)S(1)}, u32[]{:S(2)}, u32[]{:S(2)}) collective-permute-start(bf16[2048,512]{1,0:T(8,128)(2,1)S(1)} %fusion.own), channel_id=1, source_target_pairs={{0,1},{1,2},{2,3},{8,9},{9,10},{10,11},{12,13},{13,14},{14,15},{16... | collective-permute-start | bytes 6291464 | tf_op jit(solution)/shard_map/ppermute | solution.py:309
  19.9 0.7 collective-permute-start.3
  20.7 1.0 copy-start.15
  21.7 52.0 %copy-start.2 = (bf16[2048,512]{1,0:T(8,128)(2,1)}, bf16[2048,512]{1,0:T(8,128)(2,1)S(1)}, u32[]{:S(2)}) copy-start(bf16[2048,512]{1,0:T(8,128)(2,1)S(1)} %collective-permute-done.2.refs_1_) | copy-start | bytes 6291460
  21.7 53.2 %copy-start.5 = (bf16[2048,512]{1,0:T(8,128)(2,1)}, bf16[2048,512]{1,0:T(8,128)(2,1)S(1)}, u32[]{:S(2)}) copy-start(bf16[2048,512]{1,0:T(8,128)(2,1)S(1)} %collective-permute-done.1.refs_0_) | copy-start | bytes 6291460
  21.7 51.9 %collective-permute-start.6 = (bf16[8,128]{1,0:T(8,128)(2,1)S(1)}, bf16[8,128]{1,0:T(8,128)(2,1)S(1)}, u32[]{:S(2)}, u32[]{:S(2)}) collective-permute-start(bf16[8,128]{1,0:T(8,128)(2,1)S(1)} %slice_add_fusion), channel_id=1, source_target_pairs={{8,4},{9,5},{10,6},{11,7},{24,20},{25,21},{26,22},{27,23},{40,36},... | collective-permute-start | bytes 6152 | tf_op jit(solution)/shard_map/ppermute | solution.py:371
  73.6 28.2 %collective-permute-start.8 = (bf16[2048,512]{1,0:T(8,128)(2,1)S(1)}, bf16[2048,512]{1,0:T(8,128)(2,1)}, u32[]{:S(2)}, u32[]{:S(2)}) collective-permute-start(bf16[2048,512]{1,0:T(8,128)(2,1)S(1)} %fusion.own), channel_id=1, source_target_pairs={{4,7},{20,23},{36,39},{52,55},{68,71},{84,87},{100,103},{116,119}} | collective-permute-start | bytes 6291464 | tf_op jit(solution)/shard_map/ppermute | solution.py:310
  74.9 26.9 %collective-permute-start.7 = (bf16[2048,512]{1,0:T(8,128)(2,1)S(1)}, bf16[2048,512]{1,0:T(8,128)(2,1)}, u32[]{:S(2)}, u32[]{:S(2)}) collective-permute-start(bf16[2048,512]{1,0:T(8,128)(2,1)S(1)} %fusion.own), channel_id=1, source_target_pairs={{4,5},{5,6},{6,7},{20,21},{21,22},{22,23},{36,37},{37,38},{38,39},... | collective-permute-start | bytes 6291464 | tf_op jit(solution)/shard_map/ppermute | solution.py:309
  77.3 7.5 %collective-permute-start.9 = (bf16[1024,512]{1,0:T(8,128)(2,1)}, bf16[1024,512]{1,0:T(8,128)(2,1)}, u32[]{:S(2)}, u32[]{:S(2)}) collective-permute-start(bf16[1024,512]{1,0:T(8,128)(2,1)} %slice.37), channel_id=1, source_target_pairs={{5,4},{21,20},{37,36},{53,52},{69,68},{85,84},{101,100},{117,116}} | collective-permute-start | bytes 3145736 | tf_op jit(solution)/shard_map/ppermute | solution.py:311
  78.9 3.1 %copy-start.3 = (bf16[2048,512]{1,0:T(8,128)(2,1)S(1)}, bf16[2048,512]{1,0:T(8,128)(2,1)}, u32[]{:S(2)}) copy-start(bf16[2048,512]{1,0:T(8,128)(2,1)} %copy-done.2) | copy-start | bytes 6291460
  81.4 31.1 %collective-permute-start.4 = (bf16[1024,512]{1,0:T(8,128)(2,1)}, bf16[1024,512]{1,0:T(8,128)(2,1)S(1)}, u32[]{:S(2)}, u32[]{:S(2)}) collective-permute-start(bf16[1024,512]{1,0:T(8,128)(2,1)} %slice.33), channel_id=1, source_target_pairs={{1,2},{2,3},{9,10},{10,11},{13,14},{14,15},{17,18},{18,19},{25,26}... | collective-permute-start | bytes 3145736 | tf_op jit(solution)/shard_map/ppermute | solution.py:313
  83.2 29.3 %collective-permute-start.5 = (bf16[1024,512]{1,0:T(8,128)(2,1)}, bf16[1024,512]{1,0:T(8,128)(2,1)}, u32[]{:S(2)}, u32[]{:S(2)}) collective-permute-start(bf16[1024,512]{1,0:T(8,128)(2,1)} %slice_select_fusion.1), channel_id=1, source_target_pairs={{0,3},{3,2},{8,11},{11,10},{12,15},{15,14},{16,19},{19,18},{24,27}... | collective-permute-start | bytes 3145736 | tf_op jit(solution)/shard_map/ppermute | solution.py:315
  104.1 15.7 %collective-permute-start.10 = (bf16[1024,512]{1,0:T(8,128)(2,1)}, bf16[1024,512]{1,0:T(8,128)(2,1)S(1)}, u32[]{:S(2)}, u32[]{:S(2)}) collective-permute-start(bf16[1024,512]{1,0:T(8,128)(2,1)} %slice.38), channel_id=1, source_target_pairs={{5,6},{6,7},{21,22},{22,23},{37,38},{38,39},{53,54},{54,55},{69,70... | collective-permute-start | bytes 3145736 | tf_op jit(solution)/shard_map/ppermute | solution.py:313
  107.8 17.0 %collective-permute-start.11 = (bf16[1024,512]{1,0:T(8,128)(2,1)}, bf16[1024,512]{1,0:T(8,128)(2,1)S(1)}, u32[]{:S(2)}, u32[]{:S(2)}) collective-permute-start(bf16[1024,512]{1,0:T(8,128)(2,1)} %slice_select_fusion), channel_id=1, source_target_pairs={{4,7},{7,6},{20,23},{23,22},{36,39},{39,38},{52,55},{55,54},{68,71... | collective-permute-start | bytes 3145736 | tf_op jit(solution)/shard_map/ppermute | solution.py:315
  112.4 12.3 %copy-start.7 = (bf16[1024,512]{1,0:T(8,128)(2,1)}, bf16[1024,512]{1,0:T(8,128)(2,1)S(1)}, u32[]{:S(2)}) copy-start(bf16[1024,512]{1,0:T(8,128)(2,1)S(1)} %collective-permute-done.4.refs_2_) | copy-start | bytes 3145732
  119.8 6.9 %copy-start.9 = (bf16[1024,512]{1,0:T(8,128)(2,1)}, bf16[1024,512]{1,0:T(8,128)(2,1)S(1)}, u32[]{:S(2)}) copy-start(bf16[1024,512]{1,0:T(8,128)(2,1)S(1)} %collective-permute-done.10.refs_6_) | copy-start | bytes 3145732
  124.7 2.1 %copy-start.11 = (bf16[1024,512]{1,0:T(8,128)(2,1)}, bf16[1024,512]{1,0:T(8,128)(2,1)S(1)}, u32[]{:S(2)}) copy-start(bf16[1024,512]{1,0:T(8,128)(2,1)S(1)} %collective-permute-done.11.refs_7_) | copy-start | bytes 3145732
  126.8 3.4 %collective-permute-start.12 = (bf16[64,2048]{1,0:T(8,128)(2,1)}, bf16[64,2048]{1,0:T(8,128)(2,1)S(1)}, u32[]{:S(2)}, u32[]{:S(2)}) collective-permute-start(bf16[64,2048]{1,0:T(8,128)(2,1)} %get-tuple-element.47), channel_id=1, source_target_pairs={{0,16},{1,17},{2,18},{3,19}} | collective-permute-start | bytes 786440 | tf_op jit(solution)/shard_map/ppermute | solution.py:326
  127.5 3.4 %collective-permute-start.13 = (bf16[64,2048]{1,0:T(8,128)(2,1)}, bf16[64,2048]{1,0:T(8,128)(2,1)S(1)}, u32[]{:S(2)}, u32[]{:S(2)}) collective-permute-start(bf16[64,2048]{1,0:T(8,128)(2,1)} %get-tuple-element.48), channel_id=1, source_target_pairs={{0,32},{1,33},{2,34},{3,35}} | collective-permute-start | bytes 786440 | tf_op jit(solution)/shard_map/ppermute | solution.py:326
  128.2 3.5 %collective-permute-start.14 = (bf16[64,2048]{1,0:T(8,128)(2,1)}, bf16[64,2048]{1,0:T(8,128)(2,1)S(1)}, u32[]{:S(2)}, u32[]{:S(2)}) collective-permute-start(bf16[64,2048]{1,0:T(8,128)(2,1)} %get-tuple-element.49), channel_id=1, source_target_pairs={{0,48},{1,49},{2,50},{3,51}} | collective-permute-start | bytes 786440 | tf_op jit(solution)/shard_map/ppermute | solution.py:326
  128.8 2.8 %collective-permute-start.15 = (bf16[64,2048]{1,0:T(8,128)(2,1)}, bf16[64,2048]{1,0:T(8,128)(2,1)S(1)}, u32[]{:S(2)}, u32[]{:S(2)}) collective-permute-start(bf16[64,2048]{1,0:T(8,128)(2,1)} %get-tuple-element.50), channel_id=1, source_target_pairs={{0,64},{1,65},{2,66},{3,67}} | collective-permute-start | bytes 786440 | tf_op jit(solution)/shard_map/ppermute | solution.py:326
  129.5 2.1 %collective-permute-start.16 = (bf16[64,2048]{1,0:T(8,128)(2,1)}, bf16[64,2048]{1,0:T(8,128)(2,1)S(1)}, u32[]{:S(2)}, u32[]{:S(2)}) collective-permute-start(bf16[64,2048]{1,0:T(8,128)(2,1)} %get-tuple-element.51), channel_id=1, source_target_pairs={{0,80},{1,81},{2,82},{3,83}} | collective-permute-start | bytes 786440 | tf_op jit(solution)/shard_map/ppermute | solution.py:326
  130.2 1.4 collective-permute-start.17
  130.9 0.7 collective-permute-start.18
  131.7 40.5 %copy-start.8 = (bf16[1024,512]{1,0:T(8,128)(2,1)S(1)}, bf16[1024,512]{1,0:T(8,128)(2,1)}, u32[]{:S(2)}) copy-start(bf16[1024,512]{1,0:T(8,128)(2,1)} %copy-done.7) | copy-start | bytes 3145732
  132.8 39.3 %copy-start.1 = (bf16[2048,512]{1,0:T(8,128)(2,1)S(1)}, bf16[2048,512]{1,0:T(8,128)(2,1)}, u32[]{:S(2)}) copy-start(bf16[2048,512]{1,0:T(8,128)(2,1)} %copy-done) | copy-start | bytes 6291460
  132.8 39.3 %copy-start.13 = (s32[5]{0:T(128)S(1)}, s32[5]{0:T(128)}, u32[]{:S(2)}) copy-start(s32[5]{0:T(128)} %stack.37.where_ref) | copy-start | bytes 64
  132.9 2.2 %collective-permute-start.21 = (bf16[64,2048]{1,0:T(8,128)(2,1)S(1)}, bf16[64,2048]{1,0:T(8,128)(2,1)S(1)}, u32[]{:S(2)}, u32[]{:S(2)}) collective-permute-start(bf16[64,2048]{1,0:T(8,128)(2,1)S(1)} %add_select_fusion.1), channel_id=1, source_target_pairs={{0,128},{1,129},{2,130},{3,131},{16,144},{17,145},{18,146},{19,147... | collective-permute-start | bytes 786440 | tf_op jit(solution)/shard_map/ppermute | solution.py:334
  133.7 1.4 collective-permute-start.20
  134.4 0.7 collective-permute-start.19
  135.1 3.6 %collective-permute-start.22 = (bf16[64,2048]{1,0:T(8,128)(2,1)S(1)}, bf16[64,2048]{1,0:T(8,128)(2,1)}, u32[]{:S(2)}, u32[]{:S(2)}) collective-permute-start(bf16[64,2048]{1,0:T(8,128)(2,1)S(1)} %add_select_fusion), channel_id=1, source_target_pairs={{0,4},{1,5},{2,6},{3,7},{8,12},{9,13},{10,14},{11,15},{16,20},{17,... | collective-permute-start | bytes 786440 | tf_op jit(solution)/shard_map/ppermute | solution.py:337
  136.4 35.7 %copy-start.4 = (bf16[2048,512]{1,0:T(8,128)(2,1)S(1)}, bf16[2048,512]{1,0:T(8,128)(2,1)}, u32[]{:S(2)}) copy-start(bf16[2048,512]{1,0:T(8,128)(2,1)} %copy-done.2) | copy-start | bytes 6291460
  139.7 20.1 %collective-permute-start.25 = (bf16[64,2048]{1,0:T(8,128)(2,1)S(1)}, bf16[64,2048]{1,0:T(8,128)(2,1)S(1)}, u32[]{:S(2)}, u32[]{:S(2)}) collective-permute-start(bf16[64,2048]{1,0:T(8,128)(2,1)S(1)} %broadcast_select_fusion.refs_8_), channel_id=1, source_target_pairs={{0,48},{1,49},{2,50},{3,51},{4,84},{5,85},{6,86},{7,87},{8,56},{9,... | collective-permute-start | bytes 786440 | tf_op jit(solution)/shard_map/ppermute | solution.py:348
  145.2 17.4 %collective-permute-start.24 = (bf16[64,2048]{1,0:T(8,128)(2,1)S(1)}, bf16[64,2048]{1,0:T(8,128)(2,1)S(1)}, u32[]{:S(2)}, u32[]{:S(2)}) collective-permute-start(bf16[64,2048]{1,0:T(8,128)(2,1)S(1)} %broadcast_select_fusion.refs_8_), channel_id=1, source_target_pairs={{0,32},{1,33},{2,34},{3,35},{4,100},{5,101},{6,102},{7,103},{8,40}... | collective-permute-start | bytes 786440 | tf_op jit(solution)/shard_map/ppermute | solution.py:348
  145.5 22.7 %collective-permute-start.23 = (bf16[64,2048]{1,0:T(8,128)(2,1)S(1)}, bf16[64,2048]{1,0:T(8,128)(2,1)S(1)}, u32[]{:S(2)}, u32[]{:S(2)}) collective-permute-start(bf16[64,2048]{1,0:T(8,128)(2,1)S(1)} %broadcast_select_fusion.refs_8_), channel_id=1, source_target_pairs={{0,16},{1,17},{2,18},{3,19},{4,116},{5,117},{6,118},{7,119},{8,24}... | collective-permute-start | bytes 786440 | tf_op jit(solution)/shard_map/ppermute | solution.py:348
  145.9 13.8 %collective-permute-start.26 = (bf16[32,2048]{1,0:T(8,128)(2,1)S(1)}, bf16[32,2048]{1,0:T(8,128)(2,1)S(1)}, u32[]{:S(2)}, u32[]{:S(2)}) collective-permute-start(bf16[32,2048]{1,0:T(8,128)(2,1)S(1)} %constant_dynamic-slice_fusion), channel_id=1, source_target_pairs={{0,64},{1,65},{2,66},{3,67},{4,68},{5,69},{6,70},{7,71},{8,72},{9,... | collective-permute-start | bytes 393224 | tf_op jit(solution)/shard_map/ppermute | solution.py:344
  168.3 3.9 %collective-permute-start.27 = (bf16[224,2048]{1,0:T(8,128)(2,1)S(1)}, bf16[224,2048]{1,0:T(8,128)(2,1)S(1)}, u32[]{:S(2)}, u32[]{:S(2)}) collective-permute-start(bf16[224,2048]{1,0:T(8,128)(2,1)S(1)} %pad_maximum_fusion), channel_id=1, source_target_pairs={{0,4},{1,5},{2,6},{3,7},{4,0},{5,1},{6,2},{7,3},{8,12},{9,13},{10,... | collective-permute-start | bytes 2752520 | tf_op jit(solution)/shard_map/ppermute | solution.py:350
  172.2 1.6 copy-start.6
  173.8 1.2 copy-start.10
  175.0 1.2 copy-start.12

commit v9 on v8

--- a/solution.py
+++ b/solution.py
@@ -212,9 +212,9 @@
 
 
 def apply_kernel(where_ref, own, *refs):
-    main, late = refs[:4], refs[4:8]
-    chunks = refs[8 : 8 + CHUNKS]
-    out, p_ref, r_ref, psems, rsems = refs[9 + CHUNKS :]
+    near, wrap, upper, lower, late_wrap, late_upper, late_lower = refs[:7]
+    chunks = refs[7 : 7 + CHUNKS]
+    out, p_ref, r_ref, psems, rsems = refs[8 + CHUNKS :]
     second, col, z, core = where_ref[1], where_ref[2], where_ref[3], where_ref[4]
     sign = 1 - 2 * core
     copies = []
@@ -230,15 +230,24 @@
         place(swapped.at[pl.ds(by * 64 - 64, 64)], lax.rem(z + sign * by + 8, 8) * 64, 64)
     place(chunks[4], lax.rem(z + 4, 8) * 64 + core * 32, 32)
     place(swapped.at[pl.ds(192, 32)], lax.rem(z + 4, 8) * 64 + (1 - core) * 32, 32)
-    copies.append(pltpu.make_async_copy(own, p_ref.at[col], psems.at[4]))
+    copies.append(pltpu.make_async_copy(own, p_ref.at[col], psems.at[5]))
     for copy in copies:
         copy.start()
 
-    for index, parts in ((0, main), (1, late)):
-
-        @pl.when(second == index)
+    @pl.when(second == 0)
+    def _():
+        fetch_rows(col, (near, wrap, upper, lower), p_ref, psems)
+
+    for last in range(1, BLOCKS):
+        sources = [(upper, last - 1, 0, HALF), (lower, last - 1, 1, HALF)]
+        if last >= 2:
+            sources += [(late_upper, last - 2, 0, HALF), (late_lower, last - 2, 1, HALF)]
+        if last == 3:
+            sources += [(late_wrap, 0, 0, PW)]
+
+        @pl.when(jnp.logical_and(second == 1, col == last))
         def _():
-            fetch_rows(col, parts, p_ref, psems)
+            run_copies(sources, p_ref, psems)
 
     for copy in copies:
         copy.wait()
@@ -256,21 +265,21 @@
                 out[:, at] = acc.astype(jnp.bfloat16)
 
 
-def apply_rows(where, own, main, late, chunks, token):
+def apply_rows(where, own, gathered, chunks, token):
     return pl.pallas_call(
         apply_kernel,
         out_shape=jax.ShapeDtypeStruct((TILE, PW), jnp.bfloat16),
-        in_specs=[pl.BlockSpec(memory_space=pltpu.SMEM)] + [HBM] * (10 + CHUNKS),
+        in_specs=[pl.BlockSpec(memory_space=pltpu.SMEM)] + [HBM] * (9 + CHUNKS),
         out_specs=pl.BlockSpec(memory_space=pltpu.VMEM),
         scratch_shapes=[
             pltpu.VMEM((BLOCKS, PW, TILE), jnp.bfloat16),
             pltpu.VMEM((TILE, PW), jnp.bfloat16),
-            pltpu.SemaphoreType.DMA((5,)),
+            pltpu.SemaphoreType.DMA((6,)),
             pltpu.SemaphoreType.DMA((9,)),
         ],
-        compiler_params=pltpu.CompilerParams(vmem_limit_bytes=40 << 20),
+        compiler_params=pltpu.CompilerParams(vmem_limit_bytes=60 << 20),
         name="apply_rows",
-    )(where, own, *main, *late, *chunks, token)
+    )(where, own, *gathered, *chunks, token)
 
 
 def device(child, z, ylo, core, col):
@@ -303,17 +312,6 @@
 
 def is_other(c, z, y, k):
     return (c, y, k) != (0, 0, 1)
-
-
-def gather(part, member, column):
-    near = lax.ppermute(part, ALL, moves(member, (0, 1), (1, 2), (2, 3)))
-    wrap = lax.ppermute(part, ALL, moves(member, (0, 3)))
-    back = lax.ppermute(part[HALF:], ALL, moves(member, (1, 0)))
-    near, wrap, back = lax.optimization_barrier((near, wrap, back))
-    upper = lax.ppermute(near[:HALF], ALL, moves(member, (1, 2), (2, 3)))
-    mixed = jnp.where(column == 0, back, wrap[HALF:])
-    lower = lax.ppermute(mixed, ALL, moves(member, (0, 3), (3, 2)))
-    return [near, wrap, upper, lower]
 
 
 def spread_rows(chunks, z, y, core):
@@ -367,22 +365,36 @@
     factors = jnp.concatenate([kept, got], axis=2)
     update = jnp.einsum("trk,trn->tkn", factors[0], factors[1], preferred_element_type=jnp.float32)
     own = (front.astype(jnp.float32) - update.reshape(PW, TILE)).astype(jnp.bfloat16)
-    main = gather(own, is_other, column)
+    second = jnp.logical_and(y == 0, core == 1)
+    first = jnp.logical_and(jnp.logical_and(y == 0, z == 0), core == 0)
+    near = lax.ppermute(own, ALL, moves(is_other, (0, 1), (1, 2), (2, 3)))
+    wrap = lax.ppermute(own, ALL, moves(is_other, (0, 3)))
+    back = lax.ppermute(own[HALF:], ALL, moves(is_other, (1, 0)))
+    near, wrap, back = lax.optimization_barrier((near, wrap, back))
     token = lax.ppermute(
-        main[0][:8, :128] + main[1][:8, :128],
+        near[:8, :128] + wrap[:8, :128],
         ALL,
         pairs_of(lambda c, zz, yy, kk, j: (0, zz, 0, 1, j) if (c, yy, kk) == (0, 1, 0) else None),
     )
-    own_late, token = lax.optimization_barrier((own, token))
-    late = gather(own_late, is_second, column)
-    second = jnp.logical_and(y == 0, core == 1)
-    first = jnp.logical_and(jnp.logical_and(y == 0, z == 0), core == 0)
+    held, token = lax.optimization_barrier((own, token))
+    along = moves(is_second, (0, 1), (1, 2), (2, 3))
+    upper = lax.ppermute(
+        jnp.where(second, held[:HALF], near[:HALF]), ALL, moves(is_other, (1, 2), (2, 3)) + along
+    )
+    mixed = jnp.where(column == 0, back, wrap[HALF:])
+    lower = lax.ppermute(
+        jnp.where(second, held[HALF:], mixed), ALL, moves(is_other, (0, 3), (3, 2)) + along
+    )
+    late_wrap = lax.ppermute(held, ALL, moves(is_second, (0, 3)))
+    late_upper = lax.ppermute(upper, ALL, moves(is_second, (1, 2), (2, 3)))
+    late_lower = lax.ppermute(lower, ALL, moves(is_second, (1, 2), (2, 3)))
     where = jnp.stack([first, second, column, z, core]).astype(jnp.int32)
-    where, *gathered = lax.optimization_barrier((where, *main, *late))
-    main, late = gathered[:4], gathered[4:]
-    chunks = factor_rows(where, own, main)
+    where, *gathered = lax.optimization_barrier(
+        (where, near, wrap, upper, lower, late_wrap, late_upper, late_lower)
+    )
+    chunks = factor_rows(where, own, gathered[:4])
     chunks = spread_rows(chunks, z, y, core)
-    return apply_rows(where, own, main, late, chunks, token)
+    return apply_rows(where, own, gathered, chunks, token)
 
 
 def solution(mesh):

time: 187 us -> 185 us (0.989)
  waiting for transfers between devices: 113 us -> 123 us
  local copies, waits for them, and re-layouts: 13.8 us -> 3.92 us
  other arithmetic: 6.56 us -> 4.56 us
    ppermute x11 -> x9, waiting for transfers between devices: 80 us -> 90.2 us  [the longest x1 48 us: shards(): lax.ppermute(near[:8, :128] + wrap[:8, :128], ALL, pairs_of(lambda c, zz,...]
    slice x4 -> x1, local copies, waits for them, and re-layouts: 5.84 us -> 0.07 us  [shards(): back = lax.ppermute(own[HALF:], ALL, moves(is_other, (1, 0)))]
    unnamed x35 -> x23, local copies, waits for them, and re-layouts: 7.15 us -> 3.06 us
    ppermute x11 -> x9, starting transfers between devices: 15.4 us -> 13.4 us  [the longest x1 2.06 us: shards(): wrap = lax.ppermute(own, ALL, moves(is_other, (0, 3)))]
  transfers between devices with their start and end apart: 28 -> 26, of which waited for: 10 -> 11; matrix products, arithmetic and copies ran while one was open for 5% -> 0% of each run, Pallas kernels for 0% -> 0%
where the time goes in v9:
time: 185 us
  waiting for transfers between devices  123 us (66%)
  starting transfers between devices  37.9 us (20%)
  Pallas kernels  13.4 us (7%)
  other arithmetic  4.56 us (2%)
  local copies, waits for them, and re-layouts  3.92 us (2%)
    ppermute x1, waiting for transfers between devices, shards(): lax.ppermute(near[:8, :128] + wrap[:8, :128], ALL, pairs_of(lambda c, zz,...  48 us
    ppermute x1, waiting for transfers between devices, shards(): lax.ppermute(jnp.where(second, held[HALF:], mixed), ALL, moves(is_other,...  11.6 us
    ppermute x1, waiting for transfers between devices, shards(): lax.ppermute(sent, ALL, pairs_of(lambda c, zz, yy, kk, j: (1 - c, zz, yy,...  11.4 us
    pallas_call x1, Pallas kernels, apply_rows(): pl.pallas_call(apply_kernel, out_shape=jax.ShapeDtypeStruct((TILE, PW), j...  11.4 us
    ppermute x1, waiting for transfers between devices, shards(): late_upper = lax.ppermute(upper, ALL, moves(is_second, (1, 2), (2, 3)))  11.2 us
    ppermute x1, waiting for transfers between devices, shards(): lax.ppermute(jnp.where(second, held[:HALF], near[:HALF]), ALL, moves(is_o...  10 us
    ppermute x1, waiting for transfers between devices, spread_rows(): half = lax.ppermute(part, ALL, across)  9.87 us
    ppermute x1, waiting for transfers between devices, shards(): late_lower = lax.ppermute(lower, ALL, moves(is_second, (1, 2), (2, 3)))  9.28 us
  transfers between devices with their start and end apart: 26, of which 11 were waited for; matrix products, arithmetic and copies ran while one was open for 0% of the time, Pallas kernels for 0%

profile of v9, /device:TPU:7, one launch (start us, length us, event | category | flops | bytes accessed | tf_op | source)
XLA Modules:
  0.0 184.5 jit_solution(3923556365735396886)
XLA Ops:
  0.0 1.3 copy.8
  1.6 3.0 %collective-permute-start = (bf16[2,4,64,512]{3,2,1,0:T(8,128)(2,1)S(1)}, bf16[2,4,64,512]{3,2,1,0:T(8,128)(2,1)S(1)}, u32[]{:S(2)}, u32[]{:S(2)}) collective-permute-start(bf16[2,4,64,512]{3,2,1,0:T(8,128)(2,1)S(1)} %get-tuple-element.49), channel_id=1, source_target_pairs={{0,128},{1,129},{2,130},{3,131},{4,132},{5,133},{6,134},{7,135},{8... | collective-permute-start | bytes 1572872 | tf_op jit(solution)/shard_map/ppermute | solution.py:362
  4.6 11.4 %collective-permute-done = bf16[2,4,64,512]{3,2,1,0:T(8,128)(2,1)S(1)} collective-permute-done((bf16[2,4,64,512]{3,2,1,0:T(8,128)(2,1)S(1)}, bf16[2,4,64,512]{3,2,1,0:T(8,128)(2,1)S(1)}, u32[]{:S(2)}, u32[]{:S(2)}) %collective-permute-start) | collective-permute-done | bytes 524320 | tf_op jit(solution)/shard_map/ppermute | solution.py:362
  15.9 0.8 fusion.3
  16.7 0.8 copy-done.2
  17.5 0.8 fusion.own
  18.3 2.1 %collective-permute-start.2 = (bf16[2048,512]{1,0:T(8,128)(2,1)S(1)}, bf16[2048,512]{1,0:T(8,128)(2,1)}, u32[]{:S(2)}, u32[]{:S(2)}) collective-permute-start(bf16[2048,512]{1,0:T(8,128)(2,1)S(1)} %fusion.own), channel_id=1, source_target_pairs={{0,3},{8,11},{12,15},{16,19},{24,27},{28,31},{32,35},{40,43},{44,4... | collective-permute-start | bytes 6291464 | tf_op jit(solution)/shard_map/ppermute | solution.py:371
  20.4 2.0 %collective-permute-start.1 = (bf16[2048,512]{1,0:T(8,128)(2,1)S(1)}, bf16[2048,512]{1,0:T(8,128)(2,1)}, u32[]{:S(2)}, u32[]{:S(2)}) collective-permute-start(bf16[2048,512]{1,0:T(8,128)(2,1)S(1)} %fusion.own), channel_id=1, source_target_pairs={{0,1},{1,2},{2,3},{8,9},{9,10},{10,11},{12,13},{13,14},{14,15},{16... | collective-permute-start | bytes 6291464 | tf_op jit(solution)/shard_map/ppermute | solution.py:370
  22.4 1.6 collective-permute-start.3
  24.1 0.7 slice_add_fusion
  24.8 1.3 collective-permute-start.4
  26.1 48.0 %collective-permute-done.4.refs_13_ = bf16[8,128]{1,0:T(8,128)(2,1)S(1)} collective-permute-done((bf16[8,128]{1,0:T(8,128)(2,1)S(1)}, bf16[8,128]{1,0:T(8,128)(2,1)S(1)}, u32[]{:S(2)}, u32[]{:S(2)}) %collective-permute-start.4) | collective-permute-done | bytes 2080 | tf_op jit(solution)/shard_map/ppermute | solution.py:374
  74.1 1.8 select_select_fusion
  75.9 1.3 collective-permute-start.6
  77.2 1.3 collective-permute-start.5
  78.5 1.3 collective-permute-start.7
  79.8 11.6 %collective-permute-done.6.refs_3_ = bf16[1024,512]{1,0:T(8,128)(2,1)S(1)} collective-permute-done((bf16[1024,512]{1,0:T(8,128)(2,1)S(1)}, bf16[1024,512]{1,0:T(8,128)(2,1)S(1)}, u32[]{:S(2)}, u32[]{:S(2)}) %collective-permute-start.6) | collective-permute-done | bytes 1048608 | tf_op jit(solution)/shard_map/ppermute | solution.py:385
  91.4 1.3 collective-permute-start.9
  92.7 10.0 %collective-permute-done.5.refs_2_ = bf16[1024,512]{1,0:T(8,128)(2,1)} collective-permute-done((bf16[1024,512]{1,0:T(8,128)(2,1)S(1)}, bf16[1024,512]{1,0:T(8,128)(2,1)}, u32[]{:S(2)}, u32[]{:S(2)}) %collective-permute-start.5) | collective-permute-done | bytes 1048608 | tf_op jit(solution)/shard_map/ppermute | solution.py:381
  102.8 1.3 collective-permute-start.8
  104.1 0.6 stack.37.where_ref
  104.7 9.3 %collective-permute-done.9.refs_6_ = bf16[1024,512]{1,0:T(8,128)(2,1)} collective-permute-done((bf16[1024,512]{1,0:T(8,128)(2,1)S(1)}, bf16[1024,512]{1,0:T(8,128)(2,1)}, u32[]{:S(2)}, u32[]{:S(2)}) %collective-permute-start.9) | collective-permute-done | bytes 1048608 | tf_op jit(solution)/shard_map/ppermute | solution.py:390
  114.0 11.2 %collective-permute-done.8.refs_5_ = bf16[1024,512]{1,0:T(8,128)(2,1)} collective-permute-done((bf16[1024,512]{1,0:T(8,128)(2,1)}, bf16[1024,512]{1,0:T(8,128)(2,1)}, u32[]{:S(2)}, u32[]{:S(2)}) %collective-permute-start.8) | collective-permute-done | bytes 1048608 | tf_op jit(solution)/shard_map/ppermute | solution.py:389
  125.2 2.0 %factor_rows.1 = (bf16[64,2048]{1,0:T(8,128)(2,1)}, bf16[64,2048]{1,0:T(8,128)(2,1)}, bf16[64,2048]{1,0:T(8,128)(2,1)}, bf16[64,2048]{1,0:T(8,128)(2,1)}, bf16[6...) custom-call(s32[5]{0:T(128)} %stack.37.where_ref, ...), custom_call_target="tpu_custom_call" | custom-call | tf_op jit(solution)/shard_map/factor_rows/pallas_call | solution.py:190
  127.3 0.7 collective-permute-start.10
  128.0 0.7 collective-permute-start.11
  128.7 0.7 collective-permute-start.12
  129.4 0.7 collective-permute-start.13
  130.0 0.7 collective-permute-start.14
  130.7 0.7 collective-permute-start.15
  131.4 0.7 collective-permute-start.16
  132.2 1.1 add_select_fusion.1
  133.2 0.7 collective-permute-start.19
  133.9 0.7 collective-permute-start.18
  134.6 0.7 collective-permute-start.17
  135.4 1.3 collective-permute-start.20
  136.7 2.1 %collective-permute-done.20 = bf16[64,2048]{1,0:T(8,128)(2,1)S(1)} collective-permute-done((bf16[64,2048]{1,0:T(8,128)(2,1)S(1)}, bf16[64,2048]{1,0:T(8,128)(2,1)S(1)}, u32[]{:S(2)}, u32[]{:S(2)}) %collective-permute-start.20) | collective-permute-done | bytes 262176 | tf_op jit(solution)/shard_map/ppermute | solution.py:335
  138.8 5.6 %collective-permute-start.23 = (bf16[64,2048]{1,0:T(8,128)(2,1)S(1)}, bf16[64,2048]{1,0:T(8,128)(2,1)S(1)}, u32[]{:S(2)}, u32[]{:S(2)}) collective-permute-start(bf16[64,2048]{1,0:T(8,128)(2,1)S(1)} %broadcast_select_fusion.refs_7_), channel_id=1, source_target_pairs={{0,48},{1,49},{2,50},{3,51},{4,84},{5,85},{6,86},{7,87},{8,56},{9,... | collective-permute-start | bytes 786440 | tf_op jit(solution)/shard_map/ppermute | solution.py:346
  144.4 0.3 collective-permute-start.22
  144.7 0.5 collective-permute-start.21
  145.2 4.6 %collective-permute-start.24 = (bf16[32,2048]{1,0:T(8,128)(2,1)S(1)}, bf16[32,2048]{1,0:T(8,128)(2,1)S(1)}, u32[]{:S(2)}, u32[]{:S(2)}) collective-permute-start(bf16[32,2048]{1,0:T(8,128)(2,1)S(1)} %constant_dynamic-slice_fusion), channel_id=1, source_target_pairs={{0,64},{1,65},{2,66},{3,67},{4,68},{5,69},{6,70},{7,71},{8,72},{9,... | collective-permute-start | bytes 393224 | tf_op jit(solution)/shard_map/ppermute | solution.py:342
  149.8 9.9 %collective-permute-done.24.refs_11_ = bf16[32,2048]{1,0:T(8,128)(2,1)S(1)} collective-permute-done((bf16[32,2048]{1,0:T(8,128)(2,1)S(1)}, bf16[32,2048]{1,0:T(8,128)(2,1)S(1)}, u32[]{:S(2)}, u32[]{:S(2)}) %collective-permute-start.24) | collective-permute-done | bytes 131104 | tf_op jit(solution)/shard_map/ppermute | solution.py:342
  159.6 2.2 %collective-permute-done.22.refs_9_ = bf16[64,2048]{1,0:T(8,128)(2,1)S(1)} collective-permute-done((bf16[64,2048]{1,0:T(8,128)(2,1)S(1)}, bf16[64,2048]{1,0:T(8,128)(2,1)S(1)}, u32[]{:S(2)}, u32[]{:S(2)}) %collective-permute-start.22) | collective-permute-done | bytes 262176 | tf_op jit(solution)/shard_map/ppermute | solution.py:346
  161.8 5.6 %collective-permute-done.21.refs_8_ = bf16[64,2048]{1,0:T(8,128)(2,1)S(1)} collective-permute-done((bf16[64,2048]{1,0:T(8,128)(2,1)S(1)}, bf16[64,2048]{1,0:T(8,128)(2,1)S(1)}, u32[]{:S(2)}, u32[]{:S(2)}) %collective-permute-start.21) | collective-permute-done | bytes 262176 | tf_op jit(solution)/shard_map/ppermute | solution.py:346
  167.5 2.6 %collective-permute-start.25 = (bf16[224,2048]{1,0:T(8,128)(2,1)S(1)}, bf16[224,2048]{1,0:T(8,128)(2,1)S(1)}, u32[]{:S(2)}, u32[]{:S(2)}) collective-permute-start(bf16[224,2048]{1,0:T(8,128)(2,1)S(1)} %pad_maximum_fusion), channel_id=1, source_target_pairs={{0,4},{1,5},{2,6},{3,7},{4,0},{5,1},{6,2},{7,3},{8,12},{9,13},{10,... | collective-permute-start | bytes 2752520 | tf_op jit(solution)/shard_map/ppermute | solution.py:348
  170.1 2.1 %collective-permute-done.25.refs_12_ = bf16[224,2048]{1,0:T(8,128)(2,1)S(1)} collective-permute-done((bf16[224,2048]{1,0:T(8,128)(2,1)S(1)}, bf16[224,2048]{1,0:T(8,128)(2,1)S(1)}, u32[]{:S(2)}, u32[]{:S(2)}) %collective-permute-start.25) | collective-permute-done | bytes 917536 | tf_op jit(solution)/shard_map/ppermute | solution.py:348
  172.2 0.9 copy-done.7
  173.1 11.4 %apply_rows.1 = bf16[512,2048]{1,0:T(8,128)(2,1)} custom-call(s32[5]{0:T(128)} %stack.37.where_ref, bf16[2048,512]{1,0:T(8,128)(2,1)} %copy-done, bf16[2048,512]{1,0:T(8,128)(2,1)} %collective-permute-done.1.refs_0_, bf16[2048,512]{1,0:T(8,128)(2,1)} %collective-permute-done.2.refs_1_, bf16[1024,512]{1,0:T(8,128)(2,1)} %collective-permute-done.5.refs_2_, ...), custom_call_target="tpu_custom_call" | custom-call | tf_op jit(solution)/shard_map/apply_rows/pallas_call | solution.py:269
  (42 shorter events, 0.6 us)
Async XLA Ops:
  0.0 1.4 copy-start.8
  1.6 14.4 %collective-permute-start = (bf16[2,4,64,512]{3,2,1,0:T(8,128)(2,1)S(1)}, bf16[2,4,64,512]{3,2,1,0:T(8,128)(2,1)S(1)}, u32[]{:S(2)}, u32[]{:S(2)}) collective-permute-start(bf16[2,4,64,512]{3,2,1,0:T(8,128)(2,1)S(1)} %get-tuple-element.49), channel_id=1, source_target_pairs={{0,128},{1,129},{2,130},{3,131},{4,132},{5,133},{6,134},{7,135},{8... | collective-permute-start | bytes 1572872 | tf_op jit(solution)/shard_map/ppermute | solution.py:362
  15.9 1.6 copy-start.2
  18.3 60.2 %copy-start = (bf16[2048,512]{1,0:T(8,128)(2,1)}, bf16[2048,512]{1,0:T(8,128)(2,1)S(1)}, u32[]{:S(2)}) copy-start(bf16[2048,512]{1,0:T(8,128)(2,1)S(1)} %fusion.own) | copy-start | bytes 6291460
  18.3 5.8 %collective-permute-start.2 = (bf16[2048,512]{1,0:T(8,128)(2,1)S(1)}, bf16[2048,512]{1,0:T(8,128)(2,1)}, u32[]{:S(2)}, u32[]{:S(2)}) collective-permute-start(bf16[2048,512]{1,0:T(8,128)(2,1)S(1)} %fusion.own), channel_id=1, source_target_pairs={{0,3},{8,11},{12,15},{16,19},{24,27},{28,31},{32,35},{40,43},{44,4... | collective-permute-start | bytes 6291464 | tf_op jit(solution)/shard_map/ppermute | solution.py:371
  20.4 3.7 %collective-permute-start.1 = (bf16[2048,512]{1,0:T(8,128)(2,1)S(1)}, bf16[2048,512]{1,0:T(8,128)(2,1)}, u32[]{:S(2)}, u32[]{:S(2)}) collective-permute-start(bf16[2048,512]{1,0:T(8,128)(2,1)S(1)} %fusion.own), channel_id=1, source_target_pairs={{0,1},{1,2},{2,3},{8,9},{9,10},{10,11},{12,13},{13,14},{14,15},{16... | collective-permute-start | bytes 6291464 | tf_op jit(solution)/shard_map/ppermute | solution.py:370
  22.4 1.6 collective-permute-start.3
  24.8 49.3 %collective-permute-start.4 = (bf16[8,128]{1,0:T(8,128)(2,1)S(1)}, bf16[8,128]{1,0:T(8,128)(2,1)S(1)}, u32[]{:S(2)}, u32[]{:S(2)}) collective-permute-start(bf16[8,128]{1,0:T(8,128)(2,1)S(1)} %slice_add_fusion), channel_id=1, source_target_pairs={{8,4},{9,5},{10,6},{11,7},{24,20},{25,21},{26,22},{27,23},{40,36},... | collective-permute-start | bytes 6152 | tf_op jit(solution)/shard_map/ppermute | solution.py:374
  74.1 1.8 copy-start.10
  75.9 15.5 %collective-permute-start.6 = (bf16[1024,512]{1,0:T(8,128)(2,1)S(1)}, bf16[1024,512]{1,0:T(8,128)(2,1)S(1)}, u32[]{:S(2)}, u32[]{:S(2)}) collective-permute-start(bf16[1024,512]{1,0:T(8,128)(2,1)S(1)} %get-tuple-element.47), channel_id=1, source_target_pairs={{0,3},{3,2},{8,11},{11,10},{12,15},{15,14},{16,19},{19,18},{24,27}... | collective-permute-start | bytes 3145736 | tf_op jit(solution)/shard_map/ppermute | solution.py:385
  77.2 25.6 %collective-permute-start.5 = (bf16[1024,512]{1,0:T(8,128)(2,1)S(1)}, bf16[1024,512]{1,0:T(8,128)(2,1)}, u32[]{:S(2)}, u32[]{:S(2)}) collective-permute-start(bf16[1024,512]{1,0:T(8,128)(2,1)S(1)} %get-tuple-element.48), channel_id=1, source_target_pairs={{1,2},{2,3},{9,10},{10,11},{13,14},{14,15},{17,18},{18,19},{25,26}... | collective-permute-start | bytes 3145736 | tf_op jit(solution)/shard_map/ppermute | solution.py:381
  78.5 46.7 %collective-permute-start.7 = (bf16[2048,512]{1,0:T(8,128)(2,1)S(1)}, bf16[2048,512]{1,0:T(8,128)(2,1)}, u32[]{:S(2)}, u32[]{:S(2)}) collective-permute-start(bf16[2048,512]{1,0:T(8,128)(2,1)S(1)} %fusion.own), channel_id=1, source_target_pairs={{4,7},{20,23},{36,39},{52,55},{68,71},{84,87},{100,103},{116,119}} | collective-permute-start | bytes 6291464 | tf_op jit(solution)/shard_map/ppermute | solution.py:388
  91.4 33.8 %copy-start.1 = (bf16[1024,512]{1,0:T(8,128)(2,1)}, bf16[1024,512]{1,0:T(8,128)(2,1)S(1)}, u32[]{:S(2)}) copy-start(bf16[1024,512]{1,0:T(8,128)(2,1)S(1)} %collective-permute-done.6.refs_3_) | copy-start | bytes 3145732
  91.4 22.6 %collective-permute-start.9 = (bf16[1024,512]{1,0:T(8,128)(2,1)S(1)}, bf16[1024,512]{1,0:T(8,128)(2,1)}, u32[]{:S(2)}, u32[]{:S(2)}) collective-permute-start(bf16[1024,512]{1,0:T(8,128)(2,1)S(1)} %collective-permute-done.6.refs_3_), channel_id=1, source_target_pairs={{5,6},{6,7},{21,22},{22,23},{37,38},{38,39},{53,54},{54,55},{69,70... | collective-permute-start | bytes 3145736 | tf_op jit(solution)/shard_map/ppermute | solution.py:390
  102.8 22.5 %collective-permute-start.8 = (bf16[1024,512]{1,0:T(8,128)(2,1)}, bf16[1024,512]{1,0:T(8,128)(2,1)}, u32[]{:S(2)}, u32[]{:S(2)}) collective-permute-start(bf16[1024,512]{1,0:T(8,128)(2,1)} %collective-permute-done.5.refs_2_), channel_id=1, source_target_pairs={{5,6},{6,7},{21,22},{22,23},{37,38},{38,39},{53,54},{54,55},{69,70... | collective-permute-start | bytes 3145736 | tf_op jit(solution)/shard_map/ppermute | solution.py:389
  127.3 3.4 %collective-permute-start.10 = (bf16[64,2048]{1,0:T(8,128)(2,1)}, bf16[64,2048]{1,0:T(8,128)(2,1)S(1)}, u32[]{:S(2)}, u32[]{:S(2)}) collective-permute-start(bf16[64,2048]{1,0:T(8,128)(2,1)} %get-tuple-element.39), channel_id=1, source_target_pairs={{0,16},{1,17},{2,18},{3,19}} | collective-permute-start | bytes 786440 | tf_op jit(solution)/shard_map/ppermute | solution.py:324
  128.0 3.4 %collective-permute-start.11 = (bf16[64,2048]{1,0:T(8,128)(2,1)}, bf16[64,2048]{1,0:T(8,128)(2,1)S(1)}, u32[]{:S(2)}, u32[]{:S(2)}) collective-permute-start(bf16[64,2048]{1,0:T(8,128)(2,1)} %get-tuple-element.40), channel_id=1, source_target_pairs={{0,32},{1,33},{2,34},{3,35}} | collective-permute-start | bytes 786440 | tf_op jit(solution)/shard_map/ppermute | solution.py:324
  128.7 3.5 %collective-permute-start.12 = (bf16[64,2048]{1,0:T(8,128)(2,1)}, bf16[64,2048]{1,0:T(8,128)(2,1)S(1)}, u32[]{:S(2)}, u32[]{:S(2)}) collective-permute-start(bf16[64,2048]{1,0:T(8,128)(2,1)} %get-tuple-element.41), channel_id=1, source_target_pairs={{0,48},{1,49},{2,50},{3,51}} | collective-permute-start | bytes 786440 | tf_op jit(solution)/shard_map/ppermute | solution.py:324
  129.4 2.8 %collective-permute-start.13 = (bf16[64,2048]{1,0:T(8,128)(2,1)}, bf16[64,2048]{1,0:T(8,128)(2,1)S(1)}, u32[]{:S(2)}, u32[]{:S(2)}) collective-permute-start(bf16[64,2048]{1,0:T(8,128)(2,1)} %get-tuple-element.42), channel_id=1, source_target_pairs={{0,64},{1,65},{2,66},{3,67}} | collective-permute-start | bytes 786440 | tf_op jit(solution)/shard_map/ppermute | solution.py:324
  130.0 2.1 %collective-permute-start.14 = (bf16[64,2048]{1,0:T(8,128)(2,1)}, bf16[64,2048]{1,0:T(8,128)(2,1)S(1)}, u32[]{:S(2)}, u32[]{:S(2)}) collective-permute-start(bf16[64,2048]{1,0:T(8,128)(2,1)} %get-tuple-element.43), channel_id=1, source_target_pairs={{0,80},{1,81},{2,82},{3,83}} | collective-permute-start | bytes 786440 | tf_op jit(solution)/shard_map/ppermute | solution.py:324
  130.7 1.4 collective-permute-start.15
  131.4 0.7 collective-permute-start.16
  133.2 2.1 %collective-permute-start.19 = (bf16[64,2048]{1,0:T(8,128)(2,1)S(1)}, bf16[64,2048]{1,0:T(8,128)(2,1)S(1)}, u32[]{:S(2)}, u32[]{:S(2)}) collective-permute-start(bf16[64,2048]{1,0:T(8,128)(2,1)S(1)} %add_select_fusion.1), channel_id=1, source_target_pairs={{0,128},{1,129},{2,130},{3,131},{16,144},{17,145},{18,146},{19,147... | collective-permute-start | bytes 786440 | tf_op jit(solution)/shard_map/ppermute | solution.py:332
  133.9 1.4 collective-permute-start.18
  134.6 0.7 collective-permute-start.17
  135.4 3.4 %collective-permute-start.20 = (bf16[64,2048]{1,0:T(8,128)(2,1)S(1)}, bf16[64,2048]{1,0:T(8,128)(2,1)S(1)}, u32[]{:S(2)}, u32[]{:S(2)}) collective-permute-start(bf16[64,2048]{1,0:T(8,128)(2,1)S(1)} %add_select_fusion), channel_id=1, source_target_pairs={{0,4},{1,5},{2,6},{3,7},{8,12},{9,13},{10,14},{11,15},{16,20},{17,... | collective-permute-start | bytes 786440 | tf_op jit(solution)/shard_map/ppermute | solution.py:335
  138.8 33.4 %copy-start.3 = (bf16[64,2048]{1,0:T(8,128)(2,1)}, bf16[64,2048]{1,0:T(8,128)(2,1)S(1)}, u32[]{:S(2)}) copy-start(bf16[64,2048]{1,0:T(8,128)(2,1)S(1)} %broadcast_select_fusion.refs_7_) | copy-start | bytes 786436
  138.8 20.8 %collective-permute-start.23 = (bf16[64,2048]{1,0:T(8,128)(2,1)S(1)}, bf16[64,2048]{1,0:T(8,128)(2,1)S(1)}, u32[]{:S(2)}, u32[]{:S(2)}) collective-permute-start(bf16[64,2048]{1,0:T(8,128)(2,1)S(1)} %broadcast_select_fusion.refs_7_), channel_id=1, source_target_pairs={{0,48},{1,49},{2,50},{3,51},{4,84},{5,85},{6,86},{7,87},{8,56},{9,... | collective-permute-start | bytes 786440 | tf_op jit(solution)/shard_map/ppermute | solution.py:346
  144.4 17.4 %collective-permute-start.22 = (bf16[64,2048]{1,0:T(8,128)(2,1)S(1)}, bf16[64,2048]{1,0:T(8,128)(2,1)S(1)}, u32[]{:S(2)}, u32[]{:S(2)}) collective-permute-start(bf16[64,2048]{1,0:T(8,128)(2,1)S(1)} %broadcast_select_fusion.refs_7_), channel_id=1, source_target_pairs={{0,32},{1,33},{2,34},{3,35},{4,100},{5,101},{6,102},{7,103},{8,40}... | collective-permute-start | bytes 786440 | tf_op jit(solution)/shard_map/ppermute | solution.py:346
  144.7 22.7 %collective-permute-start.21 = (bf16[64,2048]{1,0:T(8,128)(2,1)S(1)}, bf16[64,2048]{1,0:T(8,128)(2,1)S(1)}, u32[]{:S(2)}, u32[]{:S(2)}) collective-permute-start(bf16[64,2048]{1,0:T(8,128)(2,1)S(1)} %broadcast_select_fusion.refs_7_), channel_id=1, source_target_pairs={{0,16},{1,17},{2,18},{3,19},{4,116},{5,117},{6,118},{7,119},{8,24}... | collective-permute-start | bytes 786440 | tf_op jit(solution)/shard_map/ppermute | solution.py:346
  145.2 14.4 %collective-permute-start.24 = (bf16[32,2048]{1,0:T(8,128)(2,1)S(1)}, bf16[32,2048]{1,0:T(8,128)(2,1)S(1)}, u32[]{:S(2)}, u32[]{:S(2)}) collective-permute-start(bf16[32,2048]{1,0:T(8,128)(2,1)S(1)} %constant_dynamic-slice_fusion), channel_id=1, source_target_pairs={{0,64},{1,65},{2,66},{3,67},{4,68},{5,69},{6,70},{7,71},{8,72},{9,... | collective-permute-start | bytes 393224 | tf_op jit(solution)/shard_map/ppermute | solution.py:342
  159.6 12.6 %copy-start.9 = (bf16[32,2048]{1,0:T(8,128)(2,1)}, bf16[32,2048]{1,0:T(8,128)(2,1)S(1)}, u32[]{:S(2)}) copy-start(bf16[32,2048]{1,0:T(8,128)(2,1)S(1)} %collective-permute-done.24.refs_11_) | copy-start | bytes 393220
  159.6 12.6 %copy-start.4 = (bf16[64,2048]{1,0:T(8,128)(2,1)}, bf16[64,2048]{1,0:T(8,128)(2,1)S(1)}, u32[]{:S(2)}) copy-start(bf16[64,2048]{1,0:T(8,128)(2,1)S(1)} %collective-permute-done.23.refs_10_) | copy-start | bytes 786436
  161.8 10.4 %copy-start.5 = (bf16[64,2048]{1,0:T(8,128)(2,1)}, bf16[64,2048]{1,0:T(8,128)(2,1)S(1)}, u32[]{:S(2)}) copy-start(bf16[64,2048]{1,0:T(8,128)(2,1)S(1)} %collective-permute-done.22.refs_9_) | copy-start | bytes 786436
  167.4 4.8 %copy-start.6 = (bf16[64,2048]{1,0:T(8,128)(2,1)}, bf16[64,2048]{1,0:T(8,128)(2,1)S(1)}, u32[]{:S(2)}) copy-start(bf16[64,2048]{1,0:T(8,128)(2,1)S(1)} %collective-permute-done.21.refs_8_) | copy-start | bytes 786436
  167.5 4.7 %collective-permute-start.25 = (bf16[224,2048]{1,0:T(8,128)(2,1)S(1)}, bf16[224,2048]{1,0:T(8,128)(2,1)S(1)}, u32[]{:S(2)}, u32[]{:S(2)}) collective-permute-start(bf16[224,2048]{1,0:T(8,128)(2,1)S(1)} %pad_maximum_fusion), channel_id=1, source_target_pairs={{0,4},{1,5},{2,6},{3,7},{4,0},{5,1},{6,2},{7,3},{8,12},{9,13},{10,... | collective-permute-start | bytes 2752520 | tf_op jit(solution)/shard_map/ppermute | solution.py:348
  172.2 0.9 copy-start.7

commit v10 on v9

--- a/solution.py
+++ b/solution.py
@@ -208,7 +208,8 @@
     )(where, own, *parts)
 
 
-CHUNKS = 6
+CHUNKS = 10
+OFFSETS = (4, 3, 5, 6, 2, 7, 1)
 
 
 def apply_kernel(where_ref, own, *refs):
@@ -216,53 +217,71 @@
     chunks = refs[7 : 7 + CHUNKS]
     out, p_ref, r_ref, psems, rsems = refs[8 + CHUNKS :]
     second, col, z, core = where_ref[1], where_ref[2], where_ref[3], where_ref[4]
-    sign = 1 - 2 * core
-    copies = []
-
-    def place(part, at, size):
-        rows = pl.ds(pl.multiple_of(at, size), size)
-        copies.append(pltpu.make_async_copy(part, r_ref.at[rows], rsems.at[len(copies)]))
-
-    swapped = chunks[5]
-    place(chunks[0], z * 64, 64)
-    for by in range(1, 4):
-        place(chunks[by], lax.rem(z - sign * by + 8, 8) * 64, 64)
-        place(swapped.at[pl.ds(by * 64 - 64, 64)], lax.rem(z + sign * by + 8, 8) * 64, 64)
-    place(chunks[4], lax.rem(z + 4, 8) * 64 + core * 32, 32)
-    place(swapped.at[pl.ds(192, 32)], lax.rem(z + 4, 8) * 64 + (1 - core) * 32, 32)
-    copies.append(pltpu.make_async_copy(own, p_ref.at[col], psems.at[5]))
-    for copy in copies:
-        copy.start()
-
-    @pl.when(second == 0)
+    parts, early, late = chunks[:8], chunks[8], chunks[9]
+
+    def piece(slot, part):
+        by = (OFFSETS + (0,))[slot]
+        rows = pl.ds(pl.multiple_of(lax.rem(z - by + 8, 8) * 64, 64), 64)
+        return pltpu.make_async_copy(part, r_ref.at[rows], rsems.at[slot])
+
+    @pl.when(core == 0)
     def _():
-        fetch_rows(col, (near, wrap, upper, lower), p_ref, psems)
-
-    for last in range(1, BLOCKS):
-        sources = [(upper, last - 1, 0, HALF), (lower, last - 1, 1, HALF)]
-        if last >= 2:
-            sources += [(late_upper, last - 2, 0, HALF), (late_lower, last - 2, 1, HALF)]
-        if last == 3:
-            sources += [(late_wrap, 0, 0, PW)]
-
-        @pl.when(jnp.logical_and(second == 1, col == last))
-        def _():
-            run_copies(sources, p_ref, psems)
-
-    for copy in copies:
-        copy.wait()
-
+        for slot in range(8):
+            piece(slot, parts[slot]).start()
+
+    @pl.when(core == 1)
+    def _():
+        for slot in range(8):
+            source = early if slot >= 4 else late
+            piece(slot, source.at[pl.ds(slot % 4 * 64, 64)]).start()
+
+    def rows_of(at):
+        return pl.ds(at * HALF, HALF)
+
+    def load(at, column, part):
+        source = part[at] if isinstance(part, tuple) else part.at[rows_of(at)]
+        return pltpu.make_async_copy(source, p_ref.at[column, rows_of(at)], psems.at[at, column])
+
+    both, late_both = (upper, lower), (late_upper, late_lower)
+    for flag in range(2):
+        for last in range(BLOCKS):
+            sources = {last: own}
+            if last >= 1:
+                sources[last - 1] = both if flag else near
+            if last >= 2:
+                sources[last - 2] = late_both if flag else both
+            if last == 3:
+                sources[0] = late_wrap if flag else wrap
+
+            @pl.when(jnp.logical_and(second == flag, col == last))
+            def _():
+                for at in range(2):
+                    for column, part in sources.items():
+                        load(at, column, part).start()
+
+    for slot in range(8):
+        piece(slot, parts[slot]).wait()
     for last in range(BLOCKS):
 
         @pl.when(col == last)
         def _():
-            @pl.loop(0, PW // TILE)
-            def _(tile):
-                at = pl.ds(pl.multiple_of(tile * TILE, TILE), TILE)
-                acc = mxu(r_ref[:, :TILE], p_ref[0, at, :], NT)
-                for k in range(1, last + 1):
-                    acc = acc + mxu(r_ref[:, k * TILE : (k + 1) * TILE], p_ref[k, at, :], NT)
-                out[:, at] = acc.astype(jnp.bfloat16)
+            @pl.loop(0, 2)
+            def _(at):
+                for column in range(last + 1):
+                    rows = pl.ds(pl.multiple_of(at * HALF, HALF), HALF)
+                    pltpu.make_async_copy(
+                        near.at[pl.ds(0, HALF)], p_ref.at[column, rows], psems.at[at, column]
+                    ).wait()
+
+                @pl.loop(0, HALF // TILE)
+                def _(tile):
+                    rows = pl.ds(pl.multiple_of(at * HALF + tile * TILE, TILE), TILE)
+                    acc = mxu(r_ref[:, :TILE], p_ref[0, rows, :], NT)
+                    for k in range(1, last + 1):
+                        acc = acc + mxu(
+                            r_ref[:, k * TILE : (k + 1) * TILE], p_ref[k, rows, :], NT
+                        )
+                    out[:, rows] = acc.astype(jnp.bfloat16)
 
 
 def apply_rows(where, own, gathered, chunks, token):
@@ -274,8 +293,8 @@
         scratch_shapes=[
             pltpu.VMEM((BLOCKS, PW, TILE), jnp.bfloat16),
             pltpu.VMEM((TILE, PW), jnp.bfloat16),
-            pltpu.SemaphoreType.DMA((6,)),
-            pltpu.SemaphoreType.DMA((9,)),
+            pltpu.SemaphoreType.DMA((2, BLOCKS)),
+            pltpu.SemaphoreType.DMA((8,)),
         ],
         compiler_params=pltpu.CompilerParams(vmem_limit_bytes=60 << 20),
         name="apply_rows",
@@ -314,7 +333,7 @@
     return (c, y, k) != (0, 0, 1)
 
 
-def spread_rows(chunks, z, y, core):
+def spread_rows(chunks, z, y):
     kept = chunks[0]
     total = None
     for k in range(1, 8):
@@ -332,21 +351,17 @@
         got = lax.ppermute(chunk, ALL, pairs)
         total = got if total is None else total + got
     chunk = jnp.where(y == 0, chunk, total)
-    got = lax.ppermute(
-        chunk, ALL, pairs_of(lambda c, zz, yy, kk, j: (c, zz, yy, 1, j) if kk == 0 else None)
-    )
-    chunk = jnp.where(core == 0, chunk, got)
-    swap = pairs_of(lambda c, zz, yy, kk, j: (c, zz, yy, 1 - kk, j))
-    across = pairs_of(lambda c, zz, yy, kk, j: (c, (zz + 4) % 8, yy, kk, j))
-    part = lax.dynamic_slice_in_dim(chunk, core * 32, 32, 0)
-    half = lax.ppermute(part, ALL, across)
     direct = {}
-    for by in (3, 2, 1):
-        pairs = pairs_of(lambda c, zz, yy, kk, j: (c, (zz + (1 - 2 * kk) * by) % 8, yy, kk, j))
+    for by in (6, 2, 5, 3, 4, 7, 1):
+        pairs = pairs_of(
+            lambda c, zz, yy, kk, j: (c, (zz + by) % 8, yy, kk, j) if kk == 0 else None
+        )
         direct[by] = lax.ppermute(chunk, ALL, pairs)
-    mine = [direct[by] for by in (1, 2, 3)] + [half]
-    theirs = lax.ppermute(jnp.concatenate(mine, axis=0), ALL, swap)
-    return [chunk] + mine + [theirs]
+    parts = [direct[by] for by in OFFSETS] + [chunk]
+    across = pairs_of(lambda c, zz, yy, kk, j: (c, zz, yy, 1, j) if kk == 0 else None)
+    early = lax.ppermute(jnp.concatenate(parts[4:], axis=0), ALL, across)
+    last = lax.ppermute(jnp.concatenate(parts[:4], axis=0), ALL, across)
+    return parts + [early, last]
 
 
 def shards(front, left_factors, right_factors):
@@ -393,7 +408,7 @@
         (where, near, wrap, upper, lower, late_wrap, late_upper, late_lower)
     )
     chunks = factor_rows(where, own, gathered[:4])
-    chunks = spread_rows(chunks, z, y, core)
+    chunks = spread_rows(chunks, z, y)
     return apply_rows(where, own, gathered, chunks, token)
 
 

time: 185 us -> 187 us (1.011)
  waiting for transfers between devices: 123 us -> 133 us
  starting transfers between devices: 37.9 us -> 30.5 us
    ppermute x3 -> x2, waiting for transfers between devices: 14.1 us -> 30.9 us  [the longest x1 17.7 us: spread_rows(): early = lax.ppermute(jnp.concatenate(parts[4:], axis=0), ALL, across)]
    ppermute x3 -> x7, waiting for transfers between devices: 7.78 us -> 0.02 us  [spread_rows(): direct[by] = lax.ppermute(chunk, ALL, pairs)]
    ppermute x3 -> x2, starting transfers between devices: 8.45 us -> 2.58 us  [the longest x1 1.29 us: spread_rows(): early = lax.ppermute(jnp.concatenate(parts[4:], axis=0), ALL, across)]
    ppermute x3 -> x7, starting transfers between devices: 6.33 us -> 4.74 us  [spread_rows(): direct[by] = lax.ppermute(chunk, ALL, pairs)]
  transfers between devices with their start and end apart: 26 -> 29, of which waited for: 11 -> 8; matrix products, arithmetic and copies ran while one was open for 0% -> 0% of each run, Pallas kernels for 0% -> 0%
where the time goes in v10:
time: 187 us; the launch traced here: 185 us
  waiting for transfers between devices  133 us (71%)
  starting transfers between devices  30.5 us (16%)
  Pallas kernels  12.7 us (7%)
  other arithmetic  4.6 us (2%)
  local copies, waits for them, and re-layouts  3.05 us (2%)
    ppermute x1, waiting for transfers between devices, shards(): lax.ppermute(near[:8, :128] + wrap[:8, :128], ALL, pairs_of(lambda c, zz,...  47.9 us
    ppermute x1, waiting for transfers between devices, spread_rows(): early = lax.ppermute(jnp.concatenate(parts[4:], axis=0), ALL, across)  17.7 us
    ppermute x1, waiting for transfers between devices, spread_rows(): last = lax.ppermute(jnp.concatenate(parts[:4], axis=0), ALL, across)  13.2 us
    ppermute x1, waiting for transfers between devices, shards(): lax.ppermute(jnp.where(second, held[HALF:], mixed), ALL, moves(is_other,...  11.6 us
    ppermute x1, waiting for transfers between devices, shards(): lax.ppermute(sent, ALL, pairs_of(lambda c, zz, yy, kk, j: (1 - c, zz, yy,...  11.4 us
    ppermute x1, waiting for transfers between devices, shards(): late_upper = lax.ppermute(upper, ALL, moves(is_second, (1, 2), (2, 3)))  11.2 us
    pallas_call x1, Pallas kernels, apply_rows(): pl.pallas_call(apply_kernel, out_shape=jax.ShapeDtypeStruct((TILE, PW), j...  10.7 us
    ppermute x1, waiting for transfers between devices, shards(): lax.ppermute(jnp.where(second, held[:HALF], near[:HALF]), ALL, moves(is_o...  10 us
  transfers between devices with their start and end apart: 29, of which 8 were waited for; matrix products, arithmetic and copies ran while one was open for 0% of the time, Pallas kernels for 0%

profile of v10, /device:TPU:7, one launch (start us, length us, event | category | flops | bytes accessed | tf_op | source)
XLA Modules:
  0.0 184.8 jit_solution(17903430002532873903)
XLA Ops:
  0.0 1.3 copy.8
  1.3 0.2 copy.10
  1.6 3.0 %collective-permute-start = (bf16[2,4,64,512]{3,2,1,0:T(8,128)(2,1)S(1)}, bf16[2,4,64,512]{3,2,1,0:T(8,128)(2,1)S(1)}, u32[]{:S(2)}, u32[]{:S(2)}) collective-permute-start(bf16[2,4,64,512]{3,2,1,0:T(8,128)(2,1)S(1)} %get-tuple-element.49), channel_id=1, source_target_pairs={{0,128},{1,129},{2,130},{3,131},{4,132},{5,133},{6,134},{7,135},{8... | collective-permute-start | bytes 1572872 | tf_op jit(solution)/shard_map/ppermute | solution.py:377
  4.6 11.4 %collective-permute-done = bf16[2,4,64,512]{3,2,1,0:T(8,128)(2,1)S(1)} collective-permute-done((bf16[2,4,64,512]{3,2,1,0:T(8,128)(2,1)S(1)}, bf16[2,4,64,512]{3,2,1,0:T(8,128)(2,1)S(1)}, u32[]{:S(2)}, u32[]{:S(2)}) %collective-permute-start) | collective-permute-done | bytes 524320 | tf_op jit(solution)/shard_map/ppermute | solution.py:377
  15.9 0.8 fusion.3
  16.7 0.8 copy-done.3
  17.5 0.8 fusion.own
  18.3 2.0 %collective-permute-start.2 = (bf16[2048,512]{1,0:T(8,128)(2,1)S(1)}, bf16[2048,512]{1,0:T(8,128)(2,1)}, u32[]{:S(2)}, u32[]{:S(2)}) collective-permute-start(bf16[2048,512]{1,0:T(8,128)(2,1)S(1)} %fusion.own), channel_id=1, source_target_pairs={{0,3},{8,11},{12,15},{16,19},{24,27},{28,31},{32,35},{40,43},{44,4... | collective-permute-start | bytes 6291464 | tf_op jit(solution)/shard_map/ppermute | solution.py:386
  20.4 2.0 %collective-permute-start.1 = (bf16[2048,512]{1,0:T(8,128)(2,1)S(1)}, bf16[2048,512]{1,0:T(8,128)(2,1)}, u32[]{:S(2)}, u32[]{:S(2)}) collective-permute-start(bf16[2048,512]{1,0:T(8,128)(2,1)S(1)} %fusion.own), channel_id=1, source_target_pairs={{0,1},{1,2},{2,3},{8,9},{9,10},{10,11},{12,13},{13,14},{14,15},{16... | collective-permute-start | bytes 6291464 | tf_op jit(solution)/shard_map/ppermute | solution.py:385
  22.4 1.6 collective-permute-start.3
  24.1 0.7 slice_add_fusion
  24.8 1.3 collective-permute-start.4
  26.1 47.9 %collective-permute-done.4.refs_17_ = bf16[8,128]{1,0:T(8,128)(2,1)S(1)} collective-permute-done((bf16[8,128]{1,0:T(8,128)(2,1)S(1)}, bf16[8,128]{1,0:T(8,128)(2,1)S(1)}, u32[]{:S(2)}, u32[]{:S(2)}) %collective-permute-start.4) | collective-permute-done | bytes 2080 | tf_op jit(solution)/shard_map/ppermute | solution.py:389
  74.1 1.8 select_select_fusion
  75.9 1.3 collective-permute-start.6
  77.2 1.3 collective-permute-start.5
  78.5 1.3 collective-permute-start.7
  79.8 11.6 %collective-permute-done.6.refs_3_ = bf16[1024,512]{1,0:T(8,128)(2,1)S(1)} collective-permute-done((bf16[1024,512]{1,0:T(8,128)(2,1)S(1)}, bf16[1024,512]{1,0:T(8,128)(2,1)S(1)}, u32[]{:S(2)}, u32[]{:S(2)}) %collective-permute-start.6) | collective-permute-done | bytes 1048608 | tf_op jit(solution)/shard_map/ppermute | solution.py:400
  91.4 1.3 collective-permute-start.9
  92.7 10.0 %collective-permute-done.5.refs_2_ = bf16[1024,512]{1,0:T(8,128)(2,1)} collective-permute-done((bf16[1024,512]{1,0:T(8,128)(2,1)S(1)}, bf16[1024,512]{1,0:T(8,128)(2,1)}, u32[]{:S(2)}, u32[]{:S(2)}) %collective-permute-start.5) | collective-permute-done | bytes 1048608 | tf_op jit(solution)/shard_map/ppermute | solution.py:396
  102.8 1.3 collective-permute-start.8
  104.1 0.7 stack.37.where_ref
  104.7 9.2 %collective-permute-done.9.refs_6_ = bf16[1024,512]{1,0:T(8,128)(2,1)} collective-permute-done((bf16[1024,512]{1,0:T(8,128)(2,1)S(1)}, bf16[1024,512]{1,0:T(8,128)(2,1)}, u32[]{:S(2)}, u32[]{:S(2)}) %collective-permute-start.9) | collective-permute-done | bytes 1048608 | tf_op jit(solution)/shard_map/ppermute | solution.py:405
  114.0 11.2 %collective-permute-done.8.refs_5_ = bf16[1024,512]{1,0:T(8,128)(2,1)} collective-permute-done((bf16[1024,512]{1,0:T(8,128)(2,1)}, bf16[1024,512]{1,0:T(8,128)(2,1)}, u32[]{:S(2)}, u32[]{:S(2)}) %collective-permute-start.8) | collective-permute-done | bytes 1048608 | tf_op jit(solution)/shard_map/ppermute | solution.py:404
  125.2 2.0 %factor_rows.1 = (bf16[64,2048]{1,0:T(8,128)(2,1)}, bf16[64,2048]{1,0:T(8,128)(2,1)}, bf16[64,2048]{1,0:T(8,128)(2,1)}, bf16[64,2048]{1,0:T(8,128)(2,1)}, bf16[6...) custom-call(s32[5]{0:T(128)} %stack.37.where_ref, ...), custom_call_target="tpu_custom_call" | custom-call | tf_op jit(solution)/shard_map/factor_rows/pallas_call | solution.py:190
  127.3 0.7 collective-permute-start.10
  128.0 0.7 collective-permute-start.11
  128.7 0.7 collective-permute-start.12
  129.3 0.7 collective-permute-start.13
  130.0 0.7 collective-permute-start.14
  130.7 0.7 collective-permute-start.15
  131.4 0.7 collective-permute-start.16
  132.2 1.1 add_select_fusion.1
  133.2 0.7 collective-permute-start.19
  133.9 0.7 collective-permute-start.18
  134.6 0.7 collective-permute-start.17
  135.4 0.7 collective-permute-start.26
  136.1 0.7 collective-permute-start.25
  136.7 0.7 collective-permute-start.24
  137.4 0.7 collective-permute-start.23
  138.1 0.7 collective-permute-start.22
  138.8 0.7 collective-permute-start.21
  139.5 0.7 collective-permute-start.20
  140.3 1.3 collective-permute-start.27
  141.8 1.3 collective-permute-start.28
  143.1 17.7 %collective-permute-done.27.refs_15_ = bf16[256,2048]{1,0:T(8,128)(2,1)S(1)} collective-permute-done((bf16[256,2048]{1,0:T(8,128)(2,1)S(1)}, bf16[256,2048]{1,0:T(8,128)(2,1)S(1)}, u32[]{:S(2)}, u32[]{:S(2)}) %collective-permute-start.27) | collective-permute-done | bytes 1048608 | tf_op jit(solution)/shard_map/ppermute | solution.py:362
  160.8 13.2 %collective-permute-done.28.refs_16_ = bf16[256,2048]{1,0:T(8,128)(2,1)} collective-permute-done((bf16[256,2048]{1,0:T(8,128)(2,1)S(1)}, bf16[256,2048]{1,0:T(8,128)(2,1)}, u32[]{:S(2)}, u32[]{:S(2)}) %collective-permute-start.28) | collective-permute-done | bytes 1048608 | tf_op jit(solution)/shard_map/ppermute | solution.py:363
  174.1 10.7 %apply_rows.1 = bf16[512,2048]{1,0:T(8,128)(2,1)} custom-call(s32[5]{0:T(128)} %stack.37.where_ref, bf16[2048,512]{1,0:T(8,128)(2,1)} %copy-done, bf16[2048,512]{1,0:T(8,128)(2,1)} %collective-permute-done.1.refs_0_, bf16[2048,512]{1,0:T(8,128)(2,1)} %collective-permute-done.2.refs_1_, bf16[1024,512]{1,0:T(8,128)(2,1)} %collective-permute-done.5.refs_2_, ...), custom_call_target="tpu_custom_call" | custom-call | tf_op jit(solution)/shard_map/apply_rows/pallas_call | solution.py:288
  (53 shorter events, 0.5 us)
Async XLA Ops:
  0.0 1.4 copy-start.12
  1.6 14.4 %collective-permute-start = (bf16[2,4,64,512]{3,2,1,0:T(8,128)(2,1)S(1)}, bf16[2,4,64,512]{3,2,1,0:T(8,128)(2,1)S(1)}, u32[]{:S(2)}, u32[]{:S(2)}) collective-permute-start(bf16[2,4,64,512]{3,2,1,0:T(8,128)(2,1)S(1)} %get-tuple-element.49), channel_id=1, source_target_pairs={{0,128},{1,129},{2,130},{3,131},{4,132},{5,133},{6,134},{7,135},{8... | collective-permute-start | bytes 1572872 | tf_op jit(solution)/shard_map/ppermute | solution.py:377
  15.9 1.6 copy-start.3
  18.3 60.1 %copy-start = (bf16[2048,512]{1,0:T(8,128)(2,1)}, bf16[2048,512]{1,0:T(8,128)(2,1)S(1)}, u32[]{:S(2)}) copy-start(bf16[2048,512]{1,0:T(8,128)(2,1)S(1)} %fusion.own) | copy-start | bytes 6291460
  18.3 5.8 %collective-permute-start.2 = (bf16[2048,512]{1,0:T(8,128)(2,1)S(1)}, bf16[2048,512]{1,0:T(8,128)(2,1)}, u32[]{:S(2)}, u32[]{:S(2)}) collective-permute-start(bf16[2048,512]{1,0:T(8,128)(2,1)S(1)} %fusion.own), channel_id=1, source_target_pairs={{0,3},{8,11},{12,15},{16,19},{24,27},{28,31},{32,35},{40,43},{44,4... | collective-permute-start | bytes 6291464 | tf_op jit(solution)/shard_map/ppermute | solution.py:386
  20.4 3.7 %collective-permute-start.1 = (bf16[2048,512]{1,0:T(8,128)(2,1)S(1)}, bf16[2048,512]{1,0:T(8,128)(2,1)}, u32[]{:S(2)}, u32[]{:S(2)}) collective-permute-start(bf16[2048,512]{1,0:T(8,128)(2,1)S(1)} %fusion.own), channel_id=1, source_target_pairs={{0,1},{1,2},{2,3},{8,9},{9,10},{10,11},{12,13},{13,14},{14,15},{16... | collective-permute-start | bytes 6291464 | tf_op jit(solution)/shard_map/ppermute | solution.py:385
  22.4 1.7 collective-permute-start.3
  24.8 49.3 %collective-permute-start.4 = (bf16[8,128]{1,0:T(8,128)(2,1)S(1)}, bf16[8,128]{1,0:T(8,128)(2,1)S(1)}, u32[]{:S(2)}, u32[]{:S(2)}) collective-permute-start(bf16[8,128]{1,0:T(8,128)(2,1)S(1)} %slice_add_fusion), channel_id=1, source_target_pairs={{8,4},{9,5},{10,6},{11,7},{24,20},{25,21},{26,22},{27,23},{40,36},... | collective-permute-start | bytes 6152 | tf_op jit(solution)/shard_map/ppermute | solution.py:389
  74.1 1.8 copy-start.13
  75.9 15.5 %collective-permute-start.6 = (bf16[1024,512]{1,0:T(8,128)(2,1)S(1)}, bf16[1024,512]{1,0:T(8,128)(2,1)S(1)}, u32[]{:S(2)}, u32[]{:S(2)}) collective-permute-start(bf16[1024,512]{1,0:T(8,128)(2,1)S(1)} %get-tuple-element.47), channel_id=1, source_target_pairs={{0,3},{3,2},{8,11},{11,10},{12,15},{15,14},{16,19},{19,18},{24,27}... | collective-permute-start | bytes 3145736 | tf_op jit(solution)/shard_map/ppermute | solution.py:400
  77.2 25.6 %collective-permute-start.5 = (bf16[1024,512]{1,0:T(8,128)(2,1)S(1)}, bf16[1024,512]{1,0:T(8,128)(2,1)}, u32[]{:S(2)}, u32[]{:S(2)}) collective-permute-start(bf16[1024,512]{1,0:T(8,128)(2,1)S(1)} %get-tuple-element.48), channel_id=1, source_target_pairs={{1,2},{2,3},{9,10},{10,11},{13,14},{14,15},{17,18},{18,19},{25,26}... | collective-permute-start | bytes 3145736 | tf_op jit(solution)/shard_map/ppermute | solution.py:396
  78.5 46.7 %collective-permute-start.7 = (bf16[2048,512]{1,0:T(8,128)(2,1)S(1)}, bf16[2048,512]{1,0:T(8,128)(2,1)}, u32[]{:S(2)}, u32[]{:S(2)}) collective-permute-start(bf16[2048,512]{1,0:T(8,128)(2,1)S(1)} %fusion.own), channel_id=1, source_target_pairs={{4,7},{20,23},{36,39},{52,55},{68,71},{84,87},{100,103},{116,119}} | collective-permute-start | bytes 6291464 | tf_op jit(solution)/shard_map/ppermute | solution.py:403
  91.4 33.8 %copy-start.1 = (bf16[1024,512]{1,0:T(8,128)(2,1)}, bf16[1024,512]{1,0:T(8,128)(2,1)S(1)}, u32[]{:S(2)}) copy-start(bf16[1024,512]{1,0:T(8,128)(2,1)S(1)} %collective-permute-done.6.refs_3_) | copy-start | bytes 3145732
  91.4 22.6 %collective-permute-start.9 = (bf16[1024,512]{1,0:T(8,128)(2,1)S(1)}, bf16[1024,512]{1,0:T(8,128)(2,1)}, u32[]{:S(2)}, u32[]{:S(2)}) collective-permute-start(bf16[1024,512]{1,0:T(8,128)(2,1)S(1)} %collective-permute-done.6.refs_3_), channel_id=1, source_target_pairs={{5,6},{6,7},{21,22},{22,23},{37,38},{38,39},{53,54},{54,55},{69,70... | collective-permute-start | bytes 3145736 | tf_op jit(solution)/shard_map/ppermute | solution.py:405
  102.8 22.5 %collective-permute-start.8 = (bf16[1024,512]{1,0:T(8,128)(2,1)}, bf16[1024,512]{1,0:T(8,128)(2,1)}, u32[]{:S(2)}, u32[]{:S(2)}) collective-permute-start(bf16[1024,512]{1,0:T(8,128)(2,1)} %collective-permute-done.5.refs_2_), channel_id=1, source_target_pairs={{5,6},{6,7},{21,22},{22,23},{37,38},{38,39},{53,54},{54,55},{69,70... | collective-permute-start | bytes 3145736 | tf_op jit(solution)/shard_map/ppermute | solution.py:404
  127.3 3.4 %collective-permute-start.10 = (bf16[64,2048]{1,0:T(8,128)(2,1)}, bf16[64,2048]{1,0:T(8,128)(2,1)S(1)}, u32[]{:S(2)}, u32[]{:S(2)}) collective-permute-start(bf16[64,2048]{1,0:T(8,128)(2,1)} %get-tuple-element.39), channel_id=1, source_target_pairs={{0,16},{1,17},{2,18},{3,19}} | collective-permute-start | bytes 786440 | tf_op jit(solution)/shard_map/ppermute | solution.py:343
  128.0 3.4 %collective-permute-start.11 = (bf16[64,2048]{1,0:T(8,128)(2,1)}, bf16[64,2048]{1,0:T(8,128)(2,1)S(1)}, u32[]{:S(2)}, u32[]{:S(2)}) collective-permute-start(bf16[64,2048]{1,0:T(8,128)(2,1)} %get-tuple-element.40), channel_id=1, source_target_pairs={{0,32},{1,33},{2,34},{3,35}} | collective-permute-start | bytes 786440 | tf_op jit(solution)/shard_map/ppermute | solution.py:343
  128.7 3.5 %collective-permute-start.12 = (bf16[64,2048]{1,0:T(8,128)(2,1)}, bf16[64,2048]{1,0:T(8,128)(2,1)S(1)}, u32[]{:S(2)}, u32[]{:S(2)}) collective-permute-start(bf16[64,2048]{1,0:T(8,128)(2,1)} %get-tuple-element.41), channel_id=1, source_target_pairs={{0,48},{1,49},{2,50},{3,51}} | collective-permute-start | bytes 786440 | tf_op jit(solution)/shard_map/ppermute | solution.py:343
  129.3 2.8 %collective-permute-start.13 = (bf16[64,2048]{1,0:T(8,128)(2,1)}, bf16[64,2048]{1,0:T(8,128)(2,1)S(1)}, u32[]{:S(2)}, u32[]{:S(2)}) collective-permute-start(bf16[64,2048]{1,0:T(8,128)(2,1)} %get-tuple-element.42), channel_id=1, source_target_pairs={{0,64},{1,65},{2,66},{3,67}} | collective-permute-start | bytes 786440 | tf_op jit(solution)/shard_map/ppermute | solution.py:343
  130.0 2.1 %collective-permute-start.14 = (bf16[64,2048]{1,0:T(8,128)(2,1)}, bf16[64,2048]{1,0:T(8,128)(2,1)S(1)}, u32[]{:S(2)}, u32[]{:S(2)}) collective-permute-start(bf16[64,2048]{1,0:T(8,128)(2,1)} %get-tuple-element.43), channel_id=1, source_target_pairs={{0,80},{1,81},{2,82},{3,83}} | collective-permute-start | bytes 786440 | tf_op jit(solution)/shard_map/ppermute | solution.py:343
  130.7 1.4 collective-permute-start.15
  131.4 0.7 collective-permute-start.16
  133.2 2.1 %collective-permute-start.19 = (bf16[64,2048]{1,0:T(8,128)(2,1)S(1)}, bf16[64,2048]{1,0:T(8,128)(2,1)S(1)}, u32[]{:S(2)}, u32[]{:S(2)}) collective-permute-start(bf16[64,2048]{1,0:T(8,128)(2,1)S(1)} %add_select_fusion.1), channel_id=1, source_target_pairs={{0,128},{1,129},{2,130},{3,131},{16,144},{17,145},{18,146},{19,147... | collective-permute-start | bytes 786440 | tf_op jit(solution)/shard_map/ppermute | solution.py:351
  133.9 1.4 collective-permute-start.18
  134.6 0.7 collective-permute-start.17
  135.4 6.4 %copy-start.2 = (bf16[64,2048]{1,0:T(8,128)(2,1)}, bf16[64,2048]{1,0:T(8,128)(2,1)S(1)}, u32[]{:S(2)}) copy-start(bf16[64,2048]{1,0:T(8,128)(2,1)S(1)} %add_select_fusion.refs_14_) | copy-start | bytes 786436
  135.4 3.4 %collective-permute-start.26 = (bf16[64,2048]{1,0:T(8,128)(2,1)S(1)}, bf16[64,2048]{1,0:T(8,128)(2,1)S(1)}, u32[]{:S(2)}, u32[]{:S(2)}) collective-permute-start(bf16[64,2048]{1,0:T(8,128)(2,1)S(1)} %add_select_fusion.refs_14_), channel_id=1, source_target_pairs={{0,16},{1,17},{2,18},{3,19},{8,24},{9,25},{10,26},{11,27},{16,32},... | collective-permute-start | bytes 786440 | tf_op jit(solution)/shard_map/ppermute | solution.py:359
  136.1 3.4 %collective-permute-start.25 = (bf16[64,2048]{1,0:T(8,128)(2,1)S(1)}, bf16[64,2048]{1,0:T(8,128)(2,1)S(1)}, u32[]{:S(2)}, u32[]{:S(2)}) collective-permute-start(bf16[64,2048]{1,0:T(8,128)(2,1)S(1)} %add_select_fusion.refs_14_), channel_id=1, source_target_pairs={{0,112},{1,113},{2,114},{3,115},{8,120},{9,121},{10,122},{11,123},... | collective-permute-start | bytes 786440 | tf_op jit(solution)/shard_map/ppermute | solution.py:359
  136.7 3.5 %collective-permute-start.24 = (bf16[64,2048]{1,0:T(8,128)(2,1)S(1)}, bf16[64,2048]{1,0:T(8,128)(2,1)S(1)}, u32[]{:S(2)}, u32[]{:S(2)}) collective-permute-start(bf16[64,2048]{1,0:T(8,128)(2,1)S(1)} %add_select_fusion.refs_14_), channel_id=1, source_target_pairs={{0,32},{1,33},{2,34},{3,35},{8,40},{9,41},{10,42},{11,43},{16,48},... | collective-permute-start | bytes 786440 | tf_op jit(solution)/shard_map/ppermute | solution.py:359
  137.4 4.2 %collective-permute-start.23 = (bf16[64,2048]{1,0:T(8,128)(2,1)S(1)}, bf16[64,2048]{1,0:T(8,128)(2,1)S(1)}, u32[]{:S(2)}, u32[]{:S(2)}) collective-permute-start(bf16[64,2048]{1,0:T(8,128)(2,1)S(1)} %add_select_fusion.refs_14_), channel_id=1, source_target_pairs={{0,96},{1,97},{2,98},{3,99},{8,104},{9,105},{10,106},{11,107},{16,... | collective-permute-start | bytes 786440 | tf_op jit(solution)/shard_map/ppermute | solution.py:359
  138.1 3.5 %collective-permute-start.22 = (bf16[64,2048]{1,0:T(8,128)(2,1)S(1)}, bf16[64,2048]{1,0:T(8,128)(2,1)S(1)}, u32[]{:S(2)}, u32[]{:S(2)}) collective-permute-start(bf16[64,2048]{1,0:T(8,128)(2,1)S(1)} %add_select_fusion.refs_14_), channel_id=1, source_target_pairs={{0,80},{1,81},{2,82},{3,83},{8,88},{9,89},{10,90},{11,91},{16,96},... | collective-permute-start | bytes 786440 | tf_op jit(solution)/shard_map/ppermute | solution.py:359
  138.8 3.0 %copy-start.4 = (bf16[64,2048]{1,0:T(8,128)(2,1)}, bf16[64,2048]{1,0:T(8,128)(2,1)S(1)}, u32[]{:S(2)}) copy-start(bf16[64,2048]{1,0:T(8,128)(2,1)S(1)} %collective-permute-done.26.refs_13_) | copy-start | bytes 786436
  138.8 2.8 %collective-permute-start.21 = (bf16[64,2048]{1,0:T(8,128)(2,1)S(1)}, bf16[64,2048]{1,0:T(8,128)(2,1)S(1)}, u32[]{:S(2)}, u32[]{:S(2)}) collective-permute-start(bf16[64,2048]{1,0:T(8,128)(2,1)S(1)} %add_select_fusion.refs_14_), channel_id=1, source_target_pairs={{0,48},{1,49},{2,50},{3,51},{8,56},{9,57},{10,58},{11,59},{16,64},... | collective-permute-start | bytes 786440 | tf_op jit(solution)/shard_map/ppermute | solution.py:359
  139.5 2.3 %copy-start.5 = (bf16[64,2048]{1,0:T(8,128)(2,1)}, bf16[64,2048]{1,0:T(8,128)(2,1)S(1)}, u32[]{:S(2)}) copy-start(bf16[64,2048]{1,0:T(8,128)(2,1)S(1)} %collective-permute-done.25.refs_12_) | copy-start | bytes 786436
  139.5 2.1 %collective-permute-start.20 = (bf16[64,2048]{1,0:T(8,128)(2,1)S(1)}, bf16[64,2048]{1,0:T(8,128)(2,1)S(1)}, u32[]{:S(2)}, u32[]{:S(2)}) collective-permute-start(bf16[64,2048]{1,0:T(8,128)(2,1)S(1)} %add_select_fusion.refs_14_), channel_id=1, source_target_pairs={{0,64},{1,65},{2,66},{3,67},{8,72},{9,73},{10,74},{11,75},{16,80},... | collective-permute-start | bytes 786440 | tf_op jit(solution)/shard_map/ppermute | solution.py:359
  140.2 1.6 copy-start.6
  140.3 20.5 %collective-permute-start.27 = (bf16[256,2048]{1,0:T(8,128)(2,1)S(1)}, bf16[256,2048]{1,0:T(8,128)(2,1)S(1)}, u32[]{:S(2)}, u32[]{:S(2)}) collective-permute-start(bf16[256,2048]{1,0:T(8,128)(2,1)S(1)} %pad_maximum_fusion), channel_id=1, source_target_pairs={{0,4},{1,5},{2,6},{3,7},{8,12},{9,13},{10,14},{11,15},{16,20},{17,... | collective-permute-start | bytes 3145736 | tf_op jit(solution)/shard_map/ppermute | solution.py:362
  141.6 32.4 %copy-start.7 = (bf16[64,2048]{1,0:T(8,128)(2,1)}, bf16[64,2048]{1,0:T(8,128)(2,1)S(1)}, u32[]{:S(2)}) copy-start(bf16[64,2048]{1,0:T(8,128)(2,1)S(1)} %collective-permute-done.23.refs_10_) | copy-start | bytes 786436
  141.6 32.4 %copy-start.8 = (bf16[64,2048]{1,0:T(8,128)(2,1)}, bf16[64,2048]{1,0:T(8,128)(2,1)S(1)}, u32[]{:S(2)}) copy-start(bf16[64,2048]{1,0:T(8,128)(2,1)S(1)} %collective-permute-done.22.refs_9_) | copy-start | bytes 786436
  141.7 32.4 %copy-start.9 = (bf16[64,2048]{1,0:T(8,128)(2,1)}, bf16[64,2048]{1,0:T(8,128)(2,1)S(1)}, u32[]{:S(2)}) copy-start(bf16[64,2048]{1,0:T(8,128)(2,1)S(1)} %collective-permute-done.21.refs_8_) | copy-start | bytes 786436
  141.7 32.4 %copy-start.10 = (bf16[64,2048]{1,0:T(8,128)(2,1)}, bf16[64,2048]{1,0:T(8,128)(2,1)S(1)}, u32[]{:S(2)}) copy-start(bf16[64,2048]{1,0:T(8,128)(2,1)S(1)} %collective-permute-done.20.refs_7_) | copy-start | bytes 786436
  141.8 32.3 %collective-permute-start.28 = (bf16[256,2048]{1,0:T(8,128)(2,1)S(1)}, bf16[256,2048]{1,0:T(8,128)(2,1)}, u32[]{:S(2)}, u32[]{:S(2)}) collective-permute-start(bf16[256,2048]{1,0:T(8,128)(2,1)S(1)} %pad_maximum_fusion.1), channel_id=1, source_target_pairs={{0,4},{1,5},{2,6},{3,7},{8,12},{9,13},{10,14},{11,15},{16,20},{17,... | collective-permute-start | bytes 3145736 | tf_op jit(solution)/shard_map/ppermute | solution.py:363
  160.8 13.2 %copy-start.11 = (bf16[256,2048]{1,0:T(8,128)(2,1)}, bf16[256,2048]{1,0:T(8,128)(2,1)S(1)}, u32[]{:S(2)}) copy-start(bf16[256,2048]{1,0:T(8,128)(2,1)S(1)} %collective-permute-done.27.refs_15_) | copy-start | bytes 3145732

commit v11 on v10

--- a/solution.py
+++ b/solution.py
@@ -98,57 +98,71 @@
 HALF = PW // 2
 
 
-def run_copies(found, dest, sems):
-    copies = [
-        pltpu.make_async_copy(part, dest.at[column, pl.ds(at * HALF, size)], sems.at[slot])
-        for slot, (part, column, at, size) in enumerate(found)
-    ]
-    for copy in copies:
-        copy.start()
-    for copy in copies:
-        copy.wait()
-
-
-def fetch_rows(col, parts, dest, sems):
-    near, wrap, upper, lower = parts
-    found = {
-        1: [(near, 0, 0, PW)],
-        2: [(near, 1, 0, PW), (upper, 0, 0, HALF), (lower, 0, 1, HALF)],
-        3: [(near, 2, 0, PW), (wrap, 0, 0, PW), (upper, 1, 0, HALF), (lower, 1, 1, HALF)],
-    }
-    for column, copies in found.items():
-
-        @pl.when(col == column)
+def start_columns(col, own, near, far, wrap, dest, sems):
+    for last in range(BLOCKS):
+        sources = {0: wrap} if last == 3 else {}
+        if last >= 2:
+            sources[last - 2] = far
+        if last >= 1:
+            sources[last - 1] = near
+        sources[last] = own
+
+        @pl.when(col == last)
         def _():
-            run_copies(copies, dest, sems)
+            for column, part in sources.items():
+                for at in range(2):
+                    rows = pl.ds(at * HALF, HALF)
+                    source = part[at] if isinstance(part, tuple) else part.at[rows]
+                    pltpu.make_async_copy(
+                        source, dest.at[column, rows], sems.at[at, column]
+                    ).start()
+
+
+def wait_column(like, column, at, dest, sems):
+    rows = pl.ds(pl.multiple_of(at * HALF, HALF), HALF)
+    pltpu.make_async_copy(
+        like.at[pl.ds(0, HALF)], dest.at[column, rows], sems.at[at, column]
+    ).wait()
 
 
 def factor_kernel(where_ref, own, *refs):
-    parts, outs = refs[:4], refs[4:12]
+    parts, outs = tuple(refs[:4]), refs[4:12]
     t_ref, s_ref, l_ref, x_ref, r_ref, g_ref, n_ref, e_ref, sems = refs[12:]
     col = where_ref[2]
 
     @pl.when(where_ref[0] == 1)
     def _():
-        mine = pltpu.make_async_copy(own, t_ref.at[col], sems.at[4])
-        mine.start()
-        fetch_rows(col, parts, t_ref, sems)
-        mine.wait()
+        start_columns(col, own, parts[0], parts[2:4], parts[1], t_ref, sems)
 
         def rows_of(i):
             return pl.ds(pl.multiple_of(i * TILE, TILE), TILE)
 
-        @pl.loop(0, col + 1)
-        def _(i):
-            @pl.loop(0, i + 1)
-            def _(j):
-                low = t_ref[j, rows_of(i), :].astype(jnp.float32)
-                high = t_ref[i, rows_of(j), :].astype(jnp.float32)
-                s_ref[i, j] = 0.5 * (low + high.T)
+        def symmetric(i, j):
+            low = t_ref[j, rows_of(i), :].astype(jnp.float32)
+            high = t_ref[i, rows_of(j), :].astype(jnp.float32)
+            s_ref[i, j] = 0.5 * (low + high.T)
+
+        wait_column(own, 0, 0, t_ref, sems)
+        symmetric(0, 0)
 
         @pl.loop(0, col + 1)
         def _(j):
             leaf_inverse(s_ref.at[j, j], x_ref.at[j], g_ref, n_ref, e_ref)
+
+            @pl.when(j == 0)
+            def _():
+                wait_column(own, 0, 1, t_ref, sems)
+
+                @pl.loop(1, col + 1)
+                def _(i):
+                    for at in range(2):
+                        wait_column(own, i, at, t_ref, sems)
+
+                @pl.loop(1, col + 1)
+                def _(i):
+                    @pl.loop(0, i + 1)
+                    def _(k):
+                        symmetric(i, k)
 
             @pl.loop(j + 1, col + 1)
             def _(i):
@@ -201,15 +215,14 @@
             pltpu.VMEM((TILE, TILE), jnp.bfloat16),
             pltpu.VMEM((TILE, TILE), jnp.float32),
             pltpu.VMEM((TILE, TILE), jnp.bfloat16),
-            pltpu.SemaphoreType.DMA((5,)),
+            pltpu.SemaphoreType.DMA((2, BLOCKS)),
         ],
         compiler_params=pltpu.CompilerParams(vmem_limit_bytes=56 << 20),
         name="factor_rows",
     )(where, own, *parts)
 
 
-CHUNKS = 10
-OFFSETS = (4, 3, 5, 6, 2, 7, 1)
+CHUNKS = 3
 
 
 def apply_kernel(where_ref, own, *refs):
@@ -217,50 +230,32 @@
     chunks = refs[7 : 7 + CHUNKS]
     out, p_ref, r_ref, psems, rsems = refs[8 + CHUNKS :]
     second, col, z, core = where_ref[1], where_ref[2], where_ref[3], where_ref[4]
-    parts, early, late = chunks[:8], chunks[8], chunks[9]
-
-    def piece(slot, part):
-        by = (OFFSETS + (0,))[slot]
-        rows = pl.ds(pl.multiple_of(lax.rem(z - by + 8, 8) * 64, 64), 64)
+    chunk, local, other = chunks
+
+    def piece(slot, part, by):
+        rows = pl.ds(pl.multiple_of(lax.rem(z + by + 8, 8) * 64, 64), 64)
         return pltpu.make_async_copy(part, r_ref.at[rows], rsems.at[slot])
 
-    @pl.when(core == 0)
-    def _():
-        for slot in range(8):
-            piece(slot, parts[slot]).start()
-
-    @pl.when(core == 1)
-    def _():
-        for slot in range(8):
-            source = early if slot >= 4 else late
-            piece(slot, source.at[pl.ds(slot % 4 * 64, 64)]).start()
-
-    def rows_of(at):
-        return pl.ds(at * HALF, HALF)
-
-    def load(at, column, part):
-        source = part[at] if isinstance(part, tuple) else part.at[rows_of(at)]
-        return pltpu.make_async_copy(source, p_ref.at[column, rows_of(at)], psems.at[at, column])
-
-    both, late_both = (upper, lower), (late_upper, late_lower)
-    for flag in range(2):
-        for last in range(BLOCKS):
-            sources = {last: own}
-            if last >= 1:
-                sources[last - 1] = both if flag else near
-            if last >= 2:
-                sources[last - 2] = late_both if flag else both
-            if last == 3:
-                sources[0] = late_wrap if flag else wrap
-
-            @pl.when(jnp.logical_and(second == flag, col == last))
-            def _():
-                for at in range(2):
-                    for column, part in sources.items():
-                        load(at, column, part).start()
+    piece(7, chunk, 0).start()
+    for here, (low, high) in enumerate(((local, other), (other, local))):
+
+        @pl.when(core == here)
+        def _():
+            for slot, by in enumerate((-3, -4, -1, -2)):
+                piece(slot, low.at[pl.ds(slot * 64, 64)], by).start()
+            for slot, by in enumerate((1, 2, 3)):
+                piece(slot + 4, high.at[pl.ds(slot * 64, 64)], by).start()
+
+    for flag, (last_near, last_far, last_wrap) in enumerate(
+        ((near, (upper, lower), wrap), ((upper, lower), (late_upper, late_lower), late_wrap))
+    ):
+
+        @pl.when(second == flag)
+        def _():
+            start_columns(col, own, last_near, last_far, last_wrap, p_ref, psems)
 
     for slot in range(8):
-        piece(slot, parts[slot]).wait()
+        piece(slot, chunk, 0).wait()
     for last in range(BLOCKS):
 
         @pl.when(col == last)
@@ -268,10 +263,7 @@
             @pl.loop(0, 2)
             def _(at):
                 for column in range(last + 1):
-                    rows = pl.ds(pl.multiple_of(at * HALF, HALF), HALF)
-                    pltpu.make_async_copy(
-                        near.at[pl.ds(0, HALF)], p_ref.at[column, rows], psems.at[at, column]
-                    ).wait()
+                    wait_column(near, column, at, p_ref, psems)
 
                 @pl.loop(0, HALF // TILE)
                 def _(tile):
@@ -333,7 +325,7 @@
     return (c, y, k) != (0, 0, 1)
 
 
-def spread_rows(chunks, z, y):
+def spread_rows(chunks, z, y, core):
     kept = chunks[0]
     total = None
     for k in range(1, 8):
@@ -351,17 +343,31 @@
         got = lax.ppermute(chunk, ALL, pairs)
         total = got if total is None else total + got
     chunk = jnp.where(y == 0, chunk, total)
-    direct = {}
-    for by in (6, 2, 5, 3, 4, 7, 1):
-        pairs = pairs_of(
-            lambda c, zz, yy, kk, j: (c, (zz + by) % 8, yy, kk, j) if kk == 0 else None
+    def ring(part, first=0, second=0):
+        steps = (first, second)
+        return lax.ppermute(
+            part,
+            ALL,
+            pairs_of(
+                lambda c, zz, yy, kk, j: (c, (zz + steps[kk]) % 8, yy, kk, j) if steps[kk] else None
+            ),
         )
-        direct[by] = lax.ppermute(chunk, ALL, pairs)
-    parts = [direct[by] for by in OFFSETS] + [chunk]
-    across = pairs_of(lambda c, zz, yy, kk, j: (c, zz, yy, 1, j) if kk == 0 else None)
-    early = lax.ppermute(jnp.concatenate(parts[4:], axis=0), ALL, across)
-    last = lax.ppermute(jnp.concatenate(parts[:4], axis=0), ALL, across)
-    return parts + [early, last]
+
+    two = ring(chunk, 2)
+    one = ring(chunk, 1)
+    chunk, one = lax.optimization_barrier((chunk, one))
+    got = lax.ppermute(
+        chunk, ALL, pairs_of(lambda c, zz, yy, kk, j: (c, zz, yy, 1, j) if kk == 0 else None)
+    )
+    chunk = jnp.where(core == 0, chunk, got)
+    four = ring(chunk, 4, -2)
+    three = ring(chunk, 3, -1)
+    below = ring(chunk, 0, -3)
+    local = jnp.concatenate([three, four, jnp.where(core == 0, one, below), two], axis=0)
+    other = lax.ppermute(
+        local, ALL, pairs_of(lambda c, zz, yy, kk, j: (c, zz, yy, 1 - kk, j))
+    )
+    return [chunk, local, other]
 
 
 def shards(front, left_factors, right_factors):
@@ -408,7 +414,7 @@
         (where, near, wrap, upper, lower, late_wrap, late_upper, late_lower)
     )
     chunks = factor_rows(where, own, gathered[:4])
-    chunks = spread_rows(chunks, z, y)
+    chunks = spread_rows(chunks, z, y, core)
     return apply_rows(where, own, gathered, chunks, token)
 
 

time: 187 us -> 186 us (level)
  waiting for transfers between devices: 133 us -> 127 us
  starting transfers between devices: 30.5 us -> 35.3 us
    ppermute x9 -> x7, waiting for transfers between devices: 31 us -> 25.8 us  [the longest x5 21.3 us: ring(): lax.ppermute(part, ALL, pairs_of(lambda c, zz, yy, kk, j: (c, (zz + steps...]
    ppermute x9 -> x7, starting transfers between devices: 7.33 us -> 12.1 us  [the longest x5 9.68 us: ring(): lax.ppermute(part, ALL, pairs_of(lambda c, zz, yy, kk, j: (c, (zz + steps...]
  transfers between devices with their start and end apart: 29 -> 27, of which waited for: 8 -> 11; matrix products, arithmetic and copies ran while one was open for 0% -> 0% of each run, Pallas kernels for 0% -> 0%
where the time goes in v11:
time: 186 us; the launch traced here: 185 us
  waiting for transfers between devices  127 us (68%)
  starting transfers between devices  35.3 us (19%)
  Pallas kernels  13 us (7%)
  other arithmetic  4.6 us (2%)
  local copies, waits for them, and re-layouts  3.96 us (2%)
    ppermute x1, waiting for transfers between devices, shards(): lax.ppermute(near[:8, :128] + wrap[:8, :128], ALL, pairs_of(lambda c, zz,...  48 us
    ppermute x5, waiting for transfers between devices, ring(): lax.ppermute(part, ALL, pairs_of(lambda c, zz, yy, kk, j: (c, (zz + steps...  21.3 us
    ppermute x1, waiting for transfers between devices, shards(): lax.ppermute(jnp.where(second, held[HALF:], mixed), ALL, moves(is_other,...  11.6 us
    ppermute x1, waiting for transfers between devices, shards(): lax.ppermute(sent, ALL, pairs_of(lambda c, zz, yy, kk, j: (1 - c, zz, yy,...  11.4 us
    ppermute x1, waiting for transfers between devices, shards(): late_upper = lax.ppermute(upper, ALL, moves(is_second, (1, 2), (2, 3)))  11.2 us
    pallas_call x1, Pallas kernels, apply_rows(): pl.pallas_call(apply_kernel, out_shape=jax.ShapeDtypeStruct((TILE, PW), j...  10.9 us
    ppermute x1, waiting for transfers between devices, shards(): lax.ppermute(jnp.where(second, held[:HALF], near[:HALF]), ALL, moves(is_o...  10 us
    ppermute x5, starting transfers between devices, ring(): lax.ppermute(part, ALL, pairs_of(lambda c, zz, yy, kk, j: (c, (zz + steps...  9.68 us
  transfers between devices with their start and end apart: 27, of which 11 were waited for; matrix products, arithmetic and copies ran while one was open for 0% of the time, Pallas kernels for 0%

profile of v11, /device:TPU:7, one launch (start us, length us, event | category | flops | bytes accessed | tf_op | source)
XLA Modules:
  0.0 185.4 jit_solution(3148628049559980720)
XLA Ops:
  0.0 1.3 copy.8
  1.6 3.0 %collective-permute-start = (bf16[2,4,64,512]{3,2,1,0:T(8,128)(2,1)S(1)}, bf16[2,4,64,512]{3,2,1,0:T(8,128)(2,1)S(1)}, u32[]{:S(2)}, u32[]{:S(2)}) collective-permute-start(bf16[2,4,64,512]{3,2,1,0:T(8,128)(2,1)S(1)} %get-tuple-element.53), channel_id=1, source_target_pairs={{0,128},{1,129},{2,130},{3,131},{4,132},{5,133},{6,134},{7,135},{8... | collective-permute-start | bytes 1572872 | tf_op jit(solution)/shard_map/ppermute | solution.py:383
  4.6 11.4 %collective-permute-done = bf16[2,4,64,512]{3,2,1,0:T(8,128)(2,1)S(1)} collective-permute-done((bf16[2,4,64,512]{3,2,1,0:T(8,128)(2,1)S(1)}, bf16[2,4,64,512]{3,2,1,0:T(8,128)(2,1)S(1)}, u32[]{:S(2)}, u32[]{:S(2)}) %collective-permute-start) | collective-permute-done | bytes 524320 | tf_op jit(solution)/shard_map/ppermute | solution.py:383
  15.9 0.8 fusion.3
  16.7 0.8 copy-done.3
  17.5 0.8 fusion.own
  18.3 2.0 %collective-permute-start.2 = (bf16[2048,512]{1,0:T(8,128)(2,1)S(1)}, bf16[2048,512]{1,0:T(8,128)(2,1)}, u32[]{:S(2)}, u32[]{:S(2)}) collective-permute-start(bf16[2048,512]{1,0:T(8,128)(2,1)S(1)} %fusion.own), channel_id=1, source_target_pairs={{0,3},{8,11},{12,15},{16,19},{24,27},{28,31},{32,35},{40,43},{44,4... | collective-permute-start | bytes 6291464 | tf_op jit(solution)/shard_map/ppermute | solution.py:392
  20.4 2.0 %collective-permute-start.1 = (bf16[2048,512]{1,0:T(8,128)(2,1)S(1)}, bf16[2048,512]{1,0:T(8,128)(2,1)}, u32[]{:S(2)}, u32[]{:S(2)}) collective-permute-start(bf16[2048,512]{1,0:T(8,128)(2,1)S(1)} %fusion.own), channel_id=1, source_target_pairs={{0,1},{1,2},{2,3},{8,9},{9,10},{10,11},{12,13},{13,14},{14,15},{16... | collective-permute-start | bytes 6291464 | tf_op jit(solution)/shard_map/ppermute | solution.py:391
  22.5 1.6 collective-permute-start.3
  24.1 0.7 slice_add_fusion
  24.8 1.3 collective-permute-start.4
  26.1 48.0 %collective-permute-done.4.refs_10_ = bf16[8,128]{1,0:T(8,128)(2,1)S(1)} collective-permute-done((bf16[8,128]{1,0:T(8,128)(2,1)S(1)}, bf16[8,128]{1,0:T(8,128)(2,1)S(1)}, u32[]{:S(2)}, u32[]{:S(2)}) %collective-permute-start.4) | collective-permute-done | bytes 2080 | tf_op jit(solution)/shard_map/ppermute | solution.py:395
  74.1 1.8 select_select_fusion
  75.9 1.3 collective-permute-start.6
  77.2 1.3 collective-permute-start.5
  78.5 1.3 collective-permute-start.7
  79.8 11.6 %collective-permute-done.6.refs_3_ = bf16[1024,512]{1,0:T(8,128)(2,1)S(1)} collective-permute-done((bf16[1024,512]{1,0:T(8,128)(2,1)S(1)}, bf16[1024,512]{1,0:T(8,128)(2,1)S(1)}, u32[]{:S(2)}, u32[]{:S(2)}) %collective-permute-start.6) | collective-permute-done | bytes 1048608 | tf_op jit(solution)/shard_map/ppermute | solution.py:406
  91.4 1.3 collective-permute-start.9
  92.7 10.0 %collective-permute-done.5.refs_2_ = bf16[1024,512]{1,0:T(8,128)(2,1)} collective-permute-done((bf16[1024,512]{1,0:T(8,128)(2,1)S(1)}, bf16[1024,512]{1,0:T(8,128)(2,1)}, u32[]{:S(2)}, u32[]{:S(2)}) %collective-permute-start.5) | collective-permute-done | bytes 1048608 | tf_op jit(solution)/shard_map/ppermute | solution.py:402
  102.8 1.3 collective-permute-start.8
  104.1 0.6 stack.37.where_ref
  104.7 9.3 %collective-permute-done.9.refs_6_ = bf16[1024,512]{1,0:T(8,128)(2,1)} collective-permute-done((bf16[1024,512]{1,0:T(8,128)(2,1)S(1)}, bf16[1024,512]{1,0:T(8,128)(2,1)}, u32[]{:S(2)}, u32[]{:S(2)}) %collective-permute-start.9) | collective-permute-done | bytes 1048608 | tf_op jit(solution)/shard_map/ppermute | solution.py:411
  114.0 11.2 %collective-permute-done.8.refs_5_ = bf16[1024,512]{1,0:T(8,128)(2,1)} collective-permute-done((bf16[1024,512]{1,0:T(8,128)(2,1)}, bf16[1024,512]{1,0:T(8,128)(2,1)}, u32[]{:S(2)}, u32[]{:S(2)}) %collective-permute-start.8) | collective-permute-done | bytes 1048608 | tf_op jit(solution)/shard_map/ppermute | solution.py:410
  125.2 2.1 %factor_rows.1 = (bf16[64,2048]{1,0:T(8,128)(2,1)}, bf16[64,2048]{1,0:T(8,128)(2,1)}, bf16[64,2048]{1,0:T(8,128)(2,1)}, bf16[64,2048]{1,0:T(8,128)(2,1)}, bf16[6...) custom-call(s32[5]{0:T(128)} %stack.37.where_ref, ...), custom_call_target="tpu_custom_call" | custom-call | tf_op jit(solution)/shard_map/factor_rows/pallas_call | solution.py:204
  127.3 0.7 collective-permute-start.10
  128.0 0.7 collective-permute-start.11
  128.7 0.7 collective-permute-start.12
  129.4 0.7 collective-permute-start.13
  130.1 0.7 collective-permute-start.14
  130.8 0.7 collective-permute-start.15
  131.5 0.7 collective-permute-start.16
  132.2 1.1 add_select_fusion.1
  133.3 0.7 collective-permute-start.19
  133.9 0.7 collective-permute-start.18
  134.6 0.7 collective-permute-start.17
  135.4 0.7 collective-permute-start.20
  136.1 1.3 collective-permute-start.21
  137.4 2.1 %collective-permute-done.21 = bf16[64,2048]{1,0:T(8,128)(2,1)S(1)} collective-permute-done((bf16[64,2048]{1,0:T(8,128)(2,1)S(1)}, bf16[64,2048]{1,0:T(8,128)(2,1)S(1)}, u32[]{:S(2)}, u32[]{:S(2)}) %collective-permute-start.21) | collective-permute-done | bytes 262176 | tf_op jit(solution)/shard_map/ppermute | solution.py:359
  139.6 7.4 %collective-permute-start.24 = (bf16[64,2048]{1,0:T(8,128)(2,1)S(1)}, bf16[64,2048]{1,0:T(8,128)(2,1)S(1)}, u32[]{:S(2)}, u32[]{:S(2)}) collective-permute-start(bf16[64,2048]{1,0:T(8,128)(2,1)S(1)} %broadcast_select_fusion.1.refs_7_), channel_id=1, source_target_pairs={{4,84},{5,85},{6,86},{7,87},{12,92},{13,93},{14,94},{15,95},{20,10... | collective-permute-start | bytes 786440 | tf_op jit(solution)/shard_map/ppermute | solution.py:348
  147.0 0.7 collective-permute-start.25
  148.0 0.5 collective-permute-start.22
  148.6 10.9 %collective-permute-done.24 = bf16[64,2048]{1,0:T(8,128)(2,1)S(1)} collective-permute-done((bf16[64,2048]{1,0:T(8,128)(2,1)S(1)}, bf16[64,2048]{1,0:T(8,128)(2,1)S(1)}, u32[]{:S(2)}, u32[]{:S(2)}) %collective-permute-start.24) | collective-permute-done | bytes 262176 | tf_op jit(solution)/shard_map/ppermute | solution.py:348
  159.5 7.7 %collective-permute-done.23 = bf16[64,2048]{1,0:T(8,128)(2,1)S(1)} collective-permute-done((bf16[64,2048]{1,0:T(8,128)(2,1)S(1)}, bf16[64,2048]{1,0:T(8,128)(2,1)S(1)}, u32[]{:S(2)}, u32[]{:S(2)}) %collective-permute-start.23) | collective-permute-done | bytes 262176 | tf_op jit(solution)/shard_map/ppermute | solution.py:348
  167.2 2.8 %collective-permute-done.22 = bf16[64,2048]{1,0:T(8,128)(2,1)S(1)} collective-permute-done((bf16[64,2048]{1,0:T(8,128)(2,1)S(1)}, bf16[64,2048]{1,0:T(8,128)(2,1)S(1)}, u32[]{:S(2)}, u32[]{:S(2)}) %collective-permute-start.22) | collective-permute-done | bytes 262176 | tf_op jit(solution)/shard_map/ppermute | solution.py:348
  170.0 1.2 collective-permute-start.26
  171.2 2.3 %collective-permute-done.26.refs_9_ = bf16[256,2048]{1,0:T(8,128)(2,1)S(1)} collective-permute-done((bf16[256,2048]{1,0:T(8,128)(2,1)S(1)}, bf16[256,2048]{1,0:T(8,128)(2,1)S(1)}, u32[]{:S(2)}, u32[]{:S(2)}) %collective-permute-start.26) | collective-permute-done | bytes 1048608 | tf_op jit(solution)/shard_map/ppermute | solution.py:367
  173.5 1.0 copy-done.5
  174.5 10.9 %apply_rows.1 = bf16[512,2048]{1,0:T(8,128)(2,1)} custom-call(s32[5]{0:T(128)} %stack.37.where_ref, bf16[2048,512]{1,0:T(8,128)(2,1)} %copy-done, bf16[2048,512]{1,0:T(8,128)(2,1)} %collective-permute-done.1.refs_0_, bf16[2048,512]{1,0:T(8,128)(2,1)} %collective-permute-done.2.refs_1_, bf16[1024,512]{1,0:T(8,128)(2,1)} %collective-permute-done.5.refs_2_, ...), custom_call_target="tpu_custom_call" | custom-call | tf_op jit(solution)/shard_map/apply_rows/pallas_call | solution.py:280
  (38 shorter events, 0.9 us)
Async XLA Ops:
  0.0 1.4 copy-start.6
  1.6 14.4 %collective-permute-start = (bf16[2,4,64,512]{3,2,1,0:T(8,128)(2,1)S(1)}, bf16[2,4,64,512]{3,2,1,0:T(8,128)(2,1)S(1)}, u32[]{:S(2)}, u32[]{:S(2)}) collective-permute-start(bf16[2,4,64,512]{3,2,1,0:T(8,128)(2,1)S(1)} %get-tuple-element.53), channel_id=1, source_target_pairs={{0,128},{1,129},{2,130},{3,131},{4,132},{5,133},{6,134},{7,135},{8... | collective-permute-start | bytes 1572872 | tf_op jit(solution)/shard_map/ppermute | solution.py:383
  15.9 1.6 copy-start.3
  18.3 60.2 %copy-start = (bf16[2048,512]{1,0:T(8,128)(2,1)}, bf16[2048,512]{1,0:T(8,128)(2,1)S(1)}, u32[]{:S(2)}) copy-start(bf16[2048,512]{1,0:T(8,128)(2,1)S(1)} %fusion.own) | copy-start | bytes 6291460
  18.3 5.7 %collective-permute-start.2 = (bf16[2048,512]{1,0:T(8,128)(2,1)S(1)}, bf16[2048,512]{1,0:T(8,128)(2,1)}, u32[]{:S(2)}, u32[]{:S(2)}) collective-permute-start(bf16[2048,512]{1,0:T(8,128)(2,1)S(1)} %fusion.own), channel_id=1, source_target_pairs={{0,3},{8,11},{12,15},{16,19},{24,27},{28,31},{32,35},{40,43},{44,4... | collective-permute-start | bytes 6291464 | tf_op jit(solution)/shard_map/ppermute | solution.py:392
  20.4 3.7 %collective-permute-start.1 = (bf16[2048,512]{1,0:T(8,128)(2,1)S(1)}, bf16[2048,512]{1,0:T(8,128)(2,1)}, u32[]{:S(2)}, u32[]{:S(2)}) collective-permute-start(bf16[2048,512]{1,0:T(8,128)(2,1)S(1)} %fusion.own), channel_id=1, source_target_pairs={{0,1},{1,2},{2,3},{8,9},{9,10},{10,11},{12,13},{13,14},{14,15},{16... | collective-permute-start | bytes 6291464 | tf_op jit(solution)/shard_map/ppermute | solution.py:391
  22.5 1.6 collective-permute-start.3
  24.8 49.3 %collective-permute-start.4 = (bf16[8,128]{1,0:T(8,128)(2,1)S(1)}, bf16[8,128]{1,0:T(8,128)(2,1)S(1)}, u32[]{:S(2)}, u32[]{:S(2)}) collective-permute-start(bf16[8,128]{1,0:T(8,128)(2,1)S(1)} %slice_add_fusion), channel_id=1, source_target_pairs={{8,4},{9,5},{10,6},{11,7},{24,20},{25,21},{26,22},{27,23},{40,36},... | collective-permute-start | bytes 6152 | tf_op jit(solution)/shard_map/ppermute | solution.py:395
  74.1 1.8 copy-start.7
  75.9 15.5 %collective-permute-start.6 = (bf16[1024,512]{1,0:T(8,128)(2,1)S(1)}, bf16[1024,512]{1,0:T(8,128)(2,1)S(1)}, u32[]{:S(2)}, u32[]{:S(2)}) collective-permute-start(bf16[1024,512]{1,0:T(8,128)(2,1)S(1)} %get-tuple-element.51), channel_id=1, source_target_pairs={{0,3},{3,2},{8,11},{11,10},{12,15},{15,14},{16,19},{19,18},{24,27}... | collective-permute-start | bytes 3145736 | tf_op jit(solution)/shard_map/ppermute | solution.py:406
  77.2 25.6 %collective-permute-start.5 = (bf16[1024,512]{1,0:T(8,128)(2,1)S(1)}, bf16[1024,512]{1,0:T(8,128)(2,1)}, u32[]{:S(2)}, u32[]{:S(2)}) collective-permute-start(bf16[1024,512]{1,0:T(8,128)(2,1)S(1)} %get-tuple-element.52), channel_id=1, source_target_pairs={{1,2},{2,3},{9,10},{10,11},{13,14},{14,15},{17,18},{18,19},{25,26}... | collective-permute-start | bytes 3145736 | tf_op jit(solution)/shard_map/ppermute | solution.py:402
  78.5 46.7 %collective-permute-start.7 = (bf16[2048,512]{1,0:T(8,128)(2,1)S(1)}, bf16[2048,512]{1,0:T(8,128)(2,1)}, u32[]{:S(2)}, u32[]{:S(2)}) collective-permute-start(bf16[2048,512]{1,0:T(8,128)(2,1)S(1)} %fusion.own), channel_id=1, source_target_pairs={{4,7},{20,23},{36,39},{52,55},{68,71},{84,87},{100,103},{116,119}} | collective-permute-start | bytes 6291464 | tf_op jit(solution)/shard_map/ppermute | solution.py:409
  91.4 33.8 %copy-start.1 = (bf16[1024,512]{1,0:T(8,128)(2,1)}, bf16[1024,512]{1,0:T(8,128)(2,1)S(1)}, u32[]{:S(2)}) copy-start(bf16[1024,512]{1,0:T(8,128)(2,1)S(1)} %collective-permute-done.6.refs_3_) | copy-start | bytes 3145732
  91.4 22.6 %collective-permute-start.9 = (bf16[1024,512]{1,0:T(8,128)(2,1)S(1)}, bf16[1024,512]{1,0:T(8,128)(2,1)}, u32[]{:S(2)}, u32[]{:S(2)}) collective-permute-start(bf16[1024,512]{1,0:T(8,128)(2,1)S(1)} %collective-permute-done.6.refs_3_), channel_id=1, source_target_pairs={{5,6},{6,7},{21,22},{22,23},{37,38},{38,39},{53,54},{54,55},{69,70... | collective-permute-start | bytes 3145736 | tf_op jit(solution)/shard_map/ppermute | solution.py:411
  102.8 22.5 %collective-permute-start.8 = (bf16[1024,512]{1,0:T(8,128)(2,1)}, bf16[1024,512]{1,0:T(8,128)(2,1)}, u32[]{:S(2)}, u32[]{:S(2)}) collective-permute-start(bf16[1024,512]{1,0:T(8,128)(2,1)} %collective-permute-done.5.refs_2_), channel_id=1, source_target_pairs={{5,6},{6,7},{21,22},{22,23},{37,38},{38,39},{53,54},{54,55},{69,70... | collective-permute-start | bytes 3145736 | tf_op jit(solution)/shard_map/ppermute | solution.py:410
  127.3 3.4 %collective-permute-start.10 = (bf16[64,2048]{1,0:T(8,128)(2,1)}, bf16[64,2048]{1,0:T(8,128)(2,1)S(1)}, u32[]{:S(2)}, u32[]{:S(2)}) collective-permute-start(bf16[64,2048]{1,0:T(8,128)(2,1)} %get-tuple-element.41), channel_id=1, source_target_pairs={{0,16},{1,17},{2,18},{3,19}} | collective-permute-start | bytes 786440 | tf_op jit(solution)/shard_map/ppermute | solution.py:335
  128.0 3.4 %collective-permute-start.11 = (bf16[64,2048]{1,0:T(8,128)(2,1)}, bf16[64,2048]{1,0:T(8,128)(2,1)S(1)}, u32[]{:S(2)}, u32[]{:S(2)}) collective-permute-start(bf16[64,2048]{1,0:T(8,128)(2,1)} %get-tuple-element.42), channel_id=1, source_target_pairs={{0,32},{1,33},{2,34},{3,35}} | collective-permute-start | bytes 786440 | tf_op jit(solution)/shard_map/ppermute | solution.py:335
  128.7 3.5 %collective-permute-start.12 = (bf16[64,2048]{1,0:T(8,128)(2,1)}, bf16[64,2048]{1,0:T(8,128)(2,1)S(1)}, u32[]{:S(2)}, u32[]{:S(2)}) collective-permute-start(bf16[64,2048]{1,0:T(8,128)(2,1)} %get-tuple-element.43), channel_id=1, source_target_pairs={{0,48},{1,49},{2,50},{3,51}} | collective-permute-start | bytes 786440 | tf_op jit(solution)/shard_map/ppermute | solution.py:335
  129.4 2.8 %collective-permute-start.13 = (bf16[64,2048]{1,0:T(8,128)(2,1)}, bf16[64,2048]{1,0:T(8,128)(2,1)S(1)}, u32[]{:S(2)}, u32[]{:S(2)}) collective-permute-start(bf16[64,2048]{1,0:T(8,128)(2,1)} %get-tuple-element.44), channel_id=1, source_target_pairs={{0,64},{1,65},{2,66},{3,67}} | collective-permute-start | bytes 786440 | tf_op jit(solution)/shard_map/ppermute | solution.py:335
  130.1 2.1 %collective-permute-start.14 = (bf16[64,2048]{1,0:T(8,128)(2,1)}, bf16[64,2048]{1,0:T(8,128)(2,1)S(1)}, u32[]{:S(2)}, u32[]{:S(2)}) collective-permute-start(bf16[64,2048]{1,0:T(8,128)(2,1)} %get-tuple-element.45), channel_id=1, source_target_pairs={{0,80},{1,81},{2,82},{3,83}} | collective-permute-start | bytes 786440 | tf_op jit(solution)/shard_map/ppermute | solution.py:335
  130.8 1.4 collective-permute-start.15
  131.5 0.7 collective-permute-start.16
  133.3 2.1 %collective-permute-start.19 = (bf16[64,2048]{1,0:T(8,128)(2,1)S(1)}, bf16[64,2048]{1,0:T(8,128)(2,1)S(1)}, u32[]{:S(2)}, u32[]{:S(2)}) collective-permute-start(bf16[64,2048]{1,0:T(8,128)(2,1)S(1)} %add_select_fusion.1), channel_id=1, source_target_pairs={{0,128},{1,129},{2,130},{3,131},{16,144},{17,145},{18,146},{19,147... | collective-permute-start | bytes 786440 | tf_op jit(solution)/shard_map/ppermute | solution.py:343
  133.9 1.4 collective-permute-start.18
  134.6 0.7 collective-permute-start.17
  135.4 0.7 collective-permute-start.20
  136.1 3.4 %collective-permute-start.21 = (bf16[64,2048]{1,0:T(8,128)(2,1)S(1)}, bf16[64,2048]{1,0:T(8,128)(2,1)S(1)}, u32[]{:S(2)}, u32[]{:S(2)}) collective-permute-start(bf16[64,2048]{1,0:T(8,128)(2,1)S(1)} %add_select_fusion), channel_id=1, source_target_pairs={{0,4},{1,5},{2,6},{3,7},{8,12},{9,13},{10,14},{11,15},{16,20},{17,... | collective-permute-start | bytes 786440 | tf_op jit(solution)/shard_map/ppermute | solution.py:359
  139.6 33.9 %copy-start.4 = (bf16[64,2048]{1,0:T(8,128)(2,1)}, bf16[64,2048]{1,0:T(8,128)(2,1)S(1)}, u32[]{:S(2)}) copy-start(bf16[64,2048]{1,0:T(8,128)(2,1)S(1)} %broadcast_select_fusion.1.refs_7_) | copy-start | bytes 786436
  139.6 19.9 %collective-permute-start.24 = (bf16[64,2048]{1,0:T(8,128)(2,1)S(1)}, bf16[64,2048]{1,0:T(8,128)(2,1)S(1)}, u32[]{:S(2)}, u32[]{:S(2)}) collective-permute-start(bf16[64,2048]{1,0:T(8,128)(2,1)S(1)} %broadcast_select_fusion.1.refs_7_), channel_id=1, source_target_pairs={{4,84},{5,85},{6,86},{7,87},{12,92},{13,93},{14,94},{15,95},{20,10... | collective-permute-start | bytes 786440 | tf_op jit(solution)/shard_map/ppermute | solution.py:348
  147.0 12.5 %collective-permute-start.25 = (bf16[64,2048]{1,0:T(8,128)(2,1)S(1)}, bf16[64,2048]{1,0:T(8,128)(2,1)S(1)}, u32[]{:S(2)}, u32[]{:S(2)}) collective-permute-start(bf16[64,2048]{1,0:T(8,128)(2,1)S(1)} %add_select_fusion), channel_id=1, source_target_pairs={{0,32},{1,33},{2,34},{3,35},{8,40},{9,41},{10,42},{11,43},{16,48},... | collective-permute-start | bytes 786440 | tf_op jit(solution)/shard_map/ppermute | solution.py:348
  147.7 19.5 %collective-permute-start.23 = (bf16[64,2048]{1,0:T(8,128)(2,1)S(1)}, bf16[64,2048]{1,0:T(8,128)(2,1)S(1)}, u32[]{:S(2)}, u32[]{:S(2)}) collective-permute-start(bf16[64,2048]{1,0:T(8,128)(2,1)S(1)} %broadcast_select_fusion.1.refs_7_), channel_id=1, source_target_pairs={{0,64},{1,65},{2,66},{3,67},{4,100},{5,101},{6,102},{7,103},{8,72}... | collective-permute-start | bytes 786440 | tf_op jit(solution)/shard_map/ppermute | solution.py:348
  148.0 21.9 %collective-permute-start.22 = (bf16[64,2048]{1,0:T(8,128)(2,1)S(1)}, bf16[64,2048]{1,0:T(8,128)(2,1)S(1)}, u32[]{:S(2)}, u32[]{:S(2)}) collective-permute-start(bf16[64,2048]{1,0:T(8,128)(2,1)S(1)} %broadcast_select_fusion.1.refs_7_), channel_id=1, source_target_pairs={{0,48},{1,49},{2,50},{3,51},{4,116},{5,117},{6,118},{7,119},{8,56}... | collective-permute-start | bytes 786440 | tf_op jit(solution)/shard_map/ppermute | solution.py:348
  170.0 3.5 %copy-start.2 = (bf16[256,2048]{1,0:T(8,128)(2,1)}, bf16[256,2048]{1,0:T(8,128)(2,1)S(1)}, u32[]{:S(2)}) copy-start(bf16[256,2048]{1,0:T(8,128)(2,1)S(1)} %pad_maximum_fusion.refs_8_) | copy-start | bytes 3145732
  170.0 3.4 %collective-permute-start.26 = (bf16[256,2048]{1,0:T(8,128)(2,1)S(1)}, bf16[256,2048]{1,0:T(8,128)(2,1)S(1)}, u32[]{:S(2)}, u32[]{:S(2)}) collective-permute-start(bf16[256,2048]{1,0:T(8,128)(2,1)S(1)} %pad_maximum_fusion.refs_8_), channel_id=1, source_target_pairs={{0,4},{1,5},{2,6},{3,7},{4,0},{5,1},{6,2},{7,3},{8,12},{9,13},{10,... | collective-permute-start | bytes 3145736 | tf_op jit(solution)/shard_map/ppermute | solution.py:367
  173.5 1.0 copy-start.5

commit v12 on v11

--- a/solution.py
+++ b/solution.py
@@ -222,40 +222,42 @@
     )(where, own, *parts)
 
 
-CHUNKS = 3
+CHUNKS = 6
 
 
 def apply_kernel(where_ref, own, *refs):
-    near, wrap, upper, lower, late_wrap, late_upper, late_lower = refs[:7]
-    chunks = refs[7 : 7 + CHUNKS]
-    out, p_ref, r_ref, psems, rsems = refs[8 + CHUNKS :]
+    near, wrap, upper, lower, late_wrap, late_far = refs[:6]
+    chunks = refs[6 : 6 + CHUNKS]
+    out, p_ref, r_ref, psems, rsems = refs[7 + CHUNKS :]
     second, col, z, core = where_ref[1], where_ref[2], where_ref[3], where_ref[4]
-    chunk, local, other = chunks
-
-    def piece(slot, part, by):
-        rows = pl.ds(pl.multiple_of(lax.rem(z + by + 8, 8) * 64, 64), 64)
+    sign = 1 - 2 * core
+    swapped = chunks[5]
+
+    def piece(slot, part, at, size):
+        rows = pl.ds(pl.multiple_of(at, size), size)
         return pltpu.make_async_copy(part, r_ref.at[rows], rsems.at[slot])
 
-    piece(7, chunk, 0).start()
-    for here, (low, high) in enumerate(((local, other), (other, local))):
-
-        @pl.when(core == here)
-        def _():
-            for slot, by in enumerate((-3, -4, -1, -2)):
-                piece(slot, low.at[pl.ds(slot * 64, 64)], by).start()
-            for slot, by in enumerate((1, 2, 3)):
-                piece(slot + 4, high.at[pl.ds(slot * 64, 64)], by).start()
+    pieces = [piece(0, chunks[0], z * 64, 64)]
+    for by in range(1, 4):
+        down, up = lax.rem(z - sign * by + 8, 8) * 64, lax.rem(z + sign * by + 8, 8) * 64
+        pieces.append(piece(by, chunks[by], down, 64))
+        pieces.append(piece(by + 3, swapped.at[pl.ds(by * 64 - 64, 64)], up, 64))
+    far = lax.rem(z + 4, 8) * 64
+    pieces.append(piece(7, chunks[4], far + core * 32, 32))
+    pieces.append(piece(8, swapped.at[pl.ds(192, 32)], far + (1 - core) * 32, 32))
+    for copy in pieces:
+        copy.start()
 
     for flag, (last_near, last_far, last_wrap) in enumerate(
-        ((near, (upper, lower), wrap), ((upper, lower), (late_upper, late_lower), late_wrap))
+        ((near, (upper, lower), wrap), ((upper, lower), late_far, late_wrap))
     ):
 
         @pl.when(second == flag)
         def _():
             start_columns(col, own, last_near, last_far, last_wrap, p_ref, psems)
 
-    for slot in range(8):
-        piece(slot, chunk, 0).wait()
+    for copy in pieces:
+        copy.wait()
     for last in range(BLOCKS):
 
         @pl.when(col == last)
@@ -280,13 +282,13 @@
     return pl.pallas_call(
         apply_kernel,
         out_shape=jax.ShapeDtypeStruct((TILE, PW), jnp.bfloat16),
-        in_specs=[pl.BlockSpec(memory_space=pltpu.SMEM)] + [HBM] * (9 + CHUNKS),
+        in_specs=[pl.BlockSpec(memory_space=pltpu.SMEM)] + [HBM] * (8 + CHUNKS),
         out_specs=pl.BlockSpec(memory_space=pltpu.VMEM),
         scratch_shapes=[
             pltpu.VMEM((BLOCKS, PW, TILE), jnp.bfloat16),
             pltpu.VMEM((TILE, PW), jnp.bfloat16),
             pltpu.SemaphoreType.DMA((2, BLOCKS)),
-            pltpu.SemaphoreType.DMA((8,)),
+            pltpu.SemaphoreType.DMA((9,)),
         ],
         compiler_params=pltpu.CompilerParams(vmem_limit_bytes=60 << 20),
         name="apply_rows",
@@ -325,7 +327,7 @@
     return (c, y, k) != (0, 0, 1)
 
 
-def spread_rows(chunks, z, y, core):
+def spread_rows(chunks, z, y, core, late_far):
     kept = chunks[0]
     total = None
     for k in range(1, 8):
@@ -343,31 +345,22 @@
         got = lax.ppermute(chunk, ALL, pairs)
         total = got if total is None else total + got
     chunk = jnp.where(y == 0, chunk, total)
-    def ring(part, first=0, second=0):
-        steps = (first, second)
-        return lax.ppermute(
-            part,
-            ALL,
-            pairs_of(
-                lambda c, zz, yy, kk, j: (c, (zz + steps[kk]) % 8, yy, kk, j) if steps[kk] else None
-            ),
-        )
-
-    two = ring(chunk, 2)
-    one = ring(chunk, 1)
-    chunk, one = lax.optimization_barrier((chunk, one))
+    chunk, late_far = lax.optimization_barrier((chunk, late_far))
     got = lax.ppermute(
         chunk, ALL, pairs_of(lambda c, zz, yy, kk, j: (c, zz, yy, 1, j) if kk == 0 else None)
     )
     chunk = jnp.where(core == 0, chunk, got)
-    four = ring(chunk, 4, -2)
-    three = ring(chunk, 3, -1)
-    below = ring(chunk, 0, -3)
-    local = jnp.concatenate([three, four, jnp.where(core == 0, one, below), two], axis=0)
-    other = lax.ppermute(
-        local, ALL, pairs_of(lambda c, zz, yy, kk, j: (c, zz, yy, 1 - kk, j))
-    )
-    return [chunk, local, other]
+    swap = pairs_of(lambda c, zz, yy, kk, j: (c, zz, yy, 1 - kk, j))
+    across = pairs_of(lambda c, zz, yy, kk, j: (c, (zz + 4) % 8, yy, kk, j))
+    part = lax.dynamic_slice_in_dim(chunk, core * 32, 32, 0)
+    half = lax.ppermute(part, ALL, across)
+    direct = {}
+    for by in (3, 2, 1):
+        pairs = pairs_of(lambda c, zz, yy, kk, j: (c, (zz + (1 - 2 * kk) * by) % 8, yy, kk, j))
+        direct[by] = lax.ppermute(chunk, ALL, pairs)
+    mine = [direct[by] for by in (1, 2, 3)] + [half]
+    theirs = lax.ppermute(jnp.concatenate(mine, axis=0), ALL, swap)
+    return [chunk] + mine + [theirs], late_far
 
 
 def shards(front, left_factors, right_factors):
@@ -407,15 +400,16 @@
         jnp.where(second, held[HALF:], mixed), ALL, moves(is_other, (0, 3), (3, 2)) + along
     )
     late_wrap = lax.ppermute(held, ALL, moves(is_second, (0, 3)))
-    late_upper = lax.ppermute(upper, ALL, moves(is_second, (1, 2), (2, 3)))
-    late_lower = lax.ppermute(lower, ALL, moves(is_second, (1, 2), (2, 3)))
+    late_far = lax.ppermute(
+        jnp.concatenate([upper, lower], axis=0), ALL, moves(is_second, (1, 2), (2, 3))
+    )
     where = jnp.stack([first, second, column, z, core]).astype(jnp.int32)
     where, *gathered = lax.optimization_barrier(
-        (where, near, wrap, upper, lower, late_wrap, late_upper, late_lower)
+        (where, near, wrap, upper, lower, late_wrap)
     )
     chunks = factor_rows(where, own, gathered[:4])
-    chunks = spread_rows(chunks, z, y, core)
-    return apply_rows(where, own, gathered, chunks, token)
+    chunks, late_far = spread_rows(chunks, z, y, core, late_far)
+    return apply_rows(where, own, gathered + [late_far], chunks, token)
 
 
 def solution(mesh):

time: 186 us -> 182 us (0.978)
  waiting for transfers between devices: 127 us -> 123 us
    ppermute x8 -> x6, waiting for transfers between devices: 44.2 us -> 34.4 us  [the longest x1 14.9 us: shards(): lax.ppermute(jnp.concatenate([upper, lower], axis=0), ALL, moves(is_secon...]
    ppermute x1, waiting for transfers between devices: 48 us -> 51.1 us  [shards(): lax.ppermute(near[:8, :128] + wrap[:8, :128], ALL, pairs_of(lambda c, zz,...]
    ppermute x8 -> x6, starting transfers between devices: 13.4 us -> 16 us  [the longest x3 7.57 us: spread_rows(): direct[by] = lax.ppermute(chunk, ALL, pairs)]
  transfers between devices with their start and end apart: 27 -> 25, of which waited for: 11 -> 10; matrix products, arithmetic and copies ran while one was open for 0% -> 3% of each run, Pallas kernels for 0% -> 1%
where the time goes in v12:
time: 182 us
  waiting for transfers between devices  123 us (68%)
  starting transfers between devices  34.5 us (19%)
  Pallas kernels  13.3 us (7%)
  other arithmetic  5.42 us (3%)
  local copies, waits for them, and re-layouts  4.13 us (2%)
    ppermute x1, waiting for transfers between devices, shards(): lax.ppermute(near[:8, :128] + wrap[:8, :128], ALL, pairs_of(lambda c, zz,...  51.1 us
    ppermute x1, waiting for transfers between devices, shards(): lax.ppermute(jnp.concatenate([upper, lower], axis=0), ALL, moves(is_secon...  14.9 us
    ppermute x1, waiting for transfers between devices, shards(): lax.ppermute(jnp.where(second, held[HALF:], mixed), ALL, moves(is_other,...  12.9 us
    ppermute x1, waiting for transfers between devices, shards(): lax.ppermute(sent, ALL, pairs_of(lambda c, zz, yy, kk, j: (1 - c, zz, yy,...  11.4 us
    pallas_call x1, Pallas kernels, apply_rows(): pl.pallas_call(apply_kernel, out_shape=jax.ShapeDtypeStruct((TILE, PW), j...  11.2 us
    ppermute x1, waiting for transfers between devices, shards(): lax.ppermute(jnp.where(second, held[:HALF], near[:HALF]), ALL, moves(is_o...  11.2 us
    ppermute x1, waiting for transfers between devices, spread_rows(): half = lax.ppermute(part, ALL, across)  10.7 us
    ppermute x3, starting transfers between devices, spread_rows(): direct[by] = lax.ppermute(chunk, ALL, pairs)  7.57 us
  transfers between devices with their start and end apart: 25, of which 10 were waited for; matrix products, arithmetic and copies ran while one was open for 3% of the time, Pallas kernels for 1%

profile of v12, /device:TPU:7, one launch (start us, length us, event | category | flops | bytes accessed | tf_op | source)
XLA Modules:
  0.0 181.9 jit_solution(1236424801698356391)
XLA Ops:
  0.0 1.3 copy.8
  1.3 0.2 copy.10
  1.5 0.1 fusion.5
  1.6 3.0 %collective-permute-start = (bf16[2,4,64,512]{3,2,1,0:T(8,128)(2,1)S(1)}, bf16[2,4,64,512]{3,2,1,0:T(8,128)(2,1)S(1)}, u32[]{:S(2)}, u32[]{:S(2)}) collective-permute-start(bf16[2,4,64,512]{3,2,1,0:T(8,128)(2,1)S(1)} %get-tuple-element.49), channel_id=1, source_target_pairs={{0,128},{1,129},{2,130},{3,131},{4,132},{5,133},{6,134},{7,135},{8... | collective-permute-start | bytes 1572872 | tf_op jit(solution)/shard_map/ppermute | solution.py:376
  4.6 11.4 %collective-permute-done = bf16[2,4,64,512]{3,2,1,0:T(8,128)(2,1)S(1)} collective-permute-done((bf16[2,4,64,512]{3,2,1,0:T(8,128)(2,1)S(1)}, bf16[2,4,64,512]{3,2,1,0:T(8,128)(2,1)S(1)}, u32[]{:S(2)}, u32[]{:S(2)}) %collective-permute-start) | collective-permute-done | bytes 524320 | tf_op jit(solution)/shard_map/ppermute | solution.py:376
  15.9 0.8 fusion.3
  16.7 0.8 copy-done.5
  17.5 0.8 fusion.own
  18.3 0.8 collective-permute-start.2
  19.1 0.8 collective-permute-start.1
  20.0 0.7 collective-permute-start.3
  20.8 1.3 collective-permute-start.4
  22.2 51.1 %collective-permute-done.4.refs_12_ = bf16[8,128]{1,0:T(8,128)(2,1)S(1)} collective-permute-done((bf16[8,128]{1,0:T(8,128)(2,1)S(1)}, bf16[8,128]{1,0:T(8,128)(2,1)S(1)}, u32[]{:S(2)}, u32[]{:S(2)}) %collective-permute-start.4) | collective-permute-done | bytes 2080 | tf_op jit(solution)/shard_map/ppermute | solution.py:388
  73.3 1.3 collective-permute-start.7
  74.6 1.8 select_select_fusion
  76.4 1.3 collective-permute-start.6
  77.7 1.3 collective-permute-start.5
  79.0 12.9 %collective-permute-done.6.refs_3_ = bf16[1024,512]{1,0:T(8,128)(2,1)S(1)} collective-permute-done((bf16[1024,512]{1,0:T(8,128)(2,1)S(1)}, bf16[1024,512]{1,0:T(8,128)(2,1)S(1)}, u32[]{:S(2)}, u32[]{:S(2)}) %collective-permute-start.6) | collective-permute-done | bytes 1048608 | tf_op jit(solution)/shard_map/ppermute | solution.py:399
  92.0 11.2 %collective-permute-done.5.refs_2_ = bf16[1024,512]{1,0:T(8,128)(2,1)S(1)} collective-permute-done((bf16[1024,512]{1,0:T(8,128)(2,1)S(1)}, bf16[1024,512]{1,0:T(8,128)(2,1)S(1)}, u32[]{:S(2)}, u32[]{:S(2)}) %collective-permute-start.5) | collective-permute-done | bytes 1048608 | tf_op jit(solution)/shard_map/ppermute | solution.py:395
  103.2 1.5 pad_maximum_fusion
  104.9 1.3 collective-permute-start.18
  106.2 0.7 stack.37.where_ref
  106.9 2.1 %factor_rows.1 = (bf16[64,2048]{1,0:T(8,128)(2,1)}, bf16[64,2048]{1,0:T(8,128)(2,1)}, bf16[64,2048]{1,0:T(8,128)(2,1)}, bf16[64,2048]{1,0:T(8,128)(2,1)}, bf16[6...) custom-call(s32[5]{0:T(128)} %stack.37.where_ref, ...), custom_call_target="tpu_custom_call" | custom-call | tf_op jit(solution)/shard_map/factor_rows/pallas_call | solution.py:204
  109.0 0.7 collective-permute-start.8
  109.7 0.7 collective-permute-start.9
  110.3 0.7 collective-permute-start.10
  111.0 0.7 collective-permute-start.11
  111.7 0.7 collective-permute-start.12
  112.4 0.7 collective-permute-start.13
  113.1 0.7 collective-permute-start.14
  113.8 1.1 add_select_fusion.1
  114.9 0.7 collective-permute-start.17
  115.6 0.7 collective-permute-start.16
  116.3 0.7 collective-permute-start.15
  117.0 14.9 %collective-permute-done.18.refs_5_ = bf16[2048,512]{1,0:T(8,128)(2,1)} collective-permute-done((bf16[2048,512]{1,0:T(8,128)(2,1)}, bf16[2048,512]{1,0:T(8,128)(2,1)}, u32[]{:S(2)}, u32[]{:S(2)}) %collective-permute-start.18) | collective-permute-done | bytes 2097184 | tf_op jit(solution)/shard_map/ppermute | solution.py:403
  132.0 1.3 collective-permute-start.19
  133.3 2.1 %collective-permute-done.19 = bf16[64,2048]{1,0:T(8,128)(2,1)S(1)} collective-permute-done((bf16[64,2048]{1,0:T(8,128)(2,1)S(1)}, bf16[64,2048]{1,0:T(8,128)(2,1)S(1)}, u32[]{:S(2)}, u32[]{:S(2)}) %collective-permute-start.19) | collective-permute-done | bytes 262176 | tf_op jit(solution)/shard_map/ppermute | solution.py:349
  135.5 6.5 %collective-permute-start.22 = (bf16[64,2048]{1,0:T(8,128)(2,1)S(1)}, bf16[64,2048]{1,0:T(8,128)(2,1)S(1)}, u32[]{:S(2)}, u32[]{:S(2)}) collective-permute-start(bf16[64,2048]{1,0:T(8,128)(2,1)S(1)} %broadcast_select_fusion.refs_6_), channel_id=1, source_target_pairs={{0,48},{1,49},{2,50},{3,51},{4,84},{5,85},{6,86},{7,87},{8,56},{9,... | collective-permute-start | bytes 786440 | tf_op jit(solution)/shard_map/ppermute | solution.py:360
  142.0 0.6 collective-permute-start.21
  142.6 0.5 collective-permute-start.20
  143.0 4.6 %collective-permute-start.23 = (bf16[32,2048]{1,0:T(8,128)(2,1)S(1)}, bf16[32,2048]{1,0:T(8,128)(2,1)S(1)}, u32[]{:S(2)}, u32[]{:S(2)}) collective-permute-start(bf16[32,2048]{1,0:T(8,128)(2,1)S(1)} %constant_dynamic-slice_fusion), channel_id=1, source_target_pairs={{0,64},{1,65},{2,66},{3,67},{4,68},{5,69},{6,70},{7,71},{8,72},{9,... | collective-permute-start | bytes 393224 | tf_op jit(solution)/shard_map/ppermute | solution.py:356
  147.6 10.7 %collective-permute-done.23.refs_10_ = bf16[32,2048]{1,0:T(8,128)(2,1)S(1)} collective-permute-done((bf16[32,2048]{1,0:T(8,128)(2,1)S(1)}, bf16[32,2048]{1,0:T(8,128)(2,1)S(1)}, u32[]{:S(2)}, u32[]{:S(2)}) %collective-permute-start.23) | collective-permute-done | bytes 131104 | tf_op jit(solution)/shard_map/ppermute | solution.py:356
  158.3 1.0 collective-permute-done.21.refs_8_
  159.4 5.6 %collective-permute-done.20.refs_7_ = bf16[64,2048]{1,0:T(8,128)(2,1)S(1)} collective-permute-done((bf16[64,2048]{1,0:T(8,128)(2,1)S(1)}, bf16[64,2048]{1,0:T(8,128)(2,1)S(1)}, u32[]{:S(2)}, u32[]{:S(2)}) %collective-permute-start.20) | collective-permute-done | bytes 262176 | tf_op jit(solution)/shard_map/ppermute | solution.py:360
  165.0 2.6 %collective-permute-start.24 = (bf16[224,2048]{1,0:T(8,128)(2,1)S(1)}, bf16[224,2048]{1,0:T(8,128)(2,1)S(1)}, u32[]{:S(2)}, u32[]{:S(2)}) collective-permute-start(bf16[224,2048]{1,0:T(8,128)(2,1)S(1)} %pad_maximum_fusion.1), channel_id=1, source_target_pairs={{0,4},{1,5},{2,6},{3,7},{4,0},{5,1},{6,2},{7,3},{8,12},{9,13},{10,... | collective-permute-start | bytes 2752520 | tf_op jit(solution)/shard_map/ppermute | solution.py:362
  167.6 2.1 %collective-permute-done.24.refs_11_ = bf16[224,2048]{1,0:T(8,128)(2,1)S(1)} collective-permute-done((bf16[224,2048]{1,0:T(8,128)(2,1)S(1)}, bf16[224,2048]{1,0:T(8,128)(2,1)S(1)}, u32[]{:S(2)}, u32[]{:S(2)}) %collective-permute-start.24) | collective-permute-done | bytes 917536 | tf_op jit(solution)/shard_map/ppermute | solution.py:362
  169.8 0.9 copy-done.10
  170.7 11.2 %apply_rows.1 = bf16[512,2048]{1,0:T(8,128)(2,1)} custom-call(s32[5]{0:T(128)} %stack.37.where_ref, bf16[2048,512]{1,0:T(8,128)(2,1)} %copy-done, bf16[2048,512]{1,0:T(8,128)(2,1)} %copy-done.2, bf16[2048,512]{1,0:T(8,128)(2,1)} %copy-done.1, bf16[1024,512]{1,0:T(8,128)(2,1)} %copy-done.4, bf16[1024,512]{1,0:T(8,128)(2,1)} %copy-done.3, ...), custom_call_target="tpu_custom_call" | custom-call | tf_op jit(solution)/shard_map/apply_rows/pallas_call | solution.py:282
  (47 shorter events, 0.5 us)
Async XLA Ops:
  0.0 1.4 copy-start.11
  1.6 14.4 %collective-permute-start = (bf16[2,4,64,512]{3,2,1,0:T(8,128)(2,1)S(1)}, bf16[2,4,64,512]{3,2,1,0:T(8,128)(2,1)S(1)}, u32[]{:S(2)}, u32[]{:S(2)}) collective-permute-start(bf16[2,4,64,512]{3,2,1,0:T(8,128)(2,1)S(1)} %get-tuple-element.49), channel_id=1, source_target_pairs={{0,128},{1,129},{2,130},{3,131},{4,132},{5,133},{6,134},{7,135},{8... | collective-permute-start | bytes 1572872 | tf_op jit(solution)/shard_map/ppermute | solution.py:376
  15.9 1.6 copy-start.5
  18.3 58.1 %copy-start = (bf16[2048,512]{1,0:T(8,128)(2,1)}, bf16[2048,512]{1,0:T(8,128)(2,1)S(1)}, u32[]{:S(2)}) copy-start(bf16[2048,512]{1,0:T(8,128)(2,1)S(1)} %fusion.own) | copy-start | bytes 6291460
  18.3 2.4 %collective-permute-start.2 = (bf16[2048,512]{1,0:T(8,128)(2,1)S(1)}, bf16[2048,512]{1,0:T(8,128)(2,1)S(1)}, u32[]{:S(2)}, u32[]{:S(2)}) collective-permute-start(bf16[2048,512]{1,0:T(8,128)(2,1)S(1)} %fusion.own), channel_id=1, source_target_pairs={{0,3},{8,11},{12,15},{16,19},{24,27},{28,31},{32,35},{40,43},{44,4... | collective-permute-start | bytes 6291464 | tf_op jit(solution)/shard_map/ppermute | solution.py:385
  19.1 1.6 collective-permute-start.1
  20.0 0.7 collective-permute-start.3
  20.8 1.4 copy-start.1
  20.8 52.5 %copy-start.2 = (bf16[2048,512]{1,0:T(8,128)(2,1)}, bf16[2048,512]{1,0:T(8,128)(2,1)S(1)}, u32[]{:S(2)}) copy-start(bf16[2048,512]{1,0:T(8,128)(2,1)S(1)} %collective-permute-done.1.refs_0_) | copy-start | bytes 6291460
  20.8 52.5 %collective-permute-start.4 = (bf16[8,128]{1,0:T(8,128)(2,1)S(1)}, bf16[8,128]{1,0:T(8,128)(2,1)S(1)}, u32[]{:S(2)}, u32[]{:S(2)}) collective-permute-start(bf16[8,128]{1,0:T(8,128)(2,1)S(1)} %slice_add_fusion), channel_id=1, source_target_pairs={{8,4},{9,5},{10,6},{11,7},{24,20},{25,21},{26,22},{27,23},{40,36},... | collective-permute-start | bytes 6152 | tf_op jit(solution)/shard_map/ppermute | solution.py:388
  73.3 3.1 %copy-start.13 = (bf16[8,128]{1,0:T(8,128)(2,1)}, bf16[8,128]{1,0:T(8,128)(2,1)S(1)}, u32[]{:S(2)}) copy-start(bf16[8,128]{1,0:T(8,128)(2,1)S(1)} %collective-permute-done.4.refs_12_) | copy-start | bytes 6148
  73.3 33.6 %collective-permute-start.7 = (bf16[2048,512]{1,0:T(8,128)(2,1)S(1)}, bf16[2048,512]{1,0:T(8,128)(2,1)}, u32[]{:S(2)}, u32[]{:S(2)}) collective-permute-start(bf16[2048,512]{1,0:T(8,128)(2,1)S(1)} %fusion.own), channel_id=1, source_target_pairs={{4,7},{20,23},{36,39},{52,55},{68,71},{84,87},{100,103},{116,119}} | collective-permute-start | bytes 6291464 | tf_op jit(solution)/shard_map/ppermute | solution.py:402
  76.4 15.5 %collective-permute-start.6 = (bf16[1024,512]{1,0:T(8,128)(2,1)S(1)}, bf16[1024,512]{1,0:T(8,128)(2,1)S(1)}, u32[]{:S(2)}, u32[]{:S(2)}) collective-permute-start(bf16[1024,512]{1,0:T(8,128)(2,1)S(1)} %get-tuple-element.47), channel_id=1, source_target_pairs={{0,3},{3,2},{8,11},{11,10},{12,15},{15,14},{16,19},{19,18},{24,27}... | collective-permute-start | bytes 3145736 | tf_op jit(solution)/shard_map/ppermute | solution.py:399
  77.7 25.5 %collective-permute-start.5 = (bf16[1024,512]{1,0:T(8,128)(2,1)S(1)}, bf16[1024,512]{1,0:T(8,128)(2,1)S(1)}, u32[]{:S(2)}, u32[]{:S(2)}) collective-permute-start(bf16[1024,512]{1,0:T(8,128)(2,1)S(1)} %get-tuple-element.48), channel_id=1, source_target_pairs={{1,2},{2,3},{9,10},{10,11},{13,14},{14,15},{17,18},{18,19},{25,26}... | collective-permute-start | bytes 3145736 | tf_op jit(solution)/shard_map/ppermute | solution.py:395
  92.0 12.8 %copy-start.3 = (bf16[1024,512]{1,0:T(8,128)(2,1)}, bf16[1024,512]{1,0:T(8,128)(2,1)S(1)}, u32[]{:S(2)}) copy-start(bf16[1024,512]{1,0:T(8,128)(2,1)S(1)} %collective-permute-done.6.refs_3_) | copy-start | bytes 3145732
  103.2 1.7 copy-start.4
  104.9 27.1 %collective-permute-start.18 = (bf16[2048,512]{1,0:T(8,128)(2,1)}, bf16[2048,512]{1,0:T(8,128)(2,1)}, u32[]{:S(2)}, u32[]{:S(2)}) collective-permute-start(bf16[2048,512]{1,0:T(8,128)(2,1)} %pad_maximum_fusion), channel_id=1, source_target_pairs={{5,6},{6,7},{21,22},{22,23},{37,38},{38,39},{53,54},{54,55},{69,70... | collective-permute-start | bytes 6291464 | tf_op jit(solution)/shard_map/ppermute | solution.py:403
  109.0 2.7 %collective-permute-start.8 = (bf16[64,2048]{1,0:T(8,128)(2,1)}, bf16[64,2048]{1,0:T(8,128)(2,1)S(1)}, u32[]{:S(2)}, u32[]{:S(2)}) collective-permute-start(bf16[64,2048]{1,0:T(8,128)(2,1)} %get-tuple-element.37), channel_id=1, source_target_pairs={{0,16},{1,17},{2,18},{3,19}} | collective-permute-start | bytes 786440 | tf_op jit(solution)/shard_map/ppermute | solution.py:337
  109.7 2.8 %collective-permute-start.9 = (bf16[64,2048]{1,0:T(8,128)(2,1)}, bf16[64,2048]{1,0:T(8,128)(2,1)S(1)}, u32[]{:S(2)}, u32[]{:S(2)}) collective-permute-start(bf16[64,2048]{1,0:T(8,128)(2,1)} %get-tuple-element.38), channel_id=1, source_target_pairs={{0,32},{1,33},{2,34},{3,35}} | collective-permute-start | bytes 786440 | tf_op jit(solution)/shard_map/ppermute | solution.py:337
  110.3 2.8 %collective-permute-start.10 = (bf16[64,2048]{1,0:T(8,128)(2,1)}, bf16[64,2048]{1,0:T(8,128)(2,1)S(1)}, u32[]{:S(2)}, u32[]{:S(2)}) collective-permute-start(bf16[64,2048]{1,0:T(8,128)(2,1)} %get-tuple-element.39), channel_id=1, source_target_pairs={{0,48},{1,49},{2,50},{3,51}} | collective-permute-start | bytes 786440 | tf_op jit(solution)/shard_map/ppermute | solution.py:337
  111.0 2.8 %collective-permute-start.11 = (bf16[64,2048]{1,0:T(8,128)(2,1)}, bf16[64,2048]{1,0:T(8,128)(2,1)S(1)}, u32[]{:S(2)}, u32[]{:S(2)}) collective-permute-start(bf16[64,2048]{1,0:T(8,128)(2,1)} %get-tuple-element.40), channel_id=1, source_target_pairs={{0,64},{1,65},{2,66},{3,67}} | collective-permute-start | bytes 786440 | tf_op jit(solution)/shard_map/ppermute | solution.py:337
  111.7 2.1 %collective-permute-start.12 = (bf16[64,2048]{1,0:T(8,128)(2,1)}, bf16[64,2048]{1,0:T(8,128)(2,1)S(1)}, u32[]{:S(2)}, u32[]{:S(2)}) collective-permute-start(bf16[64,2048]{1,0:T(8,128)(2,1)} %get-tuple-element.41), channel_id=1, source_target_pairs={{0,80},{1,81},{2,82},{3,83}} | collective-permute-start | bytes 786440 | tf_op jit(solution)/shard_map/ppermute | solution.py:337
  112.4 1.4 collective-permute-start.13
  113.1 0.7 collective-permute-start.14
  114.9 2.1 %collective-permute-start.17 = (bf16[64,2048]{1,0:T(8,128)(2,1)S(1)}, bf16[64,2048]{1,0:T(8,128)(2,1)S(1)}, u32[]{:S(2)}, u32[]{:S(2)}) collective-permute-start(bf16[64,2048]{1,0:T(8,128)(2,1)S(1)} %add_select_fusion.1), channel_id=1, source_target_pairs={{0,128},{1,129},{2,130},{3,131},{16,144},{17,145},{18,146},{19,147... | collective-permute-start | bytes 786440 | tf_op jit(solution)/shard_map/ppermute | solution.py:345
  115.6 1.4 collective-permute-start.16
  116.3 0.7 collective-permute-start.15
  132.0 3.4 %collective-permute-start.19 = (bf16[64,2048]{1,0:T(8,128)(2,1)S(1)}, bf16[64,2048]{1,0:T(8,128)(2,1)S(1)}, u32[]{:S(2)}, u32[]{:S(2)}) collective-permute-start(bf16[64,2048]{1,0:T(8,128)(2,1)S(1)} %add_select_fusion), channel_id=1, source_target_pairs={{0,4},{1,5},{2,6},{3,7},{8,12},{9,13},{10,14},{11,15},{16,20},{17,... | collective-permute-start | bytes 786440 | tf_op jit(solution)/shard_map/ppermute | solution.py:349
  135.4 34.3 %copy-start.6 = (bf16[64,2048]{1,0:T(8,128)(2,1)}, bf16[64,2048]{1,0:T(8,128)(2,1)S(1)}, u32[]{:S(2)}) copy-start(bf16[64,2048]{1,0:T(8,128)(2,1)S(1)} %broadcast_select_fusion.refs_6_) | copy-start | bytes 786436
  135.5 22.9 %collective-permute-start.22 = (bf16[64,2048]{1,0:T(8,128)(2,1)S(1)}, bf16[64,2048]{1,0:T(8,128)(2,1)S(1)}, u32[]{:S(2)}, u32[]{:S(2)}) collective-permute-start(bf16[64,2048]{1,0:T(8,128)(2,1)S(1)} %broadcast_select_fusion.refs_6_), channel_id=1, source_target_pairs={{0,48},{1,49},{2,50},{3,51},{4,84},{5,85},{6,86},{7,87},{8,56},{9,... | collective-permute-start | bytes 786440 | tf_op jit(solution)/shard_map/ppermute | solution.py:360
  142.0 17.4 %collective-permute-start.21 = (bf16[64,2048]{1,0:T(8,128)(2,1)S(1)}, bf16[64,2048]{1,0:T(8,128)(2,1)S(1)}, u32[]{:S(2)}, u32[]{:S(2)}) collective-permute-start(bf16[64,2048]{1,0:T(8,128)(2,1)S(1)} %broadcast_select_fusion.refs_6_), channel_id=1, source_target_pairs={{0,32},{1,33},{2,34},{3,35},{4,100},{5,101},{6,102},{7,103},{8,40}... | collective-permute-start | bytes 786440 | tf_op jit(solution)/shard_map/ppermute | solution.py:360
  142.6 22.4 %collective-permute-start.20 = (bf16[64,2048]{1,0:T(8,128)(2,1)S(1)}, bf16[64,2048]{1,0:T(8,128)(2,1)S(1)}, u32[]{:S(2)}, u32[]{:S(2)}) collective-permute-start(bf16[64,2048]{1,0:T(8,128)(2,1)S(1)} %broadcast_select_fusion.refs_6_), channel_id=1, source_target_pairs={{0,16},{1,17},{2,18},{3,19},{4,116},{5,117},{6,118},{7,119},{8,24}... | collective-permute-start | bytes 786440 | tf_op jit(solution)/shard_map/ppermute | solution.py:360
  143.0 15.3 %collective-permute-start.23 = (bf16[32,2048]{1,0:T(8,128)(2,1)S(1)}, bf16[32,2048]{1,0:T(8,128)(2,1)S(1)}, u32[]{:S(2)}, u32[]{:S(2)}) collective-permute-start(bf16[32,2048]{1,0:T(8,128)(2,1)S(1)} %constant_dynamic-slice_fusion), channel_id=1, source_target_pairs={{0,64},{1,65},{2,66},{3,67},{4,68},{5,69},{6,70},{7,71},{8,72},{9,... | collective-permute-start | bytes 393224 | tf_op jit(solution)/shard_map/ppermute | solution.py:356
  158.3 11.4 %copy-start.12 = (bf16[32,2048]{1,0:T(8,128)(2,1)}, bf16[32,2048]{1,0:T(8,128)(2,1)S(1)}, u32[]{:S(2)}) copy-start(bf16[32,2048]{1,0:T(8,128)(2,1)S(1)} %collective-permute-done.23.refs_10_) | copy-start | bytes 393220
  158.3 11.4 %copy-start.7 = (bf16[64,2048]{1,0:T(8,128)(2,1)}, bf16[64,2048]{1,0:T(8,128)(2,1)S(1)}, u32[]{:S(2)}) copy-start(bf16[64,2048]{1,0:T(8,128)(2,1)S(1)} %collective-permute-done.22.refs_9_) | copy-start | bytes 786436
  159.4 10.4 %copy-start.8 = (bf16[64,2048]{1,0:T(8,128)(2,1)}, bf16[64,2048]{1,0:T(8,128)(2,1)S(1)}, u32[]{:S(2)}) copy-start(bf16[64,2048]{1,0:T(8,128)(2,1)S(1)} %collective-permute-done.21.refs_8_) | copy-start | bytes 786436
  165.0 4.8 %copy-start.9 = (bf16[64,2048]{1,0:T(8,128)(2,1)}, bf16[64,2048]{1,0:T(8,128)(2,1)S(1)}, u32[]{:S(2)}) copy-start(bf16[64,2048]{1,0:T(8,128)(2,1)S(1)} %collective-permute-done.20.refs_7_) | copy-start | bytes 786436
  165.0 4.7 %collective-permute-start.24 = (bf16[224,2048]{1,0:T(8,128)(2,1)S(1)}, bf16[224,2048]{1,0:T(8,128)(2,1)S(1)}, u32[]{:S(2)}, u32[]{:S(2)}) collective-permute-start(bf16[224,2048]{1,0:T(8,128)(2,1)S(1)} %pad_maximum_fusion.1), channel_id=1, source_target_pairs={{0,4},{1,5},{2,6},{3,7},{4,0},{5,1},{6,2},{7,3},{8,12},{9,13},{10,... | collective-permute-start | bytes 2752520 | tf_op jit(solution)/shard_map/ppermute | solution.py:362
  169.8 0.9 copy-start.10

commit v13 on v12

--- a/solution.py
+++ b/solution.py
@@ -11,7 +11,8 @@
 RANK = 64
 PW = 2048
 BLOCKS = PW // TILE
-ROOT_ITERS = 3
+MOST_STEPS = 8
+STEP_BOUND = 1e-4
 ALL = ("child", "row", "col")
 NT = (((1,), (1,)), ((), ()))
 NN = (((1,), (0,)), ((), ()))
@@ -63,7 +64,7 @@
     nb_ref[low, top] = g10.astype(jnp.bfloat16)
     nb_ref[low, low] = lower(g11).astype(jnp.bfloat16)
 
-    def step(_, carry):
+    def step(state):
         n00, n10, n11 = n_ref[top, top], n_ref[low, top], n_ref[low, low]
         b00, b10, b11 = nb_ref[top, top], nb_ref[low, top], nb_ref[low, low]
         scaled00 = tile_ref[top, top] * down0 * across0 - eye
@@ -86,9 +87,13 @@
         nb_ref[top, top] = n00.astype(jnp.bfloat16)
         nb_ref[low, top] = n10.astype(jnp.bfloat16)
         nb_ref[low, low] = n11.astype(jnp.bfloat16)
-        return carry
-
-    lax.fori_loop(0, ROOT_ITERS, step, 0)
+        return state[0] + 1, jnp.sum(p00 * p00 + p11 * p11 + p10 * p10)
+
+    lax.while_loop(
+        lambda state: jnp.logical_and(state[0] < MOST_STEPS, state[1] > STEP_BOUND),
+        step,
+        (jnp.int32(0), jnp.float32(1.0)),
+    )
     x_ref[top, top] = ((eye - n_ref[top, top]) * across0).astype(jnp.bfloat16)
     x_ref[top, low] = jnp.zeros((part, part), jnp.bfloat16)
     x_ref[low, top] = (-n_ref[low, top] * across0).astype(jnp.bfloat16)

time: 182 us -> 183 us (level)
  no operation moved by 1% of the time
where the time goes in v13:
time: 183 us; the launch traced here: 182 us
  waiting for transfers between devices  124 us (68%)
  starting transfers between devices  34.6 us (19%)
  Pallas kernels  13.3 us (7%)
  other arithmetic  5.42 us (3%)
  local copies, waits for them, and re-layouts  4.13 us (2%)
    ppermute x1, waiting for transfers between devices, shards(): lax.ppermute(near[:8, :128] + wrap[:8, :128], ALL, pairs_of(lambda c, zz,...  51.1 us
    ppermute x1, waiting for transfers between devices, shards(): lax.ppermute(jnp.concatenate([upper, lower], axis=0), ALL, moves(is_secon...  14.9 us
    ppermute x1, waiting for transfers between devices, shards(): lax.ppermute(jnp.where(second, held[HALF:], mixed), ALL, moves(is_other,...  12.9 us
    ppermute x1, waiting for transfers between devices, shards(): lax.ppermute(sent, ALL, pairs_of(lambda c, zz, yy, kk, j: (1 - c, zz, yy,...  11.4 us
    pallas_call x1, Pallas kernels, apply_rows(): pl.pallas_call(apply_kernel, out_shape=jax.ShapeDtypeStruct((TILE, PW), j...  11.2 us
    ppermute x1, waiting for transfers between devices, shards(): lax.ppermute(jnp.where(second, held[:HALF], near[:HALF]), ALL, moves(is_o...  11.2 us
    ppermute x1, waiting for transfers between devices, spread_rows(): half = lax.ppermute(part, ALL, across)  10 us
    ppermute x3, waiting for transfers between devices, spread_rows(): direct[by] = lax.ppermute(chunk, ALL, pairs)  7.65 us
  transfers between devices with their start and end apart: 25, of which 10 were waited for; matrix products, arithmetic and copies ran while one was open for 3% of the time, Pallas kernels for 1%

profile of v13, /device:TPU:7, one launch (start us, length us, event | category | flops | bytes accessed | tf_op | source)
XLA Modules:
  0.0 182.3 jit_solution(4944338140508656607)
XLA Ops:
  0.0 1.3 copy.8
  1.3 0.2 copy.10
  1.5 0.1 fusion.5
  1.6 3.0 %collective-permute-start = (bf16[2,4,64,512]{3,2,1,0:T(8,128)(2,1)S(1)}, bf16[2,4,64,512]{3,2,1,0:T(8,128)(2,1)S(1)}, u32[]{:S(2)}, u32[]{:S(2)}) collective-permute-start(bf16[2,4,64,512]{3,2,1,0:T(8,128)(2,1)S(1)} %get-tuple-element.49), channel_id=1, source_target_pairs={{0,128},{1,129},{2,130},{3,131},{4,132},{5,133},{6,134},{7,135},{8... | collective-permute-start | bytes 1572872 | tf_op jit(solution)/shard_map/ppermute | solution.py:381
  4.6 11.4 %collective-permute-done = bf16[2,4,64,512]{3,2,1,0:T(8,128)(2,1)S(1)} collective-permute-done((bf16[2,4,64,512]{3,2,1,0:T(8,128)(2,1)S(1)}, bf16[2,4,64,512]{3,2,1,0:T(8,128)(2,1)S(1)}, u32[]{:S(2)}, u32[]{:S(2)}) %collective-permute-start) | collective-permute-done | bytes 524320 | tf_op jit(solution)/shard_map/ppermute | solution.py:381
  15.9 0.8 fusion.3
  16.7 0.8 copy-done.5
  17.5 0.8 fusion.own
  18.3 0.8 collective-permute-start.2
  19.1 0.8 collective-permute-start.1
  20.0 0.7 collective-permute-start.3
  20.8 1.3 collective-permute-start.4
  22.2 51.1 %collective-permute-done.4.refs_12_ = bf16[8,128]{1,0:T(8,128)(2,1)S(1)} collective-permute-done((bf16[8,128]{1,0:T(8,128)(2,1)S(1)}, bf16[8,128]{1,0:T(8,128)(2,1)S(1)}, u32[]{:S(2)}, u32[]{:S(2)}) %collective-permute-start.4) | collective-permute-done | bytes 2080 | tf_op jit(solution)/shard_map/ppermute | solution.py:393
  73.3 1.3 collective-permute-start.7
  74.6 1.8 select_select_fusion
  76.4 1.3 collective-permute-start.6
  77.7 1.3 collective-permute-start.5
  79.0 12.9 %collective-permute-done.6.refs_3_ = bf16[1024,512]{1,0:T(8,128)(2,1)S(1)} collective-permute-done((bf16[1024,512]{1,0:T(8,128)(2,1)S(1)}, bf16[1024,512]{1,0:T(8,128)(2,1)S(1)}, u32[]{:S(2)}, u32[]{:S(2)}) %collective-permute-start.6) | collective-permute-done | bytes 1048608 | tf_op jit(solution)/shard_map/ppermute | solution.py:404
  92.0 11.2 %collective-permute-done.5.refs_2_ = bf16[1024,512]{1,0:T(8,128)(2,1)S(1)} collective-permute-done((bf16[1024,512]{1,0:T(8,128)(2,1)S(1)}, bf16[1024,512]{1,0:T(8,128)(2,1)S(1)}, u32[]{:S(2)}, u32[]{:S(2)}) %collective-permute-start.5) | collective-permute-done | bytes 1048608 | tf_op jit(solution)/shard_map/ppermute | solution.py:400
  103.2 1.5 pad_maximum_fusion
  104.9 1.3 collective-permute-start.18
  106.2 0.7 stack.37.where_ref
  106.9 2.1 %factor_rows.1 = (bf16[64,2048]{1,0:T(8,128)(2,1)}, bf16[64,2048]{1,0:T(8,128)(2,1)}, bf16[64,2048]{1,0:T(8,128)(2,1)}, bf16[64,2048]{1,0:T(8,128)(2,1)}, bf16[6...) custom-call(s32[5]{0:T(128)} %stack.37.where_ref, ...), custom_call_target="tpu_custom_call" | custom-call | tf_op jit(solution)/shard_map/factor_rows/pallas_call | solution.py:209
  109.0 0.7 collective-permute-start.8
  109.7 0.7 collective-permute-start.9
  110.3 0.7 collective-permute-start.10
  111.0 0.7 collective-permute-start.11
  111.7 0.7 collective-permute-start.12
  112.4 0.7 collective-permute-start.13
  113.1 0.7 collective-permute-start.14
  113.8 1.1 add_select_fusion.1
  114.9 0.7 collective-permute-start.17
  115.6 0.7 collective-permute-start.16
  116.3 0.7 collective-permute-start.15
  117.0 14.9 %collective-permute-done.18.refs_5_ = bf16[2048,512]{1,0:T(8,128)(2,1)} collective-permute-done((bf16[2048,512]{1,0:T(8,128)(2,1)}, bf16[2048,512]{1,0:T(8,128)(2,1)}, u32[]{:S(2)}, u32[]{:S(2)}) %collective-permute-start.18) | collective-permute-done | bytes 2097184 | tf_op jit(solution)/shard_map/ppermute | solution.py:408
  132.0 1.3 collective-permute-start.19
  133.3 2.1 %collective-permute-done.19 = bf16[64,2048]{1,0:T(8,128)(2,1)S(1)} collective-permute-done((bf16[64,2048]{1,0:T(8,128)(2,1)S(1)}, bf16[64,2048]{1,0:T(8,128)(2,1)S(1)}, u32[]{:S(2)}, u32[]{:S(2)}) %collective-permute-start.19) | collective-permute-done | bytes 262176 | tf_op jit(solution)/shard_map/ppermute | solution.py:354
  135.5 6.5 %collective-permute-start.22 = (bf16[64,2048]{1,0:T(8,128)(2,1)S(1)}, bf16[64,2048]{1,0:T(8,128)(2,1)S(1)}, u32[]{:S(2)}, u32[]{:S(2)}) collective-permute-start(bf16[64,2048]{1,0:T(8,128)(2,1)S(1)} %broadcast_select_fusion.refs_6_), channel_id=1, source_target_pairs={{0,48},{1,49},{2,50},{3,51},{4,84},{5,85},{6,86},{7,87},{8,56},{9,... | collective-permute-start | bytes 786440 | tf_op jit(solution)/shard_map/ppermute | solution.py:365
  142.0 0.3 collective-permute-start.21
  142.3 0.8 collective-permute-start.20
  143.0 4.3 %collective-permute-start.23 = (bf16[32,2048]{1,0:T(8,128)(2,1)S(1)}, bf16[32,2048]{1,0:T(8,128)(2,1)S(1)}, u32[]{:S(2)}, u32[]{:S(2)}) collective-permute-start(bf16[32,2048]{1,0:T(8,128)(2,1)S(1)} %constant_dynamic-slice_fusion), channel_id=1, source_target_pairs={{0,64},{1,65},{2,66},{3,67},{4,68},{5,69},{6,70},{7,71},{8,72},{9,... | collective-permute-start | bytes 393224 | tf_op jit(solution)/shard_map/ppermute | solution.py:361
  147.3 10.0 %collective-permute-done.23.refs_10_ = bf16[32,2048]{1,0:T(8,128)(2,1)S(1)} collective-permute-done((bf16[32,2048]{1,0:T(8,128)(2,1)S(1)}, bf16[32,2048]{1,0:T(8,128)(2,1)S(1)}, u32[]{:S(2)}, u32[]{:S(2)}) %collective-permute-start.23) | collective-permute-done | bytes 131104 | tf_op jit(solution)/shard_map/ppermute | solution.py:361
  157.3 2.0 %collective-permute-done.21.refs_8_ = bf16[64,2048]{1,0:T(8,128)(2,1)S(1)} collective-permute-done((bf16[64,2048]{1,0:T(8,128)(2,1)S(1)}, bf16[64,2048]{1,0:T(8,128)(2,1)S(1)}, u32[]{:S(2)}, u32[]{:S(2)}) %collective-permute-start.21) | collective-permute-done | bytes 262176 | tf_op jit(solution)/shard_map/ppermute | solution.py:365
  159.4 5.6 %collective-permute-done.20.refs_7_ = bf16[64,2048]{1,0:T(8,128)(2,1)S(1)} collective-permute-done((bf16[64,2048]{1,0:T(8,128)(2,1)S(1)}, bf16[64,2048]{1,0:T(8,128)(2,1)S(1)}, u32[]{:S(2)}, u32[]{:S(2)}) %collective-permute-start.20) | collective-permute-done | bytes 262176 | tf_op jit(solution)/shard_map/ppermute | solution.py:365
  165.0 2.9 %collective-permute-start.24 = (bf16[224,2048]{1,0:T(8,128)(2,1)S(1)}, bf16[224,2048]{1,0:T(8,128)(2,1)S(1)}, u32[]{:S(2)}, u32[]{:S(2)}) collective-permute-start(bf16[224,2048]{1,0:T(8,128)(2,1)S(1)} %pad_maximum_fusion.1), channel_id=1, source_target_pairs={{0,4},{1,5},{2,6},{3,7},{4,0},{5,1},{6,2},{7,3},{8,12},{9,13},{10,... | collective-permute-start | bytes 2752520 | tf_op jit(solution)/shard_map/ppermute | solution.py:367
  168.0 2.1 %collective-permute-done.24.refs_11_ = bf16[224,2048]{1,0:T(8,128)(2,1)S(1)} collective-permute-done((bf16[224,2048]{1,0:T(8,128)(2,1)S(1)}, bf16[224,2048]{1,0:T(8,128)(2,1)S(1)}, u32[]{:S(2)}, u32[]{:S(2)}) %collective-permute-start.24) | collective-permute-done | bytes 917536 | tf_op jit(solution)/shard_map/ppermute | solution.py:367
  170.1 0.9 copy-done.10
  171.0 11.2 %apply_rows.1 = bf16[512,2048]{1,0:T(8,128)(2,1)} custom-call(s32[5]{0:T(128)} %stack.37.where_ref, bf16[2048,512]{1,0:T(8,128)(2,1)} %copy-done, bf16[2048,512]{1,0:T(8,128)(2,1)} %copy-done.2, bf16[2048,512]{1,0:T(8,128)(2,1)} %copy-done.1, bf16[1024,512]{1,0:T(8,128)(2,1)} %copy-done.4, bf16[1024,512]{1,0:T(8,128)(2,1)} %copy-done.3, ...), custom_call_target="tpu_custom_call" | custom-call | tf_op jit(solution)/shard_map/apply_rows/pallas_call | solution.py:287
  (47 shorter events, 0.4 us)
Async XLA Ops:
  0.0 1.4 copy-start.11
  1.6 14.4 %collective-permute-start = (bf16[2,4,64,512]{3,2,1,0:T(8,128)(2,1)S(1)}, bf16[2,4,64,512]{3,2,1,0:T(8,128)(2,1)S(1)}, u32[]{:S(2)}, u32[]{:S(2)}) collective-permute-start(bf16[2,4,64,512]{3,2,1,0:T(8,128)(2,1)S(1)} %get-tuple-element.49), channel_id=1, source_target_pairs={{0,128},{1,129},{2,130},{3,131},{4,132},{5,133},{6,134},{7,135},{8... | collective-permute-start | bytes 1572872 | tf_op jit(solution)/shard_map/ppermute | solution.py:381
  15.9 1.6 copy-start.5
  18.3 58.1 %copy-start = (bf16[2048,512]{1,0:T(8,128)(2,1)}, bf16[2048,512]{1,0:T(8,128)(2,1)S(1)}, u32[]{:S(2)}) copy-start(bf16[2048,512]{1,0:T(8,128)(2,1)S(1)} %fusion.own) | copy-start | bytes 6291460
  18.3 2.4 %collective-permute-start.2 = (bf16[2048,512]{1,0:T(8,128)(2,1)S(1)}, bf16[2048,512]{1,0:T(8,128)(2,1)S(1)}, u32[]{:S(2)}, u32[]{:S(2)}) collective-permute-start(bf16[2048,512]{1,0:T(8,128)(2,1)S(1)} %fusion.own), channel_id=1, source_target_pairs={{0,3},{8,11},{12,15},{16,19},{24,27},{28,31},{32,35},{40,43},{44,4... | collective-permute-start | bytes 6291464 | tf_op jit(solution)/shard_map/ppermute | solution.py:390
  19.1 1.6 collective-permute-start.1
  20.0 0.7 collective-permute-start.3
  20.8 1.4 copy-start.1
  20.8 52.5 %copy-start.2 = (bf16[2048,512]{1,0:T(8,128)(2,1)}, bf16[2048,512]{1,0:T(8,128)(2,1)S(1)}, u32[]{:S(2)}) copy-start(bf16[2048,512]{1,0:T(8,128)(2,1)S(1)} %collective-permute-done.1.refs_0_) | copy-start | bytes 6291460
  20.8 52.5 %collective-permute-start.4 = (bf16[8,128]{1,0:T(8,128)(2,1)S(1)}, bf16[8,128]{1,0:T(8,128)(2,1)S(1)}, u32[]{:S(2)}, u32[]{:S(2)}) collective-permute-start(bf16[8,128]{1,0:T(8,128)(2,1)S(1)} %slice_add_fusion), channel_id=1, source_target_pairs={{8,4},{9,5},{10,6},{11,7},{24,20},{25,21},{26,22},{27,23},{40,36},... | collective-permute-start | bytes 6152 | tf_op jit(solution)/shard_map/ppermute | solution.py:393
  73.3 3.1 %copy-start.13 = (bf16[8,128]{1,0:T(8,128)(2,1)}, bf16[8,128]{1,0:T(8,128)(2,1)S(1)}, u32[]{:S(2)}) copy-start(bf16[8,128]{1,0:T(8,128)(2,1)S(1)} %collective-permute-done.4.refs_12_) | copy-start | bytes 6148
  73.3 33.6 %collective-permute-start.7 = (bf16[2048,512]{1,0:T(8,128)(2,1)S(1)}, bf16[2048,512]{1,0:T(8,128)(2,1)}, u32[]{:S(2)}, u32[]{:S(2)}) collective-permute-start(bf16[2048,512]{1,0:T(8,128)(2,1)S(1)} %fusion.own), channel_id=1, source_target_pairs={{4,7},{20,23},{36,39},{52,55},{68,71},{84,87},{100,103},{116,119}} | collective-permute-start | bytes 6291464 | tf_op jit(solution)/shard_map/ppermute | solution.py:407
  76.4 15.5 %collective-permute-start.6 = (bf16[1024,512]{1,0:T(8,128)(2,1)S(1)}, bf16[1024,512]{1,0:T(8,128)(2,1)S(1)}, u32[]{:S(2)}, u32[]{:S(2)}) collective-permute-start(bf16[1024,512]{1,0:T(8,128)(2,1)S(1)} %get-tuple-element.47), channel_id=1, source_target_pairs={{0,3},{3,2},{8,11},{11,10},{12,15},{15,14},{16,19},{19,18},{24,27}... | collective-permute-start | bytes 3145736 | tf_op jit(solution)/shard_map/ppermute | solution.py:404
  77.7 25.5 %collective-permute-start.5 = (bf16[1024,512]{1,0:T(8,128)(2,1)S(1)}, bf16[1024,512]{1,0:T(8,128)(2,1)S(1)}, u32[]{:S(2)}, u32[]{:S(2)}) collective-permute-start(bf16[1024,512]{1,0:T(8,128)(2,1)S(1)} %get-tuple-element.48), channel_id=1, source_target_pairs={{1,2},{2,3},{9,10},{10,11},{13,14},{14,15},{17,18},{18,19},{25,26}... | collective-permute-start | bytes 3145736 | tf_op jit(solution)/shard_map/ppermute | solution.py:400
  92.0 12.8 %copy-start.3 = (bf16[1024,512]{1,0:T(8,128)(2,1)}, bf16[1024,512]{1,0:T(8,128)(2,1)S(1)}, u32[]{:S(2)}) copy-start(bf16[1024,512]{1,0:T(8,128)(2,1)S(1)} %collective-permute-done.6.refs_3_) | copy-start | bytes 3145732
  103.2 1.7 copy-start.4
  104.9 27.1 %collective-permute-start.18 = (bf16[2048,512]{1,0:T(8,128)(2,1)}, bf16[2048,512]{1,0:T(8,128)(2,1)}, u32[]{:S(2)}, u32[]{:S(2)}) collective-permute-start(bf16[2048,512]{1,0:T(8,128)(2,1)} %pad_maximum_fusion), channel_id=1, source_target_pairs={{5,6},{6,7},{21,22},{22,23},{37,38},{38,39},{53,54},{54,55},{69,70... | collective-permute-start | bytes 6291464 | tf_op jit(solution)/shard_map/ppermute | solution.py:408
  109.0 2.7 %collective-permute-start.8 = (bf16[64,2048]{1,0:T(8,128)(2,1)}, bf16[64,2048]{1,0:T(8,128)(2,1)S(1)}, u32[]{:S(2)}, u32[]{:S(2)}) collective-permute-start(bf16[64,2048]{1,0:T(8,128)(2,1)} %get-tuple-element.37), channel_id=1, source_target_pairs={{0,16},{1,17},{2,18},{3,19}} | collective-permute-start | bytes 786440 | tf_op jit(solution)/shard_map/ppermute | solution.py:342
  109.7 2.8 %collective-permute-start.9 = (bf16[64,2048]{1,0:T(8,128)(2,1)}, bf16[64,2048]{1,0:T(8,128)(2,1)S(1)}, u32[]{:S(2)}, u32[]{:S(2)}) collective-permute-start(bf16[64,2048]{1,0:T(8,128)(2,1)} %get-tuple-element.38), channel_id=1, source_target_pairs={{0,32},{1,33},{2,34},{3,35}} | collective-permute-start | bytes 786440 | tf_op jit(solution)/shard_map/ppermute | solution.py:342
  110.3 2.8 %collective-permute-start.10 = (bf16[64,2048]{1,0:T(8,128)(2,1)}, bf16[64,2048]{1,0:T(8,128)(2,1)S(1)}, u32[]{:S(2)}, u32[]{:S(2)}) collective-permute-start(bf16[64,2048]{1,0:T(8,128)(2,1)} %get-tuple-element.39), channel_id=1, source_target_pairs={{0,48},{1,49},{2,50},{3,51}} | collective-permute-start | bytes 786440 | tf_op jit(solution)/shard_map/ppermute | solution.py:342
  111.0 2.8 %collective-permute-start.11 = (bf16[64,2048]{1,0:T(8,128)(2,1)}, bf16[64,2048]{1,0:T(8,128)(2,1)S(1)}, u32[]{:S(2)}, u32[]{:S(2)}) collective-permute-start(bf16[64,2048]{1,0:T(8,128)(2,1)} %get-tuple-element.40), channel_id=1, source_target_pairs={{0,64},{1,65},{2,66},{3,67}} | collective-permute-start | bytes 786440 | tf_op jit(solution)/shard_map/ppermute | solution.py:342
  111.7 2.1 %collective-permute-start.12 = (bf16[64,2048]{1,0:T(8,128)(2,1)}, bf16[64,2048]{1,0:T(8,128)(2,1)S(1)}, u32[]{:S(2)}, u32[]{:S(2)}) collective-permute-start(bf16[64,2048]{1,0:T(8,128)(2,1)} %get-tuple-element.41), channel_id=1, source_target_pairs={{0,80},{1,81},{2,82},{3,83}} | collective-permute-start | bytes 786440 | tf_op jit(solution)/shard_map/ppermute | solution.py:342
  112.4 1.4 collective-permute-start.13
  113.1 0.7 collective-permute-start.14
  114.9 2.1 %collective-permute-start.17 = (bf16[64,2048]{1,0:T(8,128)(2,1)S(1)}, bf16[64,2048]{1,0:T(8,128)(2,1)S(1)}, u32[]{:S(2)}, u32[]{:S(2)}) collective-permute-start(bf16[64,2048]{1,0:T(8,128)(2,1)S(1)} %add_select_fusion.1), channel_id=1, source_target_pairs={{0,128},{1,129},{2,130},{3,131},{16,144},{17,145},{18,146},{19,147... | collective-permute-start | bytes 786440 | tf_op jit(solution)/shard_map/ppermute | solution.py:350
  115.6 1.4 collective-permute-start.16
  116.3 0.7 collective-permute-start.15
  132.0 3.4 %collective-permute-start.19 = (bf16[64,2048]{1,0:T(8,128)(2,1)S(1)}, bf16[64,2048]{1,0:T(8,128)(2,1)S(1)}, u32[]{:S(2)}, u32[]{:S(2)}) collective-permute-start(bf16[64,2048]{1,0:T(8,128)(2,1)S(1)} %add_select_fusion), channel_id=1, source_target_pairs={{0,4},{1,5},{2,6},{3,7},{8,12},{9,13},{10,14},{11,15},{16,20},{17,... | collective-permute-start | bytes 786440 | tf_op jit(solution)/shard_map/ppermute | solution.py:354
  135.4 34.6 %copy-start.6 = (bf16[64,2048]{1,0:T(8,128)(2,1)}, bf16[64,2048]{1,0:T(8,128)(2,1)S(1)}, u32[]{:S(2)}) copy-start(bf16[64,2048]{1,0:T(8,128)(2,1)S(1)} %broadcast_select_fusion.refs_6_) | copy-start | bytes 786436
  135.5 21.9 %collective-permute-start.22 = (bf16[64,2048]{1,0:T(8,128)(2,1)S(1)}, bf16[64,2048]{1,0:T(8,128)(2,1)S(1)}, u32[]{:S(2)}, u32[]{:S(2)}) collective-permute-start(bf16[64,2048]{1,0:T(8,128)(2,1)S(1)} %broadcast_select_fusion.refs_6_), channel_id=1, source_target_pairs={{0,48},{1,49},{2,50},{3,51},{4,84},{5,85},{6,86},{7,87},{8,56},{9,... | collective-permute-start | bytes 786440 | tf_op jit(solution)/shard_map/ppermute | solution.py:365
  142.0 17.4 %collective-permute-start.21 = (bf16[64,2048]{1,0:T(8,128)(2,1)S(1)}, bf16[64,2048]{1,0:T(8,128)(2,1)S(1)}, u32[]{:S(2)}, u32[]{:S(2)}) collective-permute-start(bf16[64,2048]{1,0:T(8,128)(2,1)S(1)} %broadcast_select_fusion.refs_6_), channel_id=1, source_target_pairs={{0,32},{1,33},{2,34},{3,35},{4,100},{5,101},{6,102},{7,103},{8,40}... | collective-permute-start | bytes 786440 | tf_op jit(solution)/shard_map/ppermute | solution.py:365
  142.3 22.7 %collective-permute-start.20 = (bf16[64,2048]{1,0:T(8,128)(2,1)S(1)}, bf16[64,2048]{1,0:T(8,128)(2,1)S(1)}, u32[]{:S(2)}, u32[]{:S(2)}) collective-permute-start(bf16[64,2048]{1,0:T(8,128)(2,1)S(1)} %broadcast_select_fusion.refs_6_), channel_id=1, source_target_pairs={{0,16},{1,17},{2,18},{3,19},{4,116},{5,117},{6,118},{7,119},{8,24}... | collective-permute-start | bytes 786440 | tf_op jit(solution)/shard_map/ppermute | solution.py:365
  143.0 14.3 %collective-permute-start.23 = (bf16[32,2048]{1,0:T(8,128)(2,1)S(1)}, bf16[32,2048]{1,0:T(8,128)(2,1)S(1)}, u32[]{:S(2)}, u32[]{:S(2)}) collective-permute-start(bf16[32,2048]{1,0:T(8,128)(2,1)S(1)} %constant_dynamic-slice_fusion), channel_id=1, source_target_pairs={{0,64},{1,65},{2,66},{3,67},{4,68},{5,69},{6,70},{7,71},{8,72},{9,... | collective-permute-start | bytes 393224 | tf_op jit(solution)/shard_map/ppermute | solution.py:361
  157.3 12.8 %copy-start.12 = (bf16[32,2048]{1,0:T(8,128)(2,1)}, bf16[32,2048]{1,0:T(8,128)(2,1)S(1)}, u32[]{:S(2)}) copy-start(bf16[32,2048]{1,0:T(8,128)(2,1)S(1)} %collective-permute-done.23.refs_10_) | copy-start | bytes 393220
  157.3 12.8 %copy-start.7 = (bf16[64,2048]{1,0:T(8,128)(2,1)}, bf16[64,2048]{1,0:T(8,128)(2,1)S(1)}, u32[]{:S(2)}) copy-start(bf16[64,2048]{1,0:T(8,128)(2,1)S(1)} %collective-permute-done.22.refs_9_) | copy-start | bytes 786436
  159.4 10.7 %copy-start.8 = (bf16[64,2048]{1,0:T(8,128)(2,1)}, bf16[64,2048]{1,0:T(8,128)(2,1)S(1)}, u32[]{:S(2)}) copy-start(bf16[64,2048]{1,0:T(8,128)(2,1)S(1)} %collective-permute-done.21.refs_8_) | copy-start | bytes 786436
  165.0 5.1 %copy-start.9 = (bf16[64,2048]{1,0:T(8,128)(2,1)}, bf16[64,2048]{1,0:T(8,128)(2,1)S(1)}, u32[]{:S(2)}) copy-start(bf16[64,2048]{1,0:T(8,128)(2,1)S(1)} %collective-permute-done.20.refs_7_) | copy-start | bytes 786436
  165.0 5.0 %collective-permute-start.24 = (bf16[224,2048]{1,0:T(8,128)(2,1)S(1)}, bf16[224,2048]{1,0:T(8,128)(2,1)S(1)}, u32[]{:S(2)}, u32[]{:S(2)}) collective-permute-start(bf16[224,2048]{1,0:T(8,128)(2,1)S(1)} %pad_maximum_fusion.1), channel_id=1, source_target_pairs={{0,4},{1,5},{2,6},{3,7},{4,0},{5,1},{6,2},{7,3},{8,12},{9,13},{10,... | collective-permute-start | bytes 2752520 | tf_op jit(solution)/shard_map/ppermute | solution.py:367
  170.1 0.9 copy-start.10

commit v14 on v13

--- a/solution.py
+++ b/solution.py
@@ -350,7 +350,7 @@
         got = lax.ppermute(chunk, ALL, pairs)
         total = got if total is None else total + got
     chunk = jnp.where(y == 0, chunk, total)
-    chunk, late_far = lax.optimization_barrier((chunk, late_far))
+
     got = lax.ppermute(
         chunk, ALL, pairs_of(lambda c, zz, yy, kk, j: (c, zz, yy, 1, j) if kk == 0 else None)
     )

time: 183 us -> 176 us (0.962)
  waiting for transfers between devices: 124 us -> 115 us
  other arithmetic: 5.42 us -> 7.53 us
    ppermute x1, waiting for transfers between devices: 14.9 us -> 0.01 us  [shards(): lax.ppermute(jnp.concatenate([upper, lower], axis=0), ALL, moves(is_secon...]
    ppermute x1, waiting for transfers between devices: 2.12 us -> 8.69 us  [spread_rows(): lax.ppermute(chunk, ALL, pairs_of(lambda c, zz, yy, kk, j: (c, zz, yy, 1,...]
    ppermute x3, starting transfers between devices: 7.57 us -> 4.6 us  [spread_rows(): direct[by] = lax.ppermute(chunk, ALL, pairs)]
  transfers between devices with their start and end apart: 25 -> 25, of which waited for: 10 -> 9; matrix products, arithmetic and copies ran while one was open for 3% -> 4% of each run, Pallas kernels for 1% -> 0%
where the time goes in v14:
time: 176 us; the launch traced here: 174 us
  waiting for transfers between devices  115 us (65%)
  starting transfers between devices  33.6 us (19%)
  Pallas kernels  13.3 us (8%)
  other arithmetic  7.53 us (4%)
  local copies, waits for them, and re-layouts  3.09 us (2%)
    ppermute x1, waiting for transfers between devices, shards(): lax.ppermute(near[:8, :128] + wrap[:8, :128], ALL, pairs_of(lambda c, zz,...  51.5 us
    ppermute x1, waiting for transfers between devices, shards(): lax.ppermute(jnp.where(second, held[HALF:], mixed), ALL, moves(is_other,...  12.5 us
    ppermute x1, waiting for transfers between devices, shards(): lax.ppermute(sent, ALL, pairs_of(lambda c, zz, yy, kk, j: (1 - c, zz, yy,...  11.4 us
    ppermute x1, waiting for transfers between devices, shards(): lax.ppermute(jnp.where(second, held[:HALF], near[:HALF]), ALL, moves(is_o...  11.3 us
    pallas_call x1, Pallas kernels, apply_rows(): pl.pallas_call(apply_kernel, out_shape=jax.ShapeDtypeStruct((TILE, PW), j...  11.2 us
    ppermute x1, waiting for transfers between devices, spread_rows(): half = lax.ppermute(part, ALL, across)  11.1 us
    ppermute x1, waiting for transfers between devices, spread_rows(): lax.ppermute(chunk, ALL, pairs_of(lambda c, zz, yy, kk, j: (c, zz, yy, 1,...  8.69 us
    ppermute x3, waiting for transfers between devices, spread_rows(): direct[by] = lax.ppermute(chunk, ALL, pairs)  6.64 us
  transfers between devices with their start and end apart: 25, of which 9 were waited for; matrix products, arithmetic and copies ran while one was open for 4% of the time, Pallas kernels for 0%

profile of v14, /device:TPU:7, one launch (start us, length us, event | category | flops | bytes accessed | tf_op | source)
XLA Modules:
  0.0 174.2 jit_solution(8658594459312959318)
XLA Ops:
  0.0 1.3 copy.8
  1.3 0.2 copy.10
  1.5 0.1 fusion.5
  1.6 3.0 %collective-permute-start = (bf16[2,4,64,512]{3,2,1,0:T(8,128)(2,1)S(1)}, bf16[2,4,64,512]{3,2,1,0:T(8,128)(2,1)S(1)}, u32[]{:S(2)}, u32[]{:S(2)}) collective-permute-start(bf16[2,4,64,512]{3,2,1,0:T(8,128)(2,1)S(1)} %get-tuple-element.45), channel_id=1, source_target_pairs={{0,128},{1,129},{2,130},{3,131},{4,132},{5,133},{6,134},{7,135},{8... | collective-permute-start | bytes 1572872 | tf_op jit(solution)/shard_map/ppermute | solution.py:381
  4.6 11.4 %collective-permute-done = bf16[2,4,64,512]{3,2,1,0:T(8,128)(2,1)S(1)} collective-permute-done((bf16[2,4,64,512]{3,2,1,0:T(8,128)(2,1)S(1)}, bf16[2,4,64,512]{3,2,1,0:T(8,128)(2,1)S(1)}, u32[]{:S(2)}, u32[]{:S(2)}) %collective-permute-start) | collective-permute-done | bytes 524320 | tf_op jit(solution)/shard_map/ppermute | solution.py:381
  15.9 0.8 fusion.3
  16.7 0.8 copy-done.5
  17.5 0.8 fusion.own
  18.3 0.8 collective-permute-start.2
  19.1 0.8 collective-permute-start.1
  19.9 0.1 slice.38
  20.0 0.7 collective-permute-start.3
  20.8 1.3 collective-permute-start.4
  22.2 51.5 %collective-permute-done.4.refs_12_ = bf16[8,128]{1,0:T(8,128)(2,1)S(1)} collective-permute-done((bf16[8,128]{1,0:T(8,128)(2,1)S(1)}, bf16[8,128]{1,0:T(8,128)(2,1)S(1)}, u32[]{:S(2)}, u32[]{:S(2)}) %collective-permute-start.4) | collective-permute-done | bytes 2080 | tf_op jit(solution)/shard_map/ppermute | solution.py:393
  73.7 1.3 collective-permute-start.7
  75.0 3.1 %select_select_fusion = (bf16[1024,512]{1,0:T(8,128)(2,1)}, bf16[1024,512]{1,0:T(8,128)(2,1)}) fusion(bf16[1024,512]{1,0:T(8,128)(2,1)S(1)} %collective-permute-done.3, bf16[2048,512]{1,0:T(8,128)(2,1)} %copy-done.1, bf16[2048,512]{1,0:T(8,128)(2,1)S(1)} %fusion.own, pred[]{:T(512)S(6)} %eq.26, pred[]{:T(512)S(6)} %and.36, bf16[2048,512]{1,0:T(8,128)(2,1)} %copy-done.2), kind=kLoop, calls=%fused_computation.9 | loop fusion | flops 1572864 | bytes 7340034 | tf_op jit(solution)/shard_map/jit(_where)/select_n | solution.py:405
  78.2 1.3 collective-permute-start.6
  79.5 1.3 collective-permute-start.5
  80.8 0.7 stack.37.where_ref
  81.4 12.5 %collective-permute-done.6.refs_3_ = bf16[1024,512]{1,0:T(8,128)(2,1)S(1)} collective-permute-done((bf16[1024,512]{1,0:T(8,128)(2,1)}, bf16[1024,512]{1,0:T(8,128)(2,1)S(1)}, u32[]{:S(2)}, u32[]{:S(2)}) %collective-permute-start.6) | collective-permute-done | bytes 1048608 | tf_op jit(solution)/shard_map/ppermute | solution.py:404
  93.9 11.3 %collective-permute-done.5.refs_2_ = bf16[1024,512]{1,0:T(8,128)(2,1)} collective-permute-done((bf16[1024,512]{1,0:T(8,128)(2,1)}, bf16[1024,512]{1,0:T(8,128)(2,1)}, u32[]{:S(2)}, u32[]{:S(2)}) %collective-permute-start.5) | collective-permute-done | bytes 1048608 | tf_op jit(solution)/shard_map/ppermute | solution.py:400
  105.3 2.1 %factor_rows.1 = (bf16[64,2048]{1,0:T(8,128)(2,1)}, bf16[64,2048]{1,0:T(8,128)(2,1)}, bf16[64,2048]{1,0:T(8,128)(2,1)}, bf16[64,2048]{1,0:T(8,128)(2,1)}, bf16[6...) custom-call(s32[5]{0:T(128)} %stack.37.where_ref, ...), custom_call_target="tpu_custom_call" | custom-call | tf_op jit(solution)/shard_map/factor_rows/pallas_call | solution.py:209
  107.3 0.8 collective-permute-start.9
  108.1 0.7 collective-permute-start.10
  108.8 0.7 collective-permute-start.11
  109.5 0.7 collective-permute-start.12
  110.2 0.7 collective-permute-start.13
  110.9 0.7 collective-permute-start.14
  111.6 0.7 collective-permute-start.15
  112.3 1.1 add_select_fusion.1
  113.4 0.7 collective-permute-start.18
  114.1 0.7 collective-permute-start.17
  114.8 0.7 collective-permute-start.16
  115.5 1.3 collective-permute-start.19
  116.9 1.4 pad_maximum_fusion
  118.2 1.3 collective-permute-start.8
  119.5 8.7 %collective-permute-done.19 = bf16[64,2048]{1,0:T(8,128)(2,1)} collective-permute-done((bf16[64,2048]{1,0:T(8,128)(2,1)S(1)}, bf16[64,2048]{1,0:T(8,128)(2,1)}, u32[]{:S(2)}, u32[]{:S(2)}) %collective-permute-start.19) | collective-permute-done | bytes 262176 | tf_op jit(solution)/shard_map/ppermute | solution.py:354
  128.2 1.0 broadcast_select_fusion.refs_6_
  129.2 3.9 %collective-permute-start.22 = (bf16[64,2048]{1,0:T(8,128)(2,1)S(1)}, bf16[64,2048]{1,0:T(8,128)(2,1)S(1)}, u32[]{:S(2)}, u32[]{:S(2)}) collective-permute-start(bf16[64,2048]{1,0:T(8,128)(2,1)S(1)} %broadcast_select_fusion.refs_6_), channel_id=1, source_target_pairs={{0,48},{1,49},{2,50},{3,51},{4,84},{5,85},{6,86},{7,87},{8,56},{9,... | collective-permute-start | bytes 786440 | tf_op jit(solution)/shard_map/ppermute | solution.py:365
  133.1 0.3 collective-permute-start.21
  133.4 0.5 collective-permute-start.20
  133.8 4.6 %collective-permute-start.23 = (bf16[32,2048]{1,0:T(8,128)(2,1)S(1)}, bf16[32,2048]{1,0:T(8,128)(2,1)S(1)}, u32[]{:S(2)}, u32[]{:S(2)}) collective-permute-start(bf16[32,2048]{1,0:T(8,128)(2,1)S(1)} %constant_dynamic-slice_fusion), channel_id=1, source_target_pairs={{0,64},{1,65},{2,66},{3,67},{4,68},{5,69},{6,70},{7,71},{8,72},{9,... | collective-permute-start | bytes 393224 | tf_op jit(solution)/shard_map/ppermute | solution.py:361
  138.4 11.1 %collective-permute-done.23.refs_10_ = bf16[32,2048]{1,0:T(8,128)(2,1)S(1)} collective-permute-done((bf16[32,2048]{1,0:T(8,128)(2,1)S(1)}, bf16[32,2048]{1,0:T(8,128)(2,1)S(1)}, u32[]{:S(2)}, u32[]{:S(2)}) %collective-permute-start.23) | collective-permute-done | bytes 131104 | tf_op jit(solution)/shard_map/ppermute | solution.py:361
  149.5 1.4 collective-permute-done.21.refs_8_
  150.9 5.2 %collective-permute-done.20.refs_7_ = bf16[64,2048]{1,0:T(8,128)(2,1)S(1)} collective-permute-done((bf16[64,2048]{1,0:T(8,128)(2,1)S(1)}, bf16[64,2048]{1,0:T(8,128)(2,1)S(1)}, u32[]{:S(2)}, u32[]{:S(2)}) %collective-permute-start.20) | collective-permute-done | bytes 262176 | tf_op jit(solution)/shard_map/ppermute | solution.py:365
  156.2 4.5 %collective-permute-start.24 = (bf16[224,2048]{1,0:T(8,128)(2,1)S(1)}, bf16[224,2048]{1,0:T(8,128)(2,1)}, u32[]{:S(2)}, u32[]{:S(2)}) collective-permute-start(bf16[224,2048]{1,0:T(8,128)(2,1)S(1)} %pad_maximum_fusion.1), channel_id=1, source_target_pairs={{0,4},{1,5},{2,6},{3,7},{4,0},{5,1},{6,2},{7,3},{8,12},{9,13},{10,... | collective-permute-start | bytes 2752520 | tf_op jit(solution)/shard_map/ppermute | solution.py:367
  160.7 2.2 %collective-permute-done.24.refs_11_ = bf16[224,2048]{1,0:T(8,128)(2,1)} collective-permute-done((bf16[224,2048]{1,0:T(8,128)(2,1)S(1)}, bf16[224,2048]{1,0:T(8,128)(2,1)}, u32[]{:S(2)}, u32[]{:S(2)}) %collective-permute-start.24) | collective-permute-done | bytes 917536 | tf_op jit(solution)/shard_map/ppermute | solution.py:367
  162.9 11.2 %apply_rows.1 = bf16[512,2048]{1,0:T(8,128)(2,1)} custom-call(s32[5]{0:T(128)} %stack.37.where_ref, bf16[2048,512]{1,0:T(8,128)(2,1)} %copy-done, bf16[2048,512]{1,0:T(8,128)(2,1)} %copy-done.2, bf16[2048,512]{1,0:T(8,128)(2,1)} %copy-done.1, bf16[1024,512]{1,0:T(8,128)(2,1)} %collective-permute-done.5.refs_2_, bf16[1024,512]{1,0:T(8,128)(2,1)} %copy-done.3, ...), custom_call_target="tpu_custom_call" | custom-call | tf_op jit(solution)/shard_map/apply_rows/pallas_call | solution.py:287
  (45 shorter events, 0.3 us)
Async XLA Ops:
  0.0 1.4 copy-start.10
  1.6 14.4 %collective-permute-start = (bf16[2,4,64,512]{3,2,1,0:T(8,128)(2,1)S(1)}, bf16[2,4,64,512]{3,2,1,0:T(8,128)(2,1)S(1)}, u32[]{:S(2)}, u32[]{:S(2)}) collective-permute-start(bf16[2,4,64,512]{3,2,1,0:T(8,128)(2,1)S(1)} %get-tuple-element.45), channel_id=1, source_target_pairs={{0,128},{1,129},{2,130},{3,131},{4,132},{5,133},{6,134},{7,135},{8... | collective-permute-start | bytes 1572872 | tf_op jit(solution)/shard_map/ppermute | solution.py:381
  15.9 1.6 copy-start.5
  18.3 59.8 %copy-start = (bf16[2048,512]{1,0:T(8,128)(2,1)}, bf16[2048,512]{1,0:T(8,128)(2,1)S(1)}, u32[]{:S(2)}) copy-start(bf16[2048,512]{1,0:T(8,128)(2,1)S(1)} %fusion.own) | copy-start | bytes 6291460
  18.3 2.4 %collective-permute-start.2 = (bf16[2048,512]{1,0:T(8,128)(2,1)S(1)}, bf16[2048,512]{1,0:T(8,128)(2,1)S(1)}, u32[]{:S(2)}, u32[]{:S(2)}) collective-permute-start(bf16[2048,512]{1,0:T(8,128)(2,1)S(1)} %fusion.own), channel_id=1, source_target_pairs={{0,3},{8,11},{12,15},{16,19},{24,27},{28,31},{32,35},{40,43},{44,4... | collective-permute-start | bytes 6291464 | tf_op jit(solution)/shard_map/ppermute | solution.py:390
  19.1 1.6 collective-permute-start.1
  20.0 0.7 collective-permute-start.3
  20.8 1.4 copy-start.1
  20.8 52.9 %copy-start.2 = (bf16[2048,512]{1,0:T(8,128)(2,1)}, bf16[2048,512]{1,0:T(8,128)(2,1)S(1)}, u32[]{:S(2)}) copy-start(bf16[2048,512]{1,0:T(8,128)(2,1)S(1)} %collective-permute-done.1.refs_0_) | copy-start | bytes 6291460
  20.8 52.9 %collective-permute-start.4 = (bf16[8,128]{1,0:T(8,128)(2,1)S(1)}, bf16[8,128]{1,0:T(8,128)(2,1)S(1)}, u32[]{:S(2)}, u32[]{:S(2)}) collective-permute-start(bf16[8,128]{1,0:T(8,128)(2,1)S(1)} %slice_add_fusion), channel_id=1, source_target_pairs={{8,4},{9,5},{10,6},{11,7},{24,20},{25,21},{26,22},{27,23},{40,36},... | collective-permute-start | bytes 6152 | tf_op jit(solution)/shard_map/ppermute | solution.py:393
  73.7 4.5 %copy-start.12 = (bf16[8,128]{1,0:T(8,128)(2,1)}, bf16[8,128]{1,0:T(8,128)(2,1)S(1)}, u32[]{:S(2)}) copy-start(bf16[8,128]{1,0:T(8,128)(2,1)S(1)} %collective-permute-done.4.refs_12_) | copy-start | bytes 6148
  73.7 31.6 %collective-permute-start.7 = (bf16[2048,512]{1,0:T(8,128)(2,1)S(1)}, bf16[2048,512]{1,0:T(8,128)(2,1)}, u32[]{:S(2)}, u32[]{:S(2)}) collective-permute-start(bf16[2048,512]{1,0:T(8,128)(2,1)S(1)} %fusion.own), channel_id=1, source_target_pairs={{4,7},{20,23},{36,39},{52,55},{68,71},{84,87},{100,103},{116,119}} | collective-permute-start | bytes 6291464 | tf_op jit(solution)/shard_map/ppermute | solution.py:407
  78.2 15.7 %collective-permute-start.6 = (bf16[1024,512]{1,0:T(8,128)(2,1)}, bf16[1024,512]{1,0:T(8,128)(2,1)S(1)}, u32[]{:S(2)}, u32[]{:S(2)}) collective-permute-start(bf16[1024,512]{1,0:T(8,128)(2,1)} %get-tuple-element.43), channel_id=1, source_target_pairs={{0,3},{3,2},{8,11},{11,10},{12,15},{15,14},{16,19},{19,18},{24,27}... | collective-permute-start | bytes 3145736 | tf_op jit(solution)/shard_map/ppermute | solution.py:404
  79.5 25.8 %collective-permute-start.5 = (bf16[1024,512]{1,0:T(8,128)(2,1)}, bf16[1024,512]{1,0:T(8,128)(2,1)}, u32[]{:S(2)}, u32[]{:S(2)}) collective-permute-start(bf16[1024,512]{1,0:T(8,128)(2,1)} %get-tuple-element.44), channel_id=1, source_target_pairs={{1,2},{2,3},{9,10},{10,11},{13,14},{14,15},{17,18},{18,19},{25,26}... | collective-permute-start | bytes 3145736 | tf_op jit(solution)/shard_map/ppermute | solution.py:400
  93.9 11.3 %copy-start.3 = (bf16[1024,512]{1,0:T(8,128)(2,1)}, bf16[1024,512]{1,0:T(8,128)(2,1)S(1)}, u32[]{:S(2)}) copy-start(bf16[1024,512]{1,0:T(8,128)(2,1)S(1)} %collective-permute-done.6.refs_3_) | copy-start | bytes 3145732
  107.3 9.5 %copy-start.4 = (bf16[1024,512]{1,0:T(8,128)(2,1)S(1)}, bf16[1024,512]{1,0:T(8,128)(2,1)}, u32[]{:S(2)}) copy-start(bf16[1024,512]{1,0:T(8,128)(2,1)} %copy-done.3) | copy-start | bytes 3145732
  107.3 3.6 %collective-permute-start.9 = (bf16[64,2048]{1,0:T(8,128)(2,1)}, bf16[64,2048]{1,0:T(8,128)(2,1)S(1)}, u32[]{:S(2)}, u32[]{:S(2)}) collective-permute-start(bf16[64,2048]{1,0:T(8,128)(2,1)} %get-tuple-element.35), channel_id=1, source_target_pairs={{0,16},{1,17},{2,18},{3,19}} | collective-permute-start | bytes 786440 | tf_op jit(solution)/shard_map/ppermute | solution.py:342
  108.1 3.4 %collective-permute-start.10 = (bf16[64,2048]{1,0:T(8,128)(2,1)}, bf16[64,2048]{1,0:T(8,128)(2,1)S(1)}, u32[]{:S(2)}, u32[]{:S(2)}) collective-permute-start(bf16[64,2048]{1,0:T(8,128)(2,1)} %get-tuple-element.36), channel_id=1, source_target_pairs={{0,32},{1,33},{2,34},{3,35}} | collective-permute-start | bytes 786440 | tf_op jit(solution)/shard_map/ppermute | solution.py:342
  108.8 3.5 %collective-permute-start.11 = (bf16[64,2048]{1,0:T(8,128)(2,1)}, bf16[64,2048]{1,0:T(8,128)(2,1)S(1)}, u32[]{:S(2)}, u32[]{:S(2)}) collective-permute-start(bf16[64,2048]{1,0:T(8,128)(2,1)} %get-tuple-element.37), channel_id=1, source_target_pairs={{0,48},{1,49},{2,50},{3,51}} | collective-permute-start | bytes 786440 | tf_op jit(solution)/shard_map/ppermute | solution.py:342
  109.5 2.8 %collective-permute-start.12 = (bf16[64,2048]{1,0:T(8,128)(2,1)}, bf16[64,2048]{1,0:T(8,128)(2,1)S(1)}, u32[]{:S(2)}, u32[]{:S(2)}) collective-permute-start(bf16[64,2048]{1,0:T(8,128)(2,1)} %get-tuple-element.38), channel_id=1, source_target_pairs={{0,64},{1,65},{2,66},{3,67}} | collective-permute-start | bytes 786440 | tf_op jit(solution)/shard_map/ppermute | solution.py:342
  110.2 2.1 %collective-permute-start.13 = (bf16[64,2048]{1,0:T(8,128)(2,1)}, bf16[64,2048]{1,0:T(8,128)(2,1)S(1)}, u32[]{:S(2)}, u32[]{:S(2)}) collective-permute-start(bf16[64,2048]{1,0:T(8,128)(2,1)} %get-tuple-element.39), channel_id=1, source_target_pairs={{0,80},{1,81},{2,82},{3,83}} | collective-permute-start | bytes 786440 | tf_op jit(solution)/shard_map/ppermute | solution.py:342
  110.9 1.4 collective-permute-start.14
  111.6 0.7 collective-permute-start.15
  113.4 2.1 %collective-permute-start.18 = (bf16[64,2048]{1,0:T(8,128)(2,1)S(1)}, bf16[64,2048]{1,0:T(8,128)(2,1)S(1)}, u32[]{:S(2)}, u32[]{:S(2)}) collective-permute-start(bf16[64,2048]{1,0:T(8,128)(2,1)S(1)} %add_select_fusion.1), channel_id=1, source_target_pairs={{0,128},{1,129},{2,130},{3,131},{16,144},{17,145},{18,146},{19,147... | collective-permute-start | bytes 786440 | tf_op jit(solution)/shard_map/ppermute | solution.py:350
  114.1 1.4 collective-permute-start.17
  114.8 0.7 collective-permute-start.16
  115.5 12.7 %collective-permute-start.19 = (bf16[64,2048]{1,0:T(8,128)(2,1)S(1)}, bf16[64,2048]{1,0:T(8,128)(2,1)}, u32[]{:S(2)}, u32[]{:S(2)}) collective-permute-start(bf16[64,2048]{1,0:T(8,128)(2,1)S(1)} %add_select_fusion), channel_id=1, source_target_pairs={{0,4},{1,5},{2,6},{3,7},{8,12},{9,13},{10,14},{11,15},{16,20},{17,... | collective-permute-start | bytes 786440 | tf_op jit(solution)/shard_map/ppermute | solution.py:354
  118.2 42.5 %collective-permute-start.8 = (bf16[2048,512]{1,0:T(8,128)(2,1)S(1)}, bf16[2048,512]{1,0:T(8,128)(2,1)}, u32[]{:S(2)}, u32[]{:S(2)}) collective-permute-start(bf16[2048,512]{1,0:T(8,128)(2,1)S(1)} %pad_maximum_fusion), channel_id=1, source_target_pairs={{5,6},{6,7},{21,22},{22,23},{37,38},{38,39},{53,54},{54,55},{69,70... | collective-permute-start | bytes 6291464 | tf_op jit(solution)/shard_map/ppermute | solution.py:408
  129.2 33.7 %copy-start.6 = (bf16[64,2048]{1,0:T(8,128)(2,1)}, bf16[64,2048]{1,0:T(8,128)(2,1)S(1)}, u32[]{:S(2)}) copy-start(bf16[64,2048]{1,0:T(8,128)(2,1)S(1)} %broadcast_select_fusion.refs_6_) | copy-start | bytes 786436
  129.2 20.3 %collective-permute-start.22 = (bf16[64,2048]{1,0:T(8,128)(2,1)S(1)}, bf16[64,2048]{1,0:T(8,128)(2,1)S(1)}, u32[]{:S(2)}, u32[]{:S(2)}) collective-permute-start(bf16[64,2048]{1,0:T(8,128)(2,1)S(1)} %broadcast_select_fusion.refs_6_), channel_id=1, source_target_pairs={{0,48},{1,49},{2,50},{3,51},{4,84},{5,85},{6,86},{7,87},{8,56},{9,... | collective-permute-start | bytes 786440 | tf_op jit(solution)/shard_map/ppermute | solution.py:365
  133.1 17.8 %collective-permute-start.21 = (bf16[64,2048]{1,0:T(8,128)(2,1)S(1)}, bf16[64,2048]{1,0:T(8,128)(2,1)S(1)}, u32[]{:S(2)}, u32[]{:S(2)}) collective-permute-start(bf16[64,2048]{1,0:T(8,128)(2,1)S(1)} %broadcast_select_fusion.refs_6_), channel_id=1, source_target_pairs={{0,32},{1,33},{2,34},{3,35},{4,100},{5,101},{6,102},{7,103},{8,40}... | collective-permute-start | bytes 786440 | tf_op jit(solution)/shard_map/ppermute | solution.py:365
  133.4 22.8 %collective-permute-start.20 = (bf16[64,2048]{1,0:T(8,128)(2,1)S(1)}, bf16[64,2048]{1,0:T(8,128)(2,1)S(1)}, u32[]{:S(2)}, u32[]{:S(2)}) collective-permute-start(bf16[64,2048]{1,0:T(8,128)(2,1)S(1)} %broadcast_select_fusion.refs_6_), channel_id=1, source_target_pairs={{0,16},{1,17},{2,18},{3,19},{4,116},{5,117},{6,118},{7,119},{8,24}... | collective-permute-start | bytes 786440 | tf_op jit(solution)/shard_map/ppermute | solution.py:365
  133.8 15.7 %collective-permute-start.23 = (bf16[32,2048]{1,0:T(8,128)(2,1)S(1)}, bf16[32,2048]{1,0:T(8,128)(2,1)S(1)}, u32[]{:S(2)}, u32[]{:S(2)}) collective-permute-start(bf16[32,2048]{1,0:T(8,128)(2,1)S(1)} %constant_dynamic-slice_fusion), channel_id=1, source_target_pairs={{0,64},{1,65},{2,66},{3,67},{4,68},{5,69},{6,70},{7,71},{8,72},{9,... | collective-permute-start | bytes 393224 | tf_op jit(solution)/shard_map/ppermute | solution.py:361
  149.5 13.4 %copy-start.11 = (bf16[32,2048]{1,0:T(8,128)(2,1)}, bf16[32,2048]{1,0:T(8,128)(2,1)S(1)}, u32[]{:S(2)}) copy-start(bf16[32,2048]{1,0:T(8,128)(2,1)S(1)} %collective-permute-done.23.refs_10_) | copy-start | bytes 393220
  149.5 13.4 %copy-start.7 = (bf16[64,2048]{1,0:T(8,128)(2,1)}, bf16[64,2048]{1,0:T(8,128)(2,1)S(1)}, u32[]{:S(2)}) copy-start(bf16[64,2048]{1,0:T(8,128)(2,1)S(1)} %collective-permute-done.22.refs_9_) | copy-start | bytes 786436
  150.9 12.0 %copy-start.8 = (bf16[64,2048]{1,0:T(8,128)(2,1)}, bf16[64,2048]{1,0:T(8,128)(2,1)S(1)}, u32[]{:S(2)}) copy-start(bf16[64,2048]{1,0:T(8,128)(2,1)S(1)} %collective-permute-done.21.refs_8_) | copy-start | bytes 786436
  156.1 6.8 %copy-start.9 = (bf16[64,2048]{1,0:T(8,128)(2,1)}, bf16[64,2048]{1,0:T(8,128)(2,1)S(1)}, u32[]{:S(2)}) copy-start(bf16[64,2048]{1,0:T(8,128)(2,1)S(1)} %collective-permute-done.20.refs_7_) | copy-start | bytes 786436
  156.2 6.7 %collective-permute-start.24 = (bf16[224,2048]{1,0:T(8,128)(2,1)S(1)}, bf16[224,2048]{1,0:T(8,128)(2,1)}, u32[]{:S(2)}, u32[]{:S(2)}) collective-permute-start(bf16[224,2048]{1,0:T(8,128)(2,1)S(1)} %pad_maximum_fusion.1), channel_id=1, source_target_pairs={{0,4},{1,5},{2,6},{3,7},{4,0},{5,1},{6,2},{7,3},{8,12},{9,13},{10,... | collective-permute-start | bytes 2752520 | tf_op jit(solution)/shard_map/ppermute | solution.py:367
